TPU v7x, 32 devices: a whole 2x2x4 slice. The times are simulated.
32 devices in a mesh: blk: 8 (over z, x), grp: 4 (over y, core).
Axes of the slice: x: 2, y: 2, z: 4, core: 2. Of those that a mesh axis runs over, the one named last changes fastest.
Arguments:
- tokens: bfloat16 [4, 2048, 1024], P(None, ('blk', 'grp')), may hold values from -6 to 6
- segments: int32 [4, 2048], P(None, 'blk'), may hold values from 1 to 11, as said below
- cotangent: bfloat16 [4, 2048, 1024], P(None, ('blk', 'grp')), may hold values from -6 to 6
- norm_gain: bfloat16 [1024], P(('blk', 'grp')), may hold values from 0.5 to 1.5
- entry_weight: bfloat16 [1024, 4096], P(('blk', 'grp')), may hold values from -0.1875 to 0.1875
- kernel_weight: bfloat16 [4, 2048], P(None, ('blk', 'grp')), may hold values from -3 to 3
- kernel_offset: bfloat16 [2048], P(('blk', 'grp')), may hold values from -0.5 to 0.5
- select_weight: bfloat16 [2048, 96], P(('blk', 'grp')), may hold values from -0.125 to 0.125
- delta_weight: bfloat16 [64, 2048], P(None, ('blk', 'grp')), may hold values from -0.75 to 0.75
- timestep_bias: bfloat16 [2048], P(('blk', 'grp')), may hold values from -9 to -2
- decay_log: bfloat16 [16, 2048], P(None, ('blk', 'grp')), may hold values from -1.5 to 1.5
- skip_gain: bfloat16 [2048], P(('blk', 'grp')), may hold values from 0.5 to 1.5
- exit_weight: bfloat16 [2048, 1024], P(('blk', 'grp')), may hold values from -0.375 to 0.375
Outputs:
- block_out: bfloat16 [4, 2048, 1024], P(None, ('blk', 'grp'))
- input_grad: bfloat16 [4, 2048, 1024], P(None, ('blk', 'grp'))
- gain_grad: float32 [1024], P(('blk', 'grp'))
- entry_grad: float32 [1024, 4096], P(('blk', 'grp'))
- kernel_grad: float32 [4, 2048], P(None, ('blk', 'grp'))
- offset_grad: float32 [2048], P(('blk', 'grp'))
- select_grad: float32 [2048, 96], P(('blk', 'grp'))
- delta_grad: float32 [64, 2048], P(None, ('blk', 'grp'))
- timestep_grad: float32 [2048], P(('blk', 'grp'))
- decay_grad: float32 [16, 2048], P(None, ('blk', 'grp'))
- skip_grad: float32 [2048], P(('blk', 'grp'))
- exit_grad: float32 [2048, 1024], P(('blk', 'grp'))
Inputs may be any that keep to these rules, and one draw needn't show every extreme that they name: `segments`: along each sequence the numbers never fall; a run of equal numbers is one document of 200 to 2000 tokens, save the last of a sequence, which may be shorter; the first document of a sequence has number 1 and, where there are two or more, the last has 11; in one sequence, drawn from the seed, all tokens form one document.
All inputs are finite; a program needn't handle non-finite values.
Results may differ from a plain program's by a relative error of at most 0.012.
Values may be sent and summed in bfloat16 or wider, within the bound.
No kernel may reach another device: no remote copies, remote signals or barrier semaphores. Data moves between devices by JAX's collectives and lax.ppermute only.
A program may use at most 192 MiB of HBM per device.

v0:
```python
from functools import partial

import jax
import jax.numpy as jnp
from jax import lax
from jax.sharding import PartitionSpec as P

epsilon = 1e-05
block_steps = 16
highest = lax.Precision.HIGHEST


def passed_along(block, axis, distance):
    devices = range(lax.axis_size(axis))
    route = [(i - distance, i) for i in devices if i - distance in devices]
    return lax.ppermute(block, axis, route)


def prefix(value, axis, combine, identity, reverse):
    count, index = (lax.axis_size(axis), lax.axis_index(axis))
    everything = jax.tree.map(lambda part: lax.all_gather(part, axis), value)
    start = jax.tree.map(
        lambda part, zero: jnp.broadcast_to(jnp.asarray(zero, part.dtype), part.shape),
        value,
        identity,
    )

    def lap(k, before):
        at = count - 1 - k if reverse else k
        reached = at > index if reverse else at < index
        new = combine(before, jax.tree.map(lambda part: part[at], everything))
        return jax.tree.map(lambda a, b: jnp.where(reached, a, b), new, before)

    return lax.fori_loop(0, count, lap, start)


def silu_value(values):
    return values * jax.nn.sigmoid(values)


def silu_slope(values):
    sigmoids = jax.nn.sigmoid(values)
    return sigmoids * (1.0 + values * (1.0 - sigmoids))


def step_terms(step_blocks, filter_blocks, write_blocks, reset_blocks, rate_matrix, position):
    step_now = step_blocks[:, :, position]
    decays = (
        jnp.exp(step_now[:, :, None, :] * rate_matrix)
        * (1.0 - reset_blocks[:, :, position])[:, :, None, None]
    )
    drives = (step_now * filter_blocks[:, :, position])[:, :, None, :] * write_blocks[
        :, :, position
    ][:, :, :, None]
    return (decays, drives)


def combine_pairs(earlier, following):
    return (earlier[0] * following[0], following[0] * earlier[1] + following[1])


def chain_forward(totals, block_ends, incoming):
    starts = []
    running = incoming
    for block_index in range(totals.shape[1]):
        starts.append(running)
        running = totals[:, block_index] * running + block_ends[:, block_index]
    return (jnp.stack(starts, axis=1), running)


def chain_backward(totals, block_gives, incoming):
    arrivals = []
    running = incoming
    for block_index in reversed(range(totals.shape[1])):
        arrivals.append(running)
        running = block_gives[:, block_index] + totals[:, block_index] * running
    return (jnp.stack(arrivals[::-1], axis=1), running)


def local(
    tokens,
    segments,
    cotangent,
    norm_gain,
    entry_weight,
    kernel_weight,
    kernel_offset,
    select_weight,
    delta_weight,
    timestep_bias,
    decay_log,
    skip_gain,
    exit_weight,
):
    fetched = (
        lax.all_gather(norm_gain, ("blk", "grp"), axis=0, tiled=True),
        lax.all_gather(entry_weight, ("blk", "grp"), axis=0, tiled=True),
        lax.all_gather(kernel_weight, ("blk", "grp"), axis=1, tiled=True),
        lax.all_gather(kernel_offset, ("blk", "grp"), axis=0, tiled=True),
        lax.all_gather(select_weight, ("blk", "grp"), axis=0, tiled=True),
        lax.all_gather(delta_weight, ("blk", "grp"), axis=1, tiled=True),
        lax.all_gather(timestep_bias, ("blk", "grp"), axis=0, tiled=True),
        lax.all_gather(decay_log, ("blk", "grp"), axis=1, tiled=True),
        lax.all_gather(skip_gain, ("blk", "grp"), axis=0, tiled=True),
        lax.all_gather(exit_weight, ("blk", "grp"), axis=0, tiled=True),
    )
    (
        gain_full,
        entry_full,
        kernel_full,
        offset_full,
        select_full,
        delta_full,
        bias_full,
        decay_full,
        skip_full,
        exit_full,
    ) = fetched
    sequences, piece_tokens, model_width = tokens.shape
    inner_width = exit_full.shape[0]
    groups = lax.axis_size("grp")
    group_width = inner_width // groups
    first_channel = lax.axis_index("grp") * group_width
    local_tokens = piece_tokens * groups
    rim_rows = kernel_full.shape[0] - 1
    rank_width = delta_full.shape[0]
    state_width = decay_full.shape[0]
    block_count = local_tokens // block_steps
    row_count = sequences * piece_tokens
    lane_count = sequences * local_tokens

    def group_part(values, axis):
        return lax.dynamic_slice_in_dim(values, first_channel, group_width, axis)

    kernel_group = group_part(kernel_full, 1).astype(jnp.float32)
    offset_group = group_part(offset_full, 0).astype(jnp.float32)
    select_group = group_part(select_full, 0)
    delta_group = group_part(delta_full, 1).astype(jnp.float32)
    bias_group = group_part(bias_full, 0).astype(jnp.float32)
    rate_matrix = -jnp.exp(group_part(decay_full, 1).astype(jnp.float32))
    skip_group = group_part(skip_full, 0).astype(jnp.float32)
    gain_values = gain_full.astype(jnp.float32)
    residual = tokens.astype(jnp.float32).reshape(row_count, model_width)
    root_scale = lax.rsqrt(jnp.mean(residual * residual, axis=1, keepdims=True) + epsilon)
    scaled = residual * root_scale
    normed = (scaled * gain_values).astype(jnp.bfloat16)
    projected = jnp.dot(normed, entry_full, preferred_element_type=jnp.float32)
    inner_part = (
        projected[:, :inner_width]
        .astype(jnp.bfloat16)
        .reshape(sequences, piece_tokens, inner_width)
    )
    gating = projected[:, inner_width:]
    channels = lax.all_to_all(inner_part, "grp", split_axis=2, concat_axis=1, tiled=True)
    tail_values = passed_along(channels[:, local_tokens - rim_rows :], "blk", 1)
    tail_labels = passed_along(segments[:, local_tokens - rim_rows :], "blk", 1)
    extended = jnp.concatenate([tail_values, channels], axis=1)
    labels = jnp.concatenate([tail_labels, segments], axis=1)
    same_document = [
        (labels[:, k : k + local_tokens] == segments).astype(jnp.float32)[:, :, None]
        for k in range(rim_rows + 1)
    ]
    kernel_sum = offset_group + jnp.zeros((sequences, local_tokens, group_width), jnp.float32)
    for k in range(rim_rows + 1):
        kernel_sum = (
            kernel_sum
            + kernel_group[k]
            * extended[:, k : k + local_tokens].astype(jnp.float32)
            * same_document[k]
        )
    filtered = silu_value(kernel_sum).astype(jnp.bfloat16)
    resets = (segments != labels[:, rim_rows - 1 : rim_rows - 1 + local_tokens]).astype(jnp.float32)
    flat_filtered = filtered.reshape(lane_count, group_width)
    filtered_values = flat_filtered.astype(jnp.float32)
    selected = lax.psum(
        jnp.dot(flat_filtered, select_group, preferred_element_type=jnp.float32), "grp"
    )
    low_rank = selected[:, :rank_width]
    write_gate = selected[:, rank_width : rank_width + state_width]
    read_gate = selected[:, rank_width + state_width :]
    delta_pre = jnp.dot(low_rank, delta_group, precision=highest) + bias_group
    steps_dt = jax.nn.softplus(delta_pre)

    def blocks_of(values):
        return values.reshape((sequences, block_count, block_steps) + values.shape[1:])

    step_blocks = blocks_of(steps_dt)
    filter_blocks = blocks_of(filtered_values)
    write_blocks = blocks_of(write_gate)
    read_blocks = blocks_of(read_gate)
    reset_blocks = resets.reshape(sequences, block_count, block_steps)
    make_terms = partial(
        step_terms, step_blocks, filter_blocks, write_blocks, reset_blocks, rate_matrix
    )
    state_shape = (sequences, block_count, state_width, group_width)
    totals = jnp.ones(state_shape, jnp.float32)
    block_ends = jnp.zeros(state_shape, jnp.float32)
    for position in range(block_steps):
        decays, drives = make_terms(position)
        block_ends = decays * block_ends + drives
        totals = totals * decays
    device_total = jnp.prod(totals, axis=1)
    zero_state = jnp.zeros((sequences, state_width, group_width), jnp.float32)
    one_state = jnp.ones_like(zero_state)
    unused_starts, device_end = chain_forward(totals, block_ends, zero_state)
    carried = prefix(
        (device_total, device_end), "blk", combine_pairs, (one_state, zero_state), False
    )
    starts, unused_end = chain_forward(totals, block_ends, carried[1])
    hidden = starts
    emitted = []
    for position in range(block_steps):
        decays, drives = make_terms(position)
        hidden = decays * hidden + drives
        emitted.append(jnp.sum(hidden * read_blocks[:, :, position][:, :, :, None], axis=2))
    scan_sum = jnp.stack(emitted, axis=2).reshape(lane_count, group_width)
    scan_out = (scan_sum + skip_group * filtered_values).astype(jnp.bfloat16)
    returned = lax.all_to_all(
        scan_out.reshape(sequences, local_tokens, group_width),
        "grp",
        split_axis=1,
        concat_axis=2,
        tiled=True,
    )
    scan_tokens = returned.reshape(row_count, inner_width).astype(jnp.float32)
    gate_value = silu_value(gating)
    gated = (scan_tokens * gate_value).astype(jnp.bfloat16)
    block_out = (
        (residual + jnp.dot(gated, exit_full, preferred_element_type=jnp.float32))
        .astype(jnp.bfloat16)
        .reshape(sequences, piece_tokens, model_width)
    )
    entry_back, exit_back = (
        lax.all_gather(entry_weight, ("blk", "grp"), axis=0, tiled=True),
        lax.all_gather(exit_weight, ("blk", "grp"), axis=0, tiled=True),
    )
    cotangent_rows = cotangent.reshape(row_count, model_width)
    grad_gated = lax.dot_general(
        cotangent_rows, exit_back, (((1,), (1,)), ((), ())), preferred_element_type=jnp.float32
    )
    grad_scan = (grad_gated * gate_value).astype(jnp.bfloat16)
    grad_gating = (grad_gated * scan_tokens * silu_slope(gating)).astype(jnp.bfloat16)
    grad_channels = lax.all_to_all(
        grad_scan.reshape(sequences, piece_tokens, inner_width),
        "grp",
        split_axis=2,
        concat_axis=1,
        tiled=True,
    )
    grad_flat = grad_channels.reshape(lane_count, group_width).astype(jnp.float32)
    grad_blocks = blocks_of(grad_flat)
    skip_grad_group = jnp.sum(grad_flat * filtered_values, axis=0)
    passed_back = jnp.zeros(state_shape, jnp.float32)
    for position in reversed(range(block_steps)):
        decays, drives = make_terms(position)
        adjoint = (
            read_blocks[:, :, position][:, :, :, None] * grad_blocks[:, :, position][:, :, None, :]
            + passed_back
        )
        passed_back = decays * adjoint
    block_gives = passed_back
    unused_arrivals, device_give = chain_backward(totals, block_gives, zero_state)
    carried_back = prefix(
        (device_total, device_give), "blk", combine_pairs, (one_state, zero_state), True
    )
    arrivals, unused_give = chain_backward(totals, block_gives, carried_back[1])
    hidden = starts
    saved_states = []
    read_grads = []
    for position in range(block_steps):
        decays, drives = make_terms(position)
        hidden = decays * hidden + drives
        saved_states.append(hidden)
        read_grads.append(jnp.sum(hidden * grad_blocks[:, :, position][:, :, None, :], axis=3))
    passed_back = arrivals
    rate_grad = jnp.zeros((state_width, group_width), jnp.float32)
    step_grads = [None] * block_steps
    filter_grads = [None] * block_steps
    write_grads = [None] * block_steps
    for position in reversed(range(block_steps)):
        decays, drives = make_terms(position)
        adjoint = (
            read_blocks[:, :, position][:, :, :, None] * grad_blocks[:, :, position][:, :, None, :]
            + passed_back
        )
        previous = saved_states[position - 1] if position > 0 else starts
        grad_rate = adjoint * previous * decays
        step_now = step_blocks[:, :, position]
        filter_now = filter_blocks[:, :, position]
        write_now = write_blocks[:, :, position]
        weighted = jnp.sum(adjoint * write_now[:, :, :, None], axis=2)
        step_grads[position] = jnp.sum(grad_rate * rate_matrix, axis=2) + weighted * filter_now
        filter_grads[position] = weighted * step_now
        write_grads[position] = jnp.sum(adjoint * (step_now * filter_now)[:, :, None, :], axis=3)
        rate_grad = rate_grad + jnp.sum(grad_rate * step_now[:, :, None, :], axis=(0, 1))
        passed_back = decays * adjoint

    def rows_of(pieces):
        return jnp.stack(pieces, axis=2).reshape(lane_count, -1)

    grad_steps = rows_of(step_grads)
    grad_from_scan = rows_of(filter_grads)
    grad_write = rows_of(write_grads)
    grad_read = rows_of(read_grads)
    decay_grad_group = rate_grad * rate_matrix
    grad_delta = grad_steps * jax.nn.sigmoid(delta_pre)
    bias_grad_group = jnp.sum(grad_delta, axis=0)
    delta_grad_group = lax.dot_general(
        low_rank, grad_delta, (((0,), (0,)), ((), ())), precision=highest
    )
    grad_rank = lax.dot_general(
        grad_delta, delta_group, (((1,), (1,)), ((), ())), precision=highest
    )
    grad_selected = lax.psum(
        jnp.concatenate([grad_rank, grad_write, grad_read], axis=1), "grp"
    ).astype(jnp.bfloat16)
    select_grad_group = lax.dot_general(
        flat_filtered, grad_selected, (((0,), (0,)), ((), ())), preferred_element_type=jnp.float32
    )
    grad_filter = (
        grad_from_scan
        + grad_flat * skip_group
        + lax.dot_general(
            grad_selected,
            select_group,
            (((1,), (1,)), ((), ())),
            preferred_element_type=jnp.float32,
        )
    )
    grad_kernel_sum = grad_filter.reshape(sequences, local_tokens, group_width) * silu_slope(
        kernel_sum
    )
    offset_grad_group = jnp.sum(grad_kernel_sum, axis=(0, 1))
    kernel_rows = []
    grad_extended = jnp.zeros((sequences, local_tokens + rim_rows, group_width), jnp.float32)
    for k in range(rim_rows + 1):
        masked = grad_kernel_sum * same_document[k]
        kernel_rows.append(
            jnp.sum(masked * extended[:, k : k + local_tokens].astype(jnp.float32), axis=(0, 1))
        )
        grad_extended = grad_extended + jnp.pad(
            masked * kernel_group[k], ((0, 0), (k, rim_rows - k), (0, 0))
        )
    kernel_grad_group = jnp.stack(kernel_rows, axis=0)
    spilled = passed_along(grad_extended[:, :rim_rows], "blk", -1)
    grad_inner = (
        grad_extended[:, rim_rows:]
        + jnp.pad(spilled, ((0, 0), (local_tokens - rim_rows, 0), (0, 0)))
    ).astype(jnp.bfloat16)
    grad_tokens = lax.all_to_all(grad_inner, "grp", split_axis=1, concat_axis=2, tiled=True)
    grad_projected = jnp.concatenate(
        [grad_tokens.reshape(row_count, inner_width), grad_gating], axis=1
    )
    grad_normed = lax.dot_general(
        grad_projected, entry_back, (((1,), (1,)), ((), ())), preferred_element_type=jnp.float32
    )
    gain_grad = jnp.sum(grad_normed * scaled, axis=0)
    grad_hat = grad_normed * gain_values
    grad_input = root_scale * (
        grad_hat - scaled * jnp.mean(grad_hat * scaled, axis=1, keepdims=True)
    )
    input_grad = (
        (cotangent_rows.astype(jnp.float32) + grad_input)
        .astype(jnp.bfloat16)
        .reshape(sequences, piece_tokens, model_width)
    )
    exit_grad = lax.dot_general(
        gated, cotangent_rows, (((0,), (0,)), ((), ())), preferred_element_type=jnp.float32
    )
    entry_grad = lax.dot_general(
        normed, grad_projected, (((0,), (0,)), ((), ())), preferred_element_type=jnp.float32
    )

    def full_channels(values, axis):
        full_shape = list(values.shape)
        full_shape[axis] = inner_width
        return lax.dynamic_update_slice_in_dim(
            jnp.zeros(full_shape, jnp.float32), values, first_channel, axis
        )

    reduced = (
        lax.psum_scatter(gain_grad, ("blk", "grp"), scatter_dimension=0, tiled=True),
        lax.psum_scatter(entry_grad, ("blk", "grp"), scatter_dimension=0, tiled=True),
        lax.psum_scatter(
            full_channels(kernel_grad_group, 1), ("blk", "grp"), scatter_dimension=1, tiled=True
        ),
        lax.psum_scatter(
            full_channels(offset_grad_group, 0), ("blk", "grp"), scatter_dimension=0, tiled=True
        ),
        lax.psum_scatter(
            full_channels(select_grad_group, 0), ("blk", "grp"), scatter_dimension=0, tiled=True
        ),
        lax.psum_scatter(
            full_channels(delta_grad_group, 1), ("blk", "grp"), scatter_dimension=1, tiled=True
        ),
        lax.psum_scatter(
            full_channels(bias_grad_group, 0), ("blk", "grp"), scatter_dimension=0, tiled=True
        ),
        lax.psum_scatter(
            full_channels(decay_grad_group, 1), ("blk", "grp"), scatter_dimension=1, tiled=True
        ),
        lax.psum_scatter(
            full_channels(skip_grad_group, 0), ("blk", "grp"), scatter_dimension=0, tiled=True
        ),
        lax.psum_scatter(exit_grad, ("blk", "grp"), scatter_dimension=0, tiled=True),
    )
    return (
        block_out,
        input_grad,
        reduced[0],
        reduced[1],
        reduced[2],
        reduced[3],
        reduced[4],
        reduced[5],
        reduced[6],
        reduced[7],
        reduced[8],
        reduced[9],
    )


def solution(mesh):
    placed = (
        P(None, ("blk", "grp"), None),
        P(None, "blk"),
        P(None, ("blk", "grp"), None),
        P(("blk", "grp")),
        P(("blk", "grp"), None),
        P(None, ("blk", "grp")),
        P(("blk", "grp")),
        P(("blk", "grp"), None),
        P(None, ("blk", "grp")),
        P(("blk", "grp")),
        P(None, ("blk", "grp")),
        P(("blk", "grp")),
        P(("blk", "grp"), None),
    )
    return jax.shard_map(
        local,
        mesh=mesh,
        in_specs=placed,
        out_specs=(
            P(None, ("blk", "grp"), None),
            P(None, ("blk", "grp"), None),
            P(("blk", "grp")),
            P(("blk", "grp"), None),
            P(None, ("blk", "grp")),
            P(("blk", "grp")),
            P(("blk", "grp"), None),
            P(None, ("blk", "grp")),
            P(("blk", "grp")),
            P(None, ("blk", "grp")),
            P(("blk", "grp")),
            P(("blk", "grp"), None),
        ),
        check_vma=False,
    )
```

profile of v0, /device:TPU:0, one launch (start us, length us, event | category | flops | bytes accessed | tf_op | source)
XLA Modules:
  0.0 1578.4 jit_solution(5317269750106006082)
XLA Ops:
  9.4 4.8 collective-permute-start.1
  19.0 41.2 %all-reduce.14 = (bf16[1024]{0:T(1024)(128)(2,1)S(1)}, bf16[2048]{0:T(1024)(128)(2,1)S(1)}, bf16[2048]{0:T(1024)(128)(2,1)S(1)}, bf16[2048]{0:T(1024)(128)(2,1)S(1)}) all-reduce(bf16[1024]{0:T(1024)(128)(2,1)S(1)} %dynamic-update-slice.1, bf16[2048]{0:T(1024)(128)(2,1)S(1)} %dynamic-update-slice, ...), channel_id=1, replica_groups=mesh['blk'=8,'grp'=4] {'blk','grp'}, use_global_device_ids=true, to_apply=%add.6 | all-reduce | flops 7168 | bytes 28672
  61.0 40.9 %all-gather.1 = bf16[32,64,4]{1,2,0:T(4,128)(2,1)S(1)} all-gather(bf16[1,64,4]{1,2,0:T(4,128)(2,1)} %bitcast.1328), channel_id=1, replica_groups=mesh['blk'=8,'grp'=4] {'blk','grp'}, dimensions={0}, use_global_device_ids=true | all-gather | bytes 16896 | tf_op jit(solution)/shard_map/all_gather | solution.py:98
  102.1 37.5 %all-gather.2 = bf16[32,64,16]{1,2,0:T(8,128)(2,1)S(1)} all-gather(bf16[1,64,16]{1,2,0:T(8,128)(2,1)} %bitcast.1327), channel_id=1, replica_groups=mesh['blk'=8,'grp'=4] {'blk','grp'}, dimensions={0}, use_global_device_ids=true | all-gather | bytes 67584 | tf_op jit(solution)/shard_map/all_gather | solution.py:103
  139.9 42.1 %all_gather.53 = bf16[64,2048]{0,1:T(8,128)(2,1)} all-gather(bf16[64,64]{0,1:T(8,128)(2,1)S(1)} %copy.477), channel_id=1, replica_groups=mesh['blk'=8,'grp'=4] {'blk','grp'}, dimensions={1}, use_global_device_ids=true | all-gather | bytes 270336 | tf_op jit(solution)/shard_map/all_gather | solution.py:101
  182.1 41.0 %all_gather.52 = bf16[2048,96]{1,0:T(8,128)(2,1)} all-gather(bf16[64,96]{1,0:T(8,128)(2,1)S(1)} %copy-done.270), channel_id=1, replica_groups=mesh['blk'=8,'grp'=4] {'blk','grp'}, dimensions={0}, use_global_device_ids=true | all-gather | bytes 405504 | tf_op jit(solution)/shard_map/all_gather | solution.py:100
  223.3 5.9 fusion.141
  235.3 3.6 all-to-all-start
  239.6 5.9 multiply_convert_fusion.1
  253.4 4.2 all-to-all-start.2
  275.4 4.3 reshape.1034
  301.1 28.4 %all-reduce.18.cloned.1.call-done = f32[1024,96]{0,1:T(8,128)} async-done(((f32[1024,96]{0,1:T(8,128)}), f32[1024,96]{0,1:T(8,128)}) %all-reduce.18.cloned.1.call-update) | async-done | bytes 393232 | tf_op jit(solution)/shard_map/psum | solution.py:175
  330.8 4.4 compare_select_fusion
  345.6 7.6 fusion.132
  353.3 8.8 all-gather.15.cloned.1.call-start
  362.1 5.3 fusion.137
  400.4 5.2 fusion.138
  458.5 11.6 fusion.28
  472.6 10.7 multiply_add_fusion.32
  486.4 26.5 %all-gather.15.cloned.1.call-done = f32[8,4,16,512]{3,2,1,0:T(8,128)} async-done(((f32[1,4,16,512]{3,2,1,0:T(8,128)}), f32[8,4,16,512]{3,2,1,0:T(8,128)}) %all-gather.15.cloned.1.call-update) | async-done | bytes 1048592 | tf_op jit(solution)/shard_map/all_gather | solution.py:21
  512.9 8.8 while.31
  537.9 16.7 %all-gather.11.cloned.1.call-done = f32[8,4,16,512]{3,2,1,0:T(8,128)} async-done(((f32[1,4,16,512]{3,2,1,0:T(8,128)}), f32[8,4,16,512]{3,2,1,0:T(8,128)}) %all-gather.11.cloned.1.call-update) | async-done | bytes 1048592 | tf_op jit(solution)/shard_map/all_gather | solution.py:21
  554.6 8.8 while.30
  583.4 9.7 multiply_add_fusion.35
  593.2 9.1 multiply_reduce_fusion.16
  602.5 9.6 multiply_reduce_fusion.13
  612.2 8.6 multiply_reduce_fusion.11
  620.8 8.5 multiply_reduce_fusion.9
  629.3 8.7 multiply_reduce_fusion.7
  638.0 8.5 multiply_reduce_fusion.5
  646.5 8.6 multiply_reduce_fusion.3
  655.1 8.2 multiply_reduce_fusion.1
  683.3 14.8 all-reduce.19
  732.0 4.3 all-to-all-start.1
  739.1 12.9 all-to-all-done.1
  759.7 4.5 fusion.142
  769.3 3.4 collective-permute-done.2
  773.8 18.0 %all_to_all.51 = bf16[4,256,512]{2,0,1:T(4,128)(2,1)S(1)} all-to-all(bf16[4,256,512]{2,0,1:T(4,128)(2,1)S(1)} %copy.665), channel_id=1, replica_groups=mesh['blk'=8,'grp'=4] {'grp'}, dimensions={1} | all-to-all | bytes 2097152 | tf_op jit(solution)/shard_map/all_to_all | solution.py:350
  794.1 8.1 fusion.50
  805.0 37.3 %reduce-scatter.19.cloned.1.call-done = f32[64,4]{1,0:T(8,128)} async-done(((f32[2048,4]{1,0:T(8,128)}), f32[64,4]{1,0:T(8,128)}) %reduce-scatter.19.cloned.1.call-update) | async-done | bytes 1040
  843.7 131.5 %reduce-scatter.23.cloned.1.call-done = f32[64,16]{1,0:T(8,128)} async-done(((f32[2048,16]{1,0:T(8,128)}), f32[64,16]{1,0:T(8,128)}) %reduce-scatter.23.cloned.1.call-update) | async-done | bytes 4112
  976.7 4.5 fusion.52
  981.3 6.0 multiply_reduce_fusion.96
  987.3 37.6 %all-reduce.13 = (f32[1024]{0:T(1024)S(1)}, f32[2048]{0:T(1024)S(1)}, f32[2048]{0:T(1024)S(1)}, f32[2048]{0:T(1024)S(1)}) all-reduce(f32[1024]{0:T(1024)S(1)} %get-tuple-element.397, f32[2048]{0:T(1024)S(1)} %dynamic_update_slice.22, f32[2048]{0:T(1024)S(1)} %dynamic_update_slice.25, ...), channel_id=3, replica_groups=mesh['blk'=8,'grp'=4] {'blk','grp'}, use_global_device_ids=true, to_apply=%region_90.91.clone | all-reduce | flops 7168 | bytes 57344
  1028.3 80.3 %reduce-scatter.21.cloned.1.call-done = f32[64,64]{1,0:T(8,128)} async-done(((f32[2048,64]{1,0:T(8,128)}), f32[64,64]{1,0:T(8,128)}) %reduce-scatter.21.cloned.1.call-update) | async-done | bytes 16400
  1110.1 131.9 %reduce-scatter.15.cloned.1.call-done = f32[64,96]{1,0:T(8,128)} async-done(((f32[2048,96]{1,0:T(8,128)}), f32[64,96]{1,0:T(8,128)}) %reduce-scatter.15.cloned.1.call-update) | async-done | bytes 24592 | tf_op jit(solution)/shard_map/reduce_scatter | solution.py:390
  1242.0 147.6 %reduce-scatter.17.cloned.1.call-done = f32[64,1024]{1,0:T(8,128)} async-done(((f32[2048,1024]{1,0:T(8,128)}), f32[64,1024]{1,0:T(8,128)}) %reduce-scatter.17.cloned.1.call-update) | async-done | bytes 262160 | tf_op jit(solution)/shard_map/reduce_scatter | solution.py:405
  1389.6 181.8 %reduce-scatter.13.cloned.1.call-done = f32[32,4096]{1,0:T(8,128)} async-done(((f32[1024,4096]{1,0:T(8,128)}), f32[32,4096]{1,0:T(8,128)}) %reduce-scatter.13.cloned.1.call-update) | async-done | bytes 524304 | tf_op jit(solution)/shard_map/reduce_scatter | solution.py:383
  (910 shorter events, 298.6 us)
Async XLA Ops:
  7.2 215.9 %copy-start.13 = (bf16[4,64,1024]{2,1,0:T(8,128)(2,1)S(1)}, bf16[4,64,1024]{2,1,0:T(8,128)(2,1)}, u32[]{:S(2)}) copy-start(bf16[4,64,1024]{2,1,0:T(8,128)(2,1)} %param.17) | copy-start | bytes 1572868
  7.2 174.9 %copy-start.270 = (bf16[64,96]{1,0:T(8,128)(2,1)S(1)}, bf16[64,96]{1,0:T(8,128)(2,1)}, u32[]{:S(2)}) copy-start(bf16[64,96]{1,0:T(8,128)(2,1)} %param.24) | copy-start | bytes 36868
  7.2 216.1 %all-gather.9.cloned.1.call-start = ((), (), s32[]{:S(2)}) async-start(), calls=%async_computation.10 | async-start | bytes 8650752 | tf_op jit(solution)/shard_map/all_gather | solution.py:97
  7.9 231.7 %all-gather.13.cloned.1.call-start = ((), (), s32[]{:S(2)}) async-start(), calls=%async_computation.13 | async-start | bytes 4325376 | tf_op jit(solution)/shard_map/all_gather | solution.py:105
  9.4 248.4 %collective-permute-start.1 = (s32[4,3]{1,0:T(4,128)S(1)}, s32[4,3]{1,0:T(4,128)S(1)}, u32[]{:S(2)}, u32[]{:S(2)}) collective-permute-start(s32[4,3]{1,0:T(4,128)S(1)} %slice.331), channel_id=1, source_target_pairs={{0,4},{4,8},{8,12},{12,16},{16,20},{20,24},{24,28},{1,5},{5,9},{9,... | collective-permute-start | bytes 152 | tf_op jit(solution)/shard_map/ppermute | solution.py:16
  15.6 213.5 %copy-start.271 = (f32[256]{0:T(256)}, f32[256]{0:T(256)S(1)}, u32[]{:S(2)}) copy-start(f32[256]{0:T(256)S(1)} %rsqrt.12) | copy-start | bytes 3076
  60.2 169.0 %copy-start.259 = (f32[1024]{0:T(1024)}, f32[1024]{0:T(1024)S(1)}, u32[]{:S(2)}) copy-start(f32[1024]{0:T(1024)S(1)} %convert_element_type.149) | copy-start | bytes 12292
  139.8 42.2 %copy-start.229 = (bf16[2048,16]{0,1:T(8,128)(2,1)}, bf16[2048,16]{0,1:T(8,128)(2,1)S(1)}, u32[]{:S(2)}) copy-start(bf16[2048,16]{0,1:T(8,128)(2,1)S(1)} %reshape.1023) | copy-start | bytes 196612
  139.9 190.9 %copy-start.274 = (f32[512]{0:T(512)}, f32[512]{0:T(512)S(1)}, u32[]{:S(2)}) copy-start(f32[512]{0:T(512)S(1)} %dynamic-slice_convert_fusion.1) | copy-start | bytes 6148
  235.3 18.1 %all-to-all-start = ((bf16[4,2,65536]{2,1,0:T(2,128)(2,1)}), bf16[4,2,65536]{2,1,0:T(2,128)(2,1)S(1)}, u32[]{:S(2)}, u32[]{:S(2)}) async-start(bf16[4,2,65536]{2,1,0:T(2,128)(2,1)} %reshape.1031), calls=%async_computation | async-start | bytes 2097152 | tf_op jit(solution)/shard_map/all_to_all | solution.py:154
  253.4 22.0 %all-to-all-start.2 = ((bf16[4,2,65536]{2,1,0:T(2,128)(2,1)}), bf16[4,2,65536]{2,1,0:T(2,128)(2,1)}, u32[]{:S(2)}, u32[]{:S(2)}) async-start(bf16[4,2,65536]{2,1,0:T(2,128)(2,1)} %reshape.1033), calls=%async_computation.2 | async-start | bytes 2097152 | tf_op jit(solution)/shard_map/all_to_all | solution.py:243
  257.6 71.8 %all-reduce.18.cloned.1.call-start = ((), (), s32[]{:S(2)}) async-start(), calls=%async_computation.11 | async-start | bytes 786432 | tf_op jit(solution)/shard_map/psum | solution.py:175
  257.8 34.2 %copy-start.262 = (f32[1,512]{1,0:T(1,128)}, f32[1,512]{1,0:T(1,128)S(1)}, u32[]{:S(2)}) copy-start(f32[1,512]{1,0:T(1,128)S(1)} %get-tuple-element.640) | copy-start | bytes 6148
  257.8 34.2 %copy-start.264 = (f32[1,512]{1,0:T(1,128)}, f32[1,512]{1,0:T(1,128)S(1)}, u32[]{:S(2)}) copy-start(f32[1,512]{1,0:T(1,128)S(1)} %get-tuple-element.641) | copy-start | bytes 6148
  257.8 34.2 %copy-start.266 = (f32[1,512]{1,0:T(1,128)}, f32[1,512]{1,0:T(1,128)S(1)}, u32[]{:S(2)}) copy-start(f32[1,512]{1,0:T(1,128)S(1)} %get-tuple-element.642) | copy-start | bytes 6148
  257.8 34.2 %copy-start.268 = (f32[1,512]{1,0:T(1,128)}, f32[1,512]{1,0:T(1,128)S(1)}, u32[]{:S(2)}) copy-start(f32[1,512]{1,0:T(1,128)S(1)} %get-tuple-element.643) | copy-start | bytes 6148
  257.9 34.1 %copy-start.253 = (f32[4,256]{1,0:T(4,128)}, f32[4,256]{1,0:T(4,128)S(1)}, u32[]{:S(2)}) copy-start(f32[4,256]{1,0:T(4,128)S(1)} %get-tuple-element.645) | copy-start | bytes 12292
  257.9 34.1 %copy-start.255 = (f32[4,256]{1,0:T(4,128)}, f32[4,256]{1,0:T(4,128)S(1)}, u32[]{:S(2)}) copy-start(f32[4,256]{1,0:T(4,128)S(1)} %get-tuple-element.646) | copy-start | bytes 12292
  257.9 34.1 %copy-start.257 = (f32[4,256]{1,0:T(4,128)}, f32[4,256]{1,0:T(4,128)S(1)}, u32[]{:S(2)}) copy-start(f32[4,256]{1,0:T(4,128)S(1)} %get-tuple-element.647) | copy-start | bytes 12292
  273.8 18.2 %collective-permute-start = (bf16[4,3,512]{2,1,0:T(4,128)(2,1)S(1)}, bf16[4,3,512]{2,1,0:T(4,128)(2,1)S(1)}, u32[]{:S(2)}, u32[]{:S(2)}) collective-permute-start(bf16[4,3,512]{2,1,0:T(4,128)(2,1)S(1)} %slice.492), channel_id=1, source_target_pairs={{0,4},{4,8},{8,12},{12,16},{16,20},{20,24},{24,28},{1,5},{5,9},{9,... | collective-permute-start | bytes 36872 | tf_op jit(solution)/shard_map/ppermute | solution.py:16
  298.1 188.2 %all-gather.17.cloned.1.call-start = ((), (), s32[]{:S(2)}) async-start(), calls=%async_computation.18 | async-start | bytes 1179648 | tf_op jit(solution)/shard_map/all_gather | solution.py:21
  301.0 35.9 %copy-start.94 = (f32[4,16,1,512]{3,2,1,0:T(1,128)}, f32[4,16,1,512]{3,2,1,0:T(1,128)S(1)}, u32[]{:S(2)}) copy-start(f32[4,16,1,512]{3,2,1,0:T(1,128)S(1)} %get-tuple-element.509) | copy-start | bytes 393220
  301.0 35.9 %copy-start.96 = (f32[4,16,1,512]{3,2,1,0:T(1,128)}, f32[4,16,1,512]{3,2,1,0:T(1,128)S(1)}, u32[]{:S(2)}) copy-start(f32[4,16,1,512]{3,2,1,0:T(1,128)S(1)} %get-tuple-element.494) | copy-start | bytes 393220
  301.0 36.9 %copy-start.98 = (f32[4,16,1,512]{3,2,1,0:T(1,128)}, f32[4,16,1,512]{3,2,1,0:T(1,128)S(1)}, u32[]{:S(2)}) copy-start(f32[4,16,1,512]{3,2,1,0:T(1,128)S(1)} %get-tuple-element.495) | copy-start | bytes 393220
  301.0 38.0 %copy-start.100 = (f32[4,16,1,512]{3,2,1,0:T(1,128)}, f32[4,16,1,512]{3,2,1,0:T(1,128)S(1)}, u32[]{:S(2)}) copy-start(f32[4,16,1,512]{3,2,1,0:T(1,128)S(1)} %get-tuple-element.496) | copy-start | bytes 393220
  301.1 38.0 %copy-start.104 = (f32[4,16,1,512]{3,2,1,0:T(1,128)}, f32[4,16,1,512]{3,2,1,0:T(1,128)S(1)}, u32[]{:S(2)}) copy-start(f32[4,16,1,512]{3,2,1,0:T(1,128)S(1)} %get-tuple-element.497) | copy-start | bytes 393220
  301.1 39.1 %copy-start.108 = (f32[4,16,1,512]{3,2,1,0:T(1,128)}, f32[4,16,1,512]{3,2,1,0:T(1,128)S(1)}, u32[]{:S(2)}) copy-start(f32[4,16,1,512]{3,2,1,0:T(1,128)S(1)} %get-tuple-element.498) | copy-start | bytes 393220
  353.3 210.1 %copy-start = (f32[4,16,16,512]{3,2,0,1:T(8,128)}, f32[4,16,16,512]{3,2,0,1:T(8,128)S(1)}, u32[]{:S(2)}) copy-start(f32[4,16,16,512]{3,2,0,1:T(8,128)S(1)} %get-tuple-element.469) | copy-start | bytes 6291460
  353.3 159.6 %all-gather.15.cloned.1.call-start = ((), (), s32[]{:S(2)}) async-start(), calls=%async_computation.14 | async-start | bytes 1179648 | tf_op jit(solution)/shard_map/all_gather | solution.py:21
  405.6 24.5 %copy-start.51 = (f32[4,16,1,16]{2,1,0,3:T(8,128)S(1)}, f32[4,16,1,16]{2,1,0,3:T(8,128)}, u32[]{:S(2)}) copy-start(f32[4,16,1,16]{2,1,0,3:T(8,128)} %get-tuple-element.549) | copy-start | bytes 12292
  433.7 24.8 %copy-start.24 = (f32[4,16,512]{2,0,1:T(4,128)S(1)}, f32[4,16,512]{2,0,1:T(4,128)}, u32[]{:S(2)}) copy-start(f32[4,16,512]{2,0,1:T(4,128)} %copy-done.23) | copy-start | bytes 393220
  433.7 24.8 %copy-start.26 = (f32[4,16,512]{2,0,1:T(4,128)S(1)}, f32[4,16,512]{2,0,1:T(4,128)}, u32[]{:S(2)}) copy-start(f32[4,16,512]{2,0,1:T(4,128)} %copy-done.25) | copy-start | bytes 393220
  433.7 24.8 %copy-start.28 = (f32[4,16,512]{2,0,1:T(4,128)S(1)}, f32[4,16,512]{2,0,1:T(4,128)}, u32[]{:S(2)}) copy-start(f32[4,16,512]{2,0,1:T(4,128)} %copy-done.27) | copy-start | bytes 393220
  433.7 24.8 %copy-start.30 = (f32[4,16,512]{2,0,1:T(4,128)S(1)}, f32[4,16,512]{2,0,1:T(4,128)}, u32[]{:S(2)}) copy-start(f32[4,16,512]{2,0,1:T(4,128)} %copy-done.29) | copy-start | bytes 393220
  433.7 24.8 %copy-start.32 = (f32[4,16,512]{2,0,1:T(4,128)S(1)}, f32[4,16,512]{2,0,1:T(4,128)}, u32[]{:S(2)}) copy-start(f32[4,16,512]{2,0,1:T(4,128)} %copy-done.31) | copy-start | bytes 393220
  433.7 24.8 %copy-start.34 = (f32[4,16,512]{2,0,1:T(4,128)S(1)}, f32[4,16,512]{2,0,1:T(4,128)}, u32[]{:S(2)}) copy-start(f32[4,16,512]{2,0,1:T(4,128)} %copy-done.33) | copy-start | bytes 393220
  433.7 24.8 %copy-start.36 = (f32[4,16,512]{2,0,1:T(4,128)S(1)}, f32[4,16,512]{2,0,1:T(4,128)}, u32[]{:S(2)}) copy-start(f32[4,16,512]{2,0,1:T(4,128)} %copy-done.35) | copy-start | bytes 393220
  433.7 24.8 %copy-start.38 = (f32[4,16,512]{2,0,1:T(4,128)S(1)}, f32[4,16,512]{2,0,1:T(4,128)}, u32[]{:S(2)}) copy-start(f32[4,16,512]{2,0,1:T(4,128)} %copy-done.37) | copy-start | bytes 393220
  472.6 82.1 %all-gather.11.cloned.1.call-start = ((), (), s32[]{:S(2)}) async-start(), calls=%async_computation.12 | async-start | bytes 1179648 | tf_op jit(solution)/shard_map/all_gather | solution.py:21
  485.9 356.4 %reduce-scatter.19.cloned.1.call-start = ((), (), s32[]{:S(2)}) async-start(), calls=%async_computation.19 | async-start | bytes 1081344
  708.1 267.2 %reduce-scatter.23.cloned.1.call-start = ((), (), s32[]{:S(2)}) async-start(), calls=%async_computation.21 | async-start | bytes 1081344
  711.2 397.4 %reduce-scatter.21.cloned.1.call-start = ((), (), s32[]{:S(2)}) async-start(), calls=%async_computation.20 | async-start | bytes 1081344
  732.0 20.0 %all-to-all-start.1 = ((bf16[4,256,512]{2,0,1:T(4,128)(2,1)}), bf16[4,256,512]{2,0,1:T(4,128)(2,1)}, u32[]{:S(2)}, u32[]{:S(2)}) async-start(bf16[4,256,512]{2,0,1:T(4,128)(2,1)} %copy.608), calls=%async_computation.1 | async-start | bytes 2097152 | tf_op jit(solution)/shard_map/all_to_all | solution.py:218
  736.3 505.7 %reduce-scatter.15.cloned.1.call-start = ((), (), s32[]{:S(2)}) async-start(), calls=%async_computation.16 | async-start | bytes 1081344 | tf_op jit(solution)/shard_map/reduce_scatter | solution.py:390
  738.6 651.0 %reduce-scatter.17.cloned.1.call-start = ((), (), s32[]{:S(2)}) async-start(), calls=%async_computation.17 | async-start | bytes 8650752 | tf_op jit(solution)/shard_map/reduce_scatter | solution.py:405
  764.2 807.2 %reduce-scatter.13.cloned.1.call-start = ((), (), s32[]{:S(2)}) async-start(), calls=%async_computation.15 | async-start | bytes 17301504 | tf_op jit(solution)/shard_map/reduce_scatter | solution.py:383
  766.9 5.8 collective-permute-start.2
  981.2 45.9 %copy-start.54 = (bf16[4,64,1024]{2,1,0:T(8,128)(2,1)S(1)}, bf16[4,64,1024]{2,1,0:T(8,128)(2,1)}, u32[]{:S(2)}) copy-start(bf16[4,64,1024]{2,1,0:T(8,128)(2,1)} %param.19) | copy-start | bytes 1572868
  (246 other events, 1280.6 us)
Sparse Core Ops, SparseCore 0:
  10.9 80.5 all-gather.8
  94.4 61.5 all-gather.12
  298.3 31.1 all-reduce.17
  353.4 40.1 all-gather.16
  472.7 40.1 all-gather.14
  515.7 38.8 all-gather.10
  708.2 134.1 reduce-scatter.18
  844.6 130.6 reduce-scatter.22
  977.6 130.9 reduce-scatter.20
  1111.3 130.6 reduce-scatter.14
  1245.0 144.5 reduce-scatter.16
  1392.4 178.9 reduce-scatter.12
where the time goes:
time: 1590 us; the launch traced here: 1580 us
  waiting for transfers between devices  802 us (50%)
  blocking collectives  273 us (17%)
  local copies, waits for them, and re-layouts  217 us (14%)
  other arithmetic  190 us (12%)
  matrix products  47.8 us (3%)
  starting transfers between devices  29.9 us (2%)
  between operations  18.4 us (1%)
    unnamed x15, waiting for transfers between devices  251 us
    reduce_scatter x1, waiting for transfers between devices, local(): lax.psum_scatter(entry_grad, ('blk', 'grp'), scatter_dimension=0, tiled=T...  182 us
    reduce_scatter x1, waiting for transfers between devices, local(): lax.psum_scatter(exit_grad, ('blk', 'grp'), scatter_dimension=0, tiled=True)  148 us
    reduce_scatter x1, waiting for transfers between devices, local(): lax.psum_scatter(full_channels(select_grad_group, 0), ('blk', 'grp'), sca...  132 us
    unnamed x680, local copies, waits for them, and re-layouts  121 us
    unnamed x2, blocking collectives  78.8 us
    reduce_sum x7, other arithmetic, local(): jnp.sum(grad_rate * step_now[:, :, None, :], axis=(0, 1))  60.7 us
    all_gather x3, waiting for transfers between devices, prefix(): everything = jax.tree.map(lambda part: lax.all_gather(part, axis), value)  43.3 us
  transfers between devices with their start and end apart: 18, of which 12 were waited for; matrix products, arithmetic and copies ran while one was open for 18% of the time, Pallas kernels for 0%

commit v1 on v0

v1 whole, which is shorter than its diff:
```python
import jax
import jax.numpy as jnp
from jax import lax
from jax.experimental import pallas as pl
from jax.experimental.pallas import tpu as pltpu
from jax.sharding import PartitionSpec as P

epsilon = 1e-05
log2_e = 1.4426950408889634
log_2 = 0.6931471805599453
reset_push = 1e6
f32 = jnp.float32
bf16 = jnp.bfloat16
small_rows = 192
both = ("blk", "grp")


def dot(left, right, dims=((1,), (0,))):
    return lax.dot_general(left, right, (dims, ((), ())), preferred_element_type=f32)


def sigmoid(values):
    return 1.0 / (1.0 + jnp.exp(-values))


def spread(block, axis):
    count = lax.axis_size(axis)
    copies = jnp.broadcast_to(block[None], (count,) + block.shape)
    return lax.all_to_all(copies, axis, split_axis=0, concat_axis=0, tiled=True)


def ordering(rows, chunks):
    steps = rows // chunks
    out_row = lax.broadcasted_iota(jnp.int32, (rows, rows), 0)
    in_row = lax.broadcasted_iota(jnp.int32, (rows, rows), 1)
    wanted = (out_row % chunks) * steps + out_row // chunks
    return jnp.where(in_row == wanted, 1.0, 0.0).astype(bf16)


def kernel_call(body, outs, scratch, limit, *operands):
    places = [
        pl.BlockSpec(memory_space=pltpu.SMEM)
        if value.dtype == jnp.int32
        else pl.BlockSpec(memory_space=pltpu.VMEM)
        for value in operands
    ]
    flops = 2_000_000_000
    return pl.pallas_call(
        body,
        out_shape=[jax.ShapeDtypeStruct(shape, kind) for shape, kind in outs],
        in_specs=places,
        out_specs=[pl.BlockSpec(memory_space=pltpu.VMEM) for _ in outs],
        scratch_shapes=scratch,
        compiler_params=pltpu.CompilerParams(vmem_limit_bytes=limit << 20),
        cost_estimate=pl.CostEstimate(flops=flops, bytes_accessed=8_000_000, transcendentals=0),
    )(*operands)


def read_rows(tokens_ref, order, me, block):
    groups, sequences, _, width = tokens_ref.shape
    parts = [
        tokens_ref[k ^ me, :, pl.ds(pl.multiple_of(block * 8, 8), 8), :].astype(f32)
        for k in range(groups)
    ]
    rows = jnp.concatenate(parts, axis=0).reshape(groups * sequences * 8, width)
    return rows


def small_row(small_ref, index):
    tail = small_ref[176:192, :].astype(f32)
    return tail[index : index + 1, :]


def entry_kernel(
    place_ref, tokens_ref, rim_ref, gain_ref, mask_ref, weight_ref, small_ref,
    normed_ref, inner_ref, filter_ref, chosen_ref,
):
    me = place_ref[1]
    groups, sequences, steps, width = tokens_ref.shape
    chunks = groups * sequences
    block_rows = chunks * 8
    rim_rows = 3 * chunks
    order = ordering(block_rows, chunks)

    def scaled(rows):
        root = lax.rsqrt(jnp.mean(rows * rows, axis=1, keepdims=True) + epsilon)
        return (rows * root * gain_ref[...]).astype(bf16)

    rim = scaled(rim_ref[...].astype(f32))
    inner_ref[0:rim_rows, :] = dot(rim, weight_ref[...]).astype(bf16)
    taps = [small_row(small_ref, k) for k in range(4)]
    offset = small_row(small_ref, 4)

    def lap(block, carry):
        base = pl.multiple_of(block * block_rows, block_rows)
        rows = scaled(read_rows(tokens_ref, order, me, block))
        normed = dot(order, rows).astype(bf16)
        normed_ref[pl.ds(base, block_rows), :] = normed
        inner = dot(normed, weight_ref[...]).astype(bf16)
        inner_ref[pl.ds(pl.multiple_of(base + rim_rows, 16), block_rows), :] = inner
        total = offset
        for k in range(3):
            same = mask_ref[pl.ds(base, block_rows), k : k + 1]
            part = inner_ref[pl.ds(pl.multiple_of(base + k * chunks, 16), block_rows), :]
            total = total + taps[k] * part.astype(f32) * same
        total = total + taps[3] * inner.astype(f32)
        filtered = (total * sigmoid(total)).astype(bf16)
        filter_ref[pl.ds(base, block_rows), :] = filtered.astype(f32)
        chosen = dot(small_ref[64:160, :], filtered, ((1,), (1,)))
        chosen_ref[:, pl.ds(base, block_rows)] = chosen.astype(bf16)
        return carry

    lax.fori_loop(0, steps // 8, lap, 0)


def gate_kernel(
    place_ref, cotangent_ref, normed_ref, weight_ref, exit_ref, rows_ref, value_ref, slope_ref, grad_ref
):
    me = place_ref[1]
    groups, sequences, steps, width = cotangent_ref.shape
    chunks = groups * sequences
    block_rows = chunks * 8
    order = ordering(block_rows, chunks)

    def lap(block, carry):
        at = pl.ds(pl.multiple_of(block * block_rows, block_rows), block_rows)
        rows = read_rows(cotangent_ref, order, me, block).astype(bf16)
        ordered = dot(order, rows).astype(bf16)
        rows_ref[at, :] = ordered
        gating = dot(normed_ref[at, :], weight_ref[...])
        grad_gated = dot(ordered, exit_ref[...], ((1,), (1,)))
        gate = sigmoid(gating)
        value = gating * gate
        value_ref[at, :] = value
        slope_ref[at, :] = grad_gated * (gate * (1.0 + gating * (1.0 - gate)))
        grad_ref[at, :] = (grad_gated * value).astype(bf16).astype(f32)
        return carry

    lax.fori_loop(0, steps // 8, lap, 0)


def fill_rates(small_ref, rates_ref):
    states = rates_ref.shape[0]
    rates = -jnp.exp(small_ref[160 : 160 + states, :].astype(f32)) * log2_e
    for n in range(states):
        rates_ref[n] = jnp.broadcast_to(rates[n : n + 1, :], rates_ref.shape[1:])


def fill_gates(gates_ref, write_ref, read_ref, half):
    steps, states = write_ref.shape[:2]
    at = pl.ds(pl.multiple_of(half * 8, 8), 8)

    def lap(t, carry):
        values = gates_ref[t, at, :]
        for n in range(states):
            write_ref[t, n] = jnp.broadcast_to(values[:, 64 + n : 65 + n], (8, 128))
            read_ref[t, n] = jnp.broadcast_to(values[:, 80 + n : 81 + n], (8, 128))
        return carry

    lax.fori_loop(0, steps, lap, 0)


def piece_kernel(
    chosen_ref, mask_ref, small_ref, filter_ref, grad_ref,
    gates_ref, step_ref, slope_ref, end_ref, keep_ref, give_ref, sum_ref, ahead_ref, back_ref,
    rates_ref, write_ref, read_ref,
):
    steps, chunks, width = step_ref.shape
    states = end_ref.shape[0]
    chosen = jnp.sum(chosen_ref[...].astype(f32), axis=0)
    padded = jnp.concatenate([chosen, jnp.zeros((32, chosen.shape[1]), f32)], axis=0)
    gates_ref[...] = padded.T.reshape(steps, chunks, 128)
    fill_rates(small_ref, rates_ref)
    bias = small_row(small_ref, 5)
    delta = small_ref[0:64, :]

    def delta_lap(block, carry):
        at = pl.ds(pl.multiple_of(block * 8, 8), 8)
        low = gates_ref[at, :, :].reshape(8 * chunks, 128)[:, 0:64]
        high = low.astype(bf16)
        rest = (low - high.astype(f32)).astype(bf16)
        pre = dot(high, delta) + dot(rest, delta) + bias
        grown = jnp.exp(-jnp.abs(pre))
        step = jnp.maximum(pre, 0.0) + jnp.log1p(grown)
        step_ref[at, :, :] = step.reshape(8, chunks, width)
        slope_ref[at, :, :] = (jnp.where(pre >= 0, 1.0, grown) / (1.0 + grown)).reshape(8, chunks, width)
        return carry

    lax.fori_loop(0, steps // 8, delta_lap, 0)

    end_ref[...] = jnp.zeros_like(end_ref)
    give_ref[...] = jnp.zeros_like(give_ref)
    keep_ref[...] = jnp.ones_like(keep_ref)
    sum_ref[...] = jnp.zeros_like(sum_ref)

    def half_lap(half, carry):
        fill_gates(gates_ref, write_ref, read_ref, half)
        at = pl.ds(pl.multiple_of(half * 8, 8), 8)

        def lane_lap(lane, inner_carry):
            lanes = pl.ds(pl.multiple_of(lane * 128, 128), 128)

            def lap(block, total):
                pushed, drives, grads = [], [], []
                for j in range(8):
                    t = block * 8 + j
                    step = step_ref[t, at, lanes]
                    push = step + gates_ref[t, at, 96:97]
                    total = total + push
                    pushed.append(push)
                    drives.append(step * filter_ref[t, at, lanes])
                    grads.append(grad_ref[t, at, lanes])
                for n in range(states):
                    rate = rates_ref[n, :, lanes]
                    end = end_ref[n, at, lanes]
                    keep = keep_ref[n, at, lanes]
                    give = give_ref[n, at, lanes]
                    for j in range(8):
                        t = block * 8 + j
                        decay = jnp.exp2(pushed[j] * rate)
                        end = decay * end + drives[j] * write_ref[t, n]
                        keep = keep * decay
                        give = give + keep * (read_ref[t, n] * grads[j])
                    end_ref[n, at, lanes] = end
                    keep_ref[n, at, lanes] = keep
                    give_ref[n, at, lanes] = give
                return total

            total = lax.fori_loop(0, steps // 8, lap, jnp.zeros((8, 128), f32))
            sum_ref[at, lanes] = total
            return inner_carry

        return lax.fori_loop(0, width // 128, lane_lap, carry)

    push = mask_ref[:, 3:4] * reset_push
    gates_ref[:, :, 96:97] = push.reshape(steps, chunks, 1)
    lax.fori_loop(0, chunks // 8, half_lap, 0)

    sequences = ahead_ref.shape[0] // states
    groups = chunks // sequences
    for n in range(states):
        rows = slice(n * sequences, (n + 1) * sequences)
        ahead = jnp.zeros((sequences, width), f32)
        back = jnp.zeros((sequences, width), f32)
        for k in range(groups):
            part = slice(k * sequences, (k + 1) * sequences)
            ahead = keep_ref[n, part, :] * ahead + end_ref[n, part, :]
            other = slice((groups - 1 - k) * sequences, (groups - k) * sequences)
            back = give_ref[n, other, :] + keep_ref[n, other, :] * back
        ahead_ref[rows, :] = ahead
        back_ref[rows, :] = back


def scan_kernel(
    place_ref, came_ref, sums_ref, gates_ref, small_ref, step_ref, slope_ref, filter_ref, grad_ref,
    end_ref, keep_ref, give_ref,
    out_ref, delta_ref, direct_ref, rank_ref, chosen_ref, decay_ref, skip_ref, bias_ref,
    rates_ref, write_ref, read_ref, state_ref, product_ref, pick_ref, enter_ref, arrive_ref, sums_acc_ref,
):
    me = place_ref[0]
    steps, chunks, width = step_ref.shape
    states = end_ref.shape[0]
    pieces = came_ref.shape[0]
    sequences = sums_ref.shape[1]
    groups = chunks // sequences
    fill_rates(small_ref, rates_ref)

    def state_of(piece, n):
        return came_ref[piece, n * sequences : (n + 1) * sequences, :].astype(f32)

    for n in range(states):
        rate = rates_ref[n, 0:sequences, :]

        def step_in(piece, state):
            return jnp.exp2(sums_ref[piece] * rate) * state + state_of(piece, n)

        def step_back(k, state):
            return step_in(pieces - 1 - k, state)

        zero = jnp.zeros((sequences, width), f32)
        ahead = lax.fori_loop(0, me, step_in, zero)
        back = lax.fori_loop(0, pieces - 1 - me, step_back, zero)
        for k in range(groups):
            part = slice(k * sequences, (k + 1) * sequences)
            enter_ref[n, part, :] = ahead
            ahead = keep_ref[n, part, :] * ahead + end_ref[n, part, :]
            other = slice((groups - 1 - k) * sequences, (groups - k) * sequences)
            arrive_ref[n, other, :] = back
            back = give_ref[n, other, :] + keep_ref[n, other, :] * back

    spot = lax.broadcasted_iota(jnp.int32, (2 * states * 128, 128), 0) // 128
    column = lax.broadcasted_iota(jnp.int32, (2 * states * 128, 128), 1)
    pick_ref[...] = jnp.where(column == spot + 64, 1.0, 0.0).astype(bf16)
    sums_acc_ref[...] = jnp.zeros_like(sums_acc_ref)
    decay_ref[...] = jnp.zeros_like(decay_ref)
    skip_ref[...] = jnp.zeros_like(skip_ref)
    skip_gain = small_row(small_ref, 6)
    skip_spread = jnp.broadcast_to(skip_gain, (8, width))
    rates_ref[states] = skip_spread
    span = 4

    def half_lap(half, carry):
        fill_gates(gates_ref, write_ref, read_ref, half)
        at = pl.ds(pl.multiple_of(half * 8, 8), 8)

        def lane_lap(lane, inner_carry):
            lanes = pl.ds(pl.multiple_of(lane * 128, 128), 128)

            def forward(block, states_now):
                pushed, drives, grads, outs, feeds = [], [], [], [], []
                for j in range(span):
                    t = block * span + j
                    step = step_ref[t, at, lanes]
                    feed = filter_ref[t, at, lanes]
                    pushed.append(step + gates_ref[t, at, 96:97])
                    drives.append(step * feed)
                    grads.append(grad_ref[t, at, lanes])
                    feeds.append(feed)
                    outs.append(feed * rates_ref[states, :, lanes])
                nexts = []
                for n in range(states):
                    rate = rates_ref[n, :, lanes]
                    hidden = states_now[n]
                    seen = []
                    for j in range(span):
                        t = block * span + j
                        hidden = jnp.exp2(pushed[j] * rate) * hidden + drives[j] * write_ref[t, n]
                        state_ref[t, n] = hidden
                        outs[j] = outs[j] + hidden * read_ref[t, n]
                        seen.append(grads[j] * hidden)
                    spot = slice((states + n) * 128, (states + n + 1) * 128)
                    rows = pl.ds(pl.multiple_of(block * span * 8, span * 8), span * 8)
                    product_ref[rows, spot] = jnp.concatenate(seen, axis=0).astype(bf16)
                    nexts.append(hidden)
                for j in range(span):
                    out_ref[block * span + j, at, lanes] = outs[j]
                return tuple(nexts)

            first = tuple(enter_ref[n, at, lanes] for n in range(states))
            lax.fori_loop(0, steps // span, forward, first)

            def backward(k, held):
                block = steps // span - 1 - k
                passed, totals, skip_total = held
                pushed, raw, drives, grads, weighted, slopes, feeds = [], [], [], [], [], [], []
                for j in range(span):
                    t = block * span + j
                    step = step_ref[t, at, lanes]
                    feed = filter_ref[t, at, lanes]
                    grad = grad_ref[t, at, lanes]
                    raw.append(step)
                    feeds.append(feed)
                    pushed.append(step + gates_ref[t, at, 96:97])
                    drives.append(step * feed)
                    grads.append(grad)
                    weighted.append(jnp.zeros((8, 128), f32))
                    slopes.append(jnp.zeros((8, 128), f32))
                    skip_total = skip_total + grad * feed
                next_passed, next_totals = [], []
                before = jnp.maximum(block * span - 1, 0)
                for n in range(states):
                    rate = rates_ref[n, :, lanes]
                    gone = passed[n]
                    total = totals[n]
                    seen = [None] * span
                    for j in reversed(range(span)):
                        t = block * span + j
                        adjoint = read_ref[t, n] * grads[j] + gone
                        weighted[j] = weighted[j] + adjoint * write_ref[t, n]
                        seen[j] = adjoint * drives[j]
                        gone = adjoint * jnp.exp2(pushed[j] * rate)
                        if j > 0:
                            earlier = state_ref[t - 1, n]
                        else:
                            earlier = jnp.where(block > 0, state_ref[before, n], enter_ref[n, at, lanes])
                        turn = gone * earlier
                        slopes[j] = slopes[j] + turn * rate
                        total = total + turn * raw[j]
                    spot = slice(n * 128, (n + 1) * 128)
                    rows = pl.ds(pl.multiple_of(block * span * 8, span * 8), span * 8)
                    product_ref[rows, spot] = jnp.concatenate(seen, axis=0).astype(bf16)
                    next_passed.append(gone)
                    next_totals.append(total)
                skip_now = rates_ref[states, :, lanes]
                for j in range(span):
                    t = block * span + j
                    grown = slopes[j] * log_2 + weighted[j] * feeds[j]
                    delta_ref[t, at, lanes] = grown * slope_ref[t, at, lanes]
                    direct_ref[t, at, lanes] = weighted[j] * raw[j] + grads[j] * skip_now
                return (tuple(next_passed), tuple(next_totals), skip_total)

            last = tuple(arrive_ref[n, at, lanes] for n in range(states))
            empty = tuple(jnp.zeros((8, 128), f32) for _ in range(states))
            ended = lax.fori_loop(
                0, steps // span, backward, (last, empty, jnp.zeros((8, 128), f32))
            )
            for n in range(states):
                part = jnp.sum(ended[1][n], axis=0, keepdims=True)
                decay_ref[n : n + 1, lanes] += part * rates_ref[n, 0:1, lanes] * log_2
            skip_ref[0:1, lanes] += jnp.sum(ended[2], axis=0, keepdims=True)
            summed = dot(product_ref[...], pick_ref[...])
            sums_acc_ref[:, at, :] += summed.reshape(steps, 8, 128)
            return inner_carry

        return lax.fori_loop(0, width // 128, lane_lap, carry)

    lax.fori_loop(0, chunks // 8, half_lap, 0)

    rows = steps * chunks
    grads = delta_ref[...].reshape(rows, width)
    bias_ref[...] = jnp.sum(grads, axis=0, keepdims=True)
    grads = grads.astype(bf16)
    low = gates_ref[...].reshape(rows, 128)[:, 0:64].astype(bf16)
    rank_ref[...] = dot(low, grads, ((0,), (0,)))
    back = dot(small_ref[0:64, :], grads, ((1,), (1,)))
    sums = sums_acc_ref[...].reshape(rows, 128).T
    chosen_ref[0:64, :] = back.astype(bf16)
    chosen_ref[64:96, :] = sums[64:96, :].astype(bf16)


def store_rows(out_ref, order, values, block):
    groups, sequences, _, width = out_ref.shape
    back = dot(order, values.astype(bf16), ((0,), (0,)))
    shaped = back.reshape(groups, sequences, 8, width).astype(bf16)
    out_ref[:, :, pl.ds(pl.multiple_of(block * 8, 8), 8), :] = shaped


def leave_kernel(
    scan_ref, value_ref, slope_ref, rows_ref, normed_ref, exit_ref,
    gating_ref, out_ref, exit_grad_ref, entry_grad_ref, gated_ref,
):
    groups, sequences, steps, width = out_ref.shape
    chunks = groups * sequences
    block_rows = chunks * 8
    order = ordering(block_rows, chunks)

    def lap(block, carry):
        at = pl.ds(pl.multiple_of(block * block_rows, block_rows), block_rows)
        scan_out = scan_ref[at, :].astype(bf16).astype(f32)
        gated = (scan_out * value_ref[at, :]).astype(bf16)
        gated_ref[at, :] = gated
        gating_ref[at, :] = (scan_out * slope_ref[at, :]).astype(bf16)
        store_rows(out_ref, order, dot(gated, exit_ref[...]), block)
        return carry

    lax.fori_loop(0, steps // 8, lap, 0)
    exit_grad_ref[...] = dot(gated_ref[...], rows_ref[...], ((0,), (0,))).astype(bf16)
    entry_grad_ref[...] = dot(normed_ref[...], gating_ref[...], ((0,), (0,))).astype(bf16)


def filter_kernel(
    chosen_ref, direct_ref, inner_ref, filter_ref, mask_ref, small_ref,
    grads_ref, spill_ref, select_ref, taps_ref, offset_ref, picked_ref,
):
    rows, width = grads_ref.shape
    chunks = spill_ref.shape[0] // 3
    block_rows = chunks * 8
    chosen = jnp.sum(chosen_ref[...].astype(f32), axis=0).astype(bf16)
    select_ref[...] = dot(chosen, filter_ref[...].astype(bf16))
    picked_ref[...] = chosen.astype(f32).T.astype(bf16)
    taps = [small_row(small_ref, k) for k in range(4)]
    offset = small_row(small_ref, 4)
    offset_ref[...] = jnp.zeros_like(offset_ref)
    taps_ref[...] = jnp.zeros_like(taps_ref)

    def lap(block, carry):
        base = pl.multiple_of(block * block_rows, block_rows)
        at = pl.ds(base, block_rows)
        total = offset
        shifted = []
        for k in range(4):
            part = inner_ref[pl.ds(pl.multiple_of(base + k * chunks, 16), block_rows), :].astype(f32)
            if k < 3:
                part = part * mask_ref[at, k : k + 1]
            shifted.append(part)
            total = total + taps[k] * part
        gate = sigmoid(total)
        grad = direct_ref[at, :] + dot(picked_ref[at, :], small_ref[64:160, :])
        grad = grad * (gate * (1.0 + total * (1.0 - gate)))
        grads_ref[at, :] = grad
        offset_ref[...] += jnp.sum(grad, axis=0, keepdims=True)
        for k in range(4):
            taps_ref[k : k + 1, :] += jnp.sum(grad * shifted[k], axis=0, keepdims=True)
        return carry

    lax.fori_loop(0, rows // block_rows, lap, 0)
    for u in range(3):
        total = jnp.zeros((chunks, width), f32)
        for t in range(u + 1):
            part = slice(t * chunks, (t + 1) * chunks)
            total = total + grads_ref[part, :] * taps[u - t] * mask_ref[part, u - t : u - t + 1]
        spill_ref[u * chunks : (u + 1) * chunks, :] = total


def inner_kernel(
    grads_ref, spill_ref, mask_ref, small_ref, normed_ref, gating_ref, weight_ref, gate_weight_ref,
    out_ref, entry_grad_ref, gain_ref, inner_ref, past_ref,
):
    groups, sequences, steps, width = out_ref.shape
    rows, inner_width = grads_ref.shape
    chunks = groups * sequences
    block_rows = chunks * 8
    order = ordering(block_rows, chunks)
    taps = [small_row(small_ref, k) for k in range(4)]
    gain_ref[...] = jnp.zeros_like(gain_ref)
    past_ref[0] = jnp.zeros_like(past_ref[0])
    past_ref[1] = jnp.zeros_like(past_ref[1])
    past_ref[2] = jnp.zeros_like(past_ref[2])
    rim_rows = 3 * chunks
    for k in range(3):
        past_ref[k, rows : rows + rim_rows, :] = jnp.zeros((rim_rows, inner_width), f32)

    def mask_lap(block, carry):
        at = pl.ds(pl.multiple_of(block * block_rows, block_rows), block_rows)
        grad = grads_ref[at, :]
        for k in range(3):
            past_ref[k, at, :] = grad * taps[k] * mask_ref[at, k : k + 1]
        return carry

    lax.fori_loop(0, steps // 8, mask_lap, 0)

    def lap(block, carry):
        base = pl.multiple_of(block * block_rows, block_rows)
        at = pl.ds(base, block_rows)
        total = grads_ref[at, :] * taps[3]
        for k in range(3):
            later = pl.ds(pl.multiple_of(base + (3 - k) * chunks, 16), block_rows)
            total = total + past_ref[k, later, :]
        inner_ref[at, :] = total.astype(bf16)

        @pl.when(block == steps // 8 - 1)
        def _():
            tail = total[block_rows - rim_rows :, :] + spill_ref[...]
            inner_ref[rows - rim_rows : rows, :] = tail.astype(bf16)

        grad = dot(inner_ref[at, :], weight_ref[...], ((1,), (1,)))
        grad = grad + dot(gating_ref[at, :], gate_weight_ref[...], ((1,), (1,)))
        gain_ref[...] += jnp.sum(grad * normed_ref[at, :].astype(f32), axis=0, keepdims=True)
        store_rows(out_ref, order, grad, block)
        return carry

    lax.fori_loop(0, steps // 8, lap, 0)
    entry_grad_ref[...] = dot(normed_ref[...], inner_ref[...], ((0,), (0,))).astype(bf16)


def local(
    tokens,
    segments,
    cotangent,
    norm_gain,
    entry_weight,
    kernel_weight,
    kernel_offset,
    select_weight,
    delta_weight,
    timestep_bias,
    decay_log,
    skip_gain,
    exit_weight,
):
    sequences, steps, width = tokens.shape
    pieces, groups = lax.axis_size("blk"), lax.axis_size("grp")
    piece, group = lax.axis_index("blk"), lax.axis_index("grp")
    place = jnp.stack([piece, group]).astype(jnp.int32)
    chunks = groups * sequences
    rows = steps * chunks
    slice_rows, entry_width = entry_weight.shape
    own = kernel_offset.shape[0]
    inner_width = entry_width // 2
    group_width = inner_width // groups
    states = decay_log.shape[0]
    rank = delta_weight.shape[0]

    packed = jnp.concatenate(
        [
            delta_weight,
            select_weight.T,
            decay_log,
            kernel_weight,
            kernel_offset[None],
            timestep_bias[None],
            skip_gain[None],
            jnp.zeros((small_rows - 183, own), bf16),
        ],
        axis=0,
    )
    small_came = spread(jnp.concatenate([packed.reshape(-1), norm_gain]), "blk")
    small = small_came[:, : packed.size].reshape(pieces, small_rows, own)
    small = small.transpose(1, 0, 2).reshape(small_rows, group_width)

    def meet(values):
        pair = lax.ppermute(values, "grp", [(i, i ^ 2) for i in range(groups)])
        near = lax.ppermute(values, "grp", [(i, i ^ 1) for i in range(groups)])
        far = lax.ppermute(pair, "grp", [(i, i ^ 1) for i in range(groups)])
        return jnp.stack([values, near, pair, far])

    tokens_all = meet(tokens)
    cotangent_all = meet(cotangent)

    ahead = [(i, i + 1) for i in range(pieces - 1)]
    behind = [(i + 1, i) for i in range(pieces - 1)]
    tail = tokens[:, steps - 3 :]
    tail_before = lax.ppermute(tail, "blk", ahead)
    slice_rows = norm_gain.shape[0]
    gain_part = small_came[:, packed.size :].reshape(pieces * slice_rows)
    tail_values = jnp.stack([tail, tail_before]).reshape(-1)
    tails = lax.all_gather(jnp.concatenate([tail_values, gain_part]), "grp")
    gain_all = tails[:, tail_values.size :].reshape(groups, pieces, slice_rows)
    gain_all = gain_all.transpose(1, 0, 2).reshape(1, width).astype(f32)
    tails = tails[:, : tail_values.size].reshape((groups, 2) + tail.shape)
    rim = jnp.concatenate([tails[groups - 1 :, 1], tails[: groups - 1, 0]], axis=0)
    rim = rim.transpose(2, 0, 1, 3).reshape(3 * chunks, width)
    label_tail = lax.ppermute(segments[:, -3:], "blk", ahead)
    labels = jnp.concatenate([label_tail, segments], axis=1)
    length = segments.shape[1]
    shifted = jnp.stack([labels[:, k : k + length] for k in range(3)], axis=-1)
    same = (shifted == segments[:, :, None]).astype(f32)
    columns = jnp.concatenate([same, 1.0 - same[:, :, 2:3]], axis=2)
    mask = columns.reshape(sequences, groups, steps, 4).transpose(2, 1, 0, 3).reshape(rows, 4)

    halves = entry_weight.reshape(slice_rows, 2, pieces, groups, own).transpose(1, 3, 0, 2, 4)

    def columns_of(half):
        block = halves[half].reshape(1, groups, slice_rows, group_width)
        copies = jnp.broadcast_to(block, (pieces,) + block.shape[1:])
        copies = copies.reshape(pieces * groups, slice_rows, group_width)
        parts = lax.all_to_all(copies, both, split_axis=0, concat_axis=0, tiled=True)
        return parts.reshape(width, group_width)

    inner_weight = columns_of(0)
    gate_weight = columns_of(1)
    exit_rows = spread(exit_weight, "blk").reshape(group_width, width)

    normed, inner, filtered, chosen = kernel_call(
        entry_kernel,
        [
            ((rows, width), bf16),
            ((rows + 3 * chunks, group_width), bf16),
            ((rows, group_width), f32),
            ((96, rows), bf16),
        ],
        [],
        40,
        place, tokens_all, rim, gain_all, mask, inner_weight, small,
    )
    chosen_all = lax.all_gather(chosen, "grp")
    cotangent_rows, gate_value, gate_slope, grad_scan = kernel_call(
        gate_kernel,
        [
            ((rows, width), bf16),
            ((rows, group_width), f32),
            ((rows, group_width), f32),
            ((rows, group_width), f32),
        ],
        [],
        40,
        place, cotangent_all, normed, gate_weight, exit_rows,
    )
    cube = (steps, chunks, group_width)
    bank = (states, chunks, group_width)
    gates, step_sizes, step_slopes, ends, keeps, gives, sums, ahead_state, back_state = kernel_call(
        piece_kernel,
        [
            ((steps, chunks, 128), f32),
            (cube, f32),
            (cube, f32),
            (bank, f32),
            (bank, f32),
            (bank, f32),
            ((chunks, group_width), f32),
            ((states * sequences, group_width), f32),
            ((states * sequences, group_width), f32),
        ],
        [
            pltpu.VMEM((states, 8, group_width), f32),
            pltpu.VMEM((steps, states, 8, 128), f32),
            pltpu.VMEM((steps, states, 8, 128), f32),
        ],
        48,
        chosen_all, mask, small, filtered.reshape(cube), grad_scan.reshape(cube),
    )
    piece_sum = jnp.sum(sums.reshape(groups, sequences, group_width), axis=0)
    first = lax.reduce_precision(piece_sum, 8, 7)
    second = lax.reduce_precision(piece_sum - first, 8, 7)
    third = piece_sum - first - second
    extra = jnp.concatenate([first, second, third, jnp.zeros_like(first)], axis=0)
    forward_load = jnp.concatenate([ahead_state, extra], axis=0).astype(bf16)
    back_load = jnp.concatenate([back_state, extra], axis=0).astype(bf16)
    later = (jnp.arange(pieces) > piece)[:, None, None]
    loads = jnp.where(later, forward_load[None], back_load[None])
    came = lax.all_to_all(loads, "blk", split_axis=0, concat_axis=0, tiled=True)
    at = states * sequences
    came_sums = came[:, at : at + 3 * sequences].astype(f32)
    came_sums = came_sums.reshape(pieces, 3, sequences, group_width).sum(axis=1)

    scan_out, grad_delta, grad_direct, rank_grad, chosen_grad, decay_grad, skip_grad, bias_grad = kernel_call(
        scan_kernel,
        [
            (cube, f32),
            (cube, f32),
            (cube, f32),
            ((rank, group_width), f32),
            ((96, rows), bf16),
            ((states, group_width), f32),
            ((1, group_width), f32),
            ((1, group_width), f32),
        ],
        [
            pltpu.VMEM((states + 1, 8, group_width), f32),
            pltpu.VMEM((steps, states, 8, 128), f32),
            pltpu.VMEM((steps, states, 8, 128), f32),
            pltpu.VMEM((steps, states, 8, 128), f32),
            pltpu.VMEM((steps * 8, 2 * states * 128), bf16),
            pltpu.VMEM((2 * states * 128, 128), bf16),
            pltpu.VMEM(bank, f32),
            pltpu.VMEM(bank, f32),
            pltpu.VMEM((steps, chunks, 128), f32),
        ],
        56,
        place, came, came_sums, gates, small, step_sizes, step_slopes, filtered.reshape(cube),
        grad_scan.reshape(cube), ends, keeps, gives,
    )
    chosen_grads = lax.all_gather(chosen_grad, "grp")
    shape4 = (groups, sequences, steps, width)
    grad_gating, out_parts, exit_grad, gate_entry_grad = kernel_call(
        leave_kernel,
        [
            ((rows, group_width), bf16),
            (shape4, bf16),
            ((group_width, width), bf16),
            ((width, group_width), bf16),
        ],
        [pltpu.VMEM((rows, group_width), bf16)],
        48,
        scan_out.reshape(rows, group_width), gate_value, gate_slope, cotangent_rows, normed, exit_rows,
    )
    grad_sums, spill, select_grad, taps_grad, offset_grad = kernel_call(
        filter_kernel,
        [
            ((rows, group_width), f32),
            ((3 * chunks, group_width), f32),
            ((96, group_width), f32),
            ((4, group_width), f32),
            ((1, group_width), f32),
        ],
        [pltpu.VMEM((rows, 96), bf16)],
        48,
        chosen_grads, grad_direct.reshape(rows, group_width), inner, filtered, mask, small,
    )
    spill = spill.reshape(3, groups, sequences, group_width)
    spill_after = lax.ppermute(spill[:, 0], "blk", behind)
    spill = jnp.concatenate([spill[:, 1:], spill_after[:, None]], axis=1).reshape(3 * chunks, group_width)
    grad_parts, inner_entry_grad, gain_sum = kernel_call(
        inner_kernel,
        [
            (shape4, bf16),
            ((width, group_width), bf16),
            ((1, width), f32),
        ],
        [
            pltpu.VMEM((rows, group_width), bf16),
            pltpu.VMEM((3, rows + 3 * chunks, group_width), f32),
        ],
        48,
        grad_sums, spill, mask, small, normed, grad_gating, inner_weight, gate_weight,
    )

    def gathered_sum(parts):
        came = lax.all_to_all(parts, "grp", split_axis=0, concat_axis=0, tiled=True)
        return jnp.sum(came.astype(f32), axis=0)

    residual = tokens.astype(f32)
    block_out = (residual + gathered_sum(out_parts)).astype(bf16)

    exit_parts = lax.all_to_all(
        exit_grad.reshape(pieces, own, width), "blk", split_axis=0, concat_axis=0, tiled=True
    )
    exit_out = jnp.sum(exit_parts.astype(f32), axis=0)

    def entry_half(grads):
        parts = grads.reshape(pieces * groups, slice_rows, group_width)
        came = lax.all_to_all(parts, both, split_axis=0, concat_axis=0, tiled=True)
        came = came.reshape(pieces, groups, slice_rows, pieces, own)
        summed = jnp.sum(came.astype(f32), axis=0)
        return summed.transpose(1, 2, 0, 3).reshape(slice_rows, inner_width)

    entry_out = jnp.concatenate([entry_half(inner_entry_grad), entry_half(gate_entry_grad)], axis=1)

    small_grads = jnp.concatenate(
        [rank_grad, select_grad, decay_grad, taps_grad, offset_grad, bias_grad, skip_grad], axis=0
    )
    count = small_grads.shape[0]
    split = small_grads.reshape(count, pieces, own).transpose(1, 0, 2).reshape(pieces, count * own)
    gain_split = gain_sum.reshape(pieces, groups * slice_rows)
    sent = jnp.concatenate([split, gain_split], axis=1)
    came_small = jnp.sum(
        lax.all_to_all(sent, "blk", split_axis=0, concat_axis=0, tiled=True), axis=0
    )
    gain_sums = jnp.sum(lax.all_gather(came_small[count * own :], "grp"), axis=0)
    gain_out = lax.dynamic_slice_in_dim(gain_sums, group * slice_rows, slice_rows)
    gain_out = gain_out / norm_gain.astype(f32)
    mine = came_small[: count * own].reshape(count, own)

    grad_hat = gathered_sum(grad_parts) * gain_all[0]
    root = lax.rsqrt(jnp.mean(residual * residual, axis=2, keepdims=True) + epsilon)
    hat_own = residual * root
    grad_input = root * (grad_hat - hat_own * jnp.mean(grad_hat * hat_own, axis=2, keepdims=True))
    input_grad = (cotangent.astype(f32) + grad_input).astype(bf16)
    return (
        block_out,
        input_grad,
        gain_out,
        entry_out,
        mine[176:180],
        mine[180],
        mine[64:160].T,
        mine[0:64],
        mine[181],
        mine[160:176],
        mine[182],
        exit_out,
    )


def solution(mesh):
    placed = (
        P(None, both, None),
        P(None, "blk"),
        P(None, both, None),
        P(both),
        P(both, None),
        P(None, both),
        P(both),
        P(both, None),
        P(None, both),
        P(both),
        P(None, both),
        P(both),
        P(both, None),
    )
    return jax.shard_map(
        local,
        mesh=mesh,
        in_specs=placed,
        out_specs=(
            P(None, both, None),
            P(None, both, None),
            P(both),
            P(both, None),
            P(None, both),
            P(both),
            P(both, None),
            P(None, both),
            P(both),
            P(None, both),
            P(both),
            P(both, None),
        ),
        check_vma=False,
    )
```

time: 1590 us -> 540 us (0.34)
  waiting for transfers between devices: 802 us -> 52.6 us
  other arithmetic: 190 us -> 23.5 us
  Pallas kernels: 0 us -> 165 us
  local copies, waits for them, and re-layouts: 217 us -> 74.9 us
  blocking collectives: 273 us -> 175 us
  matrix products: 47.8 us -> 0 us
  between operations: 18.4 us -> 1.31 us
    reduce_scatter x3 -> x0, waiting for transfers between devices: 461 us -> none  [the longest x1 182 us: local(): lax.psum_scatter(entry_grad, ('blk', 'grp'), scatter_dimension=0, tiled=T...]
    unnamed x15 -> x0, waiting for transfers between devices: 251 us -> none
    pallas_call x0 -> x7, Pallas kernels: none -> 165 us  [kernel_call(): pl.pallas_call(body, out_shape=[jax.ShapeDtypeStruct(shape, kind) for sha...]
    all_gather x4, blocking collectives: 162 us -> 31.7 us  [the longest x1 9.61 us: local(): tails = lax.all_gather(jnp.concatenate([tail_values, gain_part]), 'grp')]
    all_to_all x1 -> x6, blocking collectives: 18 us -> 143 us  [the longest x2 58.1 us: gathered_sum(): came = lax.all_to_all(parts, 'grp', split_axis=0, concat_axis=0, tiled=True)]
    unnamed x680 -> x100, local copies, waits for them, and re-layouts: 121 us -> 27.5 us
    unnamed x2 -> x0, blocking collectives: 78.8 us -> none
    reduce_sum x12 -> x11, other arithmetic: 76.9 us -> 10.5 us  [the longest x2 5.19 us: entry_half(): summed = jnp.sum(came.astype(f32), axis=0)]
  transfers between devices with their start and end apart: 18 -> 14, of which waited for: 12 -> 5; matrix products, arithmetic and copies ran while one was open for 18% -> 10% of each run, Pallas kernels for 0% -> 4%
where the time goes in v1:
time: 540 us; the launch traced here: 538 us
  blocking collectives  175 us (32%)
  Pallas kernels  165 us (31%)
  local copies, waits for them, and re-layouts  74.9 us (14%)
  waiting for transfers between devices  52.6 us (10%)
  starting transfers between devices  45.2 us (8%)
  other arithmetic  23.5 us (4%)
    pallas_call x7, Pallas kernels, kernel_call(): pl.pallas_call(body, out_shape=[jax.ShapeDtypeStruct(shape, kind) for sha...  165 us
    all_to_all x2, blocking collectives, gathered_sum(): came = lax.all_to_all(parts, 'grp', split_axis=0, concat_axis=0, tiled=True)  58.1 us
    all_to_all x1, blocking collectives, local(): lax.all_to_all(exit_grad.reshape(pieces, own, width), 'blk', split_axis=0...  28.8 us
    unnamed x100, local copies, waits for them, and re-layouts  27.5 us
    all_to_all x2, waiting for transfers between devices, entry_half(): came = lax.all_to_all(parts, both, split_axis=0, concat_axis=0, tiled=True)  24.9 us
    all_to_all x1, waiting for transfers between devices, spread(): return lax.all_to_all(copies, axis, split_axis=0, concat_axis=0, tiled=True)  24.4 us
    all_to_all x1, blocking collectives, local(): came = lax.all_to_all(loads, 'blk', split_axis=0, concat_axis=0, tiled=True)  24.1 us
    all_to_all x1, blocking collectives, local(): lax.all_to_all(sent, 'blk', split_axis=0, concat_axis=0, tiled=True)  17.3 us
  transfers between devices with their start and end apart: 14, of which 5 were waited for; matrix products, arithmetic and copies ran while one was open for 10% of the time, Pallas kernels for 4%

profile of v1, /device:TPU:0, one launch (start us, length us, event | category | flops | bytes accessed | tf_op | source)
XLA Modules:
  0.0 537.6 jit_solution(10409261166616566282)
XLA Ops:
  7.8 1.8 reduce.2
  9.8 15.1 %all_to_all.63 = bf16[8,2,6160]{2,1,0:T(2,128)(2,1)S(1)} all-to-all(bf16[8,2,6160]{2,1,0:T(2,128)(2,1)S(1)} %reshape.338), channel_id=1, replica_groups=mesh['blk'=8,'grp'=4] {'blk'}, dimensions={0} | all-to-all | bytes 394240 | tf_op jit(solution)/shard_map/all_to_all | solution.py:29
  26.0 3.6 all-to-all-start.3
  30.4 24.4 %all-to-all-done.3 = bf16[8,64,1024]{2,1,0:T(8,128)(2,1)S(1)} async-done(((bf16[8,64,1024]{2,1,0:T(8,128)(2,1)}), bf16[8,64,1024]{2,1,0:T(8,128)(2,1)S(1)}, u32[]{:S(2)}, u32[]{:S(2)}) %all-to-all-start.3) | async-done | bytes 1048608 | tf_op jit(solution)/shard_map/all_to_all | solution.py:29
  55.9 3.4 all-to-all-start.1
  59.7 1.7 collective-permute-start.6
  61.8 3.6 collective-permute-start.4
  66.7 13.9 %collective-permute-start.3 = (bf16[4,3,1024]{2,1,0:T(4,128)(2,1)S(1)}, bf16[4,3,1024]{2,1,0:T(4,128)(2,1)S(1)}, u32[]{:S(2)}, u32[]{:S(2)}) collective-permute-start(bf16[4,3,1024]{2,1,0:T(4,128)(2,1)S(1)} %get-tuple-element.149), channel_id=1, source_target_pairs={{0,4},{4,8},{8,12},{12,16},{16,20},{20,24},{24,28},{1,5},{5,9},{9,... | collective-permute-start | bytes 73736 | tf_op jit(solution)/shard_map/ppermute | solution.py:603
  82.7 2.9 all-to-all-done.1
  86.7 9.9 %all-to-all-start.2 = ((bf16[32,32,512]{2,1,0:T(8,128)(2,1)}), bf16[32,32,512]{2,1,0:T(8,128)(2,1)S(1)}, u32[]{:S(2)}, u32[]{:S(2)}) async-start(bf16[32,32,512]{2,1,0:T(8,128)(2,1)} %bitcast.99), calls=%async_computation.2 | async-start | bytes 2097152 | tf_op jit(solution)/shard_map/all_to_all | solution.py:627
  101.4 9.6 %all-gather.4 = bf16[4,1,24832]{2,1,0:T(2,128)(2,1)S(1)} all-gather(bf16[1,1,24832]{2,1,0:T(2,128)(2,1)} %reshape.331), channel_id=2, replica_groups=mesh['blk'=8,'grp'=4] {'grp'}, dimensions={0}, use_global_device_ids=true | all-gather | bytes 248320 | tf_op jit(solution)/shard_map/all_gather | solution.py:607
  117.4 3.1 pad_maximum_fusion.1.cotangent_ref
  120.5 1.8 pad_maximum_fusion.tokens_ref
  122.4 8.7 %shard_map.220 = (bf16[1024,1024]{1,0:T(8,128)(2,1)S(1)}, bf16[1072,512]{1,0:T(8,128)(2,1)S(1)}, f32[1024,512]{1,0:T(8,128)S(1)}, bf16[96,1024]{1,0:T(8,128)(2,1)S(1)}) custom-call(s32[2]{0:T(128)S(1)} %pad_add_fusion.1.place_ref, bf16[4,4,64,1024]{3,2,1,0:T(8,128)(2,1)S(1)} %pad_maximum_fusion.tokens_ref, bf16[48,1024]{1,0:T(8,128)(2,1)S(1)} %reshape.291.rim_ref, ...), custom_call_target="tpu_custom_call" | custom-call | flops 2000000000 | bytes 8000000 | tf_op jit(solution)/shard_map/pallas_call | solution.py:48
  132.4 1.4 copy-done.9
  134.8 9.1 %all-gather.1 = bf16[384,1024]{1,0:T(8,128)(2,1)} all-gather(bf16[96,1024]{1,0:T(8,128)(2,1)S(1)} %get-tuple-element.48), channel_id=3, replica_groups=mesh['blk'=8,'grp'=4] {'grp'}, dimensions={0}, use_global_device_ids=true | all-gather | bytes 983040 | tf_op jit(solution)/shard_map/all_gather | solution.py:646
  144.0 1.6 copy-done.5
  145.6 7.4 %shard_map.221 = (bf16[1024,1024]{1,0:T(8,128)(2,1)S(1)}, f32[1024,512]{1,0:T(8,128)S(1)}, f32[1024,512]{1,0:T(8,128)S(1)}, f32[1024,512]{1,0:T(8,128)S(1)}) custom-call(s32[2]{0:T(128)S(1)} %pad_add_fusion.1.place_ref, bf16[4,4,64,1024]{3,2,1,0:T(8,128)(2,1)S(1)} %copy-done.5, bf16[1024,1024]{1,0:T(8,128)(2,1)} %copy-done, bf16[1024,512]{1,0:T(8,128)(2,1)S(1)} %bitcast.85, ...), custom_call_target="tpu_custom_call" | custom-call | flops 2000000000 | bytes 8000000 | tf_op jit(solution)/shard_map/pallas_call | solution.py:48
  153.0 1.4 copy-done.6
  155.8 1.4 copy-done.8
  158.5 37.3 %shard_map.222 = (f32[64,16,128]{2,1,0:T(8,128)S(1)}, f32[64,16,512]{2,1,0:T(8,128)S(1)}, f32[64,16,512]{2,1,0:T(8,128)}, f32[16,16,512]{2,1,0:T(8,128)S(1)}, f3...) custom-call(bf16[4,96,1024]{2,1,0:T(8,128)(2,1)S(1)} %bitcast.96, ...), custom_call_target="tpu_custom_call" | custom-call | flops 2000000000 | bytes 8000000 | tf_op jit(solution)/shard_map/pallas_call | solution.py:48
  200.6 24.1 %all_to_all.64.came_ref = bf16[8,80,512]{2,1,0:T(8,128)(2,1)S(1)} all-to-all(bf16[8,80,512]{2,1,0:T(8,128)(2,1)S(1)} %broadcast_select_fusion), channel_id=1, replica_groups=mesh['blk'=8,'grp'=4] {'blk'}, dimensions={0} | all-to-all | bytes 1310720 | tf_op jit(solution)/shard_map/all_to_all | solution.py:691
  226.5 79.9 %shard_map.223 = (f32[64,16,512]{2,1,0:T(8,128)}, f32[64,16,512]{2,1,0:T(8,128)}, f32[64,16,512]{2,1,0:T(8,128)}, f32[64,512]{1,0:T(8,128)}, bf16[96,1024]{1,0:T...) custom-call(s32[2]{0:T(128)} %copy-done.25, bf16[8,80,512]{2,1,0:T(8,128)(2,1)} %copy-done.33, ...), custom_call_target="tpu_custom_call" | custom-call | flops 2000000000 | bytes 8000000 | tf_op jit(solution)/shard_map/pallas_call | solution.py:48
  306.4 7.7 %all-gather.2 = bf16[384,1024]{1,0:T(8,128)(2,1)S(1)} all-gather(bf16[96,1024]{1,0:T(8,128)(2,1)} %get-tuple-element.66), channel_id=4, replica_groups=mesh['blk'=8,'grp'=4] {'grp'}, dimensions={0}, use_global_device_ids=true | all-gather | bytes 983040 | tf_op jit(solution)/shard_map/all_gather | solution.py:723
  314.1 6.0 %shard_map.225 = (f32[1024,512]{1,0:T(8,128)S(1)}, f32[48,512]{1,0:T(8,128)S(1)}, f32[96,512]{1,0:T(8,128)S(1)}, f32[4,512]{1,0:T(4,128)S(1)}, f32[1,512]{1,0:T(1,128)S(1)}) custom-call(bf16[4,96,1024]{2,1,0:T(8,128)(2,1)S(1)} %bitcast.97, f32[1024,512]{1,0:T(8,128)} %bitcast.119, bf16[1072,512]{1,0:T(8,128)(2,1)S(1)} %copy-done.27, f32[1024,512]{1,0:T(8,128)} %copy-done.9, ...), custom_call_target="tpu_custom_call" | custom-call | flops 2000000000 | bytes 8000000 | tf_op jit(solution)/shard_map/pallas_call | solution.py:48
  320.2 1.4 copy-done.11
  322.2 1.6 reshape.309
  323.7 1.3 slice_bitcast_fusion.2
  326.4 11.5 %shard_map.224 = (bf16[1024,512]{1,0:T(8,128)(2,1)S(1)}, bf16[4,4,64,1024]{3,2,1,0:T(8,128)(2,1)}, bf16[512,1024]{1,0:T(8,128)(2,1)S(1)}, bf16[1024,512]{1,0:T(8,128)(2,1)}) custom-call(f32[1024,512]{1,0:T(8,128)} %bitcast.104, f32[1024,512]{1,0:T(8,128)} %copy-done.7, f32[1024,512]{1,0:T(8,128)} %copy-done.8, bf16[1024,1024]{1,0:T(8,128)(2,1)} %copy-done.6, ...), custom_call_target="tpu_custom_call" | custom-call | flops 2000000000 | bytes 8000000 | tf_op jit(solution)/shard_map/pallas_call | solution.py:48
  340.5 5.0 concatenate.58
  348.0 2.1 reshape.312
  352.1 14.2 %shard_map.226 = (bf16[4,4,64,1024]{3,2,1,0:T(8,128)(2,1)}, bf16[1024,512]{1,0:T(8,128)(2,1)}, f32[1,1024]{1,0:T(1,128)S(1)}) custom-call(f32[1024,512]{1,0:T(8,128)} %copy-done.11, f32[48,512]{1,0:T(8,128)S(1)} %reshape.310.spill_ref, f32[1024,4]{1,0:T(8,128)S(1)} %bitcast.90, bf16[192,512]{1,0:T(8,128)(2,1)S(1)} %copy-done.14, bf16[1024,1024]{1,0:T(8,128)(2,1)} %copy-done, ...), custom_call_target="tpu_custom_call" | custom-call | flops 2000000000 | bytes 8000000 | tf_op jit(solution)/shard_map/pallas_call | solution.py:48
  366.8 17.3 %all_to_all.65 = f32[8,1,11840]{2,1,0:T(1,128)S(1)} all-to-all(f32[8,1,11840]{2,1,0:T(1,128)S(1)} %copy.154), channel_id=1, replica_groups=mesh['blk'=8,'grp'=4] {'blk'}, dimensions={0} | all-to-all | bytes 757760 | tf_op jit(solution)/shard_map/all_to_all | solution.py:797
  384.1 29.0 %all_to_all.66 = bf16[4,4,64,1024]{3,2,1,0:T(8,128)(2,1)} all-to-all(bf16[4,4,64,1024]{3,2,1,0:T(8,128)(2,1)S(1)} %copy-done.34), channel_id=1, replica_groups=mesh['blk'=8,'grp'=4] {'grp'}, dimensions={0} | all-to-all | bytes 4194304 | tf_op jit(solution)/shard_map/all_to_all | solution.py:769
  413.2 29.1 %all_to_all.67 = bf16[4,4,64,1024]{3,2,1,0:T(8,128)(2,1)} all-to-all(bf16[4,4,64,1024]{3,2,1,0:T(8,128)(2,1)S(1)} %copy-done.35), channel_id=1, replica_groups=mesh['blk'=8,'grp'=4] {'grp'}, dimensions={0} | all-to-all | bytes 4194304 | tf_op jit(solution)/shard_map/all_to_all | solution.py:769
  442.3 28.8 %all_to_all.68 = bf16[8,64,1024]{2,1,0:T(8,128)(2,1)} all-to-all(bf16[8,64,1024]{2,1,0:T(8,128)(2,1)S(1)} %bitcast.95), channel_id=1, replica_groups=mesh['blk'=8,'grp'=4] {'blk'}, dimensions={0} | all-to-all | bytes 2097152 | tf_op jit(solution)/shard_map/all_to_all | solution.py:775
  471.0 2.9 all-to-all-start.9
  474.0 1.4 fusion.8
  475.3 24.8 %all-to-all-done.9 = bf16[32,32,512]{2,1,0:T(8,128)(2,1)S(1)} async-done(((bf16[32,32,512]{2,1,0:T(8,128)(2,1)}), bf16[32,32,512]{2,1,0:T(8,128)(2,1)S(1)}, u32[]{:S(2)}, u32[]{:S(2)}) %all-to-all-start.9) | async-done | bytes 1048608 | tf_op jit(solution)/shard_map/all_to_all | solution.py:782
  501.1 3.6 all-to-all-start.8
  510.1 5.2 all-gather.5
  518.0 1.4 fusion.17
  520.2 1.3 fusion.2
  521.6 2.7 fusion.6
  525.2 2.4 reshape.324
  527.6 2.6 reduce_sum.108
  531.0 2.4 reshape.323
  533.4 2.6 reduce_sum.107
  (202 shorter events, 60.7 us)
Async XLA Ops:
  0.6 24.2 %copy-start.41 = (bf16[64,1024]{1,0:T(8,128)(2,1)S(1)}, bf16[64,1024]{1,0:T(8,128)(2,1)}, u32[]{:S(2)}) copy-start(bf16[64,1024]{1,0:T(8,128)(2,1)} %param.25) | copy-start | bytes 393220
  9.6 19.9 %copy-start.39 = (bf16[32,4096]{1,0:T(8,128)(2,1)S(1)}, bf16[32,4096]{1,0:T(8,128)(2,1)}, u32[]{:S(2)}) copy-start(bf16[32,4096]{1,0:T(8,128)(2,1)} %param.17) | copy-start | bytes 786436
  26.0 28.9 %all-to-all-start.3 = ((bf16[8,64,1024]{2,1,0:T(8,128)(2,1)}), bf16[8,64,1024]{2,1,0:T(8,128)(2,1)S(1)}, u32[]{:S(2)}, u32[]{:S(2)}) async-start(bf16[8,64,1024]{2,1,0:T(8,128)(2,1)} %broadcast_in_dim.84), calls=%async_computation.3 | async-start | bytes 2097152 | tf_op jit(solution)/shard_map/all_to_all | solution.py:29
  30.2 31.5 %copy-start.42 = (s32[4,256]{1,0:T(4,128)S(1)}, s32[4,256]{1,0:T(4,128)}, u32[]{:S(2)}) copy-start(s32[4,256]{1,0:T(4,128)} %param.14) | copy-start | bytes 12292
  55.9 29.7 %all-to-all-start.1 = ((bf16[32,32,512]{2,1,0:T(8,128)(2,1)}), bf16[32,32,512]{2,1,0:T(8,128)(2,1)S(1)}, u32[]{:S(2)}, u32[]{:S(2)}) async-start(bf16[32,32,512]{2,1,0:T(8,128)(2,1)} %bitcast.22), calls=%async_computation.1 | async-start | bytes 2097152 | tf_op jit(solution)/shard_map/all_to_all | solution.py:627
  59.4 58.0 %collective-permute-start.5 = (bf16[4,64,1024]{2,1,0:T(8,128)(2,1)}, bf16[4,64,1024]{2,1,0:T(8,128)(2,1)}, u32[]{:S(2)}, u32[]{:S(2)}) collective-permute-start(bf16[4,64,1024]{2,1,0:T(8,128)(2,1)} %param.15), channel_id=1, source_target_pairs={{0,1},{1,0},{2,3},{3,2},{4,5},{5,4},{6,7},{7,6},{8,9},{9,8},{10,11... | collective-permute-start | bytes 1572872 | tf_op jit(solution)/shard_map/ppermute | solution.py:593
  59.7 55.2 %collective-permute-start.6 = (bf16[4,64,1024]{2,1,0:T(8,128)(2,1)}, bf16[4,64,1024]{2,1,0:T(8,128)(2,1)}, u32[]{:S(2)}, u32[]{:S(2)}) collective-permute-start(bf16[4,64,1024]{2,1,0:T(8,128)(2,1)} %param.15), channel_id=1, source_target_pairs={{0,2},{1,3},{2,0},{3,1},{4,6},{5,7},{6,4},{7,5},{8,10},{9,11},{10,... | collective-permute-start | bytes 1572872 | tf_op jit(solution)/shard_map/ppermute | solution.py:592
  61.4 59.2 %collective-permute-start = (bf16[4,64,1024]{2,1,0:T(8,128)(2,1)}, bf16[4,64,1024]{2,1,0:T(8,128)(2,1)}, u32[]{:S(2)}, u32[]{:S(2)}) collective-permute-start(bf16[4,64,1024]{2,1,0:T(8,128)(2,1)} %param.13), channel_id=1, source_target_pairs={{0,1},{1,0},{2,3},{3,2},{4,5},{5,4},{6,7},{7,6},{8,9},{9,8},{10,11... | collective-permute-start | bytes 1572872 | tf_op jit(solution)/shard_map/ppermute | solution.py:593
  61.4 54.8 %collective-permute-start.1 = (bf16[4,64,1024]{2,1,0:T(8,128)(2,1)}, bf16[4,64,1024]{2,1,0:T(8,128)(2,1)}, u32[]{:S(2)}, u32[]{:S(2)}) collective-permute-start(bf16[4,64,1024]{2,1,0:T(8,128)(2,1)} %param.13), channel_id=1, source_target_pairs={{0,2},{1,3},{2,0},{3,1},{4,6},{5,7},{6,4},{7,5},{8,10},{9,11},{10,... | collective-permute-start | bytes 1572872 | tf_op jit(solution)/shard_map/ppermute | solution.py:592
  61.8 4.9 collective-permute-start.4
  65.7 78.2 %copy-start.25 = (s32[2]{0:T(128)}, s32[2]{0:T(128)S(1)}, u32[]{:S(2)}) copy-start(s32[2]{0:T(128)S(1)} %pad_add_fusion.1.place_ref) | copy-start | bytes 28
  66.7 15.5 %collective-permute-start.3 = (bf16[4,3,1024]{2,1,0:T(4,128)(2,1)S(1)}, bf16[4,3,1024]{2,1,0:T(4,128)(2,1)S(1)}, u32[]{:S(2)}, u32[]{:S(2)}) collective-permute-start(bf16[4,3,1024]{2,1,0:T(4,128)(2,1)S(1)} %get-tuple-element.149), channel_id=1, source_target_pairs={{0,4},{4,8},{8,12},{12,16},{16,20},{20,24},{24,28},{1,5},{5,9},{9,... | collective-permute-start | bytes 73736 | tf_op jit(solution)/shard_map/ppermute | solution.py:603
  86.7 57.2 %all-to-all-start.2 = ((bf16[32,32,512]{2,1,0:T(8,128)(2,1)}), bf16[32,32,512]{2,1,0:T(8,128)(2,1)S(1)}, u32[]{:S(2)}, u32[]{:S(2)}) async-start(bf16[32,32,512]{2,1,0:T(8,128)(2,1)} %bitcast.99), calls=%async_computation.2 | async-start | bytes 2097152 | tf_op jit(solution)/shard_map/all_to_all | solution.py:627
  101.4 57.0 %copy-start.13 = (bf16[192,512]{1,0:T(8,128)(2,1)}, bf16[192,512]{1,0:T(8,128)(2,1)S(1)}, u32[]{:S(2)}) copy-start(bf16[192,512]{1,0:T(8,128)(2,1)S(1)} %copy.143.small_ref) | copy-start | bytes 589828
  114.9 2.5 collective-permute-start.7
  116.2 4.3 collective-permute-start.2
  120.5 1.8 copy-start.1
  131.1 1.4 copy-start
  132.4 1.4 copy-start.9
  144.0 1.6 copy-start.5
  145.6 12.9 %copy-start.2 = (f32[4,4,64,4]{3,0,1,2:T(4,128)S(1)}, f32[4,4,64,4]{3,0,1,2:T(4,128)}, u32[]{:S(2)}) copy-start(f32[4,4,64,4]{3,0,1,2:T(4,128)} %copy.140) | copy-start | bytes 49156
  145.6 12.9 %copy-start.19 = (bf16[384,1024]{1,0:T(8,128)(2,1)S(1)}, bf16[384,1024]{1,0:T(8,128)(2,1)}, u32[]{:S(2)}) copy-start(bf16[384,1024]{1,0:T(8,128)(2,1)} %all-gather.1) | copy-start | bytes 2359300
  153.0 1.4 copy-start.6
  154.4 1.3 copy-start.7
  155.8 1.4 copy-start.8
  157.1 1.3 copy-start.10
  195.7 1.3 copy-start.12
  226.5 87.6 %copy-start.3 = (f32[4,4,64,4]{3,0,1,2:T(4,128)S(1)}, f32[4,4,64,4]{3,0,1,2:T(4,128)}, u32[]{:S(2)}) copy-start(f32[4,4,64,4]{3,0,1,2:T(4,128)} %copy.140) | copy-start | bytes 49156
  226.5 87.6 %copy-start.14 = (bf16[192,512]{1,0:T(8,128)(2,1)S(1)}, bf16[192,512]{1,0:T(8,128)(2,1)}, u32[]{:S(2)}) copy-start(bf16[192,512]{1,0:T(8,128)(2,1)} %copy-done.13) | copy-start | bytes 589828
  226.5 87.6 %copy-start.27 = (bf16[1072,512]{1,0:T(8,128)(2,1)S(1)}, bf16[1072,512]{1,0:T(8,128)(2,1)}, u32[]{:S(2)}) copy-start(bf16[1072,512]{1,0:T(8,128)(2,1)} %copy-done.26) | copy-start | bytes 3293188
  320.2 1.4 copy-start.11
  325.1 25.0 %collective-permute-start.8 = (f32[3,4,512]{2,1,0:T(4,128)}, f32[3,4,512]{2,1,0:T(4,128)}, u32[]{:S(2)}, u32[]{:S(2)}) collective-permute-start(f32[3,4,512]{2,1,0:T(4,128)} %slice_bitcast_fusion.2), channel_id=1, source_target_pairs={{4,0},{8,4},{12,8},{16,12},{20,16},{24,20},{28,24},{5,1},{9,5},{13... | collective-permute-start | bytes 73736 | tf_op jit(solution)/shard_map/ppermute | solution.py:751
  326.4 13.5 %copy-start.37 = (f32[3,4,4,512]{3,2,1,0:T(4,128)S(1)}, f32[3,4,4,512]{3,2,1,0:T(4,128)}, u32[]{:S(2)}) copy-start(f32[3,4,4,512]{3,2,1,0:T(4,128)} %reshape.309) | copy-start | bytes 294916
  326.4 14.2 %copy-start.43 = (f32[1,512]{1,0:T(1,128)S(1)}, f32[1,512]{1,0:T(1,128)}, u32[]{:S(2)}) copy-start(f32[1,512]{1,0:T(1,128)} %get-tuple-element.79) | copy-start | bytes 6148
  340.5 10.3 %copy-start.4 = (f32[4,4,64,4]{3,0,1,2:T(4,128)S(1)}, f32[4,4,64,4]{3,0,1,2:T(4,128)}, u32[]{:S(2)}) copy-start(f32[4,4,64,4]{3,0,1,2:T(4,128)} %copy.140) | copy-start | bytes 49156
  345.5 4.5 copy-start.38
  352.1 14.2 %copy-start.36 = (f32[8,11712]{1,0:T(8,128)S(1)}, f32[8,11712]{1,0:T(8,128)}, u32[]{:S(2)}) copy-start(f32[8,11712]{1,0:T(8,128)} %reshape.312) | copy-start | bytes 1124356
  366.3 17.8 %copy-start.34 = (bf16[4,4,64,1024]{3,2,1,0:T(8,128)(2,1)S(1)}, bf16[4,4,64,1024]{3,2,1,0:T(8,128)(2,1)}, u32[]{:S(2)}) copy-start(bf16[4,4,64,1024]{3,2,1,0:T(8,128)(2,1)} %get-tuple-element.65) | copy-start | bytes 6291460
  384.1 29.0 %copy-start.35 = (bf16[4,4,64,1024]{3,2,1,0:T(8,128)(2,1)S(1)}, bf16[4,4,64,1024]{3,2,1,0:T(8,128)(2,1)}, u32[]{:S(2)}) copy-start(bf16[4,4,64,1024]{3,2,1,0:T(8,128)(2,1)} %get-tuple-element.72) | copy-start | bytes 6291460
  413.2 29.1 %copy-start.16 = (bf16[512,1024]{1,0:T(8,128)(2,1)S(1)}, bf16[512,1024]{1,0:T(8,128)(2,1)}, u32[]{:S(2)}) copy-start(bf16[512,1024]{1,0:T(8,128)(2,1)} %copy-done.15) | copy-start | bytes 3145732
  471.0 33.7 %copy-start.40 = (f32[8,4,32]{2,1,0:T(4,128)S(1)}, f32[8,4,32]{2,1,0:T(4,128)}, u32[]{:S(2)}) copy-start(f32[8,4,32]{2,1,0:T(4,128)} %copy.139) | copy-start | bytes 12292
  471.0 29.1 %all-to-all-start.9 = ((bf16[32,32,512]{2,1,0:T(8,128)(2,1)}), bf16[32,32,512]{2,1,0:T(8,128)(2,1)S(1)}, u32[]{:S(2)}, u32[]{:S(2)}) async-start(bf16[32,32,512]{2,1,0:T(8,128)(2,1)} %bitcast.50), calls=%async_computation.9 | async-start | bytes 2097152 | tf_op jit(solution)/shard_map/all_to_all | solution.py:782
  473.9 43.5 %copy-start.44 = (bf16[32]{0:T(256)(128)(2,1)S(1)}, bf16[32]{0:T(256)(128)(2,1)}, u32[]{:S(2)}) copy-start(bf16[32]{0:T(256)(128)(2,1)} %param.16) | copy-start | bytes 196
  473.9 45.5 %copy-start.28 = (bf16[4,4,64,1024]{3,2,1,0:T(8,128)(2,1)S(1)}, bf16[4,4,64,1024]{3,2,1,0:T(8,128)(2,1)}, u32[]{:S(2)}) copy-start(bf16[4,4,64,1024]{3,2,1,0:T(8,128)(2,1)} %all_to_all.66) | copy-start | bytes 6291460
  501.1 29.9 %all-to-all-start.8 = ((bf16[32,32,512]{2,1,0:T(8,128)(2,1)}), bf16[32,32,512]{2,1,0:T(8,128)(2,1)S(1)}, u32[]{:S(2)}, u32[]{:S(2)}) async-start(bf16[32,32,512]{2,1,0:T(8,128)(2,1)} %bitcast.48), calls=%async_computation.8 | async-start | bytes 2097152 | tf_op jit(solution)/shard_map/all_to_all | solution.py:782
  517.5 2.4 copy-start.29
  521.6 2.8 copy-start.32
  521.6 3.6 copy-start.31
  (11 other events, 10.0 us)

commit v2 on v1

v2 whole, which is shorter than its diff:
```python
import jax
import jax.numpy as jnp
from jax import lax
from jax.experimental import pallas as pl
from jax.experimental.pallas import tpu as pltpu
from jax.sharding import PartitionSpec as P

epsilon = 1e-05
log2_e = 1.4426950408889634
log_2 = 0.6931471805599453
reset_push = 1e6
f32 = jnp.float32
bf16 = jnp.bfloat16
small_rows = 192
both = ("blk", "grp")


def dot(left, right, dims=((1,), (0,))):
    return lax.dot_general(left, right, (dims, ((), ())), preferred_element_type=f32)


def sigmoid(values):
    return 1.0 / (1.0 + jnp.exp(-values))


def spread(block, axis):
    count = lax.axis_size(axis)
    copies = jnp.broadcast_to(block[None], (count,) + block.shape)
    return lax.all_to_all(copies, axis, split_axis=0, concat_axis=0, tiled=True)


def ordering(groups, sequences, me):
    chunks = groups * sequences
    rows = chunks * 8
    out_row = lax.broadcasted_iota(jnp.int32, (rows, rows), 0)
    in_row = lax.broadcasted_iota(jnp.int32, (rows, rows), 1)
    chunk = out_row % chunks
    wanted = (((chunk // sequences) ^ me) * sequences + chunk % sequences) * 8 + out_row // chunks
    return jnp.where(in_row == wanted, 1.0, 0.0).astype(bf16)


def kernel_call(body, micros, outs, scratch, limit, *operands):
    places = [
        pl.BlockSpec(memory_space=pltpu.SMEM)
        if value.dtype == jnp.int32
        else pl.BlockSpec(memory_space=pltpu.VMEM)
        for value in operands
    ]
    flops = micros * 1_150_000_000
    return pl.pallas_call(
        body,
        out_shape=[jax.ShapeDtypeStruct(shape, kind) for shape, kind in outs],
        in_specs=places,
        out_specs=[pl.BlockSpec(memory_space=pltpu.VMEM) for _ in outs],
        scratch_shapes=scratch,
        compiler_params=pltpu.CompilerParams(vmem_limit_bytes=limit << 20),
        cost_estimate=pl.CostEstimate(flops=flops, bytes_accessed=8_000_000, transcendentals=0),
    )(*operands)


def read_rows(slab_refs, block):
    sequences, _, width = slab_refs[0].shape
    at = pl.ds(pl.multiple_of(block * 8, 8), 8)
    parts = [slab[:, at, :].astype(f32) for slab in slab_refs]
    return jnp.concatenate(parts, axis=0).reshape(len(slab_refs) * sequences * 8, width)


def small_row(small_ref, index):
    tail = small_ref[176:192, :].astype(f32)
    return tail[index : index + 1, :]


def assemble(whole_ref, stacks, me):
    for side, stack_ref in enumerate(stacks):
        count = stack_ref.shape[0]
        rows = whole_ref.shape[0] // (2 * count)
        for k in range(count):
            target = pl.ds(pl.multiple_of((me ^ (2 * k + side)) * rows, 8), rows)
            whole_ref[target, :] = stack_ref[k, 0:rows, :]


def entry_kernel(
    place_ref, slab0_ref, slab1_ref, slab2_ref, slab3_ref, rim_ref, gain_ref, mask_ref, near_ref, far_ref, small_ref,
    normed_ref, inner_ref, filter_ref, chosen_ref, weight_ref,
):
    slabs = (slab0_ref, slab1_ref, slab2_ref, slab3_ref)
    groups = len(slabs)
    sequences, steps, width = slab0_ref.shape
    chunks = groups * sequences
    block_rows = chunks * 8
    inner_width = inner_ref.shape[1]
    order = ordering(groups, sequences, place_ref[1])
    assemble(weight_ref, (near_ref, far_ref), place_ref[0])

    def scaled(rows):
        root = lax.rsqrt(jnp.mean(rows * rows, axis=1, keepdims=True) + epsilon)
        return (rows * root * gain_ref[...]).astype(bf16)

    last = dot(order, scaled(read_rows(slabs, steps // 8 - 1))).astype(bf16)
    last = dot(last[block_rows - 3 * chunks :, :], weight_ref[...]).reshape(3, chunks, inner_width)
    rim = dot(scaled(rim_ref[...].astype(f32)), weight_ref[...]).reshape(3, sequences, inner_width)
    rim = jnp.concatenate([rim, last[:, : chunks - sequences, :]], axis=1)
    inner_ref[0 : 3 * chunks, :] = rim.reshape(3 * chunks, inner_width).astype(bf16)
    taps = [small_row(small_ref, k) for k in range(4)]
    offset = small_row(small_ref, 4)

    def lap(block, carry):
        base = pl.multiple_of(block * block_rows, block_rows)
        normed = dot(order, scaled(read_rows(slabs, block))).astype(bf16)
        normed_ref[pl.ds(base, block_rows), :] = normed
        inner = dot(normed, weight_ref[...]).astype(bf16)
        inner_ref[pl.ds(pl.multiple_of(base + 3 * chunks, 16), block_rows), :] = inner
        total = offset
        for k in range(3):
            same = mask_ref[pl.ds(base, block_rows), k : k + 1]
            part = inner_ref[pl.ds(pl.multiple_of(base + k * chunks, 16), block_rows), :]
            total = total + taps[k] * part.astype(f32) * same
        total = total + taps[3] * inner.astype(f32)
        filtered = (total * sigmoid(total)).astype(bf16)
        filter_ref[pl.ds(base, block_rows), :] = filtered.astype(f32)
        chosen = dot(small_ref[64:160, :], filtered, ((1,), (1,)))
        chosen_ref[:, pl.ds(base, block_rows)] = chosen.astype(bf16)
        return carry

    lax.fori_loop(0, steps // 8, lap, 0)


def gate_kernel(
    place_ref, slab0_ref, slab1_ref, slab2_ref, slab3_ref, normed_ref, near_ref, far_ref, exit_near_ref, exit_far_ref,
    rows_ref, value_ref, slope_ref, grad_ref, weight_ref, exit_ref,
):
    slabs = (slab0_ref, slab1_ref, slab2_ref, slab3_ref)
    sequences, steps, width = slab0_ref.shape
    block_rows = len(slabs) * sequences * 8
    order = ordering(len(slabs), sequences, place_ref[1])
    assemble(weight_ref, (near_ref, far_ref), place_ref[0])
    assemble(exit_ref, (exit_near_ref, exit_far_ref), place_ref[0])

    def lap(block, carry):
        at = pl.ds(pl.multiple_of(block * block_rows, block_rows), block_rows)
        ordered = dot(order, read_rows(slabs, block).astype(bf16)).astype(bf16)
        rows_ref[at, :] = ordered
        gating = dot(normed_ref[at, :], weight_ref[...])
        grad_gated = dot(ordered, exit_ref[...], ((1,), (1,)))
        gate = sigmoid(gating)
        value = gating * gate
        value_ref[at, :] = value
        slope_ref[at, :] = grad_gated * (gate * (1.0 + gating * (1.0 - gate)))
        grad_ref[at, :] = (grad_gated * value).astype(bf16).astype(f32)
        return carry

    lax.fori_loop(0, steps // 8, lap, 0)


def fill_rates(small_ref, rates_ref):
    states = rates_ref.shape[0]
    rates = -jnp.exp(small_ref[160 : 160 + states, :].astype(f32)) * log2_e
    for n in range(states):
        rates_ref[n] = jnp.broadcast_to(rates[n : n + 1, :], rates_ref.shape[1:])


def fill_picks(pick_ref):
    depth, width = pick_ref.shape
    source = lax.broadcasted_iota(jnp.int32, (depth, width), 0) % (depth // 2)
    target = lax.broadcasted_iota(jnp.int32, (depth, width), 1) // 128
    pick_ref[...] = jnp.where(source == target, 1.0, 0.0).astype(bf16)


def fill_gates(gates_ref, pick_ref, spread_ref, half):
    steps = gates_ref.shape[0]
    values = gates_ref[:, pl.ds(pl.multiple_of(half * 8, 8), 8), :].reshape(steps * 8, 128)[:, 64:96]
    high = values.astype(bf16)
    rest = (values - high.astype(f32)).astype(bf16)
    pair = jnp.concatenate([high, rest], axis=1)
    span = 2048

    def lap(k, carry):
        columns = pl.ds(pl.multiple_of(k * span, span), span)
        spread_ref[:, columns] = dot(pair, pick_ref[:, columns])
        return carry

    lax.fori_loop(0, spread_ref.shape[1] // span, lap, 0)


def gate_of(spread_ref, t, n):
    return spread_ref[pl.ds(pl.multiple_of(t * 8, 8), 8), n * 128 : (n + 1) * 128]


def lane_slices(width):
    return [slice(k * 128, (k + 1) * 128) for k in range(width // 128)]


def piece_kernel(
    place_ref, chosen_ref, other_ref, mask_ref, small_ref, filter_ref, grad_ref,
    gates_ref, step_ref, slope_ref, end_ref, keep_ref, give_ref, load_ref,
    rates_ref, spread_ref, pick_ref, sum_ref, ahead_ref, back_ref,
):
    me = place_ref[0]
    steps, chunks, width = step_ref.shape
    states = end_ref.shape[0]
    chosen = chosen_ref[...].astype(f32) + other_ref[...].astype(f32)
    padded = jnp.concatenate([chosen, jnp.zeros((32, chosen.shape[1]), f32)], axis=0)
    gates_ref[...] = padded.T.reshape(steps, chunks, 128)
    fill_rates(small_ref, rates_ref)
    fill_picks(pick_ref)
    bias = small_row(small_ref, 5)
    delta = small_ref[0:64, :]

    def delta_lap(block, carry):
        at = pl.ds(pl.multiple_of(block * 8, 8), 8)
        low = gates_ref[at, :, :].reshape(8 * chunks, 128)[:, 0:64]
        high = low.astype(bf16)
        rest = (low - high.astype(f32)).astype(bf16)
        pre = dot(high, delta) + dot(rest, delta) + bias
        grown = jnp.exp(-jnp.abs(pre))
        step = jnp.maximum(pre, 0.0) + jnp.log1p(grown)
        step_ref[at, :, :] = step.reshape(8, chunks, width)
        slope_ref[at, :, :] = (jnp.where(pre >= 0, 1.0, grown) / (1.0 + grown)).reshape(8, chunks, width)
        return carry

    lax.fori_loop(0, steps // 8, delta_lap, 0)

    push = mask_ref[:, 3:4] * reset_push
    gates_ref[:, :, 96:97] = push.reshape(steps, chunks, 1)
    end_ref[...] = jnp.zeros_like(end_ref)
    give_ref[...] = jnp.zeros_like(give_ref)
    keep_ref[...] = jnp.ones_like(keep_ref)
    span = 4
    lanes = lane_slices(width)
    spots = [(j, i) for j in range(span) for i in range(len(lanes))]

    def half_lap(half, carry):
        fill_gates(gates_ref, pick_ref, spread_ref, half)
        at = pl.ds(pl.multiple_of(half * 8, 8), 8)

        def lap(block, totals):
            totals = list(totals)
            pushed, drives, grads = {}, {}, {}
            for j, i in spots:
                t = block * span + j
                step = step_ref[t, at, lanes[i]]
                push = step + gates_ref[t, at, 96:97]
                totals[i] = totals[i] + push
                pushed[j, i] = push
                drives[j, i] = step * filter_ref[t, at, lanes[i]]
                grads[j, i] = grad_ref[t, at, lanes[i]]
            for n in range(states):
                rate = [rates_ref[n, :, one] for one in lanes]
                end = [end_ref[n, at, one] for one in lanes]
                keep = [keep_ref[n, at, one] for one in lanes]
                give = [give_ref[n, at, one] for one in lanes]
                for j in range(span):
                    write = gate_of(spread_ref, block * span + j, n)
                    read = gate_of(spread_ref, block * span + j, states + n)
                    for i in range(len(lanes)):
                        decay = jnp.exp2(pushed[j, i] * rate[i])
                        end[i] = decay * end[i] + drives[j, i] * write
                        keep[i] = keep[i] * decay
                        give[i] = give[i] + keep[i] * (read * grads[j, i])
                for i, one in enumerate(lanes):
                    end_ref[n, at, one] = end[i]
                    keep_ref[n, at, one] = keep[i]
                    give_ref[n, at, one] = give[i]
            return tuple(totals)

        start = tuple(jnp.zeros((8, 128), f32) for _ in lanes)
        totals = lax.fori_loop(0, steps // span, lap, start)
        for i, one in enumerate(lanes):
            sum_ref[at, one] = totals[i]
        return carry

    lax.fori_loop(0, chunks // 8, half_lap, 0)

    sequences = ahead_ref.shape[0] // (states + 4)
    groups = chunks // sequences
    for n in range(states):
        rows = slice(n * sequences, (n + 1) * sequences)
        ahead = jnp.zeros((sequences, width), f32)
        back = jnp.zeros((sequences, width), f32)
        for k in range(groups):
            part = slice(k * sequences, (k + 1) * sequences)
            ahead = keep_ref[n, part, :] * ahead + end_ref[n, part, :]
            other = slice((groups - 1 - k) * sequences, (groups - k) * sequences)
            back = give_ref[n, other, :] + keep_ref[n, other, :] * back
        ahead_ref[rows, :] = ahead
        back_ref[rows, :] = back
    total = jnp.zeros((sequences, width), f32)
    for k in range(groups):
        total = total + sum_ref[k * sequences : (k + 1) * sequences, :]
    held = states * sequences
    for k in range(3):
        term = total.astype(bf16).astype(f32)
        ahead_ref[held + k * sequences : held + (k + 1) * sequences, :] = term
        total = total - term
    ahead_ref[held + 3 * sequences :, :] = jnp.zeros((sequences, width), f32)
    back_ref[held:, :] = ahead_ref[held:, :]

    def load_lap(piece, carry):
        load = jnp.where(piece > me, ahead_ref[...], back_ref[...])
        load_ref[piece] = load.astype(bf16)
        return carry

    lax.fori_loop(0, load_ref.shape[0], load_lap, 0)


def fill_unpicks(unpick_ref, first):
    spot = lax.broadcasted_iota(jnp.int32, unpick_ref.shape, 0) // 128
    column = lax.broadcasted_iota(jnp.int32, unpick_ref.shape, 1)
    unpick_ref[...] = jnp.where(column == spot + first, 1.0, 0.0).astype(bf16)


def forward_kernel(
    place_ref, came_ref, gates_ref, small_ref, step_ref, filter_ref, grad_ref, end_ref, keep_ref, give_ref,
    out_ref, read_sum_ref, enter_ref, arrive_ref,
    rates_ref, spread_ref, pick_ref, product_ref, unpick_ref, passed_ref, whole_ref,
):
    me = place_ref[0]
    steps, chunks, width = step_ref.shape
    states = end_ref.shape[0]
    pieces = came_ref.shape[0]
    sequences = came_ref.shape[1] // (states + 4)
    groups = chunks // sequences
    fill_rates(small_ref, rates_ref)
    fill_picks(pick_ref)
    fill_unpicks(unpick_ref, 64 + states)

    held = states * sequences
    rates = [jnp.broadcast_to(rates_ref[n, 0:1, :], (sequences, width)) for n in range(states)]
    rates = jnp.concatenate(rates, axis=0)

    def step_in(piece, state):
        values = came_ref[piece].astype(f32)
        total = values[held : held + sequences, :]
        for k in range(1, 3):
            total = total + values[held + k * sequences : held + (k + 1) * sequences, :]
        total = jnp.concatenate([total] * states, axis=0)
        return jnp.exp2(total * rates) * state + values[:held, :]

    def step_back(k, state):
        return step_in(pieces - 1 - k, state)

    zero = jnp.zeros((held, width), f32)
    whole_ref[0] = lax.fori_loop(0, me, step_in, zero)
    whole_ref[1] = lax.fori_loop(0, pieces - 1 - me, step_back, zero)
    for n in range(states):
        ahead = whole_ref[0, n * sequences : (n + 1) * sequences, :]
        back = whole_ref[1, n * sequences : (n + 1) * sequences, :]
        for k in range(groups):
            part = slice(k * sequences, (k + 1) * sequences)
            enter_ref[n, part, :] = ahead
            ahead = keep_ref[n, part, :] * ahead + end_ref[n, part, :]
            other = slice((groups - 1 - k) * sequences, (groups - k) * sequences)
            arrive_ref[n, other, :] = back
            back = give_ref[n, other, :] + keep_ref[n, other, :] * back

    rates_ref[states] = jnp.broadcast_to(small_row(small_ref, 6), (8, width))
    span = 4
    lanes = lane_slices(width)
    spots = [(j, i) for j in range(span) for i in range(len(lanes))]

    def half_lap(half, carry):
        fill_gates(gates_ref, pick_ref, spread_ref, half)
        at = pl.ds(pl.multiple_of(half * 8, 8), 8)
        for n in range(states):
            for i, one in enumerate(lanes):
                passed_ref[n, i] = enter_ref[n, at, one]

        def forward(block, inner_carry):
            pushed, drives, grads, outs = {}, {}, {}, {}
            for j, i in spots:
                t = block * span + j
                step = step_ref[t, at, lanes[i]]
                feed = filter_ref[t, at, lanes[i]]
                pushed[j, i] = step + gates_ref[t, at, 96:97]
                drives[j, i] = step * feed
                grads[j, i] = grad_ref[t, at, lanes[i]]
                outs[j, i] = feed * rates_ref[states, :, lanes[i]]
            rows = pl.ds(pl.multiple_of(block * span * 8, span * 8), span * 8)
            for n in range(states):
                rate = [rates_ref[n, :, one] for one in lanes]
                hidden = [passed_ref[n, i] for i in range(len(lanes))]
                seen = []
                for j in range(span):
                    t = block * span + j
                    write = gate_of(spread_ref, t, n)
                    read = gate_of(spread_ref, t, states + n)
                    total = None
                    for i in range(len(lanes)):
                        hidden[i] = jnp.exp2(pushed[j, i] * rate[i]) * hidden[i] + drives[j, i] * write
                        outs[j, i] = outs[j, i] + hidden[i] * read
                        one = grads[j, i] * hidden[i]
                        total = one if total is None else total + one
                    seen.append(total)
                product_ref[rows, n * 128 : (n + 1) * 128] = jnp.concatenate(seen, axis=0).astype(bf16)
                for i in range(len(lanes)):
                    passed_ref[n, i] = hidden[i]
            for j, i in spots:
                out_ref[block * span + j, at, lanes[i]] = outs[j, i]
            return inner_carry

        lax.fori_loop(0, steps // span, forward, 0)
        summed = dot(product_ref[...], unpick_ref[...])
        read_sum_ref[:, at, :] = summed.reshape(steps, 8, 128)
        return carry

    lax.fori_loop(0, chunks // 8, half_lap, 0)


def backward_kernel(
    gates_ref, small_ref, step_ref, slope_ref, filter_ref, grad_ref, read_sum_ref, enter_ref, arrive_ref,
    direct_ref, rank_ref, chosen_ref, decay_ref, skip_ref, bias_ref,
    rates_ref, spread_ref, pick_ref, state_ref, product_ref, unpick_ref, delta_ref, sums_acc_ref,
    passed_ref, total_ref,
):
    steps, chunks, width = step_ref.shape
    states = enter_ref.shape[0]
    fill_rates(small_ref, rates_ref)
    fill_picks(pick_ref)
    fill_unpicks(unpick_ref, 64)
    decay_ref[...] = jnp.zeros_like(decay_ref)
    skip_ref[...] = jnp.zeros_like(skip_ref)
    rates_ref[states] = jnp.broadcast_to(small_row(small_ref, 6), (8, width))
    span = 4
    lanes = lane_slices(width)
    spots = [(j, i) for j in range(span) for i in range(len(lanes))]
    blocks = steps // span

    def half_lap(half, carry):
        fill_gates(gates_ref, pick_ref, spread_ref, half)
        at = pl.ds(pl.multiple_of(half * 8, 8), 8)
        for n in range(states):
            for i, one in enumerate(lanes):
                first = enter_ref[n, at, one]
                state_ref[0, n, i] = first
                passed_ref[n, i] = first

        def forward(block, inner_carry):
            pushed, drives = {}, {}
            for j, i in spots:
                t = block * span + j
                step = step_ref[t, at, lanes[i]]
                pushed[j, i] = step + gates_ref[t, at, 96:97]
                drives[j, i] = step * filter_ref[t, at, lanes[i]]
            for n in range(states):
                rate = [rates_ref[n, :, one] for one in lanes]
                hidden = [passed_ref[n, i] for i in range(len(lanes))]
                for j in range(span):
                    t = block * span + j
                    write = gate_of(spread_ref, t, n)
                    for i in range(len(lanes)):
                        hidden[i] = jnp.exp2(pushed[j, i] * rate[i]) * hidden[i] + drives[j, i] * write
                        state_ref[t + 1, n, i] = hidden[i]
                for i in range(len(lanes)):
                    passed_ref[n, i] = hidden[i]
            return inner_carry

        lax.fori_loop(0, blocks, forward, 0)
        for n in range(states):
            for i, one in enumerate(lanes):
                passed_ref[n, i] = arrive_ref[n, at, one]
                total_ref[n, i] = jnp.zeros((8, 128), f32)

        def backward(k, skips):
            block = blocks - 1 - k
            skips = list(skips)
            raw, feeds, pushed, drives, grads, weighted, slopes = {}, {}, {}, {}, {}, {}, {}
            for j, i in spots:
                t = block * span + j
                step = step_ref[t, at, lanes[i]]
                feed = filter_ref[t, at, lanes[i]]
                grad = grad_ref[t, at, lanes[i]]
                raw[j, i] = step
                feeds[j, i] = feed
                pushed[j, i] = step + gates_ref[t, at, 96:97]
                drives[j, i] = step * feed
                grads[j, i] = grad
                weighted[j, i] = jnp.zeros((8, 128), f32)
                slopes[j, i] = jnp.zeros((8, 128), f32)
                skips[i] = skips[i] + grad * feed
            rows = pl.ds(pl.multiple_of(block * span * 8, span * 8), span * 8)
            for n in range(states):
                rate = [rates_ref[n, :, one] for one in lanes]
                gone = [passed_ref[n, i] for i in range(len(lanes))]
                turns = [total_ref[n, i] for i in range(len(lanes))]
                seen = [None] * span
                for j in reversed(range(span)):
                    t = block * span + j
                    write = gate_of(spread_ref, t, n)
                    read = gate_of(spread_ref, t, states + n)
                    for i in range(len(lanes)):
                        adjoint = read * grads[j, i] + gone[i]
                        weighted[j, i] = weighted[j, i] + adjoint * write
                        one = adjoint * drives[j, i]
                        seen[j] = one if seen[j] is None else seen[j] + one
                        gone[i] = adjoint * jnp.exp2(pushed[j, i] * rate[i])
                        turn = gone[i] * state_ref[t, n, i]
                        slopes[j, i] = slopes[j, i] + turn * rate[i]
                        turns[i] = turns[i] + turn * raw[j, i]
                product_ref[rows, n * 128 : (n + 1) * 128] = jnp.concatenate(seen, axis=0).astype(bf16)
                for i in range(len(lanes)):
                    passed_ref[n, i] = gone[i]
                    total_ref[n, i] = turns[i]
            for j, i in spots:
                t = block * span + j
                grown = slopes[j, i] * log_2 + weighted[j, i] * feeds[j, i]
                delta_ref[t, at, lanes[i]] = grown * slope_ref[t, at, lanes[i]]
                direct = weighted[j, i] * raw[j, i] + grads[j, i] * rates_ref[states, :, lanes[i]]
                direct_ref[t, at, lanes[i]] = direct
            return tuple(skips)

        start = tuple(jnp.zeros((8, 128), f32) for _ in lanes)
        skips = lax.fori_loop(0, blocks, backward, start)
        for i, one in enumerate(lanes):
            skip_ref[0:1, one] += jnp.sum(skips[i], axis=0, keepdims=True)
            for n in range(states):
                part = jnp.sum(total_ref[n, i], axis=0, keepdims=True)
                decay_ref[n : n + 1, one] += part * rates_ref[n, 0:1, one] * log_2
        summed = dot(product_ref[...], unpick_ref[...])
        sums_acc_ref[:, at, :] = summed.reshape(steps, 8, 128) + read_sum_ref[:, at, :]
        return carry

    lax.fori_loop(0, chunks // 8, half_lap, 0)

    rows = steps * chunks
    grads = delta_ref[...].reshape(rows, width)
    bias_ref[...] = jnp.sum(grads, axis=0, keepdims=True)
    grads = grads.astype(bf16)
    low = gates_ref[...].reshape(rows, 128)[:, 0:64].astype(bf16)
    rank_ref[...] = dot(low, grads, ((0,), (0,)))
    back = dot(small_ref[0:64, :], grads, ((1,), (1,)))
    sums = sums_acc_ref[...].reshape(rows, 128).T
    chosen_ref[0:64, :] = back.astype(bf16)
    chosen_ref[64:96, :] = sums[64:96, :].astype(bf16)


def store_rows(keep_ref, send_ref, order, values, block):
    _, sequences, _, width = keep_ref.shape
    back = dot(order, values.astype(bf16), ((0,), (0,)))
    shaped = back.reshape(4, sequences, 8, width).astype(bf16)
    at = pl.ds(pl.multiple_of(block * 8, 8), 8)
    for k in range(4):
        target = send_ref if k % 2 else keep_ref
        target[k // 2, :, at, :] = shaped[k]


def store_blocks(keep_ref, send_ref, me, *parts):
    count = keep_ref.shape[0]
    below = 0
    for values_ref in parts:
        rows = values_ref.shape[0] // (2 * count)
        for k in range(2 * count):
            source = pl.ds(pl.multiple_of((me ^ k) * rows, 8), rows)
            target = send_ref if k % 2 else keep_ref
            target[k // 2, below : below + rows, :] = values_ref[source, :].astype(bf16)
        below += rows


def leave_kernel(
    place_ref, scan_ref, value_ref, slope_ref, rows_ref, normed_ref, exit_near_ref, exit_far_ref,
    gating_ref, out_keep_ref, out_send_ref, exit_grad_ref, keep_ref, send_ref,
    gated_ref, entry_grad_ref, exit_ref,
):
    assemble(exit_ref, (exit_near_ref, exit_far_ref), place_ref[0])
    sequences, steps = out_keep_ref.shape[1:3]
    groups = 4
    block_rows = groups * sequences * 8
    order = ordering(groups, sequences, place_ref[1])

    def lap(block, carry):
        at = pl.ds(pl.multiple_of(block * block_rows, block_rows), block_rows)
        scan_out = scan_ref[at, :].astype(bf16).astype(f32)
        gated = (scan_out * value_ref[at, :]).astype(bf16)
        gated_ref[at, :] = gated
        gating_ref[at, :] = (scan_out * slope_ref[at, :]).astype(bf16)
        store_rows(out_keep_ref, out_send_ref, order, dot(gated, exit_ref[...]), block)
        return carry

    lax.fori_loop(0, steps // 8, lap, 0)
    exit_grad_ref[...] = dot(gated_ref[...], rows_ref[...], ((0,), (0,))).astype(bf16)
    entry_grad_ref[...] = dot(normed_ref[...], gating_ref[...], ((0,), (0,)))
    store_blocks(keep_ref, send_ref, place_ref[0], entry_grad_ref)


def filter_kernel(
    place_ref, chosen_ref, other_ref, direct_ref, inner_ref, filter_ref, mask_ref, small_ref,
    rank_ref, decay_ref, bias_ref, skip_ref,
    grads_ref, spill_ref, first_ref, *refs,
):
    block_refs, (packed_ref, picked_ref, taps_ref, offset_ref) = refs[:-4], refs[-4:]
    rows, width = grads_ref.shape
    chunks = spill_ref.shape[1]
    block_rows = chunks * 8
    chosen = (chosen_ref[...].astype(f32) + other_ref[...].astype(f32)).astype(bf16)
    packed_ref[0:64, :] = rank_ref[...]
    packed_ref[64:160, :] = dot(chosen, filter_ref[...].astype(bf16))
    packed_ref[160:176, :] = decay_ref[...]
    picked_ref[...] = chosen.astype(f32).T.astype(bf16)
    taps = [small_row(small_ref, k) for k in range(4)]
    offset = small_row(small_ref, 4)
    offset_ref[...] = jnp.zeros_like(offset_ref)
    taps_ref[...] = jnp.zeros_like(taps_ref)

    def lap(block, carry):
        base = pl.multiple_of(block * block_rows, block_rows)
        at = pl.ds(base, block_rows)
        total = offset
        shifted = []
        for k in range(4):
            part = inner_ref[pl.ds(pl.multiple_of(base + k * chunks, 16), block_rows), :].astype(f32)
            if k < 3:
                part = part * mask_ref[at, k : k + 1]
            shifted.append(part)
            total = total + taps[k] * part
        gate = sigmoid(total)
        grad = direct_ref[at, :] + dot(picked_ref[at, :], small_ref[64:160, :])
        grad = grad * (gate * (1.0 + total * (1.0 - gate)))
        grads_ref[at, :] = grad
        offset_ref[...] += jnp.sum(grad, axis=0, keepdims=True)
        for k in range(4):
            taps_ref[k : k + 1, :] += jnp.sum(grad * shifted[k], axis=0, keepdims=True)
        return carry

    lax.fori_loop(0, rows // block_rows, lap, 0)
    packed_ref[176:180, :] = taps_ref[...]
    packed_ref[180:181, :] = offset_ref[...]
    packed_ref[181:182, :] = bias_ref[...]
    packed_ref[182:183, :] = skip_ref[...]
    packed_ref[183:192, :] = jnp.zeros((9, width), f32)
    if len(block_refs) == 1:
        block_refs[0][...] = packed_ref[...]
    else:
        for k, block_ref in enumerate(block_refs):
            lanes = pl.ds(pl.multiple_of(((place_ref[0] >> 1) ^ k) * 128, 128), 128)
            block_ref[...] = packed_ref[:, lanes]
    for u in range(3):
        total = jnp.zeros((chunks, width), f32)
        for t in range(u + 1):
            part = slice(t * chunks, (t + 1) * chunks)
            total = total + grads_ref[part, :] * taps[u - t] * mask_ref[part, u - t : u - t + 1]
        spill_ref[u] = total
        first_ref[u] = total[0 : first_ref.shape[1], :]


def inner_kernel(
    grads_ref, spill_ref, after_ref, mask_ref, small_ref, normed_ref,
    inner_ref, entry_grad_ref,
    past_ref,
):
    rows, inner_width = grads_ref.shape
    chunks, sequences = spill_ref.shape[1], after_ref.shape[1]
    block_rows = chunks * 8
    blocks = rows // block_rows
    later_spill = jnp.concatenate([spill_ref[:, sequences:, :], after_ref[...]], axis=1)
    later_spill = later_spill.reshape(3 * chunks, inner_width)
    taps = [small_row(small_ref, k) for k in range(4)]
    rim_rows = 3 * chunks
    for k in range(3):
        past_ref[k, rows : rows + rim_rows, :] = jnp.zeros((rim_rows, inner_width), f32)

    def mask_lap(block, carry):
        at = pl.ds(pl.multiple_of(block * block_rows, block_rows), block_rows)
        grad = grads_ref[at, :]
        for k in range(3):
            past_ref[k, at, :] = grad * taps[k] * mask_ref[at, k : k + 1]
        return carry

    lax.fori_loop(0, blocks, mask_lap, 0)

    def lap(block, carry):
        base = pl.multiple_of(block * block_rows, block_rows)
        at = pl.ds(base, block_rows)
        total = grads_ref[at, :] * taps[3]
        for k in range(3):
            later = pl.ds(pl.multiple_of(base + (3 - k) * chunks, 16), block_rows)
            total = total + past_ref[k, later, :]
        inner_ref[at, :] = total.astype(bf16)

        @pl.when(block == blocks - 1)
        def _():
            tail = total[block_rows - rim_rows :, :] + later_spill
            inner_ref[rows - rim_rows : rows, :] = tail.astype(bf16)

        return carry

    lax.fori_loop(0, blocks, lap, 0)
    entry_grad_ref[...] = dot(normed_ref[...], inner_ref[...], ((0,), (0,))).astype(bf16)


def normed_kernel(
    place_ref, inner_ref, gating_ref, near_ref, far_ref, gate_near_ref, gate_far_ref,
    out_keep_ref, out_send_ref,
    weight_ref, gate_weight_ref,
):
    assemble(weight_ref, (near_ref, far_ref), place_ref[0])
    assemble(gate_weight_ref, (gate_near_ref, gate_far_ref), place_ref[0])
    sequences, steps = out_keep_ref.shape[1:3]
    groups = 4
    block_rows = groups * sequences * 8
    order = ordering(groups, sequences, place_ref[1])

    def lap(block, carry):
        at = pl.ds(pl.multiple_of(block * block_rows, block_rows), block_rows)
        grad = dot(inner_ref[at, :], weight_ref[...], ((1,), (1,)))
        grad = grad + dot(gating_ref[at, :], gate_weight_ref[...], ((1,), (1,)))
        store_rows(out_keep_ref, out_send_ref, order, grad, block)
        return carry

    lax.fori_loop(0, steps // 8, lap, 0)


def part_kernel(keep_ref, came_ref, total_ref, *part_refs):
    total_ref[...] = keep_ref[0].astype(f32) + came_ref[0].astype(f32)
    for k, part_ref in enumerate(part_refs):
        part_ref[...] = (keep_ref[k + 1].astype(f32) + came_ref[k + 1].astype(f32)).astype(bf16)


def side_sum_kernel(place_ref, total_ref, *refs):
    part_refs, out_refs = refs[:-4], refs[-4:]
    total = total_ref[...]
    for part_ref in part_refs:
        total = total + part_ref[...].astype(f32)
    rows = out_refs[0].shape[0]
    for k, out_ref in enumerate(out_refs):
        block = total[0:rows, :]
        for j in range(1, len(out_refs)):
            block = jnp.where((place_ref[1] ^ k) == j, total[j * rows : (j + 1) * rows, :], block)
        out_ref[...] = block.astype(bf16)


def small_sum_kernel(own_ref, *refs):
    part_refs, out_ref = refs[:-1], refs[-1]
    total = own_ref[...]
    for part_ref in part_refs:
        total = total + part_ref[...]
    out_ref[...] = total


def interleave_kernel(place_ref, weight_ref, inner_ref, gate0_ref, gate1_ref, gate2_ref, gate3_ref, out_ref, gain_ref):
    gate_refs = (gate0_ref, gate1_ref, gate2_ref, gate3_ref)
    pieces, groups, rows, width = inner_ref.shape
    for k in range(groups):
        inner = inner_ref[0, k].astype(f32)
        for piece in range(1, pieces):
            inner = inner + inner_ref[piece, k].astype(f32)
        gate = gate_refs[0][...].astype(f32)
        for m in range(1, groups):
            gate = jnp.where((place_ref[1] ^ m) == k, gate_refs[m][...].astype(f32), gate)
        for half, values in enumerate((inner, gate)):
            for j in range(width // 64):
                column = half * groups * width + (j * groups + k) * 64
                out_ref[:, column : column + 64] = values[:, j * 64 : (j + 1) * 64]
    total = jnp.sum(out_ref[...] * weight_ref[...].astype(f32), axis=1, keepdims=True)
    gain_ref[...] = jnp.broadcast_to(total, gain_ref.shape)


def local(
    tokens,
    segments,
    cotangent,
    norm_gain,
    entry_weight,
    kernel_weight,
    kernel_offset,
    select_weight,
    delta_weight,
    timestep_bias,
    decay_log,
    skip_gain,
    exit_weight,
):
    sequences, steps, width = tokens.shape
    pieces, groups = lax.axis_size("blk"), lax.axis_size("grp")
    piece, group = lax.axis_index("blk"), lax.axis_index("grp")
    place = jnp.stack([piece, group]).astype(jnp.int32)
    chunks = groups * sequences
    rows = steps * chunks
    slice_rows, entry_width = entry_weight.shape
    own = kernel_offset.shape[0]
    inner_width = entry_width // 2
    group_width = inner_width // groups
    states = decay_log.shape[0]
    rank = delta_weight.shape[0]

    def flipped(value, axis, bits):
        return lax.ppermute(value, axis, [(i, i ^ bits) for i in range(lax.axis_size(axis))])

    def after(value, *others):
        return lax.optimization_barrier((value,) + others)[0]

    def rounds(*values):
        return lax.optimization_barrier(values)

    packed = jnp.concatenate(
        [
            delta_weight,
            select_weight.T,
            decay_log,
            kernel_weight,
            kernel_offset[None],
            timestep_bias[None],
            skip_gain[None],
            jnp.zeros((small_rows - 183, own), bf16),
        ],
        axis=0,
    )
    def side_blocks(block):
        return [block] + [flipped(block, "blk", 2 * k) for k in range(1, pieces // 2)]

    place_of_gain = (piece * groups + group) * slice_rows
    gain_line = lax.dynamic_update_slice_in_dim(jnp.zeros((width,), bf16), norm_gain, place_of_gain, 0)
    gain_line = jnp.pad(gain_line.reshape(1, -1, group_width), ((0, 0), (0, 8 - width // group_width), (0, 0)))
    halves = entry_weight.reshape(slice_rows, 2, pieces, groups, own).transpose(3, 1, 0, 2, 4)
    halves = halves.reshape(groups, 2 * slice_rows, group_width)
    halves = jnp.concatenate([halves, jnp.broadcast_to(gain_line, (groups,) + gain_line.shape[1:])], axis=1)
    exit_block = jnp.concatenate([exit_weight, jnp.pad(packed.reshape(-1), (0, -packed.size % (16 * width))).reshape(-1, width)])
    halves, exit_block, tokens = rounds(halves, exit_block, tokens)
    halves = lax.all_to_all(halves, "grp", split_axis=0, concat_axis=0, tiled=True)
    exit_side = side_blocks(exit_block)
    token_pair = flipped(tokens, "grp", 2)
    halves, token_pair, tokens, *exit_side = rounds(halves, token_pair, tokens, *exit_side)

    gain_rows = jnp.sum(halves[:, 2 * slice_rows :].astype(f32), axis=0).astype(bf16)
    inner_block = halves[:, :slice_rows].reshape(groups * slice_rows, group_width)
    inner_block = jnp.concatenate([inner_block, gain_rows])
    gate_block = halves[:, slice_rows : 2 * slice_rows].reshape(groups * slice_rows, group_width)
    inner_side = side_blocks(inner_block)
    exit_near = jnp.stack(exit_side)
    exit_far = flipped(exit_near, "blk", 1)
    token_slabs = (tokens, flipped(tokens, "grp", 1), token_pair, flipped(token_pair, "grp", 1))
    exit_near, exit_far, gate_block, cotangent, *rest = rounds(
        exit_near, exit_far, gate_block, cotangent, *inner_side, *token_slabs
    )
    inner_side, token_slabs = rest[: pieces // 2], rest[pieces // 2 :]
    small = jnp.stack([exit_near[:, own:], exit_far[:, own:]], axis=1).reshape(pieces, -1)[:, : packed.size]
    bits = pieces.bit_length() - 1
    small = small.reshape((2,) * bits + (small_rows, own))
    for k in range(bits):
        small = jnp.where((piece >> (bits - 1 - k)) & 1, jnp.flip(small, k), small)
    small = small.reshape(pieces, small_rows, own).transpose(1, 0, 2).reshape(small_rows, group_width)

    inner_near = jnp.stack(inner_side)
    ahead = [(i, i + 1) for i in range(pieces - 1)]
    behind = [(i + 1, i) for i in range(pieces - 1)]
    tails = jnp.stack([slab[:, steps - 3 :] for slab in token_slabs])
    tail = lax.dynamic_index_in_dim(tails, group ^ (groups - 1), 0, keepdims=False)
    rim_source = tail.transpose(1, 0, 2).reshape(3 * sequences, width)
    rim = lax.ppermute(rim_source, "blk", ahead)
    inner_far = flipped(inner_near, "blk", 1)
    gate_block, cotangent = rounds(gate_block, cotangent, inner_near, rim_source)[:2]
    gate_side = side_blocks(gate_block)
    cotangent_pair = flipped(cotangent, "grp", 2)
    label_tail = lax.ppermute(segments[:, -3:], "blk", ahead)
    labels = jnp.concatenate([label_tail, segments], axis=1)
    length = segments.shape[1]
    shifted = jnp.stack([labels[:, k : k + length] for k in range(3)], axis=-1)
    same = (shifted == segments[:, :, None]).astype(f32)
    columns = jnp.concatenate([same, 1.0 - same[:, :, 2:3]], axis=2)
    mask = columns.reshape(sequences, groups, steps, 4).transpose(2, 1, 0, 3).reshape(rows, 4)
    inner_near, inner_far, rim, cotangent_pair, cotangent, *gate_side = rounds(
        inner_near, inner_far, rim, cotangent_pair, cotangent, *gate_side
    )
    gain_all = jnp.sum(inner_near[:, -8:].astype(f32), axis=0) + jnp.sum(inner_far[:, -8:].astype(f32), axis=0)
    gain_all = gain_all[: width // group_width].reshape(1, width)

    gate_near = jnp.stack(gate_side)
    gate_far = flipped(gate_near, "blk", 1)
    cotangent_slabs = (
        cotangent,
        flipped(cotangent, "grp", 1),
        cotangent_pair,
        flipped(cotangent_pair, "grp", 1),
    )

    def group_sum(value):
        half = value.astype(f32) + flipped(value, "grp", 1).astype(f32)
        half = half.astype(bf16)
        return half, flipped(half, "grp", 2)

    normed, inner, filtered, chosen = kernel_call(
        entry_kernel,
        9,
        [
            ((rows, width), bf16),
            ((rows + 3 * chunks, group_width), bf16),
            ((rows, group_width), f32),
            ((96, rows), bf16),
        ],
        [pltpu.VMEM((width, group_width), bf16)],
        40,
        place, *token_slabs, rim, gain_all, mask, inner_near, inner_far, small,
    )
    chosen_pair = group_sum(chosen)
    cotangent_rows, gate_value, gate_slope, grad_scan = kernel_call(
        gate_kernel,
        8,
        [
            ((rows, width), bf16),
            ((rows, group_width), f32),
            ((rows, group_width), f32),
            ((rows, group_width), f32),
        ],
        [pltpu.VMEM((width, group_width), bf16), pltpu.VMEM((group_width, width), bf16)],
        40,
        place, *cotangent_slabs, normed, gate_near, gate_far, exit_near, exit_far,
    )
    cube = (steps, chunks, group_width)
    bank = (states, chunks, group_width)
    load_rows = (states + 4) * sequences
    gates, step_sizes, step_slopes, ends, keeps, gives, loads = kernel_call(
        piece_kernel,
        23,
        [
            ((steps, chunks, 128), f32),
            (cube, f32),
            (cube, f32),
            (bank, f32),
            (bank, f32),
            (bank, f32),
            ((pieces, load_rows, group_width), bf16),
        ],
        [
            pltpu.VMEM((states, 8, group_width), f32),
            pltpu.VMEM((steps * 8, 2 * states * 128), f32),
            pltpu.VMEM((4 * states, 2 * states * 128), bf16),
            pltpu.VMEM((chunks, group_width), f32),
            pltpu.VMEM((load_rows, group_width), f32),
            pltpu.VMEM((load_rows, group_width), f32),
        ],
        48,
        place, *chosen_pair, mask, small, filtered.reshape(cube), grad_scan.reshape(cube),
    )
    came = lax.all_to_all(loads, "blk", split_axis=0, concat_axis=0, tiled=True)

    lanes = group_width // 128
    gate_scratch = [
        pltpu.VMEM((states + 1, 8, group_width), f32),
        pltpu.VMEM((steps * 8, 2 * states * 128), f32),
        pltpu.VMEM((4 * states, 2 * states * 128), bf16),
    ]
    product_scratch = [pltpu.VMEM((steps * 8, states * 128), bf16), pltpu.VMEM((states * 128, 128), bf16)]
    scan_out, read_sums, enter, arrive = kernel_call(
        forward_kernel,
        18,
        [(cube, f32), ((steps, chunks, 128), f32), (bank, f32), (bank, f32)],
        gate_scratch
        + product_scratch
        + [pltpu.VMEM((states, lanes, 8, 128), f32), pltpu.VMEM((2, states * sequences, group_width), f32)],
        48,
        place, came, gates, small, step_sizes, filtered.reshape(cube), grad_scan.reshape(cube), ends, keeps, gives,
    )
    half_slabs = ((2, sequences, steps, width), bf16)
    block_height = groups * slice_rows
    entry_half = ((pieces // 2, block_height, group_width), bf16)
    grad_gating, out_keep, out_send, exit_grad, gate_keep, gate_send = kernel_call(
        leave_kernel,
        12,
        [((rows, group_width), bf16), half_slabs, half_slabs, ((group_width, width), bf16), entry_half, entry_half],
        [
            pltpu.VMEM((rows, group_width), bf16),
            pltpu.VMEM((width, group_width), f32),
            pltpu.VMEM((group_width, width), bf16),
        ],
        48,
        place, scan_out.reshape(rows, group_width), gate_value, gate_slope, cotangent_rows, normed, exit_near, exit_far,
    )

    exit_parts = lax.all_to_all(
        exit_grad.reshape(pieces, own, width), "blk", split_axis=0, concat_axis=0, tiled=True
    )
    gate_came = flipped(gate_send, "blk", 1)
    out_came = flipped(out_send, "grp", 1)
    grad_direct, rank_grad, chosen_grad, decay_grad, skip_grad, bias_grad = kernel_call(
        backward_kernel,
        35,
        [
            (cube, f32),
            ((rank, group_width), f32),
            ((96, rows), bf16),
            ((states, group_width), f32),
            ((1, group_width), f32),
            ((1, group_width), f32),
        ],
        gate_scratch
        + [pltpu.VMEM((steps + 1, states, lanes, 8, 128), f32)]
        + product_scratch
        + [
            pltpu.VMEM(cube, f32),
            pltpu.VMEM((steps, chunks, 128), f32),
            pltpu.VMEM((states, lanes, 8, 128), f32),
            pltpu.VMEM((states, lanes, 8, 128), f32),
        ],
        56,
        gates, small, step_sizes, step_slopes, filtered.reshape(cube), after(grad_scan, out_send).reshape(cube),
        read_sums, enter, arrive,
    )
    chosen_grad, exit_parts, gate_came, out_came = rounds(chosen_grad, exit_parts, gate_came, out_came)
    chosen_grads = group_sum(chosen_grad)

    def slab_part(keep, came):
        return (keep[1].astype(f32) + came[1].astype(f32)).astype(bf16)

    gate_total, *gate_side_parts = kernel_call(
        part_kernel,
        2,
        [(entry_half[0][1:], f32)] + [(entry_half[0][1:], bf16)] * (pieces // 2 - 1),
        [],
        16,
        gate_keep, gate_came,
    )
    gate_side_parts = [flipped(part, "blk", 2 * k + 2) for k, part in enumerate(gate_side_parts)]
    out_other = flipped(after(slab_part(out_keep, out_came), chosen_grads[1]), "grp", 2)

    paired = 2 * own == 128
    small_block = (small_rows, 128 if paired else group_width)
    grad_sums, spill, first_spill, *small_grads = kernel_call(
        filter_kernel,
        6,
        [
            ((rows, group_width), f32),
            ((3, chunks, group_width), f32),
            ((3, sequences, group_width), f32),
        ]
        + [(small_block, f32)] * (pieces // 2 if paired else 1),
        [
            pltpu.VMEM((small_rows, group_width), f32),
            pltpu.VMEM((rows, 96), bf16),
            pltpu.VMEM((4, group_width), f32),
            pltpu.VMEM((1, group_width), f32),
        ],
        48,
        place, *chosen_grads, grad_direct.reshape(rows, group_width), inner, filtered, mask, small,
        rank_grad, decay_grad, bias_grad, skip_grad,
    )
    spill_after = lax.ppermute(first_spill, "blk", behind)
    gate_total, grad_sums, *gate_side_parts = rounds(gate_total, grad_sums, *gate_side_parts)
    gate_blocks = kernel_call(
        side_sum_kernel,
        2,
        [((slice_rows, group_width), bf16)] * groups,
        [],
        16,
        place, gate_total, *gate_side_parts,
    )
    gate_blocks = [gate_blocks[0]] + [flipped(gate_blocks[k], "grp", k) for k in range(1, groups)]
    grad_inner, inner_entry = kernel_call(
        inner_kernel,
        6,
        [((rows, group_width), bf16), ((width, group_width), bf16)],
        [pltpu.VMEM((3, rows + 3 * chunks, group_width), f32)],
        48,
        grad_sums, spill, spill_after, mask, small, normed,
    )
    if paired:
        came_small = [small_grads[0]] + [flipped(small_grads[k], "blk", 2 * k) for k in range(1, pieces // 2)]
    else:
        came_small = small_grads
    grad_inner, inner_entry, out_other, *rest = rounds(grad_inner, inner_entry, out_other, *gate_blocks, *came_small)
    gate_blocks, came_small = rest[:groups], rest[groups:]
    inner_parts = lax.all_to_all(
        inner_entry.reshape(pieces * groups, slice_rows, group_width), both, split_axis=0, concat_axis=0, tiled=True
    )
    grad_keep, grad_send = kernel_call(
        normed_kernel,
        10,
        [half_slabs, half_slabs],
        [pltpu.VMEM((width, group_width), bf16), pltpu.VMEM((width, group_width), bf16)],
        48,
        place, grad_inner, grad_gating, inner_near, inner_far, gate_near, gate_far,
    )
    grad_came = flipped(grad_send, "grp", 1)
    grad_other = flipped(slab_part(grad_keep, grad_came), "grp", 2)
    residual = tokens.astype(f32)
    block_out = residual + out_keep[0].astype(f32) + out_came[0].astype(f32) + out_other.astype(f32)
    block_out = block_out.astype(bf16)
    exit_out = jnp.sum(exit_parts.astype(f32), axis=0)
    inner_parts = inner_parts.reshape(pieces, groups, slice_rows, group_width)
    if own == 64:
        entry_out, gain_out = kernel_call(
            interleave_kernel,
            3,
            [((slice_rows, entry_width), f32), ((slice_rows, 128), f32)],
            [],
            16,
            place, entry_weight, inner_parts, *gate_blocks,
        )
        gain_out = gain_out[:, 0]
    else:
        inner_sum = jnp.sum(inner_parts.astype(f32), axis=0)
        gate_parts = jnp.stack(gate_blocks).astype(f32)
        for k in range(2):
            pairs = gate_parts.reshape(2, 2, slice_rows, group_width)
            gate_parts = jnp.where((group >> (1 - k)) & 1, jnp.flip(pairs, k), pairs)
        entry_parts = jnp.stack([inner_sum, gate_parts.reshape(inner_sum.shape)], axis=0)
        entry_parts = entry_parts.reshape(2, groups, slice_rows, pieces, own)
        entry_out = entry_parts.transpose(2, 0, 3, 1, 4).reshape(slice_rows, entry_width)
        gain_out = jnp.sum(entry_out * entry_weight.astype(f32), axis=1)
    gain_out = gain_out / norm_gain.astype(f32)

    if paired:
        small_sum = kernel_call(small_sum_kernel, 1, [(small_block, f32)], [], 16, *came_small)[0]
        small_sum = small_sum + flipped(small_sum, "blk", 1)
        mine = lax.dynamic_slice_in_dim(small_sum, (piece & 1) * own, own, 1)
    else:
        split = came_small[0].reshape(small_rows, pieces, own).transpose(1, 0, 2)
        came_small = lax.all_to_all(split, "blk", split_axis=0, concat_axis=0, tiled=True)
        mine = jnp.sum(came_small, axis=0)

    grad_hat = grad_keep[0].astype(f32) + grad_came[0].astype(f32) + grad_other.astype(f32)
    grad_hat = grad_hat * gain_all[0]
    root = lax.rsqrt(jnp.mean(residual * residual, axis=2, keepdims=True) + epsilon)
    hat_own = residual * root
    grad_input = root * (grad_hat - hat_own * jnp.mean(grad_hat * hat_own, axis=2, keepdims=True))
    input_grad = (cotangent.astype(f32) + grad_input).astype(bf16)
    return (
        block_out,
        input_grad,
        gain_out,
        entry_out,
        mine[176:180],
        mine[180],
        mine[64:160].T,
        mine[0:64],
        mine[181],
        mine[160:176],
        mine[182],
        exit_out,
    )


def solution(mesh):
    placed = (
        P(None, both, None),
        P(None, "blk"),
        P(None, both, None),
        P(both),
        P(both, None),
        P(None, both),
        P(both),
        P(both, None),
        P(None, both),
        P(both),
        P(None, both),
        P(both),
        P(both, None),
    )
    return jax.shard_map(
        local,
        mesh=mesh,
        in_specs=placed,
        out_specs=(
            P(None, both, None),
            P(None, both, None),
            P(both),
            P(both, None),
            P(None, both),
            P(both),
            P(both, None),
            P(None, both),
            P(both),
            P(None, both),
            P(both),
            P(both, None),
        ),
        check_vma=False,
    )
```

time: 540 us -> 322 us (0.60)
  blocking collectives: 175 us -> 20.7 us
  local copies, waits for them, and re-layouts: 74.9 us -> 33.7 us
  Pallas kernels: 165 us -> 135 us
  starting transfers between devices: 45.2 us -> 65.9 us
  other arithmetic: 23.5 us -> 17.1 us
    all_to_all x5 -> x0, blocking collectives: 119 us -> none  [the longest x2 58.1 us: gathered_sum(): came = lax.all_to_all(parts, 'grp', split_axis=0, concat_axis=0, tiled=True)]
    all_to_all x5 -> x3, waiting for transfers between devices: 52.2 us -> 0.01 us  [the longest x1 0.01 us: local(): lax.all_to_all(halves, 'grp', split_axis=0, concat_axis=0, tiled=True)]
    ppermute x8 -> x39, waiting for transfers between devices: 0.33 us -> 46 us  [the longest x37 44.8 us: flipped(): lax.ppermute(value, axis, [(i, i ^ bits) for i in range(lax.axis_size(axi...]
    all_gather x4 -> x0, blocking collectives: 31.7 us -> none  [the longest x1 9.61 us: local(): tails = lax.all_gather(jnp.concatenate([tail_values, gain_part]), 'grp')]
    pallas_call x7 -> x13, Pallas kernels: 165 us -> 135 us  [kernel_call(): pl.pallas_call(body, out_shape=[jax.ShapeDtypeStruct(shape, kind) for sha...]
    ppermute x8 -> x39, starting transfers between devices: 18.1 us -> 48.5 us  [the longest x37 44 us: flipped(): lax.ppermute(value, axis, [(i, i ^ bits) for i in range(lax.axis_size(axi...]
    all_to_all x5 -> x3, starting transfers between devices: 23.4 us -> 14 us  [the longest x1 6.33 us: local(): lax.all_to_all(inner_entry.reshape(pieces * groups, slice_rows, group_wid...]
    convert_element_type x6 -> x0, local copies, waits for them, and re-layouts: 7.68 us -> none  [the longest x2 4.8 us: entry_half(): summed = jnp.sum(came.astype(f32), axis=0)]
  transfers between devices with their start and end apart: 14 -> 43, of which waited for: 5 -> 13; matrix products, arithmetic and copies ran while one was open for 10% -> 6% of each run, Pallas kernels for 4% -> 20%
where the time goes in v2:
time: 322 us; the launch traced here: 321 us
  Pallas kernels  135 us (42%)
  starting transfers between devices  65.9 us (20%)
  waiting for transfers between devices  47.2 us (15%)
  local copies, waits for them, and re-layouts  33.7 us (10%)
  blocking collectives  20.7 us (6%)
  other arithmetic  17.1 us (5%)
    pallas_call x13, Pallas kernels, kernel_call(): pl.pallas_call(body, out_shape=[jax.ShapeDtypeStruct(shape, kind) for sha...  135 us
    ppermute x37, waiting for transfers between devices, flipped(): lax.ppermute(value, axis, [(i, i ^ bits) for i in range(lax.axis_size(axi...  44.8 us
    ppermute x37, starting transfers between devices, flipped(): lax.ppermute(value, axis, [(i, i ^ bits) for i in range(lax.axis_size(axi...  44 us
    unnamed x125, local copies, waits for them, and re-layouts  22.2 us
    all_to_all x1, blocking collectives, local(): came = lax.all_to_all(loads, 'blk', split_axis=0, concat_axis=0, tiled=True)  20.7 us
  transfers between devices with their start and end apart: 43, of which 13 were waited for; matrix products, arithmetic and copies ran while one was open for 6% of the time, Pallas kernels for 20%

profile of v2, /device:TPU:0, one launch (start us, length us, event | category | flops | bytes accessed | tf_op | source)
XLA Modules:
  0.0 320.8 jit_solution(7487852414226438003)
XLA Ops:
  1.7 1.5 reshape.125
  5.5 3.0 collective-permute-start
  8.5 1.6 collective-permute-start.1
  10.1 2.6 collective-permute-start.2
  12.9 3.5 %all-to-all-start = ((bf16[4,72,512]{2,1,0:T(8,128)(2,1)}), bf16[4,72,512]{2,1,0:T(8,128)(2,1)S(1)}, u32[]{:S(2)}, u32[]{:S(2)}) async-start(bf16[4,72,512]{2,1,0:T(8,128)(2,1)} %pad_maximum_fusion.3), calls=%async_computation | async-start | bytes 589824 | tf_op jit(solution)/shard_map/all_to_all | solution.py:817
  16.4 3.4 %collective-permute-start.16 = (s32[4,3]{1,0:T(4,128)S(1)}, s32[4,3]{1,0:T(4,128)S(1)}, u32[]{:S(2)}, u32[]{:S(2)}) collective-permute-start(s32[4,3]{1,0:T(4,128)S(1)} %slice.112), channel_id=1, source_target_pairs={{0,4},{4,8},{8,12},{12,16},{16,20},{20,24},{24,28},{1,5},{5,9},{9,... | collective-permute-start | bytes 152 | tf_op jit(solution)/shard_map/ppermute | solution.py:852
  21.2 3.9 %collective-permute-done.2 = bf16[80,1024]{1,0:T(8,128)(2,1)S(1)} collective-permute-done((bf16[80,1024]{1,0:T(8,128)(2,1)S(1)}, bf16[80,1024]{1,0:T(8,128)(2,1)S(1)}, u32[]{:S(2)}, u32[]{:S(2)}) %collective-permute-start.2) | collective-permute-done | bytes 163872 | tf_op jit(solution)/shard_map/ppermute | solution.py:785
  26.0 1.6 collective-permute-start.4
  27.6 2.4 collective-permute-start.5
  31.6 1.7 collective-permute-done.5
  33.3 3.2 collective-permute-start.7
  37.0 6.4 %collective-permute-done.6 = bf16[136,512]{1,0:T(8,128)(2,1)} collective-permute-done((bf16[136,512]{1,0:T(8,128)(2,1)S(1)}, bf16[136,512]{1,0:T(8,128)(2,1)}, u32[]{:S(2)}, u32[]{:S(2)}) %collective-permute-start.6) | collective-permute-done | bytes 139296 | tf_op jit(solution)/shard_map/ppermute | solution.py:785
  46.5 3.2 collective-permute-start.13
  50.6 3.3 %collective-permute-start.11 = (bf16[12,1024]{1,0:T(8,128)(2,1)S(1)}, bf16[12,1024]{1,0:T(8,128)(2,1)S(1)}, u32[]{:S(2)}, u32[]{:S(2)}) collective-permute-start(bf16[12,1024]{1,0:T(8,128)(2,1)S(1)} %reshape.132), channel_id=1, source_target_pairs={{0,4},{4,8},{8,12},{12,16},{16,20},{20,24},{24,28},{1,5},{5,9},{9,... | collective-permute-start | bytes 73736 | tf_op jit(solution)/shard_map/ppermute | solution.py:847
  53.9 2.1 collective-permute-start.10
  60.6 6.7 %collective-permute-done.15 = bf16[128,512]{1,0:T(8,128)(2,1)} collective-permute-done((bf16[128,512]{1,0:T(8,128)(2,1)}, bf16[128,512]{1,0:T(8,128)(2,1)}, u32[]{:S(2)}, u32[]{:S(2)}) %collective-permute-start.15) | collective-permute-done | bytes 131104 | tf_op jit(solution)/shard_map/ppermute | solution.py:785
  69.7 1.4 collective-permute-start.21
  75.0 9.7 %shard_map.220 = (bf16[1024,1024]{1,0:T(8,128)(2,1)S(1)}, bf16[1072,512]{1,0:T(8,128)(2,1)S(1)}, f32[1024,512]{1,0:T(8,128)S(1)}, bf16[96,1024]{1,0:T(8,128)(2,1)S(1)}) custom-call(s32[2]{0:T(128)S(1)} %pad_add_fusion.1.place_ref, bf16[4,64,1024]{2,1,0:T(8,128)(2,1)S(1)} %copy-done, bf16[4,64,1024]{2,1,0:T(8,128)(2,1)S(1)} %copy-done.14, ...), custom_call_target="tpu_custom_call" | custom-call | flops 10350000128 | bytes 8000000 | tf_op jit(solution)/shard_map/pallas_call | solution.py:50
  88.4 1.4 collective-permute-done.17
  90.5 7.9 %shard_map.221 = (bf16[1024,1024]{1,0:T(8,128)(2,1)S(1)}, f32[1024,512]{1,0:T(8,128)S(1)}, f32[1024,512]{1,0:T(8,128)S(1)}, f32[1024,512]{1,0:T(8,128)S(1)}) custom-call(s32[2]{0:T(128)S(1)} %pad_add_fusion.1.place_ref, bf16[4,64,1024]{2,1,0:T(8,128)(2,1)S(1)} %copy-done.2, bf16[4,64,1024]{2,1,0:T(8,128)(2,1)S(1)} %collective-permute-done.19.slab1_ref, ...), custom_call_target="tpu_custom_call" | custom-call | flops 9200000000 | bytes 8000000 | tf_op jit(solution)/shard_map/pallas_call | solution.py:50
  101.1 1.4 copy-done.31
  103.8 22.6 %shard_map.222 = (f32[64,16,128]{2,1,0:T(8,128)S(1)}, f32[64,16,512]{2,1,0:T(8,128)S(1)}, f32[64,16,512]{2,1,0:T(8,128)}, f32[16,16,512]{2,1,0:T(8,128)S(1)}, f3...) custom-call(s32[2]{0:T(128)S(1)} %pad_add_fusion.1.place_ref, ...), custom_call_target="tpu_custom_call" | custom-call | flops 26449999872 | bytes 8000000 | tf_op jit(solution)/shard_map/pallas_call | solution.py:50
  127.8 20.7 %all_to_all.20.came_ref = bf16[8,80,512]{2,1,0:T(8,128)(2,1)S(1)} all-to-all(bf16[8,80,512]{2,1,0:T(8,128)(2,1)S(1)} %get-tuple-element.156), channel_id=1, replica_groups=mesh['blk'=8,'grp'=4] {'blk'}, dimensions={0} | all-to-all | bytes 1310720 | tf_op jit(solution)/shard_map/all_to_all | solution.py:932
  148.4 21.9 %shard_map.223 = (f32[64,16,512]{2,1,0:T(8,128)}, f32[64,16,128]{2,1,0:T(8,128)S(1)}, f32[16,16,512]{2,1,0:T(8,128)S(1)}, f32[16,16,512]{2,1,0:T(8,128)S(1)}) custom-call(s32[2]{0:T(128)S(1)} %pad_add_fusion.1.place_ref, bf16[8,80,512]{2,1,0:T(8,128)(2,1)S(1)} %all_to_all.20.came_ref, f32[64,16,128]{2,1,0:T(8,128)S(1)} %get-tuple-element.157.gates_ref, ...), custom_call_target="tpu_custom_call" | custom-call | flops 20700000256 | bytes 8000000 | tf_op jit(solution)/shard_map/pallas_call | solution.py:50
  172.7 11.4 %shard_map.224 = (bf16[1024,512]{1,0:T(8,128)(2,1)S(1)}, bf16[2,4,64,1024]{3,2,1,0:T(8,128)(2,1)S(1)}, bf16[2,4,64,1024]{3,2,1,0:T(8,128)(2,1)}, bf16[512,1024]{...) custom-call(s32[2]{0:T(128)S(1)} %pad_add_fusion.1.place_ref, f32[1024,512]{1,0:T(8,128)} %bitcast.138, ...), custom_call_target="tpu_custom_call" | custom-call | flops 13799999488 | bytes 8000000 | tf_op jit(solution)/shard_map/pallas_call | solution.py:50
  187.0 4.2 %all-to-all-start.2 = ((bf16[8,64,1024]{2,1,0:T(8,128)(2,1)}), bf16[8,64,1024]{2,1,0:T(8,128)(2,1)}, u32[]{:S(2)}, u32[]{:S(2)}) async-start(bf16[8,64,1024]{2,1,0:T(8,128)(2,1)} %bitcast.116), calls=%async_computation.2 | async-start | bytes 2097152 | tf_op jit(solution)/shard_map/all_to_all | solution.py:967
  191.3 36.9 %shard_map.225 = (f32[64,16,512]{2,1,0:T(8,128)}, f32[64,512]{1,0:T(8,128)}, bf16[96,1024]{1,0:T(8,128)(2,1)}, f32[16,512]{1,0:T(8,128)}, f32[1,512]{1,0:T(1,128)}, /*index=5*/f32[1,512]{1,0:T(1,128)}) custom-call(f32[64,16,128]{2,1,0:T(8,128)} %copy-done.38, bf16[192,512]{1,0:T(8,128)(2,1)} %copy-done.9, f32[64,16,512]{2,1,0:T(8,128)} %copy-done.36, ...), custom_call_target="tpu_custom_call" | custom-call | flops 40249999360 | bytes 8000000 | tf_op jit(solution)/shard_map/pallas_call | solution.py:50
  228.5 1.4 collective-permute-done.24
  230.9 1.4 collective-permute-start.25
  234.6 2.0 collective-permute-start.26
  236.5 2.4 collective-permute-start.27
  239.1 6.1 %shard_map.227 = (f32[1024,512]{1,0:T(8,128)S(1)}, f32[3,16,512]{2,1,0:T(8,128)S(1)}, f32[3,4,512]{2,1,0:T(4,128)S(1)}, f32[192,128]{1,0:T(8,128)S(1)}, f32[192,...) custom-call(s32[2]{0:T(128)S(1)} %pad_add_fusion.1.place_ref, ...), custom_call_target="tpu_custom_call" | custom-call | flops 6899999744 | bytes 8000000 | tf_op jit(solution)/shard_map/pallas_call | solution.py:50
  245.3 4.2 %collective-permute-done.27.refs_1_ = bf16[128,512]{1,0:T(8,128)(2,1)S(1)} collective-permute-done((bf16[128,512]{1,0:T(8,128)(2,1)S(1)}, bf16[128,512]{1,0:T(8,128)(2,1)S(1)}, u32[]{:S(2)}, u32[]{:S(2)}) %collective-permute-start.27) | collective-permute-done | bytes 131104 | tf_op jit(solution)/shard_map/ppermute | solution.py:785
  257.1 2.0 collective-permute-start.34
  259.1 2.8 collective-permute-start.35
  262.1 4.5 %shard_map.228 = (bf16[1024,512]{1,0:T(8,128)(2,1)S(1)}, bf16[1024,512]{1,0:T(8,128)(2,1)S(1)}) custom-call(f32[1024,512]{1,0:T(8,128)S(1)} %get-tuple-element.191.grads_ref, f32[3,16,512]{2,1,0:T(8,128)S(1)} %get-tuple-element.192.spill_ref, f32[3,4,512]{2,1,0:T(4,128)S(1)} %collective-permute-done.29.after_ref, f32[1024,4]{1,0:T(8,128)S(1)} %bitcast.105, ...), custom_call_target="tpu_custom_call" | custom-call | flops 6899999744 | bytes 8000000 | tf_op jit(solution)/shard_map/pallas_call | solution.py:50
  267.6 2.2 collective-permute-done.35.refs_1_
  269.8 10.5 %shard_map.230 = (bf16[2,4,64,1024]{3,2,1,0:T(8,128)(2,1)S(1)}, bf16[2,4,64,1024]{3,2,1,0:T(8,128)(2,1)}) custom-call(s32[2]{0:T(128)S(1)} %pad_add_fusion.1.place_ref, bf16[1024,512]{1,0:T(8,128)(2,1)S(1)} %get-tuple-element.210.inner_ref, bf16[1024,512]{1,0:T(8,128)(2,1)} %copy-done.33, bf16[4,136,512]{2,1,0:T(8,128)(2,1)S(1)} %pad_maximum_fusion.1.near_ref, ...), custom_call_target="tpu_custom_call" | custom-call | flops 11500000256 | bytes 8000000 | tf_op jit(solution)/shard_map/pallas_call | solution.py:50
  280.6 6.3 %all-to-all-start.3 = ((bf16[32,32,512]{2,1,0:T(8,128)(2,1)}), bf16[32,32,512]{2,1,0:T(8,128)(2,1)}, u32[]{:S(2)}, u32[]{:S(2)}) async-start(bf16[32,32,512]{2,1,0:T(8,128)(2,1)} %bitcast.101), calls=%async_computation.3 | async-start | bytes 2097152 | tf_op jit(solution)/shard_map/all_to_all | solution.py:1059
  287.0 2.1 convert_reduce_fusion
  289.1 1.8 collective-permute-start.39
  290.9 2.1 fusion.13
  293.0 1.5 collective-permute-start.38
  294.4 5.0 %collective-permute-done.39 = f32[192,128]{1,0:T(8,128)S(1)} collective-permute-done((f32[192,128]{1,0:T(8,128)S(1)}, f32[192,128]{1,0:T(8,128)S(1)}, u32[]{:S(2)}, u32[]{:S(2)}) %collective-permute-start.39) | collective-permute-done | bytes 98336 | tf_op jit(solution)/shard_map/ppermute | solution.py:785
  302.5 10.6 %collective-permute-done.38 = bf16[4,64,1024]{2,1,0:T(8,128)(2,1)} collective-permute-done((bf16[4,64,1024]{2,1,0:T(8,128)(2,1)}, bf16[4,64,1024]{2,1,0:T(8,128)(2,1)}, u32[]{:S(2)}, u32[]{:S(2)}) %collective-permute-start.38) | collective-permute-done | bytes 524320 | tf_op jit(solution)/shard_map/ppermute | solution.py:785
  313.1 1.6 fusion.2
  314.8 3.1 fusion.6
  317.9 2.3 shard_map.231
  (246 shorter events, 53.8 us)
Async XLA Ops:
  5.5 19.7 %collective-permute-start = (bf16[4,64,1024]{2,1,0:T(8,128)(2,1)S(1)}, bf16[4,64,1024]{2,1,0:T(8,128)(2,1)S(1)}, u32[]{:S(2)}, u32[]{:S(2)}) collective-permute-start(bf16[4,64,1024]{2,1,0:T(8,128)(2,1)S(1)} %copy-done), channel_id=1, source_target_pairs={{0,2},{1,3},{2,0},{3,1},{4,6},{5,7},{6,4},{7,5},{8,10},{9,11},{10,... | collective-permute-start | bytes 1572872 | tf_op jit(solution)/shard_map/ppermute | solution.py:785
  8.5 12.7 %collective-permute-start.1 = (bf16[80,1024]{1,0:T(8,128)(2,1)S(1)}, bf16[80,1024]{1,0:T(8,128)(2,1)S(1)}, u32[]{:S(2)}, u32[]{:S(2)}) collective-permute-start(bf16[80,1024]{1,0:T(8,128)(2,1)S(1)} %pad_maximum_fusion.5), channel_id=1, source_target_pairs={{0,8},{4,12},{8,0},{12,4},{16,24},{20,28},{24,16},{28,20},{1,9},{5... | collective-permute-start | bytes 491528 | tf_op jit(solution)/shard_map/ppermute | solution.py:785
  10.1 15.1 %collective-permute-start.2 = (bf16[80,1024]{1,0:T(8,128)(2,1)S(1)}, bf16[80,1024]{1,0:T(8,128)(2,1)S(1)}, u32[]{:S(2)}, u32[]{:S(2)}) collective-permute-start(bf16[80,1024]{1,0:T(8,128)(2,1)S(1)} %pad_maximum_fusion.5), channel_id=1, source_target_pairs={{0,16},{4,20},{8,24},{12,28},{16,0},{20,4},{24,8},{28,12},{1,17},{... | collective-permute-start | bytes 491528 | tf_op jit(solution)/shard_map/ppermute | solution.py:785
  12.7 12.5 %collective-permute-start.3 = (bf16[80,1024]{1,0:T(8,128)(2,1)S(1)}, bf16[80,1024]{1,0:T(8,128)(2,1)S(1)}, u32[]{:S(2)}, u32[]{:S(2)}) collective-permute-start(bf16[80,1024]{1,0:T(8,128)(2,1)S(1)} %pad_maximum_fusion.5), channel_id=1, source_target_pairs={{0,24},{4,28},{8,16},{12,20},{16,8},{20,12},{24,0},{28,4},{1,25},{... | collective-permute-start | bytes 491528 | tf_op jit(solution)/shard_map/ppermute | solution.py:785
  12.9 12.3 %all-to-all-start = ((bf16[4,72,512]{2,1,0:T(8,128)(2,1)}), bf16[4,72,512]{2,1,0:T(8,128)(2,1)S(1)}, u32[]{:S(2)}, u32[]{:S(2)}) async-start(bf16[4,72,512]{2,1,0:T(8,128)(2,1)} %pad_maximum_fusion.3), calls=%async_computation | async-start | bytes 589824 | tf_op jit(solution)/shard_map/all_to_all | solution.py:817
  16.4 4.7 %collective-permute-start.16 = (s32[4,3]{1,0:T(4,128)S(1)}, s32[4,3]{1,0:T(4,128)S(1)}, u32[]{:S(2)}, u32[]{:S(2)}) collective-permute-start(s32[4,3]{1,0:T(4,128)S(1)} %slice.112), channel_id=1, source_target_pairs={{0,4},{4,8},{8,12},{12,16},{16,20},{20,24},{24,28},{1,5},{5,9},{9,... | collective-permute-start | bytes 152 | tf_op jit(solution)/shard_map/ppermute | solution.py:852
  25.9 30.1 %copy-start.2 = (bf16[4,64,1024]{2,1,0:T(8,128)(2,1)S(1)}, bf16[4,64,1024]{2,1,0:T(8,128)(2,1)}, u32[]{:S(2)}) copy-start(bf16[4,64,1024]{2,1,0:T(8,128)(2,1)} %slab0_ref.1) | copy-start | bytes 1572868
  26.0 17.4 %collective-permute-start.4 = (bf16[4,80,1024]{2,1,0:T(8,128)(2,1)S(1)}, bf16[4,80,1024]{2,1,0:T(8,128)(2,1)}, u32[]{:S(2)}, u32[]{:S(2)}) collective-permute-start(bf16[4,80,1024]{2,1,0:T(8,128)(2,1)S(1)} %pad_maximum_fusion.exit_near_ref), channel_id=1, source_target_pairs={{0,4},{4,0},{8,12},{12,8},{16,20},{20,16},{24,28},{28,24},{1,5},{5... | collective-permute-start | bytes 1966088 | tf_op jit(solution)/shard_map/ppermute | solution.py:785
  27.6 5.8 %collective-permute-start.5 = (bf16[136,512]{1,0:T(8,128)(2,1)S(1)}, bf16[136,512]{1,0:T(8,128)(2,1)S(1)}, u32[]{:S(2)}, u32[]{:S(2)}) collective-permute-start(bf16[136,512]{1,0:T(8,128)(2,1)S(1)} %pad_maximum_fusion.6), channel_id=1, source_target_pairs={{0,8},{4,12},{8,0},{12,4},{16,24},{20,28},{24,16},{28,20},{1,9},{5... | collective-permute-start | bytes 417800 | tf_op jit(solution)/shard_map/ppermute | solution.py:785
  30.0 13.5 %collective-permute-start.8 = (bf16[4,64,1024]{2,1,0:T(8,128)(2,1)S(1)}, bf16[4,64,1024]{2,1,0:T(8,128)(2,1)S(1)}, u32[]{:S(2)}, u32[]{:S(2)}) collective-permute-start(bf16[4,64,1024]{2,1,0:T(8,128)(2,1)S(1)} %copy-done), channel_id=1, source_target_pairs={{0,1},{1,0},{2,3},{3,2},{4,5},{5,4},{6,7},{7,6},{8,9},{9,8},{10,11... | collective-permute-start | bytes 1572872 | tf_op jit(solution)/shard_map/ppermute | solution.py:785
  30.0 13.5 %collective-permute-start.9 = (bf16[4,64,1024]{2,1,0:T(8,128)(2,1)S(1)}, bf16[4,64,1024]{2,1,0:T(8,128)(2,1)}, u32[]{:S(2)}, u32[]{:S(2)}) collective-permute-start(bf16[4,64,1024]{2,1,0:T(8,128)(2,1)S(1)} %collective-permute-done.slab2_ref), channel_id=1, source_target_pairs={{0,1},{1,0},{2,3},{3,2},{4,5},{5,4},{6,7},{7,6},{8,9},{9,8},{10,11... | collective-permute-start | bytes 1572872 | tf_op jit(solution)/shard_map/ppermute | solution.py:785
  30.5 12.9 %collective-permute-start.6 = (bf16[136,512]{1,0:T(8,128)(2,1)S(1)}, bf16[136,512]{1,0:T(8,128)(2,1)}, u32[]{:S(2)}, u32[]{:S(2)}) collective-permute-start(bf16[136,512]{1,0:T(8,128)(2,1)S(1)} %pad_maximum_fusion.6), channel_id=1, source_target_pairs={{0,16},{4,20},{8,24},{12,28},{16,0},{20,4},{24,8},{28,12},{1,17},{... | collective-permute-start | bytes 417800 | tf_op jit(solution)/shard_map/ppermute | solution.py:785
  33.3 10.1 %collective-permute-start.7 = (bf16[136,512]{1,0:T(8,128)(2,1)S(1)}, bf16[136,512]{1,0:T(8,128)(2,1)}, u32[]{:S(2)}, u32[]{:S(2)}) collective-permute-start(bf16[136,512]{1,0:T(8,128)(2,1)S(1)} %pad_maximum_fusion.6), channel_id=1, source_target_pairs={{0,24},{4,28},{8,16},{12,20},{16,8},{20,12},{24,0},{28,4},{1,25},{... | collective-permute-start | bytes 417800 | tf_op jit(solution)/shard_map/ppermute | solution.py:785
  37.0 66.8 %copy-start.4 = (f32[4,4,64,4]{3,0,1,2:T(4,128)}, f32[4,4,64,4]{3,0,1,2:T(4,128)S(1)}, u32[]{:S(2)}) copy-start(f32[4,4,64,4]{3,0,1,2:T(4,128)S(1)} %copy.43) | copy-start | bytes 49156
  46.5 14.1 %collective-permute-start.13 = (bf16[128,512]{1,0:T(8,128)(2,1)}, bf16[128,512]{1,0:T(8,128)(2,1)}, u32[]{:S(2)}, u32[]{:S(2)}) collective-permute-start(bf16[128,512]{1,0:T(8,128)(2,1)} %bitcast.122), channel_id=1, source_target_pairs={{0,8},{4,12},{8,0},{12,4},{16,24},{20,28},{24,16},{28,20},{1,9},{5... | collective-permute-start | bytes 393224 | tf_op jit(solution)/shard_map/ppermute | solution.py:785
  49.6 10.9 %collective-permute-start.14 = (bf16[128,512]{1,0:T(8,128)(2,1)}, bf16[128,512]{1,0:T(8,128)(2,1)}, u32[]{:S(2)}, u32[]{:S(2)}) collective-permute-start(bf16[128,512]{1,0:T(8,128)(2,1)} %bitcast.123), channel_id=1, source_target_pairs={{0,16},{4,20},{8,24},{12,28},{16,0},{20,4},{24,8},{28,12},{1,17},{... | collective-permute-start | bytes 393224 | tf_op jit(solution)/shard_map/ppermute | solution.py:785
  50.6 9.4 %collective-permute-start.11 = (bf16[12,1024]{1,0:T(8,128)(2,1)S(1)}, bf16[12,1024]{1,0:T(8,128)(2,1)S(1)}, u32[]{:S(2)}, u32[]{:S(2)}) collective-permute-start(bf16[12,1024]{1,0:T(8,128)(2,1)S(1)} %reshape.132), channel_id=1, source_target_pairs={{0,4},{4,8},{8,12},{12,16},{16,20},{20,24},{24,28},{1,5},{5,9},{9,... | collective-permute-start | bytes 73736 | tf_op jit(solution)/shard_map/ppermute | solution.py:847
  53.9 14.6 %collective-permute-start.10 = (bf16[4,136,512]{2,1,0:T(8,128)(2,1)S(1)}, bf16[4,136,512]{2,1,0:T(8,128)(2,1)}, u32[]{:S(2)}, u32[]{:S(2)}) collective-permute-start(bf16[4,136,512]{2,1,0:T(8,128)(2,1)S(1)} %pad_maximum_fusion.1.near_ref), channel_id=1, source_target_pairs={{0,4},{4,0},{8,12},{12,8},{16,20},{20,16},{24,28},{28,24},{1,5},{5... | collective-permute-start | bytes 1671176 | tf_op jit(solution)/shard_map/ppermute | solution.py:785
  56.0 12.5 %collective-permute-start.12 = (bf16[4,64,1024]{2,1,0:T(8,128)(2,1)S(1)}, bf16[4,64,1024]{2,1,0:T(8,128)(2,1)}, u32[]{:S(2)}, u32[]{:S(2)}) collective-permute-start(bf16[4,64,1024]{2,1,0:T(8,128)(2,1)S(1)} %copy-done.2), channel_id=1, source_target_pairs={{0,2},{1,3},{2,0},{3,1},{4,6},{5,7},{6,4},{7,5},{8,10},{9,11},{10,... | collective-permute-start | bytes 1572872 | tf_op jit(solution)/shard_map/ppermute | solution.py:785
  60.0 7.3 %collective-permute-start.15 = (bf16[128,512]{1,0:T(8,128)(2,1)}, bf16[128,512]{1,0:T(8,128)(2,1)}, u32[]{:S(2)}, u32[]{:S(2)}) collective-permute-start(bf16[128,512]{1,0:T(8,128)(2,1)} %bitcast.124), channel_id=1, source_target_pairs={{0,24},{4,28},{8,16},{12,20},{16,8},{20,12},{24,0},{28,4},{1,25},{... | collective-permute-start | bytes 393224 | tf_op jit(solution)/shard_map/ppermute | solution.py:785
  60.6 87.9 %copy-start.9 = (bf16[192,512]{1,0:T(8,128)(2,1)}, bf16[192,512]{1,0:T(8,128)(2,1)S(1)}, u32[]{:S(2)}) copy-start(bf16[192,512]{1,0:T(8,128)(2,1)S(1)} %copy.46.small_ref) | copy-start | bytes 589828
  69.7 20.8 %collective-permute-start.21 = (bf16[4,128,512]{2,1,0:T(8,128)(2,1)S(1)}, bf16[4,128,512]{2,1,0:T(8,128)(2,1)S(1)}, u32[]{:S(2)}, u32[]{:S(2)}) collective-permute-start(bf16[4,128,512]{2,1,0:T(8,128)(2,1)S(1)} %pad_maximum_fusion.2.near_ref.gate_near_ref), channel_id=1, source_target_pairs={{0,4},{4,0},{8,12},{12,8},{16,20},{20,16},{24,28},{28,24},{1,5},{5... | collective-permute-start | bytes 1572872 | tf_op jit(solution)/shard_map/ppermute | solution.py:785
  72.4 18.1 %collective-permute-start.19 = (bf16[4,64,1024]{2,1,0:T(8,128)(2,1)S(1)}, bf16[4,64,1024]{2,1,0:T(8,128)(2,1)S(1)}, u32[]{:S(2)}, u32[]{:S(2)}) collective-permute-start(bf16[4,64,1024]{2,1,0:T(8,128)(2,1)S(1)} %copy-done.2), channel_id=1, source_target_pairs={{0,1},{1,0},{2,3},{3,2},{4,5},{5,4},{6,7},{7,6},{8,9},{9,8},{10,11... | collective-permute-start | bytes 1572872 | tf_op jit(solution)/shard_map/ppermute | solution.py:785
  72.4 18.1 %collective-permute-start.20 = (bf16[4,64,1024]{2,1,0:T(8,128)(2,1)}, bf16[4,64,1024]{2,1,0:T(8,128)(2,1)S(1)}, u32[]{:S(2)}, u32[]{:S(2)}) collective-permute-start(bf16[4,64,1024]{2,1,0:T(8,128)(2,1)} %collective-permute-done.12.slab2_ref), channel_id=1, source_target_pairs={{0,1},{1,0},{2,3},{3,2},{4,5},{5,4},{6,7},{7,6},{8,9},{9,8},{10,11... | collective-permute-start | bytes 1572872 | tf_op jit(solution)/shard_map/ppermute | solution.py:785
  88.4 1.4 collective-permute-start.17
  89.9 13.9 %collective-permute-start.18 = (bf16[96,1024]{1,0:T(8,128)(2,1)S(1)}, bf16[96,1024]{1,0:T(8,128)(2,1)S(1)}, u32[]{:S(2)}, u32[]{:S(2)}) collective-permute-start(bf16[96,1024]{1,0:T(8,128)(2,1)S(1)} %add_convert_fusion.3.chosen_ref), channel_id=1, source_target_pairs={{0,2},{1,3},{2,0},{3,1},{4,6},{5,7},{6,4},{7,5},{8,10},{9,11},{10,... | collective-permute-start | bytes 589832 | tf_op jit(solution)/shard_map/ppermute | solution.py:785
  127.7 42.6 %copy-start.38 = (f32[64,16,128]{2,1,0:T(8,128)}, f32[64,16,128]{2,1,0:T(8,128)S(1)}, u32[]{:S(2)}) copy-start(f32[64,16,128]{2,1,0:T(8,128)S(1)} %get-tuple-element.157.gates_ref) | copy-start | bytes 1572868
  185.9 42.3 %collective-permute-start.23 = (bf16[2,4,64,1024]{3,2,1,0:T(8,128)(2,1)}, bf16[2,4,64,1024]{3,2,1,0:T(8,128)(2,1)}, u32[]{:S(2)}, u32[]{:S(2)}) collective-permute-start(bf16[2,4,64,1024]{3,2,1,0:T(8,128)(2,1)} %get-tuple-element.168), channel_id=1, source_target_pairs={{0,1},{1,0},{2,3},{3,2},{4,5},{5,4},{6,7},{7,6},{8,9},{9,8},{10,11... | collective-permute-start | bytes 3145736 | tf_op jit(solution)/shard_map/ppermute | solution.py:785
  185.9 42.2 %collective-permute-start.22 = (bf16[4,128,512]{2,1,0:T(8,128)(2,1)}, bf16[4,128,512]{2,1,0:T(8,128)(2,1)S(1)}, u32[]{:S(2)}, u32[]{:S(2)}) collective-permute-start(bf16[4,128,512]{2,1,0:T(8,128)(2,1)} %get-tuple-element.175), channel_id=1, source_target_pairs={{0,4},{4,0},{8,12},{12,8},{16,20},{20,16},{24,28},{28,24},{1,5},{5... | collective-permute-start | bytes 1572872 | tf_op jit(solution)/shard_map/ppermute | solution.py:785
  187.0 41.2 %all-to-all-start.2 = ((bf16[8,64,1024]{2,1,0:T(8,128)(2,1)}), bf16[8,64,1024]{2,1,0:T(8,128)(2,1)}, u32[]{:S(2)}, u32[]{:S(2)}) async-start(bf16[8,64,1024]{2,1,0:T(8,128)(2,1)} %bitcast.116), calls=%async_computation.2 | async-start | bytes 2097152 | tf_op jit(solution)/shard_map/all_to_all | solution.py:967
  228.2 1.7 collective-permute-start.24
  230.9 8.2 %collective-permute-start.25 = (bf16[96,1024]{1,0:T(8,128)(2,1)S(1)}, bf16[96,1024]{1,0:T(8,128)(2,1)S(1)}, u32[]{:S(2)}, u32[]{:S(2)}) collective-permute-start(bf16[96,1024]{1,0:T(8,128)(2,1)S(1)} %add_convert_fusion.2.chosen_ref), channel_id=1, source_target_pairs={{0,2},{1,3},{2,0},{3,1},{4,6},{5,7},{6,4},{7,5},{8,10},{9,11},{10,... | collective-permute-start | bytes 589832 | tf_op jit(solution)/shard_map/ppermute | solution.py:785
  234.6 10.7 %collective-permute-start.26 = (bf16[128,512]{1,0:T(8,128)(2,1)S(1)}, bf16[128,512]{1,0:T(8,128)(2,1)S(1)}, u32[]{:S(2)}, u32[]{:S(2)}) collective-permute-start(bf16[128,512]{1,0:T(8,128)(2,1)S(1)} %get-tuple-element.188), channel_id=1, source_target_pairs={{0,8},{4,12},{8,0},{12,4},{16,24},{20,28},{24,16},{28,20},{1,9},{5... | collective-permute-start | bytes 393224 | tf_op jit(solution)/shard_map/ppermute | solution.py:785
  236.5 12.9 %collective-permute-start.27 = (bf16[128,512]{1,0:T(8,128)(2,1)S(1)}, bf16[128,512]{1,0:T(8,128)(2,1)S(1)}, u32[]{:S(2)}, u32[]{:S(2)}) collective-permute-start(bf16[128,512]{1,0:T(8,128)(2,1)S(1)} %get-tuple-element.189), channel_id=1, source_target_pairs={{0,16},{4,20},{8,24},{12,28},{16,0},{20,4},{24,8},{28,12},{1,17},{... | collective-permute-start | bytes 393224 | tf_op jit(solution)/shard_map/ppermute | solution.py:785
  238.9 10.6 %collective-permute-start.28 = (bf16[128,512]{1,0:T(8,128)(2,1)S(1)}, bf16[128,512]{1,0:T(8,128)(2,1)S(1)}, u32[]{:S(2)}, u32[]{:S(2)}) collective-permute-start(bf16[128,512]{1,0:T(8,128)(2,1)S(1)} %get-tuple-element.190), channel_id=1, source_target_pairs={{0,24},{4,28},{8,16},{12,20},{16,8},{20,12},{24,0},{28,4},{1,25},{... | collective-permute-start | bytes 393224 | tf_op jit(solution)/shard_map/ppermute | solution.py:785
  250.7 8.4 %collective-permute-start.31 = (bf16[32,512]{1,0:T(8,128)(2,1)S(1)}, bf16[32,512]{1,0:T(8,128)(2,1)S(1)}, u32[]{:S(2)}, u32[]{:S(2)}) collective-permute-start(bf16[32,512]{1,0:T(8,128)(2,1)S(1)} %get-tuple-element.202), channel_id=1, source_target_pairs={{0,1},{1,0},{2,3},{3,2},{4,5},{5,4},{6,7},{7,6},{8,9},{9,8},{10,11... | collective-permute-start | bytes 98312 | tf_op jit(solution)/shard_map/ppermute | solution.py:785
  250.7 11.2 %collective-permute-start.32 = (bf16[32,512]{1,0:T(8,128)(2,1)S(1)}, bf16[32,512]{1,0:T(8,128)(2,1)S(1)}, u32[]{:S(2)}, u32[]{:S(2)}) collective-permute-start(bf16[32,512]{1,0:T(8,128)(2,1)S(1)} %get-tuple-element.203), channel_id=1, source_target_pairs={{0,2},{1,3},{2,0},{3,1},{4,6},{5,7},{6,4},{7,5},{8,10},{9,11},{10,... | collective-permute-start | bytes 98312 | tf_op jit(solution)/shard_map/ppermute | solution.py:785
  251.4 5.7 %collective-permute-start.29 = (f32[3,4,512]{2,1,0:T(4,128)S(1)}, f32[3,4,512]{2,1,0:T(4,128)S(1)}, u32[]{:S(2)}, u32[]{:S(2)}) collective-permute-start(f32[3,4,512]{2,1,0:T(4,128)S(1)} %get-tuple-element.193), channel_id=1, source_target_pairs={{4,0},{8,4},{12,8},{16,12},{20,16},{24,20},{28,24},{5,1},{9,5},{13... | collective-permute-start | bytes 73736 | tf_op jit(solution)/shard_map/ppermute | solution.py:1034
  253.9 13.7 %collective-permute-start.33 = (bf16[32,512]{1,0:T(8,128)(2,1)S(1)}, bf16[32,512]{1,0:T(8,128)(2,1)S(1)}, u32[]{:S(2)}, u32[]{:S(2)}) collective-permute-start(bf16[32,512]{1,0:T(8,128)(2,1)S(1)} %get-tuple-element.204), channel_id=1, source_target_pairs={{0,3},{1,2},{2,1},{3,0},{4,7},{5,6},{6,5},{7,4},{8,11},{9,10},{10,... | collective-permute-start | bytes 98312 | tf_op jit(solution)/shard_map/ppermute | solution.py:785
  255.2 14.6 %collective-permute-start.30 = (bf16[4,64,1024]{2,1,0:T(8,128)(2,1)S(1)}, bf16[4,64,1024]{2,1,0:T(8,128)(2,1)S(1)}, u32[]{:S(2)}, u32[]{:S(2)}) collective-permute-start(bf16[4,64,1024]{2,1,0:T(8,128)(2,1)S(1)} %fusion.12), channel_id=1, source_target_pairs={{0,2},{1,3},{2,0},{3,1},{4,6},{5,7},{6,4},{7,5},{8,10},{9,11},{10,... | collective-permute-start | bytes 1572872 | tf_op jit(solution)/shard_map/ppermute | solution.py:785
  257.1 10.5 %collective-permute-start.34 = (f32[192,128]{1,0:T(8,128)S(1)}, f32[192,128]{1,0:T(8,128)S(1)}, u32[]{:S(2)}, u32[]{:S(2)}) collective-permute-start(f32[192,128]{1,0:T(8,128)S(1)} %get-tuple-element.206), channel_id=1, source_target_pairs={{0,8},{4,12},{8,0},{12,4},{16,24},{20,28},{24,16},{28,20},{1,9},{5... | collective-permute-start | bytes 294920 | tf_op jit(solution)/shard_map/ppermute | solution.py:785
  259.1 10.7 %collective-permute-start.35 = (f32[192,128]{1,0:T(8,128)S(1)}, f32[192,128]{1,0:T(8,128)S(1)}, u32[]{:S(2)}, u32[]{:S(2)}) collective-permute-start(f32[192,128]{1,0:T(8,128)S(1)} %get-tuple-element.207), channel_id=1, source_target_pairs={{0,16},{4,20},{8,24},{12,28},{16,0},{20,4},{24,8},{28,12},{1,17},{... | collective-permute-start | bytes 294920 | tf_op jit(solution)/shard_map/ppermute | solution.py:785
  262.0 7.8 %collective-permute-start.36 = (f32[192,128]{1,0:T(8,128)S(1)}, f32[192,128]{1,0:T(8,128)S(1)}, u32[]{:S(2)}, u32[]{:S(2)}) collective-permute-start(f32[192,128]{1,0:T(8,128)S(1)} %get-tuple-element.208), channel_id=1, source_target_pairs={{0,24},{4,28},{8,16},{12,20},{16,8},{20,12},{24,0},{28,4},{1,25},{... | collective-permute-start | bytes 294920 | tf_op jit(solution)/shard_map/ppermute | solution.py:785
  280.3 10.6 %collective-permute-start.37 = (bf16[2,4,64,1024]{3,2,1,0:T(8,128)(2,1)}, bf16[2,4,64,1024]{3,2,1,0:T(8,128)(2,1)}, u32[]{:S(2)}, u32[]{:S(2)}) collective-permute-start(bf16[2,4,64,1024]{3,2,1,0:T(8,128)(2,1)} %get-tuple-element.213), channel_id=1, source_target_pairs={{0,1},{1,0},{2,3},{3,2},{4,5},{5,4},{6,7},{7,6},{8,9},{9,8},{10,11... | collective-permute-start | bytes 3145736 | tf_op jit(solution)/shard_map/ppermute | solution.py:785
  280.6 37.3 %all-to-all-start.3 = ((bf16[32,32,512]{2,1,0:T(8,128)(2,1)}), bf16[32,32,512]{2,1,0:T(8,128)(2,1)}, u32[]{:S(2)}, u32[]{:S(2)}) async-start(bf16[32,32,512]{2,1,0:T(8,128)(2,1)} %bitcast.101), calls=%async_computation.3 | async-start | bytes 2097152 | tf_op jit(solution)/shard_map/all_to_all | solution.py:1059
  289.1 10.3 %collective-permute-start.39 = (f32[192,128]{1,0:T(8,128)S(1)}, f32[192,128]{1,0:T(8,128)S(1)}, u32[]{:S(2)}, u32[]{:S(2)}) collective-permute-start(f32[192,128]{1,0:T(8,128)S(1)} %shard_map.232), channel_id=1, source_target_pairs={{0,4},{4,0},{8,12},{12,8},{16,20},{20,16},{24,28},{28,24},{1,5},{5... | collective-permute-start | bytes 294920 | tf_op jit(solution)/shard_map/ppermute | solution.py:785
  290.9 23.9 %copy-start.3 = (bf16[4,64,1024]{2,1,0:T(8,128)(2,1)S(1)}, bf16[4,64,1024]{2,1,0:T(8,128)(2,1)}, u32[]{:S(2)}) copy-start(bf16[4,64,1024]{2,1,0:T(8,128)(2,1)} %slab0_ref.1) | copy-start | bytes 1572868
  293.0 20.1 %collective-permute-start.38 = (bf16[4,64,1024]{2,1,0:T(8,128)(2,1)}, bf16[4,64,1024]{2,1,0:T(8,128)(2,1)}, u32[]{:S(2)}, u32[]{:S(2)}) collective-permute-start(bf16[4,64,1024]{2,1,0:T(8,128)(2,1)} %fusion.13), channel_id=1, source_target_pairs={{0,2},{1,3},{2,0},{3,1},{4,6},{5,7},{6,4},{7,5},{8,10},{9,11},{10,... | collective-permute-start | bytes 1572872 | tf_op jit(solution)/shard_map/ppermute | solution.py:785
  (54 other events, 238.8 us)

commit v3 on v2

--- a/solution.py
+++ b/solution.py
@@ -39,22 +39,34 @@
     return jnp.where(in_row == wanted, 1.0, 0.0).astype(bf16)
 
 
-def kernel_call(body, micros, outs, scratch, limit, *operands):
-    places = [
-        pl.BlockSpec(memory_space=pltpu.SMEM)
-        if value.dtype == jnp.int32
-        else pl.BlockSpec(memory_space=pltpu.VMEM)
-        for value in operands
-    ]
-    flops = micros * 1_150_000_000
+def kernel_call(body, micros, outs, scratch, limit, *operands, halves=None, free=False):
+    whole = pl.BlockSpec(memory_space=pltpu.VMEM)
+    kinds = [(value.shape, value.dtype) for value in operands] + list(outs)
+
+    def place(index):
+        shape, kind = kinds[index]
+        if kind == jnp.int32:
+            return pl.BlockSpec(memory_space=pltpu.SMEM)
+        axis = halves[index] if halves else None
+        if axis is None and free:
+            return pl.BlockSpec(shape, lambda *_: (0,) * len(shape))
+        if axis is None:
+            return whole
+        block = tuple(size // 2 if k == axis else size for k, size in enumerate(shape))
+        return pl.BlockSpec(block, lambda half: tuple(half if k == axis else 0 for k in range(len(block))))
+
+    places = [place(k) for k in range(len(kinds))]
     return pl.pallas_call(
         body,
         out_shape=[jax.ShapeDtypeStruct(shape, kind) for shape, kind in outs],
-        in_specs=places,
-        out_specs=[pl.BlockSpec(memory_space=pltpu.VMEM) for _ in outs],
+        grid=(2,) if halves else (),
+        in_specs=places[: len(operands)],
+        out_specs=places[len(operands) :],
         scratch_shapes=scratch,
         compiler_params=pltpu.CompilerParams(vmem_limit_bytes=limit << 20),
-        cost_estimate=pl.CostEstimate(flops=flops, bytes_accessed=8_000_000, transcendentals=0),
+        cost_estimate=pl.CostEstimate(
+            flops=micros * 1_150_000_000, bytes_accessed=8_000_000, transcendentals=0
+        ),
     )(*operands)
 
 
@@ -96,25 +108,30 @@
         root = lax.rsqrt(jnp.mean(rows * rows, axis=1, keepdims=True) + epsilon)
         return (rows * root * gain_ref[...]).astype(bf16)
 
-    last = dot(order, scaled(read_rows(slabs, steps // 8 - 1))).astype(bf16)
-    last = dot(last[block_rows - 3 * chunks :, :], weight_ref[...]).reshape(3, chunks, inner_width)
+    taps = [small_row(small_ref, k) for k in range(4)]
+    offset = small_row(small_ref, 4)
+
+    def norm_lap(block, carry):
+        base = pl.multiple_of(block * block_rows, block_rows)
+        normed = dot(order, scaled(read_rows(slabs, block))).astype(bf16)
+        normed_ref[pl.ds(base, block_rows), :] = normed
+        return carry
+
+    lax.fori_loop(0, steps // 8, norm_lap, 0)
+    inner_ref[3 * chunks :, :] = dot(normed_ref[...], weight_ref[...]).astype(bf16)
+    last = inner_ref[steps * chunks :, :].astype(f32).reshape(3, chunks, inner_width)
     rim = dot(scaled(rim_ref[...].astype(f32)), weight_ref[...]).reshape(3, sequences, inner_width)
     rim = jnp.concatenate([rim, last[:, : chunks - sequences, :]], axis=1)
     inner_ref[0 : 3 * chunks, :] = rim.reshape(3 * chunks, inner_width).astype(bf16)
-    taps = [small_row(small_ref, k) for k in range(4)]
-    offset = small_row(small_ref, 4)
 
     def lap(block, carry):
         base = pl.multiple_of(block * block_rows, block_rows)
-        normed = dot(order, scaled(read_rows(slabs, block))).astype(bf16)
-        normed_ref[pl.ds(base, block_rows), :] = normed
-        inner = dot(normed, weight_ref[...]).astype(bf16)
-        inner_ref[pl.ds(pl.multiple_of(base + 3 * chunks, 16), block_rows), :] = inner
         total = offset
         for k in range(3):
             same = mask_ref[pl.ds(base, block_rows), k : k + 1]
             part = inner_ref[pl.ds(pl.multiple_of(base + k * chunks, 16), block_rows), :]
             total = total + taps[k] * part.astype(f32) * same
+        inner = inner_ref[pl.ds(pl.multiple_of(base + 3 * chunks, 16), block_rows), :]
         total = total + taps[3] * inner.astype(f32)
         filtered = (total * sigmoid(total)).astype(bf16)
         filter_ref[pl.ds(base, block_rows), :] = filtered.astype(f32)
@@ -127,7 +144,7 @@
 
 def gate_kernel(
     place_ref, slab0_ref, slab1_ref, slab2_ref, slab3_ref, normed_ref, near_ref, far_ref, exit_near_ref, exit_far_ref,
-    rows_ref, value_ref, slope_ref, grad_ref, weight_ref, exit_ref,
+    rows_ref, value_ref, slope_ref, grad_ref, weight_ref, exit_ref, gating_ref, gated_ref,
 ):
     slabs = (slab0_ref, slab1_ref, slab2_ref, slab3_ref)
     sequences, steps, width = slab0_ref.shape
@@ -136,12 +153,19 @@
     assemble(weight_ref, (near_ref, far_ref), place_ref[0])
     assemble(exit_ref, (exit_near_ref, exit_far_ref), place_ref[0])
 
+    def order_lap(block, carry):
+        at = pl.ds(pl.multiple_of(block * block_rows, block_rows), block_rows)
+        rows_ref[at, :] = dot(order, read_rows(slabs, block).astype(bf16)).astype(bf16)
+        return carry
+
+    lax.fori_loop(0, steps // 8, order_lap, 0)
+    gating_ref[...] = dot(normed_ref[...], weight_ref[...])
+    gated_ref[...] = dot(rows_ref[...], exit_ref[...], ((1,), (1,)))
+
     def lap(block, carry):
         at = pl.ds(pl.multiple_of(block * block_rows, block_rows), block_rows)
-        ordered = dot(order, read_rows(slabs, block).astype(bf16)).astype(bf16)
-        rows_ref[at, :] = ordered
-        gating = dot(normed_ref[at, :], weight_ref[...])
-        grad_gated = dot(ordered, exit_ref[...], ((1,), (1,)))
+        gating = gating_ref[at, :]
+        grad_gated = gated_ref[at, :]
         gate = sigmoid(gating)
         value = gating * gate
         value_ref[at, :] = value
@@ -166,9 +190,9 @@
     pick_ref[...] = jnp.where(source == target, 1.0, 0.0).astype(bf16)
 
 
-def fill_gates(gates_ref, pick_ref, spread_ref, half):
+def fill_gates(gates_ref, pick_ref, spread_ref, at):
     steps = gates_ref.shape[0]
-    values = gates_ref[:, pl.ds(pl.multiple_of(half * 8, 8), 8), :].reshape(steps * 8, 128)[:, 64:96]
+    values = gates_ref[:, at, :].reshape(steps * 8, 128)[:, 64:96]
     high = values.astype(bf16)
     rest = (values - high.astype(f32)).astype(bf16)
     pair = jnp.concatenate([high, rest], axis=1)
@@ -230,8 +254,8 @@
     spots = [(j, i) for j in range(span) for i in range(len(lanes))]
 
     def half_lap(half, carry):
-        fill_gates(gates_ref, pick_ref, spread_ref, half)
         at = pl.ds(pl.multiple_of(half * 8, 8), 8)
+        fill_gates(gates_ref, pick_ref, spread_ref, at)
 
         def lap(block, totals):
             totals = list(totals)
@@ -311,226 +335,216 @@
 
 def forward_kernel(
     place_ref, came_ref, gates_ref, small_ref, step_ref, filter_ref, grad_ref, end_ref, keep_ref, give_ref,
-    out_ref, read_sum_ref, enter_ref, arrive_ref,
-    rates_ref, spread_ref, pick_ref, product_ref, unpick_ref, passed_ref, whole_ref,
+    out_ref, read_sum_ref, start_ref, arrive_ref,
+    rates_ref, spread_ref, pick_ref, product_ref, unpick_ref, passed_ref, whole_ref, enter_ref,
 ):
     me = place_ref[0]
-    steps, chunks, width = step_ref.shape
-    states = end_ref.shape[0]
+    half = pl.program_id(0)
+    steps, _, width = step_ref.shape
+    states, chunks = end_ref.shape[:2]
     pieces = came_ref.shape[0]
     sequences = came_ref.shape[1] // (states + 4)
     groups = chunks // sequences
-    fill_rates(small_ref, rates_ref)
-    fill_picks(pick_ref)
-    fill_unpicks(unpick_ref, 64 + states)
-
-    held = states * sequences
-    rates = [jnp.broadcast_to(rates_ref[n, 0:1, :], (sequences, width)) for n in range(states)]
-    rates = jnp.concatenate(rates, axis=0)
-
-    def step_in(piece, state):
-        values = came_ref[piece].astype(f32)
-        total = values[held : held + sequences, :]
-        for k in range(1, 3):
-            total = total + values[held + k * sequences : held + (k + 1) * sequences, :]
-        total = jnp.concatenate([total] * states, axis=0)
-        return jnp.exp2(total * rates) * state + values[:held, :]
-
-    def step_back(k, state):
-        return step_in(pieces - 1 - k, state)
-
-    zero = jnp.zeros((held, width), f32)
-    whole_ref[0] = lax.fori_loop(0, me, step_in, zero)
-    whole_ref[1] = lax.fori_loop(0, pieces - 1 - me, step_back, zero)
-    for n in range(states):
-        ahead = whole_ref[0, n * sequences : (n + 1) * sequences, :]
-        back = whole_ref[1, n * sequences : (n + 1) * sequences, :]
-        for k in range(groups):
-            part = slice(k * sequences, (k + 1) * sequences)
-            enter_ref[n, part, :] = ahead
-            ahead = keep_ref[n, part, :] * ahead + end_ref[n, part, :]
-            other = slice((groups - 1 - k) * sequences, (groups - k) * sequences)
-            arrive_ref[n, other, :] = back
-            back = give_ref[n, other, :] + keep_ref[n, other, :] * back
-
-    rates_ref[states] = jnp.broadcast_to(small_row(small_ref, 6), (8, width))
+    @pl.when(half == 0)
+    def _():
+        fill_rates(small_ref, rates_ref)
+        fill_picks(pick_ref)
+        fill_unpicks(unpick_ref, 64 + states)
+        rates_ref[states] = jnp.broadcast_to(small_row(small_ref, 6), (8, width))
+
+        held = states * sequences
+        rates = [jnp.broadcast_to(rates_ref[n, 0:1, :], (sequences, width)) for n in range(states)]
+        rates = jnp.concatenate(rates, axis=0)
+
+        def step_in(piece, state):
+            values = came_ref[piece].astype(f32)
+            total = values[held : held + sequences, :]
+            for k in range(1, 3):
+                total = total + values[held + k * sequences : held + (k + 1) * sequences, :]
+            total = jnp.concatenate([total] * states, axis=0)
+            return jnp.exp2(total * rates) * state + values[:held, :]
+
+        def step_back(k, state):
+            return step_in(pieces - 1 - k, state)
+
+        zero = jnp.zeros((held, width), f32)
+        whole_ref[0] = lax.fori_loop(0, me, step_in, zero)
+        whole_ref[1] = lax.fori_loop(0, pieces - 1 - me, step_back, zero)
+        for n in range(states):
+            ahead = whole_ref[0, n * sequences : (n + 1) * sequences, :]
+            back = whole_ref[1, n * sequences : (n + 1) * sequences, :]
+            for k in range(groups):
+                part = slice(k * sequences, (k + 1) * sequences)
+                enter_ref[n, part, :] = ahead
+                ahead = keep_ref[n, part, :] * ahead + end_ref[n, part, :]
+                other = slice((groups - 1 - k) * sequences, (groups - k) * sequences)
+                arrive_ref[n, other, :] = back
+                back = give_ref[n, other, :] + keep_ref[n, other, :] * back
+
     span = 4
     lanes = lane_slices(width)
     spots = [(j, i) for j in range(span) for i in range(len(lanes))]
 
-    def half_lap(half, carry):
-        fill_gates(gates_ref, pick_ref, spread_ref, half)
-        at = pl.ds(pl.multiple_of(half * 8, 8), 8)
+    fill_gates(gates_ref, pick_ref, spread_ref, slice(None))
+    at = pl.ds(pl.multiple_of(half * 8, 8), 8)
+    for n in range(states):
+        for i, one in enumerate(lanes):
+            passed_ref[n, i] = enter_ref[n, at, one]
+
+    def forward(block, inner_carry):
+        pushed, drives, grads, outs = {}, {}, {}, {}
+        for j, i in spots:
+            t = block * span + j
+            step = step_ref[t, :, lanes[i]]
+            feed = filter_ref[t, :, lanes[i]]
+            pushed[j, i] = step + gates_ref[t, :, 96:97]
+            drives[j, i] = step * feed
+            grads[j, i] = grad_ref[t, :, lanes[i]]
+            outs[j, i] = feed * rates_ref[states, :, lanes[i]]
+        rows = pl.ds(pl.multiple_of(block * span * 8, span * 8), span * 8)
         for n in range(states):
+            rate = [rates_ref[n, :, one] for one in lanes]
+            hidden = [passed_ref[n, i] for i in range(len(lanes))]
             for i, one in enumerate(lanes):
-                passed_ref[n, i] = enter_ref[n, at, one]
-
-        def forward(block, inner_carry):
-            pushed, drives, grads, outs = {}, {}, {}, {}
-            for j, i in spots:
+                start_ref[block, n, :, one] = hidden[i]
+            seen = []
+            for j in range(span):
                 t = block * span + j
-                step = step_ref[t, at, lanes[i]]
-                feed = filter_ref[t, at, lanes[i]]
-                pushed[j, i] = step + gates_ref[t, at, 96:97]
-                drives[j, i] = step * feed
-                grads[j, i] = grad_ref[t, at, lanes[i]]
-                outs[j, i] = feed * rates_ref[states, :, lanes[i]]
-            rows = pl.ds(pl.multiple_of(block * span * 8, span * 8), span * 8)
-            for n in range(states):
-                rate = [rates_ref[n, :, one] for one in lanes]
-                hidden = [passed_ref[n, i] for i in range(len(lanes))]
-                seen = []
-                for j in range(span):
-                    t = block * span + j
-                    write = gate_of(spread_ref, t, n)
-                    read = gate_of(spread_ref, t, states + n)
-                    total = None
-                    for i in range(len(lanes)):
-                        hidden[i] = jnp.exp2(pushed[j, i] * rate[i]) * hidden[i] + drives[j, i] * write
-                        outs[j, i] = outs[j, i] + hidden[i] * read
-                        one = grads[j, i] * hidden[i]
-                        total = one if total is None else total + one
-                    seen.append(total)
-                product_ref[rows, n * 128 : (n + 1) * 128] = jnp.concatenate(seen, axis=0).astype(bf16)
+                write = gate_of(spread_ref, t, n)
+                read = gate_of(spread_ref, t, states + n)
+                total = None
                 for i in range(len(lanes)):
-                    passed_ref[n, i] = hidden[i]
-            for j, i in spots:
-                out_ref[block * span + j, at, lanes[i]] = outs[j, i]
-            return inner_carry
-
-        lax.fori_loop(0, steps // span, forward, 0)
-        summed = dot(product_ref[...], unpick_ref[...])
-        read_sum_ref[:, at, :] = summed.reshape(steps, 8, 128)
-        return carry
-
-    lax.fori_loop(0, chunks // 8, half_lap, 0)
+                    hidden[i] = jnp.exp2(pushed[j, i] * rate[i]) * hidden[i] + drives[j, i] * write
+                    outs[j, i] = outs[j, i] + hidden[i] * read
+                    one = grads[j, i] * hidden[i]
+                    total = one if total is None else total + one
+                seen.append(total)
+            product_ref[rows, n * 128 : (n + 1) * 128] = jnp.concatenate(seen, axis=0).astype(bf16)
+            for i in range(len(lanes)):
+                passed_ref[n, i] = hidden[i]
+        for j, i in spots:
+            out_ref[block * span + j, :, lanes[i]] = outs[j, i]
+        return inner_carry
+
+    lax.fori_loop(0, steps // span, forward, 0)
+    summed = dot(product_ref[...], unpick_ref[...])
+    read_sum_ref[...] = summed.reshape(steps, 8, 128)
 
 
 def backward_kernel(
-    gates_ref, small_ref, step_ref, slope_ref, filter_ref, grad_ref, read_sum_ref, enter_ref, arrive_ref,
+    gates_ref, small_ref, step_ref, slope_ref, filter_ref, grad_ref, read_sum_ref, start_ref, arrive_ref,
     direct_ref, rank_ref, chosen_ref, decay_ref, skip_ref, bias_ref,
-    rates_ref, spread_ref, pick_ref, state_ref, product_ref, unpick_ref, delta_ref, sums_acc_ref,
+    rates_ref, spread_ref, pick_ref, product_ref, unpick_ref, delta_ref, sums_acc_ref,
     passed_ref, total_ref,
 ):
-    steps, chunks, width = step_ref.shape
-    states = enter_ref.shape[0]
-    fill_rates(small_ref, rates_ref)
-    fill_picks(pick_ref)
-    fill_unpicks(unpick_ref, 64)
-    decay_ref[...] = jnp.zeros_like(decay_ref)
-    skip_ref[...] = jnp.zeros_like(skip_ref)
-    rates_ref[states] = jnp.broadcast_to(small_row(small_ref, 6), (8, width))
-    span = 4
+    half = pl.program_id(0)
+    steps, _, width = step_ref.shape
+    chunks = delta_ref.shape[1]
+    blocks, states = start_ref.shape[:2]
+    span = steps // blocks
+
+    @pl.when(half == 0)
+    def _():
+        fill_rates(small_ref, rates_ref)
+        fill_picks(pick_ref)
+        fill_unpicks(unpick_ref, 64)
+        decay_ref[...] = jnp.zeros_like(decay_ref)
+        skip_ref[...] = jnp.zeros_like(skip_ref)
+        rank_ref[...] = jnp.zeros_like(rank_ref)
+        bias_ref[...] = jnp.zeros_like(bias_ref)
+        rates_ref[states] = jnp.broadcast_to(small_row(small_ref, 6), (8, width))
+
     lanes = lane_slices(width)
     spots = [(j, i) for j in range(span) for i in range(len(lanes))]
-    blocks = steps // span
-
-    def half_lap(half, carry):
-        fill_gates(gates_ref, pick_ref, spread_ref, half)
-        at = pl.ds(pl.multiple_of(half * 8, 8), 8)
+
+    fill_gates(gates_ref, pick_ref, spread_ref, slice(None))
+    at = pl.ds(pl.multiple_of(half * 8, 8), 8)
+    for n in range(states):
+        for i, one in enumerate(lanes):
+            passed_ref[n, i] = arrive_ref[n, :, one]
+            total_ref[n, i] = jnp.zeros((8, 128), f32)
+
+    def backward(k, skips):
+        block = blocks - 1 - k
+        skips = list(skips)
+        raw, feeds, pushed, drives, grads, weighted, slopes = {}, {}, {}, {}, {}, {}, {}
+        for j, i in spots:
+            t = block * span + j
+            step = step_ref[t, :, lanes[i]]
+            feed = filter_ref[t, :, lanes[i]]
+            grad = grad_ref[t, :, lanes[i]]
+            raw[j, i] = step
+            feeds[j, i] = feed
+            pushed[j, i] = step + gates_ref[t, :, 96:97]
+            drives[j, i] = step * feed
+            grads[j, i] = grad
+            weighted[j, i] = jnp.zeros((8, 128), f32)
+            slopes[j, i] = jnp.zeros((8, 128), f32)
+            skips[i] = skips[i] + grad * feed
+        rows = pl.ds(pl.multiple_of(block * span * 8, span * 8), span * 8)
         for n in range(states):
-            for i, one in enumerate(lanes):
-                first = enter_ref[n, at, one]
-                state_ref[0, n, i] = first
-                passed_ref[n, i] = first
-
-        def forward(block, inner_carry):
-            pushed, drives = {}, {}
-            for j, i in spots:
+            rate = [rates_ref[n, :, one] for one in lanes]
+            gone = [passed_ref[n, i] for i in range(len(lanes))]
+            turns = [total_ref[n, i] for i in range(len(lanes))]
+            hidden = [[start_ref[block, n, :, one] for one in lanes]]
+            decays = []
+            for j in range(span):
+                decays.append([jnp.exp2(pushed[j, i] * rate[i]) for i in range(len(lanes))])
+                if j < span - 1:
+                    write = gate_of(spread_ref, block * span + j, n)
+                    last = hidden[-1]
+                    hidden.append(
+                        [decays[j][i] * last[i] + drives[j, i] * write for i in range(len(lanes))]
+                    )
+            seen = [None] * span
+            for j in reversed(range(span)):
                 t = block * span + j
-                step = step_ref[t, at, lanes[i]]
-                pushed[j, i] = step + gates_ref[t, at, 96:97]
-                drives[j, i] = step * filter_ref[t, at, lanes[i]]
-            for n in range(states):
-                rate = [rates_ref[n, :, one] for one in lanes]
-                hidden = [passed_ref[n, i] for i in range(len(lanes))]
-                for j in range(span):
-                    t = block * span + j
-                    write = gate_of(spread_ref, t, n)
-                    for i in range(len(lanes)):
-                        hidden[i] = jnp.exp2(pushed[j, i] * rate[i]) * hidden[i] + drives[j, i] * write
-                        state_ref[t + 1, n, i] = hidden[i]
+                write = gate_of(spread_ref, t, n)
+                read = gate_of(spread_ref, t, states + n)
                 for i in range(len(lanes)):
-                    passed_ref[n, i] = hidden[i]
-            return inner_carry
-
-        lax.fori_loop(0, blocks, forward, 0)
+                    adjoint = read * grads[j, i] + gone[i]
+                    weighted[j, i] = weighted[j, i] + adjoint * write
+                    one = adjoint * drives[j, i]
+                    seen[j] = one if seen[j] is None else seen[j] + one
+                    gone[i] = adjoint * decays[j][i]
+                    turn = gone[i] * hidden[j][i]
+                    slopes[j, i] = slopes[j, i] + turn * rate[i]
+                    turns[i] = turns[i] + turn * raw[j, i]
+            product_ref[rows, n * 128 : (n + 1) * 128] = jnp.concatenate(seen, axis=0).astype(bf16)
+            for i in range(len(lanes)):
+                passed_ref[n, i] = gone[i]
+                total_ref[n, i] = turns[i]
+        for j, i in spots:
+            t = block * span + j
+            grown = slopes[j, i] * log_2 + weighted[j, i] * feeds[j, i]
+            delta_ref[t, at, lanes[i]] = grown * slope_ref[t, :, lanes[i]]
+            direct = weighted[j, i] * raw[j, i] + grads[j, i] * rates_ref[states, :, lanes[i]]
+            direct_ref[t, :, lanes[i]] = direct
+        return tuple(skips)
+
+    start = tuple(jnp.zeros((8, 128), f32) for _ in lanes)
+    skips = lax.fori_loop(0, blocks, backward, start)
+    for i, one in enumerate(lanes):
+        skip_ref[0:1, one] += jnp.sum(skips[i], axis=0, keepdims=True)
         for n in range(states):
-            for i, one in enumerate(lanes):
-                passed_ref[n, i] = arrive_ref[n, at, one]
-                total_ref[n, i] = jnp.zeros((8, 128), f32)
-
-        def backward(k, skips):
-            block = blocks - 1 - k
-            skips = list(skips)
-            raw, feeds, pushed, drives, grads, weighted, slopes = {}, {}, {}, {}, {}, {}, {}
-            for j, i in spots:
-                t = block * span + j
-                step = step_ref[t, at, lanes[i]]
-                feed = filter_ref[t, at, lanes[i]]
-                grad = grad_ref[t, at, lanes[i]]
-                raw[j, i] = step
-                feeds[j, i] = feed
-                pushed[j, i] = step + gates_ref[t, at, 96:97]
-                drives[j, i] = step * feed
-                grads[j, i] = grad
-                weighted[j, i] = jnp.zeros((8, 128), f32)
-                slopes[j, i] = jnp.zeros((8, 128), f32)
-                skips[i] = skips[i] + grad * feed
-            rows = pl.ds(pl.multiple_of(block * span * 8, span * 8), span * 8)
-            for n in range(states):
-                rate = [rates_ref[n, :, one] for one in lanes]
-                gone = [passed_ref[n, i] for i in range(len(lanes))]
-                turns = [total_ref[n, i] for i in range(len(lanes))]
-                seen = [None] * span
-                for j in reversed(range(span)):
-                    t = block * span + j
-                    write = gate_of(spread_ref, t, n)
-                    read = gate_of(spread_ref, t, states + n)
-                    for i in range(len(lanes)):
-                        adjoint = read * grads[j, i] + gone[i]
-                        weighted[j, i] = weighted[j, i] + adjoint * write
-                        one = adjoint * drives[j, i]
-                        seen[j] = one if seen[j] is None else seen[j] + one
-                        gone[i] = adjoint * jnp.exp2(pushed[j, i] * rate[i])
-                        turn = gone[i] * state_ref[t, n, i]
-                        slopes[j, i] = slopes[j, i] + turn * rate[i]
-                        turns[i] = turns[i] + turn * raw[j, i]
-                product_ref[rows, n * 128 : (n + 1) * 128] = jnp.concatenate(seen, axis=0).astype(bf16)
-                for i in range(len(lanes)):
-                    passed_ref[n, i] = gone[i]
-                    total_ref[n, i] = turns[i]
-            for j, i in spots:
-                t = block * span + j
-                grown = slopes[j, i] * log_2 + weighted[j, i] * feeds[j, i]
-                delta_ref[t, at, lanes[i]] = grown * slope_ref[t, at, lanes[i]]
-                direct = weighted[j, i] * raw[j, i] + grads[j, i] * rates_ref[states, :, lanes[i]]
-                direct_ref[t, at, lanes[i]] = direct
-            return tuple(skips)
-
-        start = tuple(jnp.zeros((8, 128), f32) for _ in lanes)
-        skips = lax.fori_loop(0, blocks, backward, start)
-        for i, one in enumerate(lanes):
-            skip_ref[0:1, one] += jnp.sum(skips[i], axis=0, keepdims=True)
-            for n in range(states):
-                part = jnp.sum(total_ref[n, i], axis=0, keepdims=True)
-                decay_ref[n : n + 1, one] += part * rates_ref[n, 0:1, one] * log_2
-        summed = dot(product_ref[...], unpick_ref[...])
-        sums_acc_ref[:, at, :] = summed.reshape(steps, 8, 128) + read_sum_ref[:, at, :]
-        return carry
-
-    lax.fori_loop(0, chunks // 8, half_lap, 0)
-
-    rows = steps * chunks
-    grads = delta_ref[...].reshape(rows, width)
-    bias_ref[...] = jnp.sum(grads, axis=0, keepdims=True)
-    grads = grads.astype(bf16)
-    low = gates_ref[...].reshape(rows, 128)[:, 0:64].astype(bf16)
-    rank_ref[...] = dot(low, grads, ((0,), (0,)))
-    back = dot(small_ref[0:64, :], grads, ((1,), (1,)))
-    sums = sums_acc_ref[...].reshape(rows, 128).T
-    chosen_ref[0:64, :] = back.astype(bf16)
-    chosen_ref[64:96, :] = sums[64:96, :].astype(bf16)
+            part = jnp.sum(total_ref[n, i], axis=0, keepdims=True)
+            decay_ref[n : n + 1, one] += part * rates_ref[n, 0:1, one] * log_2
+    summed = dot(product_ref[...], unpick_ref[...])
+    sums_acc_ref[:, at, :] = summed.reshape(steps, 8, 128) + read_sum_ref[...]
+
+    grads = delta_ref[:, at, :].reshape(steps * 8, width)
+    bias_ref[...] += jnp.sum(grads, axis=0, keepdims=True)
+    low = gates_ref[...].reshape(steps * 8, 128)[:, 0:64].astype(bf16)
+    rank_ref[...] += dot(low, grads.astype(bf16), ((0,), (0,)))
+
+    @pl.when(half == 1)
+    def _():
+        rows = steps * chunks
+        whole = delta_ref[...].reshape(rows, width).astype(bf16)
+        back = dot(small_ref[0:64, :], whole, ((1,), (1,)))
+        sums = sums_acc_ref[...].reshape(rows, 128).T
+        chosen_ref[0:64, :] = back.astype(bf16)
+        chosen_ref[64:96, :] = sums[64:96, :].astype(bf16)
 
 
 def store_rows(keep_ref, send_ref, order, values, block):
@@ -558,7 +572,7 @@
 def leave_kernel(
     place_ref, scan_ref, value_ref, slope_ref, rows_ref, normed_ref, exit_near_ref, exit_far_ref,
     gating_ref, out_keep_ref, out_send_ref, exit_grad_ref, keep_ref, send_ref,
-    gated_ref, entry_grad_ref, exit_ref,
+    gated_ref, entry_grad_ref, exit_ref, out_ref,
 ):
     assemble(exit_ref, (exit_near_ref, exit_far_ref), place_ref[0])
     sequences, steps = out_keep_ref.shape[1:3]
@@ -572,10 +586,24 @@
         gated = (scan_out * value_ref[at, :]).astype(bf16)
         gated_ref[at, :] = gated
         gating_ref[at, :] = (scan_out * slope_ref[at, :]).astype(bf16)
-        store_rows(out_keep_ref, out_send_ref, order, dot(gated, exit_ref[...]), block)
         return carry
 
     lax.fori_loop(0, steps // 8, lap, 0)
+    span = 256
+
+    def column_lap(block, carry):
+        at = pl.ds(pl.multiple_of(block * span, span), span)
+        out_ref[:, at] = dot(gated_ref[...], exit_ref[:, at]).astype(bf16)
+        return carry
+
+    lax.fori_loop(0, out_ref.shape[1] // span, column_lap, 0)
+
+    def store_lap(block, carry):
+        at = pl.ds(pl.multiple_of(block * block_rows, block_rows), block_rows)
+        store_rows(out_keep_ref, out_send_ref, order, out_ref[at, :], block)
+        return carry
+
+    lax.fori_loop(0, steps // 8, store_lap, 0)
     exit_grad_ref[...] = dot(gated_ref[...], rows_ref[...], ((0,), (0,))).astype(bf16)
     entry_grad_ref[...] = dot(normed_ref[...], gating_ref[...], ((0,), (0,)))
     store_blocks(keep_ref, send_ref, place_ref[0], entry_grad_ref)
@@ -583,10 +611,10 @@
 
 def filter_kernel(
     place_ref, chosen_ref, other_ref, direct_ref, inner_ref, filter_ref, mask_ref, small_ref,
-    rank_ref, decay_ref, bias_ref, skip_ref,
-    grads_ref, spill_ref, first_ref, *refs,
+    rank_ref, decay_ref, bias_ref, skip_ref, gate_keep_ref, gate_came_ref,
+    grads_ref, spill_ref, first_ref, small_out_ref, total_ref, *refs,
 ):
-    block_refs, (packed_ref, picked_ref, taps_ref, offset_ref) = refs[:-4], refs[-4:]
+    part_refs, (packed_ref, picked_ref, taps_ref, offset_ref) = refs[:-4], refs[-4:]
     rows, width = grads_ref.shape
     chunks = spill_ref.shape[1]
     block_rows = chunks * 8
@@ -626,12 +654,16 @@
     packed_ref[181:182, :] = bias_ref[...]
     packed_ref[182:183, :] = skip_ref[...]
     packed_ref[183:192, :] = jnp.zeros((9, width), f32)
-    if len(block_refs) == 1:
-        block_refs[0][...] = packed_ref[...]
-    else:
-        for k, block_ref in enumerate(block_refs):
+    small_out_ref[...] = packed_ref[...]
+    height = gate_keep_ref.shape[1]
+    below = (total_ref.shape[0] - height) * 4
+    for k, target in enumerate((total_ref,) + part_refs):
+        target[0:height, :] = (gate_keep_ref[k].astype(f32) + gate_came_ref[k].astype(f32)).astype(target.dtype)
+        if below:
             lanes = pl.ds(pl.multiple_of(((place_ref[0] >> 1) ^ k) * 128, 128), 128)
-            block_ref[...] = packed_ref[:, lanes]
+            for q in range(4):
+                values = packed_ref[q * below // 4 : (q + 1) * below // 4, lanes]
+                target[height:, q * 128 : (q + 1) * 128] = values.astype(target.dtype)
     for u in range(3):
         total = jnp.zeros((chunks, width), f32)
         for t in range(u + 1):
@@ -689,7 +721,7 @@
 def normed_kernel(
     place_ref, inner_ref, gating_ref, near_ref, far_ref, gate_near_ref, gate_far_ref,
     out_keep_ref, out_send_ref,
-    weight_ref, gate_weight_ref,
+    weight_ref, gate_weight_ref, grad_ref,
 ):
     assemble(weight_ref, (near_ref, far_ref), place_ref[0])
     assemble(gate_weight_ref, (gate_near_ref, gate_far_ref), place_ref[0])
@@ -698,24 +730,27 @@
     block_rows = groups * sequences * 8
     order = ordering(groups, sequences, place_ref[1])
 
+    span = 256
+
+    def column_lap(block, carry):
+        at = pl.ds(pl.multiple_of(block * span, span), span)
+        grad = dot(inner_ref[...], weight_ref[at, :], ((1,), (1,)))
+        grad = grad + dot(gating_ref[...], gate_weight_ref[at, :], ((1,), (1,)))
+        grad_ref[:, at] = grad.astype(bf16)
+        return carry
+
+    lax.fori_loop(0, grad_ref.shape[1] // span, column_lap, 0)
+
     def lap(block, carry):
         at = pl.ds(pl.multiple_of(block * block_rows, block_rows), block_rows)
-        grad = dot(inner_ref[at, :], weight_ref[...], ((1,), (1,)))
-        grad = grad + dot(gating_ref[at, :], gate_weight_ref[...], ((1,), (1,)))
-        store_rows(out_keep_ref, out_send_ref, order, grad, block)
+        store_rows(out_keep_ref, out_send_ref, order, grad_ref[at, :], block)
         return carry
 
     lax.fori_loop(0, steps // 8, lap, 0)
 
 
-def part_kernel(keep_ref, came_ref, total_ref, *part_refs):
-    total_ref[...] = keep_ref[0].astype(f32) + came_ref[0].astype(f32)
-    for k, part_ref in enumerate(part_refs):
-        part_ref[...] = (keep_ref[k + 1].astype(f32) + came_ref[k + 1].astype(f32)).astype(bf16)
-
-
 def side_sum_kernel(place_ref, total_ref, *refs):
-    part_refs, out_refs = refs[:-4], refs[-4:]
+    part_refs, out_refs, small_ref = refs[:-5], refs[-5:-1], refs[-1]
     total = total_ref[...]
     for part_ref in part_refs:
         total = total + part_ref[...].astype(f32)
@@ -725,14 +760,13 @@
         for j in range(1, len(out_refs)):
             block = jnp.where((place_ref[1] ^ k) == j, total[j * rows : (j + 1) * rows, :], block)
         out_ref[...] = block.astype(bf16)
-
-
-def small_sum_kernel(own_ref, *refs):
-    part_refs, out_ref = refs[:-1], refs[-1]
-    total = own_ref[...]
-    for part_ref in part_refs:
-        total = total + part_ref[...]
-    out_ref[...] = total
+    height = rows * len(out_refs)
+    below = total.shape[0] - height
+    if below:
+        for q in range(4):
+            small_ref[q * below : (q + 1) * below, :] = total[height:, q * 128 : (q + 1) * 128]
+    else:
+        small_ref[...] = jnp.zeros_like(small_ref)
 
 
 def interleave_kernel(place_ref, weight_ref, inner_ref, gate0_ref, gate1_ref, gate2_ref, gate3_ref, out_ref, gain_ref):
@@ -886,7 +920,7 @@
             ((96, rows), bf16),
         ],
         [pltpu.VMEM((width, group_width), bf16)],
-        40,
+        12,
         place, *token_slabs, rim, gain_all, mask, inner_near, inner_far, small,
     )
     chosen_pair = group_sum(chosen)
@@ -899,8 +933,13 @@
             ((rows, group_width), f32),
             ((rows, group_width), f32),
         ],
-        [pltpu.VMEM((width, group_width), bf16), pltpu.VMEM((group_width, width), bf16)],
-        40,
+        [
+            pltpu.VMEM((width, group_width), bf16),
+            pltpu.VMEM((group_width, width), bf16),
+            pltpu.VMEM((rows, group_width), f32),
+            pltpu.VMEM((rows, group_width), f32),
+        ],
+        16,
         place, *cotangent_slabs, normed, gate_near, gate_far, exit_near, exit_far,
     )
     cube = (steps, chunks, group_width)
@@ -926,7 +965,7 @@
             pltpu.VMEM((load_rows, group_width), f32),
             pltpu.VMEM((load_rows, group_width), f32),
         ],
-        48,
+        16,
         place, *chosen_pair, mask, small, filtered.reshape(cube), grad_scan.reshape(cube),
     )
     came = lax.all_to_all(loads, "blk", split_axis=0, concat_axis=0, tiled=True)
@@ -938,15 +977,17 @@
         pltpu.VMEM((4 * states, 2 * states * 128), bf16),
     ]
     product_scratch = [pltpu.VMEM((steps * 8, states * 128), bf16), pltpu.VMEM((states * 128, 128), bf16)]
-    scan_out, read_sums, enter, arrive = kernel_call(
+    starts = (steps // 4, states, chunks, group_width)
+    scan_out, read_sums, block_starts, arrive = kernel_call(
         forward_kernel,
         18,
-        [(cube, f32), ((steps, chunks, 128), f32), (bank, f32), (bank, f32)],
+        [(cube, f32), ((steps, chunks, 128), f32), (starts, f32), (bank, f32)],
         gate_scratch
         + product_scratch
-        + [pltpu.VMEM((states, lanes, 8, 128), f32), pltpu.VMEM((2, states * sequences, group_width), f32)],
-        48,
+        + [pltpu.VMEM((states, lanes, 8, 128), f32), pltpu.VMEM((2, states * sequences, group_width), f32), pltpu.VMEM(bank, f32)],
+        36,
         place, came, gates, small, step_sizes, filtered.reshape(cube), grad_scan.reshape(cube), ends, keeps, gives,
+        halves=(None, None, 1, None, 1, 1, 1) + (None,) * 3 + (1, 1, 2, None),
     )
     half_slabs = ((2, sequences, steps, width), bf16)
     block_height = groups * slice_rows
@@ -959,8 +1000,9 @@
             pltpu.VMEM((rows, group_width), bf16),
             pltpu.VMEM((width, group_width), f32),
             pltpu.VMEM((group_width, width), bf16),
+            pltpu.VMEM((rows, width), bf16),
         ],
-        48,
+        14,
         place, scan_out.reshape(rows, group_width), gate_value, gate_slope, cotangent_rows, normed, exit_near, exit_far,
     )
 
@@ -981,7 +1023,6 @@
             ((1, group_width), f32),
         ],
         gate_scratch
-        + [pltpu.VMEM((steps + 1, states, lanes, 8, 128), f32)]
         + product_scratch
         + [
             pltpu.VMEM(cube, f32),
@@ -989,9 +1030,10 @@
             pltpu.VMEM((states, lanes, 8, 128), f32),
             pltpu.VMEM((states, lanes, 8, 128), f32),
         ],
-        56,
+        50,
         gates, small, step_sizes, step_slopes, filtered.reshape(cube), after(grad_scan, out_send).reshape(cube),
-        read_sums, enter, arrive,
+        read_sums, block_starts, arrive,
+        halves=(1, None, 1, 1, 1, 1, 1, 2, 1, 1) + (None,) * 5,
     )
     chosen_grad, exit_parts, gate_came, out_came = rounds(chosen_grad, exit_parts, gate_came, out_came)
     chosen_grads = group_sum(chosen_grad)
@@ -999,63 +1041,46 @@
     def slab_part(keep, came):
         return (keep[1].astype(f32) + came[1].astype(f32)).astype(bf16)
 
-    gate_total, *gate_side_parts = kernel_call(
-        part_kernel,
-        2,
-        [(entry_half[0][1:], f32)] + [(entry_half[0][1:], bf16)] * (pieces // 2 - 1),
-        [],
-        16,
-        gate_keep, gate_came,
-    )
-    gate_side_parts = [flipped(part, "blk", 2 * k + 2) for k, part in enumerate(gate_side_parts)]
-    out_other = flipped(after(slab_part(out_keep, out_came), chosen_grads[1]), "grp", 2)
+    exit_out = jnp.sum(exit_parts.astype(f32), axis=0)
+    grad_direct, exit_out = rounds(grad_direct, exit_out)
+    out_part = after(slab_part(out_keep, out_came), chosen_grads[0])
+    out_other = flipped(out_part, "grp", 2)
 
     paired = 2 * own == 128
-    small_block = (small_rows, 128 if paired else group_width)
-    grad_sums, spill, first_spill, *small_grads = kernel_call(
+    side_block = (block_height + (small_rows // 4 if paired else 0), group_width)
+    grad_sums, spill, first_spill, small_grads, side_total, *side_parts = kernel_call(
         filter_kernel,
         6,
         [
             ((rows, group_width), f32),
             ((3, chunks, group_width), f32),
             ((3, sequences, group_width), f32),
+            ((small_rows, group_width), f32),
+            (side_block, f32),
         ]
-        + [(small_block, f32)] * (pieces // 2 if paired else 1),
+        + [(side_block, bf16)] * (pieces // 2 - 1),
         [
             pltpu.VMEM((small_rows, group_width), f32),
             pltpu.VMEM((rows, 96), bf16),
             pltpu.VMEM((4, group_width), f32),
             pltpu.VMEM((1, group_width), f32),
         ],
-        48,
+        62,
         place, *chosen_grads, grad_direct.reshape(rows, group_width), inner, filtered, mask, small,
-        rank_grad, decay_grad, bias_grad, skip_grad,
+        rank_grad, decay_grad, bias_grad, skip_grad, gate_keep, gate_came,
+        free=True,
     )
     spill_after = lax.ppermute(first_spill, "blk", behind)
-    gate_total, grad_sums, *gate_side_parts = rounds(gate_total, grad_sums, *gate_side_parts)
-    gate_blocks = kernel_call(
-        side_sum_kernel,
-        2,
-        [((slice_rows, group_width), bf16)] * groups,
-        [],
-        16,
-        place, gate_total, *gate_side_parts,
-    )
-    gate_blocks = [gate_blocks[0]] + [flipped(gate_blocks[k], "grp", k) for k in range(1, groups)]
+    side_parts = [flipped(part, "blk", 2 * k + 2) for k, part in enumerate(side_parts)]
     grad_inner, inner_entry = kernel_call(
         inner_kernel,
         6,
         [((rows, group_width), bf16), ((width, group_width), bf16)],
         [pltpu.VMEM((3, rows + 3 * chunks, group_width), f32)],
-        48,
+        14,
         grad_sums, spill, spill_after, mask, small, normed,
     )
-    if paired:
-        came_small = [small_grads[0]] + [flipped(small_grads[k], "blk", 2 * k) for k in range(1, pieces // 2)]
-    else:
-        came_small = small_grads
-    grad_inner, inner_entry, out_other, *rest = rounds(grad_inner, inner_entry, out_other, *gate_blocks, *came_small)
-    gate_blocks, came_small = rest[:groups], rest[groups:]
+    grad_inner, inner_entry, out_other = rounds(grad_inner, inner_entry, out_other)
     inner_parts = lax.all_to_all(
         inner_entry.reshape(pieces * groups, slice_rows, group_width), both, split_axis=0, concat_axis=0, tiled=True
     )
@@ -1063,16 +1088,30 @@
         normed_kernel,
         10,
         [half_slabs, half_slabs],
-        [pltpu.VMEM((width, group_width), bf16), pltpu.VMEM((width, group_width), bf16)],
-        48,
+        [
+            pltpu.VMEM((width, group_width), bf16),
+            pltpu.VMEM((width, group_width), bf16),
+            pltpu.VMEM((rows, width), bf16),
+        ],
+        14,
         place, grad_inner, grad_gating, inner_near, inner_far, gate_near, gate_far,
     )
+    grad_send, *side_parts = rounds(grad_send, *side_parts)
     grad_came = flipped(grad_send, "grp", 1)
-    grad_other = flipped(slab_part(grad_keep, grad_came), "grp", 2)
+    grad_part = slab_part(grad_keep, grad_came)
+    grad_other = flipped(grad_part, "grp", 2)
+    *gate_blocks, small_sum = kernel_call(
+        side_sum_kernel,
+        2,
+        [((slice_rows, group_width), bf16)] * groups + [((small_rows, 128), f32)],
+        [],
+        16,
+        place, after(side_total, grad_part), *side_parts,
+    )
+    gate_blocks = [gate_blocks[0]] + [flipped(gate_blocks[k], "grp", k) for k in range(1, groups)]
     residual = tokens.astype(f32)
     block_out = residual + out_keep[0].astype(f32) + out_came[0].astype(f32) + out_other.astype(f32)
     block_out = block_out.astype(bf16)
-    exit_out = jnp.sum(exit_parts.astype(f32), axis=0)
     inner_parts = inner_parts.reshape(pieces, groups, slice_rows, group_width)
     if own == 64:
         entry_out, gain_out = kernel_call(
@@ -1097,11 +1136,10 @@
     gain_out = gain_out / norm_gain.astype(f32)
 
     if paired:
-        small_sum = kernel_call(small_sum_kernel, 1, [(small_block, f32)], [], 16, *came_small)[0]
         small_sum = small_sum + flipped(small_sum, "blk", 1)
         mine = lax.dynamic_slice_in_dim(small_sum, (piece & 1) * own, own, 1)
     else:
-        split = came_small[0].reshape(small_rows, pieces, own).transpose(1, 0, 2)
+        split = small_grads.reshape(small_rows, pieces, own).transpose(1, 0, 2)
         came_small = lax.all_to_all(split, "blk", split_axis=0, concat_axis=0, tiled=True)
         mine = jnp.sum(came_small, axis=0)
 

time: 322 us -> 297 us (0.922)
  Pallas kernels: 135 us -> 120 us
  waiting for transfers between devices: 47.2 us -> 38.5 us
  starting transfers between devices: 65.9 us -> 61.1 us
    pallas_call x13 -> x11, Pallas kernels: 135 us -> 120 us  [kernel_call(): pl.pallas_call(body, out_shape=[jax.ShapeDtypeStruct(shape, kind) for sha...]
    ppermute x37 -> x34, waiting for transfers between devices: 44.8 us -> 37.2 us  [flipped(): lax.ppermute(value, axis, [(i, i ^ bits) for i in range(lax.axis_size(axi...]
    ppermute x37 -> x34, starting transfers between devices: 44 us -> 39.5 us  [flipped(): lax.ppermute(value, axis, [(i, i ^ bits) for i in range(lax.axis_size(axi...]
    unnamed x125 -> x139, local copies, waits for them, and re-layouts: 22.2 us -> 19.8 us
  transfers between devices with their start and end apart: 43 -> 40, of which waited for: 13 -> 11; matrix products, arithmetic and copies ran while one was open for 6% -> 8% of each run, Pallas kernels for 20% -> 20%
where the time goes in v3:
time: 297 us; the launch traced here: 295 us
  Pallas kernels  120 us (40%)
  starting transfers between devices  61.1 us (21%)
  waiting for transfers between devices  38.5 us (13%)
  local copies, waits for them, and re-layouts  33.6 us (11%)
  blocking collectives  22.4 us (8%)
  other arithmetic  18.5 us (6%)
    pallas_call x11, Pallas kernels, kernel_call(): pl.pallas_call(body, out_shape=[jax.ShapeDtypeStruct(shape, kind) for sha...  120 us
    ppermute x34, starting transfers between devices, flipped(): lax.ppermute(value, axis, [(i, i ^ bits) for i in range(lax.axis_size(axi...  39.5 us
    ppermute x34, waiting for transfers between devices, flipped(): lax.ppermute(value, axis, [(i, i ^ bits) for i in range(lax.axis_size(axi...  37.2 us
    all_to_all x1, blocking collectives, local(): came = lax.all_to_all(loads, 'blk', split_axis=0, concat_axis=0, tiled=True)  22.4 us
    unnamed x139, local copies, waits for them, and re-layouts  19.8 us
    all_to_all x1, starting transfers between devices, local(): lax.all_to_all(inner_entry.reshape(pieces * groups, slice_rows, group_wid...  6.26 us
  transfers between devices with their start and end apart: 40, of which 11 were waited for; matrix products, arithmetic and copies ran while one was open for 8% of the time, Pallas kernels for 20%

profile of v3, /device:TPU:0, one launch (start us, length us, event | category | flops | bytes accessed | tf_op | source)
XLA Modules:
  0.0 295.2 jit_solution(1040795374368389498)
XLA Ops:
  1.7 1.5 reshape.125
  5.5 3.0 %collective-permute-start = (bf16[4,64,1024]{2,1,0:T(8,128)(2,1)S(1)}, bf16[4,64,1024]{2,1,0:T(8,128)(2,1)S(1)}, u32[]{:S(2)}, u32[]{:S(2)}) collective-permute-start(bf16[4,64,1024]{2,1,0:T(8,128)(2,1)S(1)} %copy-done), channel_id=1, source_target_pairs={{0,2},{1,3},{2,0},{3,1},{4,6},{5,7},{6,4},{7,5},{8,10},{9,11},{10,... | collective-permute-start | bytes 1572872 | tf_op jit(solution)/shard_map/ppermute | solution.py:819
  8.5 1.6 collective-permute-start.1
  10.1 2.6 collective-permute-start.2
  12.9 3.5 %all-to-all-start = ((bf16[4,72,512]{2,1,0:T(8,128)(2,1)}), bf16[4,72,512]{2,1,0:T(8,128)(2,1)S(1)}, u32[]{:S(2)}, u32[]{:S(2)}) async-start(bf16[4,72,512]{2,1,0:T(8,128)(2,1)} %pad_maximum_fusion.3), calls=%async_computation | async-start | bytes 589824 | tf_op jit(solution)/shard_map/all_to_all | solution.py:851
  16.4 3.4 %collective-permute-start.16 = (s32[4,3]{1,0:T(4,128)S(1)}, s32[4,3]{1,0:T(4,128)S(1)}, u32[]{:S(2)}, u32[]{:S(2)}) collective-permute-start(s32[4,3]{1,0:T(4,128)S(1)} %slice.112), channel_id=1, source_target_pairs={{0,4},{4,8},{8,12},{12,16},{16,20},{20,24},{24,28},{1,5},{5,9},{9,... | collective-permute-start | bytes 152 | tf_op jit(solution)/shard_map/ppermute | solution.py:886
  21.2 3.9 %collective-permute-done.2 = bf16[80,1024]{1,0:T(8,128)(2,1)S(1)} collective-permute-done((bf16[80,1024]{1,0:T(8,128)(2,1)S(1)}, bf16[80,1024]{1,0:T(8,128)(2,1)S(1)}, u32[]{:S(2)}, u32[]{:S(2)}) %collective-permute-start.2) | collective-permute-done | bytes 163872 | tf_op jit(solution)/shard_map/ppermute | solution.py:819
  26.0 1.6 collective-permute-start.4
  28.2 2.3 collective-permute-start.5
  32.1 2.2 collective-permute-done.5
  34.4 3.1 %collective-permute-start.7 = (bf16[136,512]{1,0:T(8,128)(2,1)}, bf16[136,512]{1,0:T(8,128)(2,1)}, u32[]{:S(2)}, u32[]{:S(2)}) collective-permute-start(bf16[136,512]{1,0:T(8,128)(2,1)} %pad_maximum_fusion.6), channel_id=1, source_target_pairs={{0,24},{4,28},{8,16},{12,20},{16,8},{20,12},{24,0},{28,4},{1,25},{... | collective-permute-start | bytes 417800 | tf_op jit(solution)/shard_map/ppermute | solution.py:819
  37.9 6.3 %collective-permute-done.6 = bf16[136,512]{1,0:T(8,128)(2,1)} collective-permute-done((bf16[136,512]{1,0:T(8,128)(2,1)}, bf16[136,512]{1,0:T(8,128)(2,1)}, u32[]{:S(2)}, u32[]{:S(2)}) %collective-permute-start.6) | collective-permute-done | bytes 139296 | tf_op jit(solution)/shard_map/ppermute | solution.py:819
  48.8 2.8 collective-permute-start.11
  51.6 3.2 %collective-permute-start.13 = (bf16[128,512]{1,0:T(8,128)(2,1)}, bf16[128,512]{1,0:T(8,128)(2,1)}, u32[]{:S(2)}, u32[]{:S(2)}) collective-permute-start(bf16[128,512]{1,0:T(8,128)(2,1)} %bitcast.121), channel_id=1, source_target_pairs={{0,8},{4,12},{8,0},{12,4},{16,24},{20,28},{24,16},{28,20},{1,9},{5... | collective-permute-start | bytes 393224 | tf_op jit(solution)/shard_map/ppermute | solution.py:819
  57.5 2.1 reshape.137
  61.0 1.5 collective-permute-start.15
  64.5 3.7 %collective-permute-done.15 = bf16[128,512]{1,0:T(8,128)(2,1)} collective-permute-done((bf16[128,512]{1,0:T(8,128)(2,1)}, bf16[128,512]{1,0:T(8,128)(2,1)}, u32[]{:S(2)}, u32[]{:S(2)}) %collective-permute-start.15) | collective-permute-done | bytes 131104 | tf_op jit(solution)/shard_map/ppermute | solution.py:819
  71.6 1.6 collective-permute-start.21
  74.3 8.6 %shard_map.220 = (bf16[1024,1024]{1,0:T(8,128)(2,1)S(1)}, bf16[1072,512]{1,0:T(8,128)(2,1)S(1)}, f32[1024,512]{1,0:T(8,128)S(1)}, bf16[96,1024]{1,0:T(8,128)(2,1)S(1)}) custom-call(s32[2]{0:T(128)S(1)} %pad_add_fusion.1.place_ref, bf16[4,64,1024]{2,1,0:T(8,128)(2,1)S(1)} %copy-done, bf16[4,64,1024]{2,1,0:T(8,128)(2,1)} %collective-permute-done.8.slab1_ref, ...), custom_call_target="tpu_custom_call" | custom-call | flops 10350000128 | bytes 8000000 | tf_op jit(solution)/shard_map/pallas_call | solution.py:59
  83.9 1.4 collective-permute-done.17
  86.2 6.6 %shard_map.221 = (bf16[1024,1024]{1,0:T(8,128)(2,1)S(1)}, f32[1024,512]{1,0:T(8,128)S(1)}, f32[1024,512]{1,0:T(8,128)S(1)}, f32[1024,512]{1,0:T(8,128)S(1)}) custom-call(s32[2]{0:T(128)S(1)} %pad_add_fusion.1.place_ref, bf16[4,64,1024]{2,1,0:T(8,128)(2,1)S(1)} %copy-done.4, bf16[4,64,1024]{2,1,0:T(8,128)(2,1)S(1)} %collective-permute-done.19.slab1_ref, ...), custom_call_target="tpu_custom_call" | custom-call | flops 9200000000 | bytes 8000000 | tf_op jit(solution)/shard_map/pallas_call | solution.py:59
  92.8 19.6 %shard_map.222 = (f32[64,16,128]{2,1,0:T(8,128)S(1)}, f32[64,16,512]{2,1,0:T(8,128)S(1)}, f32[64,16,512]{2,1,0:T(8,128)S(1)}, f32[16,16,512]{2,1,0:T(8,128)S(1)}...) custom-call(s32[2]{0:T(128)S(1)} %pad_add_fusion.1.place_ref, ...), custom_call_target="tpu_custom_call" | custom-call | flops 26449999872 | bytes 8000000 | tf_op jit(solution)/shard_map/pallas_call | solution.py:59
  113.7 22.4 %all_to_all.20.came_ref = bf16[8,80,512]{2,1,0:T(8,128)(2,1)S(1)} all-to-all(bf16[8,80,512]{2,1,0:T(8,128)(2,1)S(1)} %get-tuple-element.147), channel_id=1, replica_groups=mesh['blk'=8,'grp'=4] {'blk'}, dimensions={0} | all-to-all | bytes 1310720 | tf_op jit(solution)/shard_map/all_to_all | solution.py:971
  136.1 21.6 %shard_map.223 = (f32[64,16,512]{2,1,0:T(8,128)S(1)}, f32[64,16,128]{2,1,0:T(8,128)S(1)}, f32[16,16,16,512]{3,2,1,0:T(8,128)}, f32[16,16,512]{2,1,0:T(8,128)S(1)}) custom-call(s32[2]{0:T(128)S(1)} %pad_add_fusion.1.place_ref, bf16[8,80,512]{2,1,0:T(8,128)(2,1)S(1)} %all_to_all.20.came_ref, f32[64,16,128]{2,1,0:T(8,128)S(1)} %get-tuple-element.148.gates_ref, ...), custom_call_target="tpu_custom_call" | custom-call | flops 20700000256 | bytes 8000000 | tf_op jit(solution)/shard_map/pallas_call | solution.py:59
  157.7 8.7 %shard_map.224 = (bf16[1024,512]{1,0:T(8,128)(2,1)S(1)}, bf16[2,4,64,1024]{3,2,1,0:T(8,128)(2,1)S(1)}, bf16[2,4,64,1024]{3,2,1,0:T(8,128)(2,1)}, bf16[512,1024]{...) custom-call(s32[2]{0:T(128)S(1)} %pad_add_fusion.1.place_ref, ...), custom_call_target="tpu_custom_call" | custom-call | flops 13799999488 | bytes 8000000 | tf_op jit(solution)/shard_map/pallas_call | solution.py:59
  168.2 4.2 %all-to-all-start.2 = ((bf16[8,64,1024]{2,1,0:T(8,128)(2,1)}), bf16[8,64,1024]{2,1,0:T(8,128)(2,1)}, u32[]{:S(2)}, u32[]{:S(2)}) async-start(bf16[8,64,1024]{2,1,0:T(8,128)(2,1)} %bitcast.43), calls=%async_computation.2 | async-start | bytes 2097152 | tf_op jit(solution)/shard_map/all_to_all | solution.py:1009
  172.5 1.9 collective-permute-start.22
  177.5 32.0 %shard_map.225 = (f32[64,16,512]{2,1,0:T(8,128)}, f32[64,512]{1,0:T(8,128)S(1)}, bf16[96,1024]{1,0:T(8,128)(2,1)S(1)}, f32[16,512]{1,0:T(8,128)S(1)}, f32[1,512]{1,0:T(1,128)S(1)}, /*index=5*/f32[1,512]{1,0:T(1,128)S(1)}) custom-call(f32[64,16,128]{2,1,0:T(8,128)S(1)} %copy-done.41, bf16[192,512]{1,0:T(8,128)(2,1)S(1)} %copy.46.small_ref, ...), custom_call_target="tpu_custom_call" | custom-call | flops 40249999360 | bytes 8000000 | tf_op jit(solution)/shard_map/pallas_call | solution.py:59
  210.4 1.4 collective-permute-done.24
  212.5 2.1 convert_reduce_fusion
  214.6 4.3 %collective-permute-done.25.other_ref = bf16[96,1024]{1,0:T(8,128)(2,1)S(1)} collective-permute-done((bf16[96,1024]{1,0:T(8,128)(2,1)S(1)}, bf16[96,1024]{1,0:T(8,128)(2,1)S(1)}, u32[]{:S(2)}, u32[]{:S(2)}) %collective-permute-start.25) | collective-permute-done | bytes 196640 | tf_op jit(solution)/shard_map/ppermute | solution.py:819
  219.6 8.8 %shard_map.226 = (f32[1024,512]{1,0:T(8,128)}, f32[3,16,512]{2,1,0:T(8,128)}, f32[3,4,512]{2,1,0:T(4,128)}, f32[192,512]{1,0:T(8,128)}, f32[176,512]{1,0:T(8,128...) custom-call(s32[2]{0:T(128)} %copy-done.24, bf16[96,1024]{1,0:T(8,128)(2,1)} %copy-done.51, ...), custom_call_target="tpu_custom_call" | custom-call | flops 6899999744 | bytes 8000000 | tf_op jit(solution)/shard_map/pallas_call | solution.py:59
  228.4 1.5 collective-permute-start.26
  231.8 2.3 collective-permute-start.28
  234.1 2.7 collective-permute-start.29
  237.8 1.6 copy-done.26
  239.4 1.6 copy-done.29
  241.9 2.8 shard_map.227
  245.8 7.3 %shard_map.228 = (bf16[2,4,64,1024]{3,2,1,0:T(8,128)(2,1)S(1)}, bf16[2,4,64,1024]{3,2,1,0:T(8,128)(2,1)}) custom-call(s32[2]{0:T(128)S(1)} %copy-done.25, bf16[1024,512]{1,0:T(8,128)(2,1)S(1)} %get-tuple-element.186.inner_ref, bf16[1024,512]{1,0:T(8,128)(2,1)S(1)} %copy-done.33, bf16[4,136,512]{2,1,0:T(8,128)(2,1)S(1)} %copy-done.3, ...), custom_call_target="tpu_custom_call" | custom-call | flops 11500000256 | bytes 8000000 | tf_op jit(solution)/shard_map/pallas_call | solution.py:59
  254.0 6.3 %all-to-all-start.3 = ((bf16[32,32,512]{2,1,0:T(8,128)(2,1)}), bf16[32,32,512]{2,1,0:T(8,128)(2,1)}, u32[]{:S(2)}, u32[]{:S(2)}) async-start(bf16[32,32,512]{2,1,0:T(8,128)(2,1)} %bitcast.101), calls=%async_computation.3 | async-start | bytes 2097152 | tf_op jit(solution)/shard_map/all_to_all | solution.py:1084
  260.3 2.0 fusion.13
  265.5 1.7 collective-permute-start.36
  267.2 1.5 collective-permute-start.32
  270.5 2.6 collective-permute-done.36
  276.3 10.9 %collective-permute-done.32 = bf16[4,64,1024]{2,1,0:T(8,128)(2,1)} collective-permute-done((bf16[4,64,1024]{2,1,0:T(8,128)(2,1)}, bf16[4,64,1024]{2,1,0:T(8,128)(2,1)}, u32[]{:S(2)}, u32[]{:S(2)}) %collective-permute-start.32) | collective-permute-done | bytes 524320 | tf_op jit(solution)/shard_map/ppermute | solution.py:819
  287.2 1.6 fusion.2
  288.8 3.4 %fusion.6 = (bf16[4,64,1024]{2,1,0:T(8,128)(2,1)}, bf16[4,64,1024]{2,1,0:T(8,128)(2,1)}) fusion(bf16[4,64,1024]{2,1,0:T(8,128)(2,1)S(1)} %copy-done, bf16[4,64,1024]{2,1,0:T(8,128)(2,1)} %slab0_ref.1, bf16[4,64,1024]{2,1,0:T(8,128)(2,1)} %collective-permute-done.32, f32[4,64]{1,0:T(4,128)S(1)} %broadcast_multiply_fusion, f32[1024]{0:T(1024)S(1)} %bitcast.131, ...), kind=kLoop, calls=%fused_computation.10 | loop fusion | flops 5505024 | bytes 5249024 | tf_op jit(solution)/shard_map/convert_element_type | solution.py:1151
  292.3 2.3 shard_map.230
  (252 shorter events, 48.0 us)
Async XLA Ops:
  5.5 19.7 %collective-permute-start = (bf16[4,64,1024]{2,1,0:T(8,128)(2,1)S(1)}, bf16[4,64,1024]{2,1,0:T(8,128)(2,1)S(1)}, u32[]{:S(2)}, u32[]{:S(2)}) collective-permute-start(bf16[4,64,1024]{2,1,0:T(8,128)(2,1)S(1)} %copy-done), channel_id=1, source_target_pairs={{0,2},{1,3},{2,0},{3,1},{4,6},{5,7},{6,4},{7,5},{8,10},{9,11},{10,... | collective-permute-start | bytes 1572872 | tf_op jit(solution)/shard_map/ppermute | solution.py:819
  8.5 12.7 %collective-permute-start.1 = (bf16[80,1024]{1,0:T(8,128)(2,1)S(1)}, bf16[80,1024]{1,0:T(8,128)(2,1)S(1)}, u32[]{:S(2)}, u32[]{:S(2)}) collective-permute-start(bf16[80,1024]{1,0:T(8,128)(2,1)S(1)} %pad_maximum_fusion.5), channel_id=1, source_target_pairs={{0,8},{4,12},{8,0},{12,4},{16,24},{20,28},{24,16},{28,20},{1,9},{5... | collective-permute-start | bytes 491528 | tf_op jit(solution)/shard_map/ppermute | solution.py:819
  10.1 15.1 %collective-permute-start.2 = (bf16[80,1024]{1,0:T(8,128)(2,1)S(1)}, bf16[80,1024]{1,0:T(8,128)(2,1)S(1)}, u32[]{:S(2)}, u32[]{:S(2)}) collective-permute-start(bf16[80,1024]{1,0:T(8,128)(2,1)S(1)} %pad_maximum_fusion.5), channel_id=1, source_target_pairs={{0,16},{4,20},{8,24},{12,28},{16,0},{20,4},{24,8},{28,12},{1,17},{... | collective-permute-start | bytes 491528 | tf_op jit(solution)/shard_map/ppermute | solution.py:819
  12.7 12.5 %collective-permute-start.3 = (bf16[80,1024]{1,0:T(8,128)(2,1)S(1)}, bf16[80,1024]{1,0:T(8,128)(2,1)S(1)}, u32[]{:S(2)}, u32[]{:S(2)}) collective-permute-start(bf16[80,1024]{1,0:T(8,128)(2,1)S(1)} %pad_maximum_fusion.5), channel_id=1, source_target_pairs={{0,24},{4,28},{8,16},{12,20},{16,8},{20,12},{24,0},{28,4},{1,25},{... | collective-permute-start | bytes 491528 | tf_op jit(solution)/shard_map/ppermute | solution.py:819
  12.9 12.3 %all-to-all-start = ((bf16[4,72,512]{2,1,0:T(8,128)(2,1)}), bf16[4,72,512]{2,1,0:T(8,128)(2,1)S(1)}, u32[]{:S(2)}, u32[]{:S(2)}) async-start(bf16[4,72,512]{2,1,0:T(8,128)(2,1)} %pad_maximum_fusion.3), calls=%async_computation | async-start | bytes 589824 | tf_op jit(solution)/shard_map/all_to_all | solution.py:851
  16.4 4.7 %collective-permute-start.16 = (s32[4,3]{1,0:T(4,128)S(1)}, s32[4,3]{1,0:T(4,128)S(1)}, u32[]{:S(2)}, u32[]{:S(2)}) collective-permute-start(s32[4,3]{1,0:T(4,128)S(1)} %slice.112), channel_id=1, source_target_pairs={{0,4},{4,8},{8,12},{12,16},{16,20},{20,24},{24,28},{1,5},{5,9},{9,... | collective-permute-start | bytes 152 | tf_op jit(solution)/shard_map/ppermute | solution.py:886
  19.9 137.8 %copy-start.24 = (s32[2]{0:T(128)}, s32[2]{0:T(128)S(1)}, u32[]{:S(2)}) copy-start(s32[2]{0:T(128)S(1)} %pad_add_fusion.1.place_ref) | copy-start | bytes 28
  26.0 18.2 %collective-permute-start.4 = (bf16[4,80,1024]{2,1,0:T(8,128)(2,1)S(1)}, bf16[4,80,1024]{2,1,0:T(8,128)(2,1)S(1)}, u32[]{:S(2)}, u32[]{:S(2)}) collective-permute-start(bf16[4,80,1024]{2,1,0:T(8,128)(2,1)S(1)} %pad_maximum_fusion.exit_near_ref), channel_id=1, source_target_pairs={{0,4},{4,0},{8,12},{12,8},{16,20},{20,16},{24,28},{28,24},{1,5},{5... | collective-permute-start | bytes 1966088 | tf_op jit(solution)/shard_map/ppermute | solution.py:819
  28.2 6.1 %collective-permute-start.5 = (bf16[136,512]{1,0:T(8,128)(2,1)}, bf16[136,512]{1,0:T(8,128)(2,1)S(1)}, u32[]{:S(2)}, u32[]{:S(2)}) collective-permute-start(bf16[136,512]{1,0:T(8,128)(2,1)} %pad_maximum_fusion.6), channel_id=1, source_target_pairs={{0,8},{4,12},{8,0},{12,4},{16,24},{20,28},{24,16},{28,20},{1,9},{5... | collective-permute-start | bytes 417800 | tf_op jit(solution)/shard_map/ppermute | solution.py:819
  30.6 13.7 %collective-permute-start.8 = (bf16[4,64,1024]{2,1,0:T(8,128)(2,1)S(1)}, bf16[4,64,1024]{2,1,0:T(8,128)(2,1)}, u32[]{:S(2)}, u32[]{:S(2)}) collective-permute-start(bf16[4,64,1024]{2,1,0:T(8,128)(2,1)S(1)} %copy-done), channel_id=1, source_target_pairs={{0,1},{1,0},{2,3},{3,2},{4,5},{5,4},{6,7},{7,6},{8,9},{9,8},{10,11... | collective-permute-start | bytes 1572872 | tf_op jit(solution)/shard_map/ppermute | solution.py:819
  30.6 13.7 %collective-permute-start.9 = (bf16[4,64,1024]{2,1,0:T(8,128)(2,1)S(1)}, bf16[4,64,1024]{2,1,0:T(8,128)(2,1)}, u32[]{:S(2)}, u32[]{:S(2)}) collective-permute-start(bf16[4,64,1024]{2,1,0:T(8,128)(2,1)S(1)} %collective-permute-done.slab2_ref), channel_id=1, source_target_pairs={{0,1},{1,0},{2,3},{3,2},{4,5},{5,4},{6,7},{7,6},{8,9},{9,8},{10,11... | collective-permute-start | bytes 1572872 | tf_op jit(solution)/shard_map/ppermute | solution.py:819
  31.1 13.1 %collective-permute-start.6 = (bf16[136,512]{1,0:T(8,128)(2,1)}, bf16[136,512]{1,0:T(8,128)(2,1)}, u32[]{:S(2)}, u32[]{:S(2)}) collective-permute-start(bf16[136,512]{1,0:T(8,128)(2,1)} %pad_maximum_fusion.6), channel_id=1, source_target_pairs={{0,16},{4,20},{8,24},{12,28},{16,0},{20,4},{24,8},{28,12},{1,17},{... | collective-permute-start | bytes 417800 | tf_op jit(solution)/shard_map/ppermute | solution.py:819
  34.4 9.9 %collective-permute-start.7 = (bf16[136,512]{1,0:T(8,128)(2,1)}, bf16[136,512]{1,0:T(8,128)(2,1)}, u32[]{:S(2)}, u32[]{:S(2)}) collective-permute-start(bf16[136,512]{1,0:T(8,128)(2,1)} %pad_maximum_fusion.6), channel_id=1, source_target_pairs={{0,24},{4,28},{8,16},{12,20},{16,8},{20,12},{24,0},{28,4},{1,25},{... | collective-permute-start | bytes 417800 | tf_op jit(solution)/shard_map/ppermute | solution.py:819
  37.9 54.8 %copy-start.5 = (f32[4,4,64,4]{3,0,1,2:T(4,128)}, f32[4,4,64,4]{3,0,1,2:T(4,128)S(1)}, u32[]{:S(2)}) copy-start(f32[4,4,64,4]{3,0,1,2:T(4,128)S(1)} %copy.43) | copy-start | bytes 49156
  45.7 22.9 %collective-permute-start.10 = (bf16[4,136,512]{2,1,0:T(8,128)(2,1)S(1)}, bf16[4,136,512]{2,1,0:T(8,128)(2,1)}, u32[]{:S(2)}, u32[]{:S(2)}) collective-permute-start(bf16[4,136,512]{2,1,0:T(8,128)(2,1)S(1)} %pad_maximum_fusion.1.near_ref), channel_id=1, source_target_pairs={{0,4},{4,0},{8,12},{12,8},{16,20},{20,16},{24,28},{28,24},{1,5},{5... | collective-permute-start | bytes 1671176 | tf_op jit(solution)/shard_map/ppermute | solution.py:819
  48.8 12.2 %collective-permute-start.11 = (bf16[12,1024]{1,0:T(8,128)(2,1)S(1)}, bf16[12,1024]{1,0:T(8,128)(2,1)S(1)}, u32[]{:S(2)}, u32[]{:S(2)}) collective-permute-start(bf16[12,1024]{1,0:T(8,128)(2,1)S(1)} %reshape.132), channel_id=1, source_target_pairs={{0,4},{4,8},{8,12},{12,16},{16,20},{20,24},{24,28},{1,5},{5,9},{9,... | collective-permute-start | bytes 73736 | tf_op jit(solution)/shard_map/ppermute | solution.py:881
  51.6 12.9 %collective-permute-start.13 = (bf16[128,512]{1,0:T(8,128)(2,1)}, bf16[128,512]{1,0:T(8,128)(2,1)}, u32[]{:S(2)}, u32[]{:S(2)}) collective-permute-start(bf16[128,512]{1,0:T(8,128)(2,1)} %bitcast.121), channel_id=1, source_target_pairs={{0,8},{4,12},{8,0},{12,4},{16,24},{20,28},{24,16},{28,20},{1,9},{5... | collective-permute-start | bytes 393224 | tf_op jit(solution)/shard_map/ppermute | solution.py:819
  54.8 9.7 %collective-permute-start.14 = (bf16[128,512]{1,0:T(8,128)(2,1)}, bf16[128,512]{1,0:T(8,128)(2,1)}, u32[]{:S(2)}, u32[]{:S(2)}) collective-permute-start(bf16[128,512]{1,0:T(8,128)(2,1)} %bitcast.122), channel_id=1, source_target_pairs={{0,16},{4,20},{8,24},{12,28},{16,0},{20,4},{24,8},{28,12},{1,17},{... | collective-permute-start | bytes 393224 | tf_op jit(solution)/shard_map/ppermute | solution.py:819
  55.8 12.9 %collective-permute-start.12 = (bf16[4,64,1024]{2,1,0:T(8,128)(2,1)S(1)}, bf16[4,64,1024]{2,1,0:T(8,128)(2,1)}, u32[]{:S(2)}, u32[]{:S(2)}) collective-permute-start(bf16[4,64,1024]{2,1,0:T(8,128)(2,1)S(1)} %copy-done.4), channel_id=1, source_target_pairs={{0,2},{1,3},{2,0},{3,1},{4,6},{5,7},{6,4},{7,5},{8,10},{9,11},{10,... | collective-permute-start | bytes 1572872 | tf_op jit(solution)/shard_map/ppermute | solution.py:819
  61.0 7.3 %collective-permute-start.15 = (bf16[128,512]{1,0:T(8,128)(2,1)}, bf16[128,512]{1,0:T(8,128)(2,1)}, u32[]{:S(2)}, u32[]{:S(2)}) collective-permute-start(bf16[128,512]{1,0:T(8,128)(2,1)} %bitcast.123), channel_id=1, source_target_pairs={{0,24},{4,28},{8,16},{12,20},{16,8},{20,12},{24,0},{28,4},{1,25},{... | collective-permute-start | bytes 393224 | tf_op jit(solution)/shard_map/ppermute | solution.py:819
  64.5 109.9 %copy-start.10 = (bf16[192,512]{1,0:T(8,128)(2,1)}, bf16[192,512]{1,0:T(8,128)(2,1)S(1)}, u32[]{:S(2)}) copy-start(bf16[192,512]{1,0:T(8,128)(2,1)S(1)} %copy.46.small_ref) | copy-start | bytes 589828
  70.0 16.1 %collective-permute-start.19 = (bf16[4,64,1024]{2,1,0:T(8,128)(2,1)S(1)}, bf16[4,64,1024]{2,1,0:T(8,128)(2,1)S(1)}, u32[]{:S(2)}, u32[]{:S(2)}) collective-permute-start(bf16[4,64,1024]{2,1,0:T(8,128)(2,1)S(1)} %copy-done.4), channel_id=1, source_target_pairs={{0,1},{1,0},{2,3},{3,2},{4,5},{5,4},{6,7},{7,6},{8,9},{9,8},{10,11... | collective-permute-start | bytes 1572872 | tf_op jit(solution)/shard_map/ppermute | solution.py:819
  70.0 16.1 %collective-permute-start.20 = (bf16[4,64,1024]{2,1,0:T(8,128)(2,1)}, bf16[4,64,1024]{2,1,0:T(8,128)(2,1)S(1)}, u32[]{:S(2)}, u32[]{:S(2)}) collective-permute-start(bf16[4,64,1024]{2,1,0:T(8,128)(2,1)} %collective-permute-done.12.slab2_ref), channel_id=1, source_target_pairs={{0,1},{1,0},{2,3},{3,2},{4,5},{5,4},{6,7},{7,6},{8,9},{9,8},{10,11... | collective-permute-start | bytes 1572872 | tf_op jit(solution)/shard_map/ppermute | solution.py:819
  71.6 14.5 %collective-permute-start.21 = (bf16[4,128,512]{2,1,0:T(8,128)(2,1)S(1)}, bf16[4,128,512]{2,1,0:T(8,128)(2,1)S(1)}, u32[]{:S(2)}, u32[]{:S(2)}) collective-permute-start(bf16[4,128,512]{2,1,0:T(8,128)(2,1)S(1)} %pad_maximum_fusion.2.near_ref.gate_near_ref), channel_id=1, source_target_pairs={{0,4},{4,0},{8,12},{12,8},{16,20},{20,16},{24,28},{28,24},{1,5},{5... | collective-permute-start | bytes 1572872 | tf_op jit(solution)/shard_map/ppermute | solution.py:819
  83.9 52.2 %copy-start.22 = (f32[1024,512]{1,0:T(8,128)}, f32[1024,512]{1,0:T(8,128)S(1)}, u32[]{:S(2)}) copy-start(f32[1024,512]{1,0:T(8,128)S(1)} %get-tuple-element.138.filter_ref) | copy-start | bytes 6291460
  83.9 73.8 %copy-start.28 = (bf16[1024,1024]{1,0:T(8,128)(2,1)}, bf16[1024,1024]{1,0:T(8,128)(2,1)S(1)}, u32[]{:S(2)}) copy-start(bf16[1024,1024]{1,0:T(8,128)(2,1)S(1)} %get-tuple-element.141.normed_ref) | copy-start | bytes 6291460
  83.9 1.4 collective-permute-start.17
  85.4 7.3 %collective-permute-start.18 = (bf16[96,1024]{1,0:T(8,128)(2,1)S(1)}, bf16[96,1024]{1,0:T(8,128)(2,1)S(1)}, u32[]{:S(2)}, u32[]{:S(2)}) collective-permute-start(bf16[96,1024]{1,0:T(8,128)(2,1)S(1)} %add_convert_fusion.3.chosen_ref), channel_id=1, source_target_pairs={{0,2},{1,3},{2,0},{3,1},{4,6},{5,7},{6,4},{7,5},{8,10},{9,11},{10,... | collective-permute-start | bytes 589832 | tf_op jit(solution)/shard_map/ppermute | solution.py:819
  92.8 43.3 %copy-start.23 = (f32[1024,512]{1,0:T(8,128)}, f32[1024,512]{1,0:T(8,128)S(1)}, u32[]{:S(2)}) copy-start(f32[1024,512]{1,0:T(8,128)S(1)} %get-tuple-element.160) | copy-start | bytes 6291460
  113.7 44.0 %copy-start.36 = (f32[64,16,512]{2,1,0:T(8,128)}, f32[64,16,512]{2,1,0:T(8,128)S(1)}, u32[]{:S(2)}) copy-start(f32[64,16,512]{2,1,0:T(8,128)S(1)} %get-tuple-element.149.step_ref) | copy-start | bytes 6291460
  113.7 44.0 %copy-start.40 = (f32[64,16,128]{2,1,0:T(8,128)}, f32[64,16,128]{2,1,0:T(8,128)S(1)}, u32[]{:S(2)}) copy-start(f32[64,16,128]{2,1,0:T(8,128)S(1)} %get-tuple-element.148.gates_ref) | copy-start | bytes 1572868
  168.2 42.1 %collective-permute-start.23 = (bf16[2,4,64,1024]{3,2,1,0:T(8,128)(2,1)}, bf16[2,4,64,1024]{3,2,1,0:T(8,128)(2,1)}, u32[]{:S(2)}, u32[]{:S(2)}) collective-permute-start(bf16[2,4,64,1024]{3,2,1,0:T(8,128)(2,1)} %get-tuple-element.159), channel_id=1, source_target_pairs={{0,1},{1,0},{2,3},{3,2},{4,5},{5,4},{6,7},{7,6},{8,9},{9,8},{10,11... | collective-permute-start | bytes 3145736 | tf_op jit(solution)/shard_map/ppermute | solution.py:819
  168.2 42.1 %all-to-all-start.2 = ((bf16[8,64,1024]{2,1,0:T(8,128)(2,1)}), bf16[8,64,1024]{2,1,0:T(8,128)(2,1)}, u32[]{:S(2)}, u32[]{:S(2)}) async-start(bf16[8,64,1024]{2,1,0:T(8,128)(2,1)} %bitcast.43), calls=%async_computation.2 | async-start | bytes 2097152 | tf_op jit(solution)/shard_map/all_to_all | solution.py:1009
  172.5 37.0 %collective-permute-start.22 = (bf16[4,128,512]{2,1,0:T(8,128)(2,1)S(1)}, bf16[4,128,512]{2,1,0:T(8,128)(2,1)S(1)}, u32[]{:S(2)}, u32[]{:S(2)}) collective-permute-start(bf16[4,128,512]{2,1,0:T(8,128)(2,1)S(1)} %get-tuple-element.166), channel_id=1, source_target_pairs={{0,4},{4,0},{8,12},{12,8},{16,20},{20,16},{24,28},{28,24},{1,5},{5... | collective-permute-start | bytes 1572872 | tf_op jit(solution)/shard_map/ppermute | solution.py:819
  210.4 1.4 collective-permute-start.24
  211.9 7.0 %collective-permute-start.25 = (bf16[96,1024]{1,0:T(8,128)(2,1)S(1)}, bf16[96,1024]{1,0:T(8,128)(2,1)S(1)}, u32[]{:S(2)}, u32[]{:S(2)}) collective-permute-start(bf16[96,1024]{1,0:T(8,128)(2,1)S(1)} %add_convert_fusion.2.chosen_ref), channel_id=1, source_target_pairs={{0,2},{1,3},{2,0},{3,1},{4,6},{5,7},{6,4},{7,5},{8,10},{9,11},{10,... | collective-permute-start | bytes 589832 | tf_op jit(solution)/shard_map/ppermute | solution.py:819
  228.4 8.4 %collective-permute-start.26 = (f32[3,4,512]{2,1,0:T(4,128)}, f32[3,4,512]{2,1,0:T(4,128)S(1)}, u32[]{:S(2)}, u32[]{:S(2)}) collective-permute-start(f32[3,4,512]{2,1,0:T(4,128)} %get-tuple-element.181), channel_id=1, source_target_pairs={{4,0},{8,4},{12,8},{16,12},{20,16},{24,20},{28,24},{5,1},{9,5},{13... | collective-permute-start | bytes 73736 | tf_op jit(solution)/shard_map/ppermute | solution.py:1073
  231.1 14.6 %collective-permute-start.27 = (bf16[4,64,1024]{2,1,0:T(8,128)(2,1)S(1)}, bf16[4,64,1024]{2,1,0:T(8,128)(2,1)S(1)}, u32[]{:S(2)}, u32[]{:S(2)}) collective-permute-start(bf16[4,64,1024]{2,1,0:T(8,128)(2,1)S(1)} %fusion.12), channel_id=1, source_target_pairs={{0,2},{1,3},{2,0},{3,1},{4,6},{5,7},{6,4},{7,5},{8,10},{9,11},{10,... | collective-permute-start | bytes 1572872 | tf_op jit(solution)/shard_map/ppermute | solution.py:819
  231.8 21.4 %collective-permute-start.28 = (bf16[176,512]{1,0:T(8,128)(2,1)}, bf16[176,512]{1,0:T(8,128)(2,1)S(1)}, u32[]{:S(2)}, u32[]{:S(2)}) collective-permute-start(bf16[176,512]{1,0:T(8,128)(2,1)} %get-tuple-element.190), channel_id=1, source_target_pairs={{0,8},{4,12},{8,0},{12,4},{16,24},{20,28},{24,16},{28,20},{1,9},{5... | collective-permute-start | bytes 540680 | tf_op jit(solution)/shard_map/ppermute | solution.py:819
  234.1 19.0 %collective-permute-start.29 = (bf16[176,512]{1,0:T(8,128)(2,1)}, bf16[176,512]{1,0:T(8,128)(2,1)S(1)}, u32[]{:S(2)}, u32[]{:S(2)}) collective-permute-start(bf16[176,512]{1,0:T(8,128)(2,1)} %get-tuple-element.191), channel_id=1, source_target_pairs={{0,16},{4,20},{8,24},{12,28},{16,0},{20,4},{24,8},{28,12},{1,17},{... | collective-permute-start | bytes 540680 | tf_op jit(solution)/shard_map/ppermute | solution.py:819
  236.8 17.0 %collective-permute-start.30 = (bf16[176,512]{1,0:T(8,128)(2,1)}, bf16[176,512]{1,0:T(8,128)(2,1)S(1)}, u32[]{:S(2)}, u32[]{:S(2)}) collective-permute-start(bf16[176,512]{1,0:T(8,128)(2,1)} %get-tuple-element.192), channel_id=1, source_target_pairs={{0,24},{4,28},{8,16},{12,20},{16,8},{20,12},{24,0},{28,4},{1,25},{... | collective-permute-start | bytes 540680 | tf_op jit(solution)/shard_map/ppermute | solution.py:819
  253.8 6.5 %collective-permute-start.31 = (bf16[2,4,64,1024]{3,2,1,0:T(8,128)(2,1)}, bf16[2,4,64,1024]{3,2,1,0:T(8,128)(2,1)}, u32[]{:S(2)}, u32[]{:S(2)}) collective-permute-start(bf16[2,4,64,1024]{3,2,1,0:T(8,128)(2,1)} %get-tuple-element.193), channel_id=1, source_target_pairs={{0,1},{1,0},{2,3},{3,2},{4,5},{5,4},{6,7},{7,6},{8,9},{9,8},{10,11... | collective-permute-start | bytes 3145736 | tf_op jit(solution)/shard_map/ppermute | solution.py:819
  254.0 38.2 %all-to-all-start.3 = ((bf16[32,32,512]{2,1,0:T(8,128)(2,1)}), bf16[32,32,512]{2,1,0:T(8,128)(2,1)}, u32[]{:S(2)}, u32[]{:S(2)}) async-start(bf16[32,32,512]{2,1,0:T(8,128)(2,1)} %bitcast.101), calls=%async_computation.3 | async-start | bytes 2097152 | tf_op jit(solution)/shard_map/all_to_all | solution.py:1084
  265.5 7.7 %collective-permute-start.36 = (f32[192,128]{1,0:T(8,128)S(1)}, f32[192,128]{1,0:T(8,128)S(1)}, u32[]{:S(2)}, u32[]{:S(2)}) collective-permute-start(f32[192,128]{1,0:T(8,128)S(1)} %get-tuple-element.206), channel_id=1, source_target_pairs={{0,4},{4,0},{8,12},{12,8},{16,20},{20,16},{24,28},{28,24},{1,5},{5... | collective-permute-start | bytes 294920 | tf_op jit(solution)/shard_map/ppermute | solution.py:819
  267.2 20.0 %collective-permute-start.32 = (bf16[4,64,1024]{2,1,0:T(8,128)(2,1)}, bf16[4,64,1024]{2,1,0:T(8,128)(2,1)}, u32[]{:S(2)}, u32[]{:S(2)}) collective-permute-start(bf16[4,64,1024]{2,1,0:T(8,128)(2,1)} %fusion.13), channel_id=1, source_target_pairs={{0,2},{1,3},{2,0},{3,1},{4,6},{5,7},{6,4},{7,5},{8,10},{9,11},{10,... | collective-permute-start | bytes 1572872 | tf_op jit(solution)/shard_map/ppermute | solution.py:819
  268.7 23.6 %collective-permute-start.33 = (bf16[32,512]{1,0:T(8,128)(2,1)}, bf16[32,512]{1,0:T(8,128)(2,1)S(1)}, u32[]{:S(2)}, u32[]{:S(2)}) collective-permute-start(bf16[32,512]{1,0:T(8,128)(2,1)} %get-tuple-element.201), channel_id=1, source_target_pairs={{0,1},{1,0},{2,3},{3,2},{4,5},{5,4},{6,7},{7,6},{8,9},{9,8},{10,11... | collective-permute-start | bytes 98312 | tf_op jit(solution)/shard_map/ppermute | solution.py:819
  268.7 23.6 %collective-permute-start.34 = (bf16[32,512]{1,0:T(8,128)(2,1)S(1)}, bf16[32,512]{1,0:T(8,128)(2,1)S(1)}, u32[]{:S(2)}, u32[]{:S(2)}) collective-permute-start(bf16[32,512]{1,0:T(8,128)(2,1)S(1)} %get-tuple-element.202), channel_id=1, source_target_pairs={{0,2},{1,3},{2,0},{3,1},{4,6},{5,7},{6,4},{7,5},{8,10},{9,11},{10,... | collective-permute-start | bytes 98312 | tf_op jit(solution)/shard_map/ppermute | solution.py:819
  269.3 23.0 %collective-permute-start.35 = (bf16[32,512]{1,0:T(8,128)(2,1)S(1)}, bf16[32,512]{1,0:T(8,128)(2,1)S(1)}, u32[]{:S(2)}, u32[]{:S(2)}) collective-permute-start(bf16[32,512]{1,0:T(8,128)(2,1)S(1)} %get-tuple-element.203), channel_id=1, source_target_pairs={{0,3},{1,2},{2,1},{3,0},{4,7},{5,6},{6,5},{7,4},{8,11},{9,10},{10,... | collective-permute-start | bytes 98312 | tf_op jit(solution)/shard_map/ppermute | solution.py:819
  (58 other events, 345.1 us)

commit v4 on v3

--- a/solution.py
+++ b/solution.py
@@ -295,7 +295,7 @@
 
     lax.fori_loop(0, chunks // 8, half_lap, 0)
 
-    sequences = ahead_ref.shape[0] // (states + 4)
+    sequences = ahead_ref.shape[0] // (states + 2)
     groups = chunks // sequences
     for n in range(states):
         rows = slice(n * sequences, (n + 1) * sequences)
@@ -312,11 +312,10 @@
     for k in range(groups):
         total = total + sum_ref[k * sequences : (k + 1) * sequences, :]
     held = states * sequences
-    for k in range(3):
+    for k in range(2):
         term = total.astype(bf16).astype(f32)
         ahead_ref[held + k * sequences : held + (k + 1) * sequences, :] = term
         total = total - term
-    ahead_ref[held + 3 * sequences :, :] = jnp.zeros((sequences, width), f32)
     back_ref[held:, :] = ahead_ref[held:, :]
 
     def load_lap(piece, carry):
@@ -343,7 +342,7 @@
     steps, _, width = step_ref.shape
     states, chunks = end_ref.shape[:2]
     pieces = came_ref.shape[0]
-    sequences = came_ref.shape[1] // (states + 4)
+    sequences = came_ref.shape[1] // (states + 2)
     groups = chunks // sequences
     @pl.when(half == 0)
     def _():
@@ -359,8 +358,7 @@
         def step_in(piece, state):
             values = came_ref[piece].astype(f32)
             total = values[held : held + sequences, :]
-            for k in range(1, 3):
-                total = total + values[held + k * sequences : held + (k + 1) * sequences, :]
+            total = total + values[held + sequences :, :]
             total = jnp.concatenate([total] * states, axis=0)
             return jnp.exp2(total * rates) * state + values[:held, :]
 
@@ -612,11 +610,14 @@
 def filter_kernel(
     place_ref, chosen_ref, other_ref, direct_ref, inner_ref, filter_ref, mask_ref, small_ref,
     rank_ref, decay_ref, bias_ref, skip_ref, gate_keep_ref, gate_came_ref,
-    grads_ref, spill_ref, first_ref, small_out_ref, total_ref, *refs,
+    back_ref, tail_ref, first_ref, small_out_ref, total_ref, *refs,
 ):
-    part_refs, (packed_ref, picked_ref, taps_ref, offset_ref) = refs[:-4], refs[-4:]
+    part_refs, (packed_ref, picked_ref, taps_ref, offset_ref, grads_ref, past_ref) = refs[:-6], refs[-6:]
     rows, width = grads_ref.shape
-    chunks = spill_ref.shape[1]
+    chunks, sequences = tail_ref.shape[1], first_ref.shape[1]
+    rim_rows = 3 * chunks
+    for k in range(3):
+        past_ref[k, rows : rows + rim_rows, :] = jnp.zeros((rim_rows, width), f32)
     block_rows = chunks * 8
     chosen = (chosen_ref[...].astype(f32) + other_ref[...].astype(f32)).astype(bf16)
     packed_ref[0:64, :] = rank_ref[...]
@@ -643,6 +644,8 @@
         grad = direct_ref[at, :] + dot(picked_ref[at, :], small_ref[64:160, :])
         grad = grad * (gate * (1.0 + total * (1.0 - gate)))
         grads_ref[at, :] = grad
+        for k in range(3):
+            past_ref[k, at, :] = grad * taps[k] * mask_ref[at, k : k + 1]
         offset_ref[...] += jnp.sum(grad, axis=0, keepdims=True)
         for k in range(4):
             taps_ref[k : k + 1, :] += jnp.sum(grad * shifted[k], axis=0, keepdims=True)
@@ -664,57 +667,42 @@
             for q in range(4):
                 values = packed_ref[q * below // 4 : (q + 1) * below // 4, lanes]
                 target[height:, q * 128 : (q + 1) * 128] = values.astype(target.dtype)
+    spills = []
     for u in range(3):
         total = jnp.zeros((chunks, width), f32)
         for t in range(u + 1):
-            part = slice(t * chunks, (t + 1) * chunks)
-            total = total + grads_ref[part, :] * taps[u - t] * mask_ref[part, u - t : u - t + 1]
-        spill_ref[u] = total
-        first_ref[u] = total[0 : first_ref.shape[1], :]
-
-
-def inner_kernel(
-    grads_ref, spill_ref, after_ref, mask_ref, small_ref, normed_ref,
-    inner_ref, entry_grad_ref,
-    past_ref,
-):
-    rows, inner_width = grads_ref.shape
-    chunks, sequences = spill_ref.shape[1], after_ref.shape[1]
-    block_rows = chunks * 8
-    blocks = rows // block_rows
-    later_spill = jnp.concatenate([spill_ref[:, sequences:, :], after_ref[...]], axis=1)
-    later_spill = later_spill.reshape(3 * chunks, inner_width)
-    taps = [small_row(small_ref, k) for k in range(4)]
-    rim_rows = 3 * chunks
-    for k in range(3):
-        past_ref[k, rows : rows + rim_rows, :] = jnp.zeros((rim_rows, inner_width), f32)
-
-    def mask_lap(block, carry):
-        at = pl.ds(pl.multiple_of(block * block_rows, block_rows), block_rows)
-        grad = grads_ref[at, :]
-        for k in range(3):
-            past_ref[k, at, :] = grad * taps[k] * mask_ref[at, k : k + 1]
-        return carry
-
-    lax.fori_loop(0, blocks, mask_lap, 0)
-
-    def lap(block, carry):
+            total = total + past_ref[u - t, t * chunks : (t + 1) * chunks, :]
+        first_ref[u] = total[0:sequences, :]
+        spills.append(jnp.concatenate([total[sequences:, :], jnp.zeros((sequences, width), f32)], axis=0))
+
+    def back_lap(block, carry):
         base = pl.multiple_of(block * block_rows, block_rows)
         at = pl.ds(base, block_rows)
         total = grads_ref[at, :] * taps[3]
         for k in range(3):
             later = pl.ds(pl.multiple_of(base + (3 - k) * chunks, 16), block_rows)
             total = total + past_ref[k, later, :]
-        inner_ref[at, :] = total.astype(bf16)
-
-        @pl.when(block == blocks - 1)
+        back_ref[at, :] = total.astype(bf16)
+
+        @pl.when(block == rows // block_rows - 1)
         def _():
-            tail = total[block_rows - rim_rows :, :] + later_spill
-            inner_ref[rows - rim_rows : rows, :] = tail.astype(bf16)
-
-        return carry
-
-    lax.fori_loop(0, blocks, lap, 0)
+            for u in range(3):
+                first = block_rows - rim_rows + u * chunks
+                tail_ref[u] = total[first : first + chunks, :] + spills[u]
+
+        return carry
+
+    lax.fori_loop(0, rows // block_rows, back_lap, 0)
+
+
+def inner_kernel(back_ref, tail_ref, after_ref, normed_ref, inner_ref, entry_grad_ref):
+    rows, width = back_ref.shape
+    chunks, sequences = tail_ref.shape[1], after_ref.shape[1]
+    rim_rows = 3 * chunks
+    inner_ref[0 : rows - rim_rows, :] = back_ref[0 : rows - rim_rows, :]
+    later = jnp.concatenate([jnp.zeros((3, chunks - sequences, width), f32), after_ref[...]], axis=1)
+    tail = (tail_ref[...] + later).reshape(rim_rows, width)
+    inner_ref[rows - rim_rows :, :] = tail.astype(bf16)
     entry_grad_ref[...] = dot(normed_ref[...], inner_ref[...], ((0,), (0,))).astype(bf16)
 
 
@@ -890,9 +878,6 @@
     same = (shifted == segments[:, :, None]).astype(f32)
     columns = jnp.concatenate([same, 1.0 - same[:, :, 2:3]], axis=2)
     mask = columns.reshape(sequences, groups, steps, 4).transpose(2, 1, 0, 3).reshape(rows, 4)
-    inner_near, inner_far, rim, cotangent_pair, cotangent, *gate_side = rounds(
-        inner_near, inner_far, rim, cotangent_pair, cotangent, *gate_side
-    )
     gain_all = jnp.sum(inner_near[:, -8:].astype(f32), axis=0) + jnp.sum(inner_far[:, -8:].astype(f32), axis=0)
     gain_all = gain_all[: width // group_width].reshape(1, width)
 
@@ -944,7 +929,7 @@
     )
     cube = (steps, chunks, group_width)
     bank = (states, chunks, group_width)
-    load_rows = (states + 4) * sequences
+    load_rows = (states + 2) * sequences
     gates, step_sizes, step_slopes, ends, keeps, gives, loads = kernel_call(
         piece_kernel,
         23,
@@ -1048,11 +1033,11 @@
 
     paired = 2 * own == 128
     side_block = (block_height + (small_rows // 4 if paired else 0), group_width)
-    grad_sums, spill, first_spill, small_grads, side_total, *side_parts = kernel_call(
+    grad_back, tail_back, first_spill, small_grads, side_total, *side_parts = kernel_call(
         filter_kernel,
         6,
         [
-            ((rows, group_width), f32),
+            ((rows, group_width), bf16),
             ((3, chunks, group_width), f32),
             ((3, sequences, group_width), f32),
             ((small_rows, group_width), f32),
@@ -1064,6 +1049,8 @@
             pltpu.VMEM((rows, 96), bf16),
             pltpu.VMEM((4, group_width), f32),
             pltpu.VMEM((1, group_width), f32),
+            pltpu.VMEM((rows, group_width), f32),
+            pltpu.VMEM((3, rows + 3 * chunks, group_width), f32),
         ],
         62,
         place, *chosen_grads, grad_direct.reshape(rows, group_width), inner, filtered, mask, small,
@@ -1074,11 +1061,11 @@
     side_parts = [flipped(part, "blk", 2 * k + 2) for k, part in enumerate(side_parts)]
     grad_inner, inner_entry = kernel_call(
         inner_kernel,
-        6,
+        4,
         [((rows, group_width), bf16), ((width, group_width), bf16)],
-        [pltpu.VMEM((3, rows + 3 * chunks, group_width), f32)],
-        14,
-        grad_sums, spill, spill_after, mask, small, normed,
+        [],
+        12,
+        grad_back, tail_back, spill_after, normed,
     )
     grad_inner, inner_entry, out_other = rounds(grad_inner, inner_entry, out_other)
     inner_parts = lax.all_to_all(

time: 297 us -> 290 us (0.976)
    unnamed x139 -> x133, local copies, waits for them, and re-layouts: 19.8 us -> 19.6 us
  transfers between devices with their start and end apart: 40 -> 40, of which waited for: 11 -> 11; matrix products, arithmetic and copies ran while one was open for 8% -> 9% of each run, Pallas kernels for 20% -> 23%
where the time goes in v4:
time: 290 us; the launch traced here: 289 us
  Pallas kernels  118 us (41%)
  starting transfers between devices  61 us (21%)
  waiting for transfers between devices  36 us (12%)
  local copies, waits for them, and re-layouts  32.6 us (11%)
  blocking collectives  20.5 us (7%)
  other arithmetic  19.1 us (7%)
    pallas_call x11, Pallas kernels, kernel_call(): pl.pallas_call(body, out_shape=[jax.ShapeDtypeStruct(shape, kind) for sha...  118 us
    ppermute x34, starting transfers between devices, flipped(): lax.ppermute(value, axis, [(i, i ^ bits) for i in range(lax.axis_size(axi...  39.7 us
    ppermute x34, waiting for transfers between devices, flipped(): lax.ppermute(value, axis, [(i, i ^ bits) for i in range(lax.axis_size(axi...  34.8 us
    all_to_all x1, blocking collectives, local(): came = lax.all_to_all(loads, 'blk', split_axis=0, concat_axis=0, tiled=True)  20.5 us
    unnamed x133, local copies, waits for them, and re-layouts  19.6 us
    all_to_all x1, starting transfers between devices, local(): lax.all_to_all(inner_entry.reshape(pieces * groups, slice_rows, group_wid...  5.98 us
  transfers between devices with their start and end apart: 40, of which 11 were waited for; matrix products, arithmetic and copies ran while one was open for 9% of the time, Pallas kernels for 23%

profile of v4, /device:TPU:0, one launch (start us, length us, event | category | flops | bytes accessed | tf_op | source)
XLA Modules:
  0.0 288.7 jit_solution(7745876179265818541)
XLA Ops:
  1.7 1.5 reshape.125
  5.5 3.0 %collective-permute-start = (bf16[4,64,1024]{2,1,0:T(8,128)(2,1)S(1)}, bf16[4,64,1024]{2,1,0:T(8,128)(2,1)S(1)}, u32[]{:S(2)}, u32[]{:S(2)}) collective-permute-start(bf16[4,64,1024]{2,1,0:T(8,128)(2,1)S(1)} %copy-done), channel_id=1, source_target_pairs={{0,2},{1,3},{2,0},{3,1},{4,6},{5,7},{6,4},{7,5},{8,10},{9,11},{10,... | collective-permute-start | bytes 1572872 | tf_op jit(solution)/shard_map/ppermute | solution.py:807
  8.5 1.6 collective-permute-start.1
  10.1 2.6 collective-permute-start.2
  12.9 3.5 %all-to-all-start = ((bf16[4,72,512]{2,1,0:T(8,128)(2,1)}), bf16[4,72,512]{2,1,0:T(8,128)(2,1)S(1)}, u32[]{:S(2)}, u32[]{:S(2)}) async-start(bf16[4,72,512]{2,1,0:T(8,128)(2,1)} %pad_maximum_fusion.3), calls=%async_computation | async-start | bytes 589824 | tf_op jit(solution)/shard_map/all_to_all | solution.py:839
  16.4 3.4 %collective-permute-start.12 = (s32[4,3]{1,0:T(4,128)S(1)}, s32[4,3]{1,0:T(4,128)S(1)}, u32[]{:S(2)}, u32[]{:S(2)}) collective-permute-start(s32[4,3]{1,0:T(4,128)S(1)} %slice.112), channel_id=1, source_target_pairs={{0,4},{4,8},{8,12},{12,16},{16,20},{20,24},{24,28},{1,5},{5,9},{9,... | collective-permute-start | bytes 152 | tf_op jit(solution)/shard_map/ppermute | solution.py:874
  21.2 3.9 %collective-permute-done.2 = bf16[80,1024]{1,0:T(8,128)(2,1)S(1)} collective-permute-done((bf16[80,1024]{1,0:T(8,128)(2,1)S(1)}, bf16[80,1024]{1,0:T(8,128)(2,1)S(1)}, u32[]{:S(2)}, u32[]{:S(2)}) %collective-permute-start.2) | collective-permute-done | bytes 163872 | tf_op jit(solution)/shard_map/ppermute | solution.py:807
  26.0 1.6 collective-permute-start.4
  28.2 2.4 collective-permute-start.5
  32.1 2.2 collective-permute-done.5
  34.4 3.1 %collective-permute-start.7 = (bf16[136,512]{1,0:T(8,128)(2,1)}, bf16[136,512]{1,0:T(8,128)(2,1)}, u32[]{:S(2)}, u32[]{:S(2)}) collective-permute-start(bf16[136,512]{1,0:T(8,128)(2,1)} %pad_maximum_fusion.6), channel_id=1, source_target_pairs={{0,24},{4,28},{8,16},{12,20},{16,8},{20,12},{24,0},{28,4},{1,25},{... | collective-permute-start | bytes 417800 | tf_op jit(solution)/shard_map/ppermute | solution.py:807
  37.9 6.3 %collective-permute-done.6 = bf16[136,512]{1,0:T(8,128)(2,1)} collective-permute-done((bf16[136,512]{1,0:T(8,128)(2,1)}, bf16[136,512]{1,0:T(8,128)(2,1)}, u32[]{:S(2)}, u32[]{:S(2)}) %collective-permute-start.6) | collective-permute-done | bytes 139296 | tf_op jit(solution)/shard_map/ppermute | solution.py:807
  48.6 2.2 collective-permute-start.20
  50.8 2.0 collective-permute-start.19
  54.3 2.1 reshape.137
  60.4 2.8 collective-permute-start.10
  64.7 1.9 collective-permute-start.21
  66.6 2.9 %collective-permute-done.16.slab2_ref = bf16[4,64,1024]{2,1,0:T(8,128)(2,1)} collective-permute-done((bf16[4,64,1024]{2,1,0:T(8,128)(2,1)S(1)}, bf16[4,64,1024]{2,1,0:T(8,128)(2,1)}, u32[]{:S(2)}, u32[]{:S(2)}) %collective-permute-start.16) | collective-permute-done | bytes 524320 | tf_op jit(solution)/shard_map/ppermute | solution.py:807
  73.0 8.5 %shard_map.220 = (bf16[1024,1024]{1,0:T(8,128)(2,1)S(1)}, bf16[1072,512]{1,0:T(8,128)(2,1)S(1)}, f32[1024,512]{1,0:T(8,128)S(1)}, bf16[96,1024]{1,0:T(8,128)(2,1)S(1)}) custom-call(s32[2]{0:T(128)S(1)} %pad_add_fusion.1.place_ref, bf16[4,64,1024]{2,1,0:T(8,128)(2,1)S(1)} %copy-done, bf16[4,64,1024]{2,1,0:T(8,128)(2,1)S(1)} %copy-done.15, ...), custom_call_target="tpu_custom_call" | custom-call | flops 10350000128 | bytes 8000000 | tf_op jit(solution)/shard_map/pallas_call | solution.py:59
  84.8 6.5 %shard_map.221 = (bf16[1024,1024]{1,0:T(8,128)(2,1)S(1)}, f32[1024,512]{1,0:T(8,128)S(1)}, f32[1024,512]{1,0:T(8,128)S(1)}, f32[1024,512]{1,0:T(8,128)S(1)}) custom-call(s32[2]{0:T(128)S(1)} %pad_add_fusion.1.place_ref, bf16[4,64,1024]{2,1,0:T(8,128)(2,1)S(1)} %copy-done.4, bf16[4,64,1024]{2,1,0:T(8,128)(2,1)S(1)} %collective-permute-done.15.slab1_ref, ...), custom_call_target="tpu_custom_call" | custom-call | flops 9200000000 | bytes 8000000 | tf_op jit(solution)/shard_map/pallas_call | solution.py:59
  91.4 19.6 %shard_map.222 = (f32[64,16,128]{2,1,0:T(8,128)S(1)}, f32[64,16,512]{2,1,0:T(8,128)S(1)}, f32[64,16,512]{2,1,0:T(8,128)S(1)}, f32[16,16,512]{2,1,0:T(8,128)S(1)}...) custom-call(s32[2]{0:T(128)S(1)} %pad_add_fusion.1.place_ref, ...), custom_call_target="tpu_custom_call" | custom-call | flops 26449999872 | bytes 8000000 | tf_op jit(solution)/shard_map/pallas_call | solution.py:59
  111.0 1.3 copy-done.37
  112.3 20.5 %all_to_all.20.came_ref = bf16[8,72,512]{2,1,0:T(8,128)(2,1)S(1)} all-to-all(bf16[8,72,512]{2,1,0:T(8,128)(2,1)S(1)} %get-tuple-element.129), channel_id=1, replica_groups=mesh['blk'=8,'grp'=4] {'blk'}, dimensions={0} | all-to-all | bytes 1179648 | tf_op jit(solution)/shard_map/all_to_all | solution.py:956
  132.8 21.5 %shard_map.223 = (f32[64,16,512]{2,1,0:T(8,128)S(1)}, f32[64,16,128]{2,1,0:T(8,128)S(1)}, f32[16,16,16,512]{3,2,1,0:T(8,128)}, f32[16,16,512]{2,1,0:T(8,128)S(1)}) custom-call(s32[2]{0:T(128)S(1)} %pad_add_fusion.1.place_ref, bf16[8,72,512]{2,1,0:T(8,128)(2,1)S(1)} %all_to_all.20.came_ref, f32[64,16,128]{2,1,0:T(8,128)S(1)} %get-tuple-element.130.gates_ref, ...), custom_call_target="tpu_custom_call" | custom-call | flops 20700000256 | bytes 8000000 | tf_op jit(solution)/shard_map/pallas_call | solution.py:59
  154.4 8.7 %shard_map.224 = (bf16[1024,512]{1,0:T(8,128)(2,1)S(1)}, bf16[2,4,64,1024]{3,2,1,0:T(8,128)(2,1)S(1)}, bf16[2,4,64,1024]{3,2,1,0:T(8,128)(2,1)}, bf16[512,1024]{...) custom-call(s32[2]{0:T(128)S(1)} %pad_add_fusion.1.place_ref, ...), custom_call_target="tpu_custom_call" | custom-call | flops 13799999488 | bytes 8000000 | tf_op jit(solution)/shard_map/pallas_call | solution.py:59
  164.9 4.2 %all-to-all-start.2 = ((bf16[8,64,1024]{2,1,0:T(8,128)(2,1)}), bf16[8,64,1024]{2,1,0:T(8,128)(2,1)}, u32[]{:S(2)}, u32[]{:S(2)}) async-start(bf16[8,64,1024]{2,1,0:T(8,128)(2,1)} %bitcast.43), calls=%async_computation.2 | async-start | bytes 2097152 | tf_op jit(solution)/shard_map/all_to_all | solution.py:994
  169.2 1.9 collective-permute-start.22
  174.2 32.0 %shard_map.225 = (f32[64,16,512]{2,1,0:T(8,128)}, f32[64,512]{1,0:T(8,128)S(1)}, bf16[96,1024]{1,0:T(8,128)(2,1)S(1)}, f32[16,512]{1,0:T(8,128)S(1)}, f32[1,512]{1,0:T(1,128)S(1)}, /*index=5*/f32[1,512]{1,0:T(1,128)S(1)}) custom-call(f32[64,16,128]{2,1,0:T(8,128)S(1)} %copy-done.39, bf16[192,512]{1,0:T(8,128)(2,1)S(1)} %copy.46.small_ref, ...), custom_call_target="tpu_custom_call" | custom-call | flops 40249999360 | bytes 8000000 | tf_op jit(solution)/shard_map/pallas_call | solution.py:59
  207.1 2.1 convert_reduce_fusion
  209.3 1.6 collective-permute-start.25
  210.9 2.0 fusion.12
  213.4 3.6 %collective-permute-done.25.other_ref = bf16[96,1024]{1,0:T(8,128)(2,1)S(1)} collective-permute-done((bf16[96,1024]{1,0:T(8,128)(2,1)S(1)}, bf16[96,1024]{1,0:T(8,128)(2,1)S(1)}, u32[]{:S(2)}, u32[]{:S(2)}) %collective-permute-start.25) | collective-permute-done | bytes 196640 | tf_op jit(solution)/shard_map/ppermute | solution.py:807
  217.7 9.7 %shard_map.226 = (bf16[1024,512]{1,0:T(8,128)(2,1)}, f32[3,16,512]{2,1,0:T(8,128)}, f32[3,4,512]{2,1,0:T(4,128)}, f32[192,512]{1,0:T(8,128)}, f32[176,512]{1,0:T...) custom-call(s32[2]{0:T(128)} %copy-done.22, bf16[96,1024]{1,0:T(8,128)(2,1)} %copy-done.48, ...), custom_call_target="tpu_custom_call" | custom-call | flops 6899999744 | bytes 8000000 | tf_op jit(solution)/shard_map/pallas_call | solution.py:59
  227.4 1.5 collective-permute-start.26
  228.9 2.6 collective-permute-start.28
  231.5 2.5 collective-permute-start.29
  234.0 1.6 copy-done.25
  240.0 7.2 %shard_map.228 = (bf16[2,4,64,1024]{3,2,1,0:T(8,128)(2,1)S(1)}, bf16[2,4,64,1024]{3,2,1,0:T(8,128)(2,1)}) custom-call(s32[2]{0:T(128)S(1)} %copy-done.23, bf16[1024,512]{1,0:T(8,128)(2,1)S(1)} %get-tuple-element.168.inner_ref, bf16[1024,512]{1,0:T(8,128)(2,1)S(1)} %copy-done.31, bf16[4,136,512]{2,1,0:T(8,128)(2,1)S(1)} %copy-done.3, ...), custom_call_target="tpu_custom_call" | custom-call | flops 11500000256 | bytes 8000000 | tf_op jit(solution)/shard_map/pallas_call | solution.py:59
  247.8 6.0 %all-to-all-start.3 = ((bf16[32,32,512]{2,1,0:T(8,128)(2,1)}), bf16[32,32,512]{2,1,0:T(8,128)(2,1)}, u32[]{:S(2)}, u32[]{:S(2)}) async-start(bf16[32,32,512]{2,1,0:T(8,128)(2,1)} %bitcast.101), calls=%async_computation.3 | async-start | bytes 2097152 | tf_op jit(solution)/shard_map/all_to_all | solution.py:1071
  253.8 2.0 fusion.13
  258.4 1.8 collective-permute-start.36
  260.2 1.5 collective-permute-start.32
  262.3 1.3 collective-permute-start.35
  263.6 2.9 collective-permute-done.36
  269.6 11.0 %collective-permute-done.32 = bf16[4,64,1024]{2,1,0:T(8,128)(2,1)} collective-permute-done((bf16[4,64,1024]{2,1,0:T(8,128)(2,1)}, bf16[4,64,1024]{2,1,0:T(8,128)(2,1)}, u32[]{:S(2)}, u32[]{:S(2)}) %collective-permute-start.32) | collective-permute-done | bytes 524320 | tf_op jit(solution)/shard_map/ppermute | solution.py:807
  280.6 1.6 fusion.2
  282.3 3.4 %fusion.6 = (bf16[4,64,1024]{2,1,0:T(8,128)(2,1)}, bf16[4,64,1024]{2,1,0:T(8,128)(2,1)}) fusion(bf16[4,64,1024]{2,1,0:T(8,128)(2,1)S(1)} %copy-done, bf16[4,64,1024]{2,1,0:T(8,128)(2,1)} %slab0_ref.1, bf16[4,64,1024]{2,1,0:T(8,128)(2,1)} %collective-permute-done.32, f32[4,64]{1,0:T(4,128)S(1)} %broadcast_multiply_fusion, f32[1024]{0:T(1024)S(1)} %bitcast.130, ...), kind=kLoop, calls=%fused_computation.10 | loop fusion | flops 5505024 | bytes 5249024 | tf_op jit(solution)/shard_map/convert_element_type | solution.py:1138
  285.7 2.3 shard_map.230
  (246 shorter events, 45.3 us)
Async XLA Ops:
  5.5 19.7 %collective-permute-start = (bf16[4,64,1024]{2,1,0:T(8,128)(2,1)S(1)}, bf16[4,64,1024]{2,1,0:T(8,128)(2,1)S(1)}, u32[]{:S(2)}, u32[]{:S(2)}) collective-permute-start(bf16[4,64,1024]{2,1,0:T(8,128)(2,1)S(1)} %copy-done), channel_id=1, source_target_pairs={{0,2},{1,3},{2,0},{3,1},{4,6},{5,7},{6,4},{7,5},{8,10},{9,11},{10,... | collective-permute-start | bytes 1572872 | tf_op jit(solution)/shard_map/ppermute | solution.py:807
  8.5 12.7 %collective-permute-start.1 = (bf16[80,1024]{1,0:T(8,128)(2,1)S(1)}, bf16[80,1024]{1,0:T(8,128)(2,1)S(1)}, u32[]{:S(2)}, u32[]{:S(2)}) collective-permute-start(bf16[80,1024]{1,0:T(8,128)(2,1)S(1)} %pad_maximum_fusion.5), channel_id=1, source_target_pairs={{0,8},{4,12},{8,0},{12,4},{16,24},{20,28},{24,16},{28,20},{1,9},{5... | collective-permute-start | bytes 491528 | tf_op jit(solution)/shard_map/ppermute | solution.py:807
  10.1 15.1 %collective-permute-start.2 = (bf16[80,1024]{1,0:T(8,128)(2,1)S(1)}, bf16[80,1024]{1,0:T(8,128)(2,1)S(1)}, u32[]{:S(2)}, u32[]{:S(2)}) collective-permute-start(bf16[80,1024]{1,0:T(8,128)(2,1)S(1)} %pad_maximum_fusion.5), channel_id=1, source_target_pairs={{0,16},{4,20},{8,24},{12,28},{16,0},{20,4},{24,8},{28,12},{1,17},{... | collective-permute-start | bytes 491528 | tf_op jit(solution)/shard_map/ppermute | solution.py:807
  12.7 12.5 %collective-permute-start.3 = (bf16[80,1024]{1,0:T(8,128)(2,1)S(1)}, bf16[80,1024]{1,0:T(8,128)(2,1)S(1)}, u32[]{:S(2)}, u32[]{:S(2)}) collective-permute-start(bf16[80,1024]{1,0:T(8,128)(2,1)S(1)} %pad_maximum_fusion.5), channel_id=1, source_target_pairs={{0,24},{4,28},{8,16},{12,20},{16,8},{20,12},{24,0},{28,4},{1,25},{... | collective-permute-start | bytes 491528 | tf_op jit(solution)/shard_map/ppermute | solution.py:807
  12.9 12.3 %all-to-all-start = ((bf16[4,72,512]{2,1,0:T(8,128)(2,1)}), bf16[4,72,512]{2,1,0:T(8,128)(2,1)S(1)}, u32[]{:S(2)}, u32[]{:S(2)}) async-start(bf16[4,72,512]{2,1,0:T(8,128)(2,1)} %pad_maximum_fusion.3), calls=%async_computation | async-start | bytes 589824 | tf_op jit(solution)/shard_map/all_to_all | solution.py:839
  16.4 4.7 %collective-permute-start.12 = (s32[4,3]{1,0:T(4,128)S(1)}, s32[4,3]{1,0:T(4,128)S(1)}, u32[]{:S(2)}, u32[]{:S(2)}) collective-permute-start(s32[4,3]{1,0:T(4,128)S(1)} %slice.112), channel_id=1, source_target_pairs={{0,4},{4,8},{8,12},{12,16},{16,20},{20,24},{24,28},{1,5},{5,9},{9,... | collective-permute-start | bytes 152 | tf_op jit(solution)/shard_map/ppermute | solution.py:874
  19.9 134.5 %copy-start.22 = (s32[2]{0:T(128)}, s32[2]{0:T(128)S(1)}, u32[]{:S(2)}) copy-start(s32[2]{0:T(128)S(1)} %pad_add_fusion.1.place_ref) | copy-start | bytes 28
  26.0 18.2 %collective-permute-start.4 = (bf16[4,80,1024]{2,1,0:T(8,128)(2,1)S(1)}, bf16[4,80,1024]{2,1,0:T(8,128)(2,1)S(1)}, u32[]{:S(2)}, u32[]{:S(2)}) collective-permute-start(bf16[4,80,1024]{2,1,0:T(8,128)(2,1)S(1)} %pad_maximum_fusion.exit_near_ref), channel_id=1, source_target_pairs={{0,4},{4,0},{8,12},{12,8},{16,20},{20,16},{24,28},{28,24},{1,5},{5... | collective-permute-start | bytes 1966088 | tf_op jit(solution)/shard_map/ppermute | solution.py:807
  28.2 6.1 %collective-permute-start.5 = (bf16[136,512]{1,0:T(8,128)(2,1)}, bf16[136,512]{1,0:T(8,128)(2,1)S(1)}, u32[]{:S(2)}, u32[]{:S(2)}) collective-permute-start(bf16[136,512]{1,0:T(8,128)(2,1)} %pad_maximum_fusion.6), channel_id=1, source_target_pairs={{0,8},{4,12},{8,0},{12,4},{16,24},{20,28},{24,16},{28,20},{1,9},{5... | collective-permute-start | bytes 417800 | tf_op jit(solution)/shard_map/ppermute | solution.py:807
  30.6 13.7 %collective-permute-start.8 = (bf16[4,64,1024]{2,1,0:T(8,128)(2,1)S(1)}, bf16[4,64,1024]{2,1,0:T(8,128)(2,1)S(1)}, u32[]{:S(2)}, u32[]{:S(2)}) collective-permute-start(bf16[4,64,1024]{2,1,0:T(8,128)(2,1)S(1)} %copy-done), channel_id=1, source_target_pairs={{0,1},{1,0},{2,3},{3,2},{4,5},{5,4},{6,7},{7,6},{8,9},{9,8},{10,11... | collective-permute-start | bytes 1572872 | tf_op jit(solution)/shard_map/ppermute | solution.py:807
  30.6 13.7 %collective-permute-start.9 = (bf16[4,64,1024]{2,1,0:T(8,128)(2,1)S(1)}, bf16[4,64,1024]{2,1,0:T(8,128)(2,1)}, u32[]{:S(2)}, u32[]{:S(2)}) collective-permute-start(bf16[4,64,1024]{2,1,0:T(8,128)(2,1)S(1)} %collective-permute-done.slab2_ref), channel_id=1, source_target_pairs={{0,1},{1,0},{2,3},{3,2},{4,5},{5,4},{6,7},{7,6},{8,9},{9,8},{10,11... | collective-permute-start | bytes 1572872 | tf_op jit(solution)/shard_map/ppermute | solution.py:807
  31.1 13.1 %collective-permute-start.6 = (bf16[136,512]{1,0:T(8,128)(2,1)}, bf16[136,512]{1,0:T(8,128)(2,1)}, u32[]{:S(2)}, u32[]{:S(2)}) collective-permute-start(bf16[136,512]{1,0:T(8,128)(2,1)} %pad_maximum_fusion.6), channel_id=1, source_target_pairs={{0,16},{4,20},{8,24},{12,28},{16,0},{20,4},{24,8},{28,12},{1,17},{... | collective-permute-start | bytes 417800 | tf_op jit(solution)/shard_map/ppermute | solution.py:807
  34.4 9.9 %collective-permute-start.7 = (bf16[136,512]{1,0:T(8,128)(2,1)}, bf16[136,512]{1,0:T(8,128)(2,1)}, u32[]{:S(2)}, u32[]{:S(2)}) collective-permute-start(bf16[136,512]{1,0:T(8,128)(2,1)} %pad_maximum_fusion.6), channel_id=1, source_target_pairs={{0,24},{4,28},{8,16},{12,20},{16,8},{20,12},{24,0},{28,4},{1,25},{... | collective-permute-start | bytes 417800 | tf_op jit(solution)/shard_map/ppermute | solution.py:807
  37.9 53.5 %copy-start.5 = (f32[4,4,64,4]{3,0,1,2:T(4,128)}, f32[4,4,64,4]{3,0,1,2:T(4,128)S(1)}, u32[]{:S(2)}) copy-start(f32[4,4,64,4]{3,0,1,2:T(4,128)S(1)} %copy.43) | copy-start | bytes 49156
  47.5 22.1 %collective-permute-start.11 = (bf16[4,136,512]{2,1,0:T(8,128)(2,1)S(1)}, bf16[4,136,512]{2,1,0:T(8,128)(2,1)}, u32[]{:S(2)}, u32[]{:S(2)}) collective-permute-start(bf16[4,136,512]{2,1,0:T(8,128)(2,1)S(1)} %pad_maximum_fusion.1.near_ref), channel_id=1, source_target_pairs={{0,4},{4,0},{8,12},{12,8},{16,20},{20,16},{24,28},{28,24},{1,5},{5... | collective-permute-start | bytes 1671176 | tf_op jit(solution)/shard_map/ppermute | solution.py:807
  48.6 11.7 %collective-permute-start.20 = (bf16[128,512]{1,0:T(8,128)(2,1)}, bf16[128,512]{1,0:T(8,128)(2,1)}, u32[]{:S(2)}, u32[]{:S(2)}) collective-permute-start(bf16[128,512]{1,0:T(8,128)(2,1)} %bitcast.120), channel_id=1, source_target_pairs={{0,24},{4,28},{8,16},{12,20},{16,8},{20,12},{24,0},{28,4},{1,25},{... | collective-permute-start | bytes 393224 | tf_op jit(solution)/shard_map/ppermute | solution.py:807
  50.8 12.7 %collective-permute-start.19 = (bf16[128,512]{1,0:T(8,128)(2,1)}, bf16[128,512]{1,0:T(8,128)(2,1)}, u32[]{:S(2)}, u32[]{:S(2)}) collective-permute-start(bf16[128,512]{1,0:T(8,128)(2,1)} %bitcast.121), channel_id=1, source_target_pairs={{0,16},{4,20},{8,24},{12,28},{16,0},{20,4},{24,8},{28,12},{1,17},{... | collective-permute-start | bytes 393224 | tf_op jit(solution)/shard_map/ppermute | solution.py:807
  52.8 10.7 %collective-permute-start.18 = (bf16[128,512]{1,0:T(8,128)(2,1)}, bf16[128,512]{1,0:T(8,128)(2,1)}, u32[]{:S(2)}, u32[]{:S(2)}) collective-permute-start(bf16[128,512]{1,0:T(8,128)(2,1)} %bitcast.122), channel_id=1, source_target_pairs={{0,8},{4,12},{8,0},{12,4},{16,24},{20,28},{24,16},{28,20},{1,9},{5... | collective-permute-start | bytes 393224 | tf_op jit(solution)/shard_map/ppermute | solution.py:807
  56.4 13.1 %collective-permute-start.16 = (bf16[4,64,1024]{2,1,0:T(8,128)(2,1)S(1)}, bf16[4,64,1024]{2,1,0:T(8,128)(2,1)}, u32[]{:S(2)}, u32[]{:S(2)}) collective-permute-start(bf16[4,64,1024]{2,1,0:T(8,128)(2,1)S(1)} %copy-done.4), channel_id=1, source_target_pairs={{0,2},{1,3},{2,0},{3,1},{4,6},{5,7},{6,4},{7,5},{8,10},{9,11},{10,... | collective-permute-start | bytes 1572872 | tf_op jit(solution)/shard_map/ppermute | solution.py:807
  60.4 110.7 %copy-start.9 = (bf16[192,512]{1,0:T(8,128)(2,1)}, bf16[192,512]{1,0:T(8,128)(2,1)S(1)}, u32[]{:S(2)}) copy-start(bf16[192,512]{1,0:T(8,128)(2,1)S(1)} %copy.46.small_ref) | copy-start | bytes 589828
  60.4 10.5 %collective-permute-start.10 = (bf16[12,1024]{1,0:T(8,128)(2,1)S(1)}, bf16[12,1024]{1,0:T(8,128)(2,1)S(1)}, u32[]{:S(2)}, u32[]{:S(2)}) collective-permute-start(bf16[12,1024]{1,0:T(8,128)(2,1)S(1)} %reshape.132), channel_id=1, source_target_pairs={{0,4},{4,8},{8,12},{12,16},{16,20},{20,24},{24,28},{1,5},{5,9},{9,... | collective-permute-start | bytes 73736 | tf_op jit(solution)/shard_map/ppermute | solution.py:869
  63.6 21.2 %collective-permute-start.15 = (bf16[4,64,1024]{2,1,0:T(8,128)(2,1)S(1)}, bf16[4,64,1024]{2,1,0:T(8,128)(2,1)S(1)}, u32[]{:S(2)}, u32[]{:S(2)}) collective-permute-start(bf16[4,64,1024]{2,1,0:T(8,128)(2,1)S(1)} %copy-done.4), channel_id=1, source_target_pairs={{0,1},{1,0},{2,3},{3,2},{4,5},{5,4},{6,7},{7,6},{8,9},{9,8},{10,11... | collective-permute-start | bytes 1572872 | tf_op jit(solution)/shard_map/ppermute | solution.py:807
  64.7 20.1 %collective-permute-start.21 = (bf16[4,128,512]{2,1,0:T(8,128)(2,1)S(1)}, bf16[4,128,512]{2,1,0:T(8,128)(2,1)S(1)}, u32[]{:S(2)}, u32[]{:S(2)}) collective-permute-start(bf16[4,128,512]{2,1,0:T(8,128)(2,1)S(1)} %pad_maximum_fusion.2.near_ref.gate_near_ref), channel_id=1, source_target_pairs={{0,4},{4,0},{8,12},{12,8},{16,20},{20,16},{24,28},{28,24},{1,5},{5... | collective-permute-start | bytes 1572872 | tf_op jit(solution)/shard_map/ppermute | solution.py:807
  69.5 15.2 %collective-permute-start.17 = (bf16[4,64,1024]{2,1,0:T(8,128)(2,1)}, bf16[4,64,1024]{2,1,0:T(8,128)(2,1)S(1)}, u32[]{:S(2)}, u32[]{:S(2)}) collective-permute-start(bf16[4,64,1024]{2,1,0:T(8,128)(2,1)} %collective-permute-done.16.slab2_ref), channel_id=1, source_target_pairs={{0,1},{1,0},{2,3},{3,2},{4,5},{5,4},{6,7},{7,6},{8,9},{9,8},{10,11... | collective-permute-start | bytes 1572872 | tf_op jit(solution)/shard_map/ppermute | solution.py:807
  82.5 50.3 %copy-start.20 = (f32[1024,512]{1,0:T(8,128)}, f32[1024,512]{1,0:T(8,128)S(1)}, u32[]{:S(2)}) copy-start(f32[1024,512]{1,0:T(8,128)S(1)} %get-tuple-element.122.filter_ref) | copy-start | bytes 6291460
  82.5 71.8 %copy-start.24 = (bf16[1024,1024]{1,0:T(8,128)(2,1)}, bf16[1024,1024]{1,0:T(8,128)(2,1)S(1)}, u32[]{:S(2)}) copy-start(bf16[1024,1024]{1,0:T(8,128)(2,1)S(1)} %get-tuple-element.126.normed_ref) | copy-start | bytes 6291460
  82.5 1.6 collective-permute-start.13
  84.2 7.2 %collective-permute-start.14 = (bf16[96,1024]{1,0:T(8,128)(2,1)S(1)}, bf16[96,1024]{1,0:T(8,128)(2,1)S(1)}, u32[]{:S(2)}, u32[]{:S(2)}) collective-permute-start(bf16[96,1024]{1,0:T(8,128)(2,1)S(1)} %add_convert_fusion.3.chosen_ref), channel_id=1, source_target_pairs={{0,2},{1,3},{2,0},{3,1},{4,6},{5,7},{6,4},{7,5},{8,10},{9,11},{10,... | collective-permute-start | bytes 589832 | tf_op jit(solution)/shard_map/ppermute | solution.py:807
  91.4 41.5 %copy-start.21 = (f32[1024,512]{1,0:T(8,128)}, f32[1024,512]{1,0:T(8,128)S(1)}, u32[]{:S(2)}) copy-start(f32[1024,512]{1,0:T(8,128)S(1)} %get-tuple-element.142) | copy-start | bytes 6291460
  112.3 42.0 %copy-start.35 = (f32[64,16,512]{2,1,0:T(8,128)}, f32[64,16,512]{2,1,0:T(8,128)S(1)}, u32[]{:S(2)}) copy-start(f32[64,16,512]{2,1,0:T(8,128)S(1)} %get-tuple-element.131.step_ref) | copy-start | bytes 6291460
  112.3 42.0 %copy-start.38 = (f32[64,16,128]{2,1,0:T(8,128)}, f32[64,16,128]{2,1,0:T(8,128)S(1)}, u32[]{:S(2)}) copy-start(f32[64,16,128]{2,1,0:T(8,128)S(1)} %get-tuple-element.130.gates_ref) | copy-start | bytes 1572868
  164.9 42.2 %collective-permute-start.23 = (bf16[2,4,64,1024]{3,2,1,0:T(8,128)(2,1)}, bf16[2,4,64,1024]{3,2,1,0:T(8,128)(2,1)}, u32[]{:S(2)}, u32[]{:S(2)}) collective-permute-start(bf16[2,4,64,1024]{3,2,1,0:T(8,128)(2,1)} %get-tuple-element.141), channel_id=1, source_target_pairs={{0,1},{1,0},{2,3},{3,2},{4,5},{5,4},{6,7},{7,6},{8,9},{9,8},{10,11... | collective-permute-start | bytes 3145736 | tf_op jit(solution)/shard_map/ppermute | solution.py:807
  164.9 42.2 %all-to-all-start.2 = ((bf16[8,64,1024]{2,1,0:T(8,128)(2,1)}), bf16[8,64,1024]{2,1,0:T(8,128)(2,1)}, u32[]{:S(2)}, u32[]{:S(2)}) async-start(bf16[8,64,1024]{2,1,0:T(8,128)(2,1)} %bitcast.43), calls=%async_computation.2 | async-start | bytes 2097152 | tf_op jit(solution)/shard_map/all_to_all | solution.py:994
  169.2 37.1 %collective-permute-start.22 = (bf16[4,128,512]{2,1,0:T(8,128)(2,1)S(1)}, bf16[4,128,512]{2,1,0:T(8,128)(2,1)S(1)}, u32[]{:S(2)}, u32[]{:S(2)}) collective-permute-start(bf16[4,128,512]{2,1,0:T(8,128)(2,1)S(1)} %get-tuple-element.148), channel_id=1, source_target_pairs={{0,4},{4,0},{8,12},{12,8},{16,20},{20,16},{24,28},{28,24},{1,5},{5... | collective-permute-start | bytes 1572872 | tf_op jit(solution)/shard_map/ppermute | solution.py:807
  207.1 2.1 collective-permute-start.24
  209.3 7.8 %collective-permute-start.25 = (bf16[96,1024]{1,0:T(8,128)(2,1)S(1)}, bf16[96,1024]{1,0:T(8,128)(2,1)S(1)}, u32[]{:S(2)}, u32[]{:S(2)}) collective-permute-start(bf16[96,1024]{1,0:T(8,128)(2,1)S(1)} %add_convert_fusion.2.chosen_ref), channel_id=1, source_target_pairs={{0,2},{1,3},{2,0},{3,1},{4,6},{5,7},{6,4},{7,5},{8,10},{9,11},{10,... | collective-permute-start | bytes 589832 | tf_op jit(solution)/shard_map/ppermute | solution.py:807
  212.9 27.1 %collective-permute-start.27 = (bf16[4,64,1024]{2,1,0:T(8,128)(2,1)}, bf16[4,64,1024]{2,1,0:T(8,128)(2,1)}, u32[]{:S(2)}, u32[]{:S(2)}) collective-permute-start(bf16[4,64,1024]{2,1,0:T(8,128)(2,1)} %fusion.12), channel_id=1, source_target_pairs={{0,2},{1,3},{2,0},{3,1},{4,6},{5,7},{6,4},{7,5},{8,10},{9,11},{10,... | collective-permute-start | bytes 1572872 | tf_op jit(solution)/shard_map/ppermute | solution.py:807
  227.4 6.6 %collective-permute-start.26 = (f32[3,4,512]{2,1,0:T(4,128)}, f32[3,4,512]{2,1,0:T(4,128)S(1)}, u32[]{:S(2)}, u32[]{:S(2)}) collective-permute-start(f32[3,4,512]{2,1,0:T(4,128)} %get-tuple-element.163), channel_id=1, source_target_pairs={{4,0},{8,4},{12,8},{16,12},{20,16},{24,20},{28,24},{5,1},{9,5},{13... | collective-permute-start | bytes 73736 | tf_op jit(solution)/shard_map/ppermute | solution.py:1060
  228.9 18.3 %collective-permute-start.28 = (bf16[176,512]{1,0:T(8,128)(2,1)}, bf16[176,512]{1,0:T(8,128)(2,1)S(1)}, u32[]{:S(2)}, u32[]{:S(2)}) collective-permute-start(bf16[176,512]{1,0:T(8,128)(2,1)} %get-tuple-element.172), channel_id=1, source_target_pairs={{0,8},{4,12},{8,0},{12,4},{16,24},{20,28},{24,16},{28,20},{1,9},{5... | collective-permute-start | bytes 540680 | tf_op jit(solution)/shard_map/ppermute | solution.py:807
  231.5 16.1 %collective-permute-start.29 = (bf16[176,512]{1,0:T(8,128)(2,1)}, bf16[176,512]{1,0:T(8,128)(2,1)S(1)}, u32[]{:S(2)}, u32[]{:S(2)}) collective-permute-start(bf16[176,512]{1,0:T(8,128)(2,1)} %get-tuple-element.173), channel_id=1, source_target_pairs={{0,16},{4,20},{8,24},{12,28},{16,0},{20,4},{24,8},{28,12},{1,17},{... | collective-permute-start | bytes 540680 | tf_op jit(solution)/shard_map/ppermute | solution.py:807
  234.0 13.6 %collective-permute-start.30 = (bf16[176,512]{1,0:T(8,128)(2,1)}, bf16[176,512]{1,0:T(8,128)(2,1)S(1)}, u32[]{:S(2)}, u32[]{:S(2)}) collective-permute-start(bf16[176,512]{1,0:T(8,128)(2,1)} %get-tuple-element.174), channel_id=1, source_target_pairs={{0,24},{4,28},{8,16},{12,20},{16,8},{20,12},{24,0},{28,4},{1,25},{... | collective-permute-start | bytes 540680 | tf_op jit(solution)/shard_map/ppermute | solution.py:807
  247.6 6.2 %collective-permute-start.31 = (bf16[2,4,64,1024]{3,2,1,0:T(8,128)(2,1)}, bf16[2,4,64,1024]{3,2,1,0:T(8,128)(2,1)}, u32[]{:S(2)}, u32[]{:S(2)}) collective-permute-start(bf16[2,4,64,1024]{3,2,1,0:T(8,128)(2,1)} %get-tuple-element.175), channel_id=1, source_target_pairs={{0,1},{1,0},{2,3},{3,2},{4,5},{5,4},{6,7},{7,6},{8,9},{9,8},{10,11... | collective-permute-start | bytes 3145736 | tf_op jit(solution)/shard_map/ppermute | solution.py:807
  247.8 37.9 %all-to-all-start.3 = ((bf16[32,32,512]{2,1,0:T(8,128)(2,1)}), bf16[32,32,512]{2,1,0:T(8,128)(2,1)}, u32[]{:S(2)}, u32[]{:S(2)}) async-start(bf16[32,32,512]{2,1,0:T(8,128)(2,1)} %bitcast.101), calls=%async_computation.3 | async-start | bytes 2097152 | tf_op jit(solution)/shard_map/all_to_all | solution.py:1071
  258.4 8.0 %collective-permute-start.36 = (f32[192,128]{1,0:T(8,128)S(1)}, f32[192,128]{1,0:T(8,128)S(1)}, u32[]{:S(2)}, u32[]{:S(2)}) collective-permute-start(f32[192,128]{1,0:T(8,128)S(1)} %get-tuple-element.188), channel_id=1, source_target_pairs={{0,4},{4,0},{8,12},{12,8},{16,20},{20,16},{24,28},{28,24},{1,5},{5... | collective-permute-start | bytes 294920 | tf_op jit(solution)/shard_map/ppermute | solution.py:807
  260.2 20.4 %collective-permute-start.32 = (bf16[4,64,1024]{2,1,0:T(8,128)(2,1)}, bf16[4,64,1024]{2,1,0:T(8,128)(2,1)}, u32[]{:S(2)}, u32[]{:S(2)}) collective-permute-start(bf16[4,64,1024]{2,1,0:T(8,128)(2,1)} %fusion.13), channel_id=1, source_target_pairs={{0,2},{1,3},{2,0},{3,1},{4,6},{5,7},{6,4},{7,5},{8,10},{9,11},{10,... | collective-permute-start | bytes 1572872 | tf_op jit(solution)/shard_map/ppermute | solution.py:807
  261.7 23.9 %collective-permute-start.33 = (bf16[32,512]{1,0:T(8,128)(2,1)S(1)}, bf16[32,512]{1,0:T(8,128)(2,1)S(1)}, u32[]{:S(2)}, u32[]{:S(2)}) collective-permute-start(bf16[32,512]{1,0:T(8,128)(2,1)S(1)} %get-tuple-element.183), channel_id=1, source_target_pairs={{0,1},{1,0},{2,3},{3,2},{4,5},{5,4},{6,7},{7,6},{8,9},{9,8},{10,11... | collective-permute-start | bytes 98312 | tf_op jit(solution)/shard_map/ppermute | solution.py:807
  261.7 23.9 %collective-permute-start.34 = (bf16[32,512]{1,0:T(8,128)(2,1)S(1)}, bf16[32,512]{1,0:T(8,128)(2,1)S(1)}, u32[]{:S(2)}, u32[]{:S(2)}) collective-permute-start(bf16[32,512]{1,0:T(8,128)(2,1)S(1)} %get-tuple-element.184), channel_id=1, source_target_pairs={{0,2},{1,3},{2,0},{3,1},{4,6},{5,7},{6,4},{7,5},{8,10},{9,11},{10,... | collective-permute-start | bytes 98312 | tf_op jit(solution)/shard_map/ppermute | solution.py:807
  262.3 23.4 %collective-permute-start.35 = (bf16[32,512]{1,0:T(8,128)(2,1)S(1)}, bf16[32,512]{1,0:T(8,128)(2,1)S(1)}, u32[]{:S(2)}, u32[]{:S(2)}) collective-permute-start(bf16[32,512]{1,0:T(8,128)(2,1)S(1)} %get-tuple-element.185), channel_id=1, source_target_pairs={{0,3},{1,2},{2,1},{3,0},{4,7},{5,6},{6,5},{7,4},{8,11},{9,10},{10,... | collective-permute-start | bytes 98312 | tf_op jit(solution)/shard_map/ppermute | solution.py:807
  (55 other events, 278.4 us)

commit v5 on v4

--- a/solution.py
+++ b/solution.py
@@ -757,6 +757,16 @@
         small_ref[...] = jnp.zeros_like(small_ref)
 
 
+def input_kernel(keep_ref, came_ref, other_ref, tokens_ref, cotangent_ref, gain_ref, out_ref):
+    grad_hat = keep_ref[0].astype(f32) + came_ref[0].astype(f32) + other_ref[...].astype(f32)
+    grad_hat = grad_hat * gain_ref[...]
+    rows = tokens_ref[...].astype(f32)
+    root = lax.rsqrt(jnp.mean(rows * rows, axis=2, keepdims=True) + epsilon)
+    hat = rows * root
+    grad = root * (grad_hat - hat * jnp.mean(grad_hat * hat, axis=2, keepdims=True))
+    out_ref[...] = (cotangent_ref[...].astype(f32) + grad).astype(bf16)
+
+
 def interleave_kernel(place_ref, weight_ref, inner_ref, gate0_ref, gate1_ref, gate2_ref, gate3_ref, out_ref, gain_ref):
     gate_refs = (gate0_ref, gate1_ref, gate2_ref, gate3_ref)
     pieces, groups, rows, width = inner_ref.shape
@@ -1026,7 +1036,7 @@
     def slab_part(keep, came):
         return (keep[1].astype(f32) + came[1].astype(f32)).astype(bf16)
 
-    exit_out = jnp.sum(exit_parts.astype(f32), axis=0)
+    exit_out = jnp.sum(after(exit_parts, chosen_grads[0]).astype(f32), axis=0)
     grad_direct, exit_out = rounds(grad_direct, exit_out)
     out_part = after(slab_part(out_keep, out_came), chosen_grads[0])
     out_other = flipped(out_part, "grp", 2)
@@ -1097,6 +1107,7 @@
     )
     gate_blocks = [gate_blocks[0]] + [flipped(gate_blocks[k], "grp", k) for k in range(1, groups)]
     residual = tokens.astype(f32)
+    out_other, gate_blocks[3], small_sum = rounds(out_other, gate_blocks[3], small_sum)
     block_out = residual + out_keep[0].astype(f32) + out_came[0].astype(f32) + out_other.astype(f32)
     block_out = block_out.astype(bf16)
     inner_parts = inner_parts.reshape(pieces, groups, slice_rows, group_width)
@@ -1130,12 +1141,14 @@
         came_small = lax.all_to_all(split, "blk", split_axis=0, concat_axis=0, tiled=True)
         mine = jnp.sum(came_small, axis=0)
 
-    grad_hat = grad_keep[0].astype(f32) + grad_came[0].astype(f32) + grad_other.astype(f32)
-    grad_hat = grad_hat * gain_all[0]
-    root = lax.rsqrt(jnp.mean(residual * residual, axis=2, keepdims=True) + epsilon)
-    hat_own = residual * root
-    grad_input = root * (grad_hat - hat_own * jnp.mean(grad_hat * hat_own, axis=2, keepdims=True))
-    input_grad = (cotangent.astype(f32) + grad_input).astype(bf16)
+    input_grad = kernel_call(
+        input_kernel,
+        2,
+        [((sequences, steps, width), bf16)],
+        [],
+        16,
+        grad_keep, grad_came, after(grad_other, entry_out), tokens, cotangent, gain_all,
+    )[0]
     return (
         block_out,
         input_grad,

time: 290 us -> 287 us (0.990)
  waiting for transfers between devices: 36 us -> 32.5 us
  other arithmetic: 19.1 us -> 15.8 us
    unnamed x133 -> x104, local copies, waits for them, and re-layouts: 19.6 us -> 16 us
    pallas_call x11 -> x12, Pallas kernels: 118 us -> 120 us  [kernel_call(): pl.pallas_call(body, out_shape=[jax.ShapeDtypeStruct(shape, kind) for sha...]
  transfers between devices with their start and end apart: 40 -> 40, of which waited for: 11 -> 12; matrix products, arithmetic and copies ran while one was open for 9% -> 7% of each run, Pallas kernels for 23% -> 24%
where the time goes in v5:
time: 287 us; the launch traced here: 286 us
  Pallas kernels  120 us (42%)
  starting transfers between devices  63.8 us (22%)
  waiting for transfers between devices  32.5 us (11%)
  local copies, waits for them, and re-layouts  30.1 us (10%)
  blocking collectives  21.6 us (8%)
  other arithmetic  15.8 us (6%)
    pallas_call x12, Pallas kernels, kernel_call(): pl.pallas_call(body, out_shape=[jax.ShapeDtypeStruct(shape, kind) for sha...  120 us
    ppermute x34, starting transfers between devices, flipped(): lax.ppermute(value, axis, [(i, i ^ bits) for i in range(lax.axis_size(axi...  41.1 us
    ppermute x34, waiting for transfers between devices, flipped(): lax.ppermute(value, axis, [(i, i ^ bits) for i in range(lax.axis_size(axi...  32 us
    all_to_all x1, blocking collectives, local(): came = lax.all_to_all(loads, 'blk', split_axis=0, concat_axis=0, tiled=True)  21.6 us
    unnamed x104, local copies, waits for them, and re-layouts  16 us
    all_to_all x1, starting transfers between devices, local(): lax.all_to_all(inner_entry.reshape(pieces * groups, slice_rows, group_wid...  6.03 us
  transfers between devices with their start and end apart: 40, of which 12 were waited for; matrix products, arithmetic and copies ran while one was open for 7% of the time, Pallas kernels for 24%

profile of v5, /device:TPU:0, one launch (start us, length us, event | category | flops | bytes accessed | tf_op | source)
XLA Modules:
  0.0 285.7 jit_solution(367356609040113392)
XLA Ops:
  7.4 1.5 reshape.109
  10.0 3.0 %collective-permute-start = (bf16[4,64,1024]{2,1,0:T(8,128)(2,1)S(1)}, bf16[4,64,1024]{2,1,0:T(8,128)(2,1)S(1)}, u32[]{:S(2)}, u32[]{:S(2)}) collective-permute-start(bf16[4,64,1024]{2,1,0:T(8,128)(2,1)S(1)} %copy-done), channel_id=1, source_target_pairs={{0,2},{1,3},{2,0},{3,1},{4,6},{5,7},{6,4},{7,5},{8,10},{9,11},{10,... | collective-permute-start | bytes 1572872 | tf_op jit(solution)/shard_map/ppermute | solution.py:817
  13.0 3.6 %collective-permute-start.3 = (bf16[80,1024]{1,0:T(8,128)(2,1)S(1)}, bf16[80,1024]{1,0:T(8,128)(2,1)S(1)}, u32[]{:S(2)}, u32[]{:S(2)}) collective-permute-start(bf16[80,1024]{1,0:T(8,128)(2,1)S(1)} %pad_maximum_fusion.5), channel_id=1, source_target_pairs={{0,24},{4,28},{8,16},{12,20},{16,8},{20,12},{24,0},{28,4},{1,25},{... | collective-permute-start | bytes 491528 | tf_op jit(solution)/shard_map/ppermute | solution.py:817
  17.5 3.4 %collective-permute-start.12 = (s32[4,3]{1,0:T(4,128)S(1)}, s32[4,3]{1,0:T(4,128)S(1)}, u32[]{:S(2)}, u32[]{:S(2)}) collective-permute-start(s32[4,3]{1,0:T(4,128)S(1)} %slice.106), channel_id=1, source_target_pairs={{0,4},{4,8},{8,12},{12,16},{16,20},{20,24},{24,28},{1,5},{5,9},{9,... | collective-permute-start | bytes 152 | tf_op jit(solution)/shard_map/ppermute | solution.py:884
  20.9 3.5 %all-to-all-start = ((bf16[4,72,512]{2,1,0:T(8,128)(2,1)}), bf16[4,72,512]{2,1,0:T(8,128)(2,1)S(1)}, u32[]{:S(2)}, u32[]{:S(2)}) async-start(bf16[4,72,512]{2,1,0:T(8,128)(2,1)} %pad_maximum_fusion.3), calls=%async_computation | async-start | bytes 589824 | tf_op jit(solution)/shard_map/all_to_all | solution.py:849
  24.5 5.7 %collective-permute-done.2 = bf16[80,1024]{1,0:T(8,128)(2,1)S(1)} collective-permute-done((bf16[80,1024]{1,0:T(8,128)(2,1)S(1)}, bf16[80,1024]{1,0:T(8,128)(2,1)S(1)}, u32[]{:S(2)}, u32[]{:S(2)}) %collective-permute-start.2) | collective-permute-done | bytes 163872 | tf_op jit(solution)/shard_map/ppermute | solution.py:817
  31.5 1.3 collective-permute-start.4
  32.8 2.5 collective-permute-start.7
  36.4 3.4 %collective-permute-done.7 = bf16[136,512]{1,0:T(8,128)(2,1)S(1)} collective-permute-done((bf16[136,512]{1,0:T(8,128)(2,1)S(1)}, bf16[136,512]{1,0:T(8,128)(2,1)S(1)}, u32[]{:S(2)}, u32[]{:S(2)}) %collective-permute-start.7) | collective-permute-done | bytes 139296 | tf_op jit(solution)/shard_map/ppermute | solution.py:817
  39.8 6.5 %collective-permute-start.5 = (bf16[136,512]{1,0:T(8,128)(2,1)S(1)}, bf16[136,512]{1,0:T(8,128)(2,1)}, u32[]{:S(2)}, u32[]{:S(2)}) collective-permute-start(bf16[136,512]{1,0:T(8,128)(2,1)S(1)} %pad_maximum_fusion.6), channel_id=1, source_target_pairs={{0,8},{4,12},{8,0},{12,4},{16,24},{20,28},{24,16},{28,20},{1,9},{5... | collective-permute-start | bytes 417800 | tf_op jit(solution)/shard_map/ppermute | solution.py:817
  46.8 1.3 collective-permute-done.6
  48.1 3.0 %collective-permute-done.5 = bf16[136,512]{1,0:T(8,128)(2,1)} collective-permute-done((bf16[136,512]{1,0:T(8,128)(2,1)S(1)}, bf16[136,512]{1,0:T(8,128)(2,1)}, u32[]{:S(2)}, u32[]{:S(2)}) %collective-permute-start.5) | collective-permute-done | bytes 139296 | tf_op jit(solution)/shard_map/ppermute | solution.py:817
  54.2 2.6 collective-permute-start.20
  56.9 1.8 collective-permute-start.18
  64.2 3.9 %collective-permute-start.10 = (bf16[12,1024]{1,0:T(8,128)(2,1)S(1)}, bf16[12,1024]{1,0:T(8,128)(2,1)S(1)}, u32[]{:S(2)}, u32[]{:S(2)}) collective-permute-start(bf16[12,1024]{1,0:T(8,128)(2,1)S(1)} %reshape.116), channel_id=1, source_target_pairs={{0,4},{4,8},{8,12},{12,16},{16,20},{20,24},{24,28},{1,5},{5,9},{9,... | collective-permute-start | bytes 73736 | tf_op jit(solution)/shard_map/ppermute | solution.py:879
  70.2 3.2 %collective-permute-done.16.slab2_ref = bf16[4,64,1024]{2,1,0:T(8,128)(2,1)} collective-permute-done((bf16[4,64,1024]{2,1,0:T(8,128)(2,1)}, bf16[4,64,1024]{2,1,0:T(8,128)(2,1)}, u32[]{:S(2)}, u32[]{:S(2)}) %collective-permute-start.16) | collective-permute-done | bytes 524320 | tf_op jit(solution)/shard_map/ppermute | solution.py:817
  74.2 8.7 %shard_map.220 = (bf16[1024,1024]{1,0:T(8,128)(2,1)S(1)}, bf16[1072,512]{1,0:T(8,128)(2,1)S(1)}, f32[1024,512]{1,0:T(8,128)S(1)}, bf16[96,1024]{1,0:T(8,128)(2,1)S(1)}) custom-call(s32[2]{0:T(128)S(1)} %pad_add_fusion.1.place_ref, bf16[4,64,1024]{2,1,0:T(8,128)(2,1)S(1)} %copy-done, bf16[4,64,1024]{2,1,0:T(8,128)(2,1)} %collective-permute-done.8.slab1_ref, ...), custom_call_target="tpu_custom_call" | custom-call | flops 10350000128 | bytes 8000000 | tf_op jit(solution)/shard_map/pallas_call | solution.py:59
  86.3 6.5 %shard_map.221 = (bf16[1024,1024]{1,0:T(8,128)(2,1)S(1)}, f32[1024,512]{1,0:T(8,128)S(1)}, f32[1024,512]{1,0:T(8,128)S(1)}, f32[1024,512]{1,0:T(8,128)S(1)}) custom-call(s32[2]{0:T(128)S(1)} %pad_add_fusion.1.place_ref, bf16[4,64,1024]{2,1,0:T(8,128)(2,1)S(1)} %copy-done.13, bf16[4,64,1024]{2,1,0:T(8,128)(2,1)S(1)} %collective-permute-done.15.slab1_ref, ...), custom_call_target="tpu_custom_call" | custom-call | flops 9200000000 | bytes 8000000 | tf_op jit(solution)/shard_map/pallas_call | solution.py:59
  92.9 19.6 %shard_map.222 = (f32[64,16,128]{2,1,0:T(8,128)S(1)}, f32[64,16,512]{2,1,0:T(8,128)S(1)}, f32[64,16,512]{2,1,0:T(8,128)S(1)}, f32[16,16,512]{2,1,0:T(8,128)S(1)}...) custom-call(s32[2]{0:T(128)S(1)} %pad_add_fusion.1.place_ref, ...), custom_call_target="tpu_custom_call" | custom-call | flops 26449999872 | bytes 8000000 | tf_op jit(solution)/shard_map/pallas_call | solution.py:59
  112.5 1.3 copy-done.32
  113.8 21.6 %all_to_all.20.came_ref = bf16[8,72,512]{2,1,0:T(8,128)(2,1)S(1)} all-to-all(bf16[8,72,512]{2,1,0:T(8,128)(2,1)S(1)} %get-tuple-element.134), channel_id=1, replica_groups=mesh['blk'=8,'grp'=4] {'blk'}, dimensions={0} | all-to-all | bytes 1179648 | tf_op jit(solution)/shard_map/all_to_all | solution.py:966
  135.3 21.5 %shard_map.223 = (f32[64,16,512]{2,1,0:T(8,128)S(1)}, f32[64,16,128]{2,1,0:T(8,128)S(1)}, f32[16,16,16,512]{3,2,1,0:T(8,128)}, f32[16,16,512]{2,1,0:T(8,128)S(1)}) custom-call(s32[2]{0:T(128)S(1)} %pad_add_fusion.1.place_ref, bf16[8,72,512]{2,1,0:T(8,128)(2,1)S(1)} %all_to_all.20.came_ref, f32[64,16,128]{2,1,0:T(8,128)S(1)} %get-tuple-element.135.gates_ref, ...), custom_call_target="tpu_custom_call" | custom-call | flops 20700000256 | bytes 8000000 | tf_op jit(solution)/shard_map/pallas_call | solution.py:59
  156.9 8.1 %shard_map.224 = (bf16[1024,512]{1,0:T(8,128)(2,1)S(1)}, bf16[2,4,64,1024]{3,2,1,0:T(8,128)(2,1)S(1)}, bf16[2,4,64,1024]{3,2,1,0:T(8,128)(2,1)}, bf16[512,1024]{...) custom-call(s32[2]{0:T(128)S(1)} %pad_add_fusion.1.place_ref, ...), custom_call_target="tpu_custom_call" | custom-call | flops 13799999488 | bytes 8000000 | tf_op jit(solution)/shard_map/pallas_call | solution.py:59
  166.9 4.4 %all-to-all-start.2 = ((bf16[8,64,1024]{2,1,0:T(8,128)(2,1)}), bf16[8,64,1024]{2,1,0:T(8,128)(2,1)}, u32[]{:S(2)}, u32[]{:S(2)}) async-start(bf16[8,64,1024]{2,1,0:T(8,128)(2,1)} %bitcast.43), calls=%async_computation.2 | async-start | bytes 2097152 | tf_op jit(solution)/shard_map/all_to_all | solution.py:1004
  171.3 1.9 collective-permute-start.22
  175.3 32.0 %shard_map.225 = (f32[64,16,512]{2,1,0:T(8,128)}, f32[64,512]{1,0:T(8,128)S(1)}, bf16[96,1024]{1,0:T(8,128)(2,1)S(1)}, f32[16,512]{1,0:T(8,128)S(1)}, f32[1,512]{1,0:T(1,128)S(1)}, /*index=5*/f32[1,512]{1,0:T(1,128)S(1)}) custom-call(f32[64,16,128]{2,1,0:T(8,128)S(1)} %copy-done.34, bf16[192,512]{1,0:T(8,128)(2,1)S(1)} %copy.46.small_ref, ...), custom_call_target="tpu_custom_call" | custom-call | flops 40249999360 | bytes 8000000 | tf_op jit(solution)/shard_map/pallas_call | solution.py:59
  207.4 1.4 collective-permute-done.24
  208.9 1.4 collective-permute-start.25
  210.4 2.0 fusion.2
  212.4 2.1 convert_reduce_fusion
  216.6 9.6 %shard_map.226 = (bf16[1024,512]{1,0:T(8,128)(2,1)}, f32[3,16,512]{2,1,0:T(8,128)}, f32[3,4,512]{2,1,0:T(4,128)}, f32[192,512]{1,0:T(8,128)}, f32[176,512]{1,0:T...) custom-call(s32[2]{0:T(128)} %copy-done.19, bf16[96,1024]{1,0:T(8,128)(2,1)} %copy-done.42, ...), custom_call_target="tpu_custom_call" | custom-call | flops 6899999744 | bytes 8000000 | tf_op jit(solution)/shard_map/pallas_call | solution.py:59
  226.2 1.5 collective-permute-start.26
  227.7 2.3 collective-permute-start.28
  230.1 2.7 collective-permute-start.29
  232.8 1.6 copy-done.22
  236.5 2.3 shard_map.227
  238.8 7.2 %shard_map.228 = (bf16[2,4,64,1024]{3,2,1,0:T(8,128)(2,1)S(1)}, bf16[2,4,64,1024]{3,2,1,0:T(8,128)(2,1)}) custom-call(s32[2]{0:T(128)S(1)} %copy-done.20, bf16[1024,512]{1,0:T(8,128)(2,1)S(1)} %get-tuple-element.175.inner_ref, bf16[1024,512]{1,0:T(8,128)(2,1)S(1)} %copy-done.28, bf16[4,136,512]{2,1,0:T(8,128)(2,1)S(1)} %pad_maximum_fusion.1.near_ref, ...), custom_call_target="tpu_custom_call" | custom-call | flops 11500000256 | bytes 8000000 | tf_op jit(solution)/shard_map/pallas_call | solution.py:59
  247.1 6.0 %all-to-all-start.3 = ((bf16[32,32,512]{2,1,0:T(8,128)(2,1)}), bf16[32,32,512]{2,1,0:T(8,128)(2,1)S(1)}, u32[]{:S(2)}, u32[]{:S(2)}) async-start(bf16[32,32,512]{2,1,0:T(8,128)(2,1)} %bitcast.49), calls=%async_computation.3 | async-start | bytes 2097152 | tf_op jit(solution)/shard_map/all_to_all | solution.py:1081
  253.1 2.2 fusion.3
  256.9 1.6 collective-permute-start.32
  258.9 1.7 collective-permute-start.35
  260.7 2.8 collective-permute-done.32.gate3_ref
  263.5 2.4 collective-permute-start.36
  265.9 2.4 fusion.1
  268.3 1.9 collective-permute-done.36
  273.3 7.4 %collective-permute-done.35.gate2_ref = bf16[32,512]{1,0:T(8,128)(2,1)S(1)} collective-permute-done((bf16[32,512]{1,0:T(8,128)(2,1)S(1)}, bf16[32,512]{1,0:T(8,128)(2,1)S(1)}, u32[]{:S(2)}, u32[]{:S(2)}) %collective-permute-start.35) | collective-permute-done | bytes 32800 | tf_op jit(solution)/shard_map/ppermute | solution.py:817
  280.7 1.6 shard_map.230
  283.0 2.8 shard_map.231
  (214 shorter events, 41.7 us)
Async XLA Ops:
  10.0 20.7 %collective-permute-start = (bf16[4,64,1024]{2,1,0:T(8,128)(2,1)S(1)}, bf16[4,64,1024]{2,1,0:T(8,128)(2,1)S(1)}, u32[]{:S(2)}, u32[]{:S(2)}) collective-permute-start(bf16[4,64,1024]{2,1,0:T(8,128)(2,1)S(1)} %copy-done), channel_id=1, source_target_pairs={{0,2},{1,3},{2,0},{3,1},{4,6},{5,7},{6,4},{7,5},{8,10},{9,11},{10,... | collective-permute-start | bytes 1572872 | tf_op jit(solution)/shard_map/ppermute | solution.py:817
  13.0 11.5 %collective-permute-start.3 = (bf16[80,1024]{1,0:T(8,128)(2,1)S(1)}, bf16[80,1024]{1,0:T(8,128)(2,1)S(1)}, u32[]{:S(2)}, u32[]{:S(2)}) collective-permute-start(bf16[80,1024]{1,0:T(8,128)(2,1)S(1)} %pad_maximum_fusion.5), channel_id=1, source_target_pairs={{0,24},{4,28},{8,16},{12,20},{16,8},{20,12},{24,0},{28,4},{1,25},{... | collective-permute-start | bytes 491528 | tf_op jit(solution)/shard_map/ppermute | solution.py:817
  16.6 13.6 %collective-permute-start.2 = (bf16[80,1024]{1,0:T(8,128)(2,1)S(1)}, bf16[80,1024]{1,0:T(8,128)(2,1)S(1)}, u32[]{:S(2)}, u32[]{:S(2)}) collective-permute-start(bf16[80,1024]{1,0:T(8,128)(2,1)S(1)} %pad_maximum_fusion.5), channel_id=1, source_target_pairs={{0,16},{4,20},{8,24},{12,28},{16,0},{20,4},{24,8},{28,12},{1,17},{... | collective-permute-start | bytes 491528 | tf_op jit(solution)/shard_map/ppermute | solution.py:817
  16.6 13.6 %collective-permute-start.1 = (bf16[80,1024]{1,0:T(8,128)(2,1)S(1)}, bf16[80,1024]{1,0:T(8,128)(2,1)S(1)}, u32[]{:S(2)}, u32[]{:S(2)}) collective-permute-start(bf16[80,1024]{1,0:T(8,128)(2,1)S(1)} %pad_maximum_fusion.5), channel_id=1, source_target_pairs={{0,8},{4,12},{8,0},{12,4},{16,24},{20,28},{24,16},{28,20},{1,9},{5... | collective-permute-start | bytes 491528 | tf_op jit(solution)/shard_map/ppermute | solution.py:817
  17.5 6.9 %collective-permute-start.12 = (s32[4,3]{1,0:T(4,128)S(1)}, s32[4,3]{1,0:T(4,128)S(1)}, u32[]{:S(2)}, u32[]{:S(2)}) collective-permute-start(s32[4,3]{1,0:T(4,128)S(1)} %slice.106), channel_id=1, source_target_pairs={{0,4},{4,8},{8,12},{12,16},{16,20},{20,24},{24,28},{1,5},{5,9},{9,... | collective-permute-start | bytes 152 | tf_op jit(solution)/shard_map/ppermute | solution.py:884
  20.9 9.8 %all-to-all-start = ((bf16[4,72,512]{2,1,0:T(8,128)(2,1)}), bf16[4,72,512]{2,1,0:T(8,128)(2,1)S(1)}, u32[]{:S(2)}, u32[]{:S(2)}) async-start(bf16[4,72,512]{2,1,0:T(8,128)(2,1)} %pad_maximum_fusion.3), calls=%async_computation | async-start | bytes 589824 | tf_op jit(solution)/shard_map/all_to_all | solution.py:849
  24.4 132.5 %copy-start.19 = (s32[2]{0:T(128)}, s32[2]{0:T(128)S(1)}, u32[]{:S(2)}) copy-start(s32[2]{0:T(128)S(1)} %pad_add_fusion.1.place_ref) | copy-start | bytes 28
  31.5 19.5 %collective-permute-start.4 = (bf16[4,80,1024]{2,1,0:T(8,128)(2,1)S(1)}, bf16[4,80,1024]{2,1,0:T(8,128)(2,1)S(1)}, u32[]{:S(2)}, u32[]{:S(2)}) collective-permute-start(bf16[4,80,1024]{2,1,0:T(8,128)(2,1)S(1)} %pad_maximum_fusion.exit_near_ref), channel_id=1, source_target_pairs={{0,4},{4,0},{8,12},{12,8},{16,20},{20,16},{24,28},{28,24},{1,5},{5... | collective-permute-start | bytes 1966088 | tf_op jit(solution)/shard_map/ppermute | solution.py:817
  32.8 7.0 %collective-permute-start.7 = (bf16[136,512]{1,0:T(8,128)(2,1)S(1)}, bf16[136,512]{1,0:T(8,128)(2,1)S(1)}, u32[]{:S(2)}, u32[]{:S(2)}) collective-permute-start(bf16[136,512]{1,0:T(8,128)(2,1)S(1)} %pad_maximum_fusion.6), channel_id=1, source_target_pairs={{0,24},{4,28},{8,16},{12,20},{16,8},{20,12},{24,0},{28,4},{1,25},{... | collective-permute-start | bytes 417800 | tf_op jit(solution)/shard_map/ppermute | solution.py:817
  35.3 15.8 %collective-permute-start.9 = (bf16[4,64,1024]{2,1,0:T(8,128)(2,1)S(1)}, bf16[4,64,1024]{2,1,0:T(8,128)(2,1)}, u32[]{:S(2)}, u32[]{:S(2)}) collective-permute-start(bf16[4,64,1024]{2,1,0:T(8,128)(2,1)S(1)} %collective-permute-done.slab2_ref), channel_id=1, source_target_pairs={{0,1},{1,0},{2,3},{3,2},{4,5},{5,4},{6,7},{7,6},{8,9},{9,8},{10,11... | collective-permute-start | bytes 1572872 | tf_op jit(solution)/shard_map/ppermute | solution.py:817
  35.3 15.8 %collective-permute-start.8 = (bf16[4,64,1024]{2,1,0:T(8,128)(2,1)S(1)}, bf16[4,64,1024]{2,1,0:T(8,128)(2,1)}, u32[]{:S(2)}, u32[]{:S(2)}) collective-permute-start(bf16[4,64,1024]{2,1,0:T(8,128)(2,1)S(1)} %copy-done), channel_id=1, source_target_pairs={{0,1},{1,0},{2,3},{3,2},{4,5},{5,4},{6,7},{7,6},{8,9},{9,8},{10,11... | collective-permute-start | bytes 1572872 | tf_op jit(solution)/shard_map/ppermute | solution.py:817
  35.8 12.3 %collective-permute-start.6 = (bf16[136,512]{1,0:T(8,128)(2,1)S(1)}, bf16[136,512]{1,0:T(8,128)(2,1)S(1)}, u32[]{:S(2)}, u32[]{:S(2)}) collective-permute-start(bf16[136,512]{1,0:T(8,128)(2,1)S(1)} %pad_maximum_fusion.6), channel_id=1, source_target_pairs={{0,16},{4,20},{8,24},{12,28},{16,0},{20,4},{24,8},{28,12},{1,17},{... | collective-permute-start | bytes 417800 | tf_op jit(solution)/shard_map/ppermute | solution.py:817
  39.8 11.2 %collective-permute-start.5 = (bf16[136,512]{1,0:T(8,128)(2,1)S(1)}, bf16[136,512]{1,0:T(8,128)(2,1)}, u32[]{:S(2)}, u32[]{:S(2)}) collective-permute-start(bf16[136,512]{1,0:T(8,128)(2,1)S(1)} %pad_maximum_fusion.6), channel_id=1, source_target_pairs={{0,8},{4,12},{8,0},{12,4},{16,24},{20,28},{24,16},{28,20},{1,9},{5... | collective-permute-start | bytes 417800 | tf_op jit(solution)/shard_map/ppermute | solution.py:817
  46.8 46.1 %copy-start.2 = (f32[4,4,64,4]{3,0,1,2:T(4,128)}, f32[4,4,64,4]{3,0,1,2:T(4,128)S(1)}, u32[]{:S(2)}) copy-start(f32[4,4,64,4]{3,0,1,2:T(4,128)S(1)} %copy.43) | copy-start | bytes 49156
  54.2 10.0 %collective-permute-start.20 = (bf16[128,512]{1,0:T(8,128)(2,1)}, bf16[128,512]{1,0:T(8,128)(2,1)}, u32[]{:S(2)}, u32[]{:S(2)}) collective-permute-start(bf16[128,512]{1,0:T(8,128)(2,1)} %bitcast.111), channel_id=1, source_target_pairs={{0,24},{4,28},{8,16},{12,20},{16,8},{20,12},{24,0},{28,4},{1,25},{... | collective-permute-start | bytes 393224 | tf_op jit(solution)/shard_map/ppermute | solution.py:817
  56.9 11.3 %collective-permute-start.19 = (bf16[128,512]{1,0:T(8,128)(2,1)}, bf16[128,512]{1,0:T(8,128)(2,1)}, u32[]{:S(2)}, u32[]{:S(2)}) collective-permute-start(bf16[128,512]{1,0:T(8,128)(2,1)} %bitcast.112), channel_id=1, source_target_pairs={{0,16},{4,20},{8,24},{12,28},{16,0},{20,4},{24,8},{28,12},{1,17},{... | collective-permute-start | bytes 393224 | tf_op jit(solution)/shard_map/ppermute | solution.py:817
  56.9 11.4 %collective-permute-start.18 = (bf16[128,512]{1,0:T(8,128)(2,1)}, bf16[128,512]{1,0:T(8,128)(2,1)}, u32[]{:S(2)}, u32[]{:S(2)}) collective-permute-start(bf16[128,512]{1,0:T(8,128)(2,1)} %bitcast.113), channel_id=1, source_target_pairs={{0,8},{4,12},{8,0},{12,4},{16,24},{20,28},{24,16},{28,20},{1,9},{5... | collective-permute-start | bytes 393224 | tf_op jit(solution)/shard_map/ppermute | solution.py:817
  58.7 14.7 %collective-permute-start.11 = (bf16[4,136,512]{2,1,0:T(8,128)(2,1)S(1)}, bf16[4,136,512]{2,1,0:T(8,128)(2,1)}, u32[]{:S(2)}, u32[]{:S(2)}) collective-permute-start(bf16[4,136,512]{2,1,0:T(8,128)(2,1)S(1)} %pad_maximum_fusion.1.near_ref), channel_id=1, source_target_pairs={{0,4},{4,0},{8,12},{12,8},{16,20},{20,16},{24,28},{28,24},{1,5},{5... | collective-permute-start | bytes 1671176 | tf_op jit(solution)/shard_map/ppermute | solution.py:817
  60.1 13.3 %collective-permute-start.16 = (bf16[4,64,1024]{2,1,0:T(8,128)(2,1)}, bf16[4,64,1024]{2,1,0:T(8,128)(2,1)}, u32[]{:S(2)}, u32[]{:S(2)}) collective-permute-start(bf16[4,64,1024]{2,1,0:T(8,128)(2,1)} %cotangent_ref), channel_id=1, source_target_pairs={{0,2},{1,3},{2,0},{3,1},{4,6},{5,7},{6,4},{7,5},{8,10},{9,11},{10,... | collective-permute-start | bytes 1572872 | tf_op jit(solution)/shard_map/ppermute | solution.py:817
  64.2 109.0 %copy-start.8 = (bf16[192,512]{1,0:T(8,128)(2,1)}, bf16[192,512]{1,0:T(8,128)(2,1)S(1)}, u32[]{:S(2)}) copy-start(bf16[192,512]{1,0:T(8,128)(2,1)S(1)} %copy.46.small_ref) | copy-start | bytes 589828
  64.2 10.0 %collective-permute-start.10 = (bf16[12,1024]{1,0:T(8,128)(2,1)S(1)}, bf16[12,1024]{1,0:T(8,128)(2,1)S(1)}, u32[]{:S(2)}, u32[]{:S(2)}) collective-permute-start(bf16[12,1024]{1,0:T(8,128)(2,1)S(1)} %reshape.116), channel_id=1, source_target_pairs={{0,4},{4,8},{8,12},{12,16},{16,20},{20,24},{24,28},{1,5},{5,9},{9,... | collective-permute-start | bytes 73736 | tf_op jit(solution)/shard_map/ppermute | solution.py:879
  68.2 18.1 %collective-permute-start.15 = (bf16[4,64,1024]{2,1,0:T(8,128)(2,1)}, bf16[4,64,1024]{2,1,0:T(8,128)(2,1)S(1)}, u32[]{:S(2)}, u32[]{:S(2)}) collective-permute-start(bf16[4,64,1024]{2,1,0:T(8,128)(2,1)} %cotangent_ref), channel_id=1, source_target_pairs={{0,1},{1,0},{2,3},{3,2},{4,5},{5,4},{6,7},{7,6},{8,9},{9,8},{10,11... | collective-permute-start | bytes 1572872 | tf_op jit(solution)/shard_map/ppermute | solution.py:817
  69.5 16.8 %collective-permute-start.21 = (bf16[4,128,512]{2,1,0:T(8,128)(2,1)S(1)}, bf16[4,128,512]{2,1,0:T(8,128)(2,1)S(1)}, u32[]{:S(2)}, u32[]{:S(2)}) collective-permute-start(bf16[4,128,512]{2,1,0:T(8,128)(2,1)S(1)} %pad_maximum_fusion.2.near_ref.gate_near_ref), channel_id=1, source_target_pairs={{0,4},{4,0},{8,12},{12,8},{16,20},{20,16},{24,28},{28,24},{1,5},{5... | collective-permute-start | bytes 1572872 | tf_op jit(solution)/shard_map/ppermute | solution.py:817
  73.4 12.9 %collective-permute-start.17 = (bf16[4,64,1024]{2,1,0:T(8,128)(2,1)}, bf16[4,64,1024]{2,1,0:T(8,128)(2,1)S(1)}, u32[]{:S(2)}, u32[]{:S(2)}) collective-permute-start(bf16[4,64,1024]{2,1,0:T(8,128)(2,1)} %collective-permute-done.16.slab2_ref), channel_id=1, source_target_pairs={{0,1},{1,0},{2,3},{3,2},{4,5},{5,4},{6,7},{7,6},{8,9},{9,8},{10,11... | collective-permute-start | bytes 1572872 | tf_op jit(solution)/shard_map/ppermute | solution.py:817
  83.9 51.4 %copy-start.17 = (f32[1024,512]{1,0:T(8,128)}, f32[1024,512]{1,0:T(8,128)S(1)}, u32[]{:S(2)}) copy-start(f32[1024,512]{1,0:T(8,128)S(1)} %get-tuple-element.127.filter_ref) | copy-start | bytes 6291460
  83.9 72.9 %copy-start.21 = (bf16[1024,1024]{1,0:T(8,128)(2,1)}, bf16[1024,1024]{1,0:T(8,128)(2,1)S(1)}, u32[]{:S(2)}) copy-start(bf16[1024,1024]{1,0:T(8,128)(2,1)S(1)} %get-tuple-element.131.normed_ref) | copy-start | bytes 6291460
  83.9 1.6 collective-permute-start.13
  85.6 7.3 %collective-permute-start.14 = (bf16[96,1024]{1,0:T(8,128)(2,1)S(1)}, bf16[96,1024]{1,0:T(8,128)(2,1)S(1)}, u32[]{:S(2)}, u32[]{:S(2)}) collective-permute-start(bf16[96,1024]{1,0:T(8,128)(2,1)S(1)} %add_convert_fusion.3.chosen_ref), channel_id=1, source_target_pairs={{0,2},{1,3},{2,0},{3,1},{4,6},{5,7},{6,4},{7,5},{8,10},{9,11},{10,... | collective-permute-start | bytes 589832 | tf_op jit(solution)/shard_map/ppermute | solution.py:817
  92.9 42.5 %copy-start.18 = (f32[1024,512]{1,0:T(8,128)}, f32[1024,512]{1,0:T(8,128)S(1)}, u32[]{:S(2)}) copy-start(f32[1024,512]{1,0:T(8,128)S(1)} %get-tuple-element.147) | copy-start | bytes 6291460
  113.8 43.1 %copy-start.30 = (f32[64,16,512]{2,1,0:T(8,128)}, f32[64,16,512]{2,1,0:T(8,128)S(1)}, u32[]{:S(2)}) copy-start(f32[64,16,512]{2,1,0:T(8,128)S(1)} %get-tuple-element.136.step_ref) | copy-start | bytes 6291460
  113.8 43.1 %copy-start.33 = (f32[64,16,128]{2,1,0:T(8,128)}, f32[64,16,128]{2,1,0:T(8,128)S(1)}, u32[]{:S(2)}) copy-start(f32[64,16,128]{2,1,0:T(8,128)S(1)} %get-tuple-element.135.gates_ref) | copy-start | bytes 1572868
  166.9 40.5 %collective-permute-start.23 = (bf16[2,4,64,1024]{3,2,1,0:T(8,128)(2,1)}, bf16[2,4,64,1024]{3,2,1,0:T(8,128)(2,1)}, u32[]{:S(2)}, u32[]{:S(2)}) collective-permute-start(bf16[2,4,64,1024]{3,2,1,0:T(8,128)(2,1)} %get-tuple-element.146), channel_id=1, source_target_pairs={{0,1},{1,0},{2,3},{3,2},{4,5},{5,4},{6,7},{7,6},{8,9},{9,8},{10,11... | collective-permute-start | bytes 3145736 | tf_op jit(solution)/shard_map/ppermute | solution.py:817
  166.9 40.5 %all-to-all-start.2 = ((bf16[8,64,1024]{2,1,0:T(8,128)(2,1)}), bf16[8,64,1024]{2,1,0:T(8,128)(2,1)}, u32[]{:S(2)}, u32[]{:S(2)}) async-start(bf16[8,64,1024]{2,1,0:T(8,128)(2,1)} %bitcast.43), calls=%async_computation.2 | async-start | bytes 2097152 | tf_op jit(solution)/shard_map/all_to_all | solution.py:1004
  171.3 36.0 %collective-permute-start.22 = (bf16[4,128,512]{2,1,0:T(8,128)(2,1)}, bf16[4,128,512]{2,1,0:T(8,128)(2,1)}, u32[]{:S(2)}, u32[]{:S(2)}) collective-permute-start(bf16[4,128,512]{2,1,0:T(8,128)(2,1)} %get-tuple-element.153), channel_id=1, source_target_pairs={{0,4},{4,0},{8,12},{12,8},{16,20},{20,16},{24,28},{28,24},{1,5},{5... | collective-permute-start | bytes 1572872 | tf_op jit(solution)/shard_map/ppermute | solution.py:817
  207.3 1.5 collective-permute-start.24
  208.9 7.0 %collective-permute-start.25 = (bf16[96,1024]{1,0:T(8,128)(2,1)S(1)}, bf16[96,1024]{1,0:T(8,128)(2,1)S(1)}, u32[]{:S(2)}, u32[]{:S(2)}) collective-permute-start(bf16[96,1024]{1,0:T(8,128)(2,1)S(1)} %add_convert_fusion.2.chosen_ref), channel_id=1, source_target_pairs={{0,2},{1,3},{2,0},{3,1},{4,6},{5,7},{6,4},{7,5},{8,10},{9,11},{10,... | collective-permute-start | bytes 589832 | tf_op jit(solution)/shard_map/ppermute | solution.py:817
  214.5 24.3 %collective-permute-start.27 = (bf16[4,64,1024]{2,1,0:T(8,128)(2,1)}, bf16[4,64,1024]{2,1,0:T(8,128)(2,1)}, u32[]{:S(2)}, u32[]{:S(2)}) collective-permute-start(bf16[4,64,1024]{2,1,0:T(8,128)(2,1)} %fusion.2), channel_id=1, source_target_pairs={{0,2},{1,3},{2,0},{3,1},{4,6},{5,7},{6,4},{7,5},{8,10},{9,11},{10,... | collective-permute-start | bytes 1572872 | tf_op jit(solution)/shard_map/ppermute | solution.py:817
  226.2 6.6 %collective-permute-start.26 = (f32[3,4,512]{2,1,0:T(4,128)}, f32[3,4,512]{2,1,0:T(4,128)S(1)}, u32[]{:S(2)}, u32[]{:S(2)}) collective-permute-start(f32[3,4,512]{2,1,0:T(4,128)} %get-tuple-element.169), channel_id=1, source_target_pairs={{4,0},{8,4},{12,8},{16,12},{20,16},{24,20},{28,24},{5,1},{9,5},{13... | collective-permute-start | bytes 73736 | tf_op jit(solution)/shard_map/ppermute | solution.py:1070
  227.7 19.2 %collective-permute-start.28 = (bf16[176,512]{1,0:T(8,128)(2,1)}, bf16[176,512]{1,0:T(8,128)(2,1)S(1)}, u32[]{:S(2)}, u32[]{:S(2)}) collective-permute-start(bf16[176,512]{1,0:T(8,128)(2,1)} %get-tuple-element.179), channel_id=1, source_target_pairs={{0,8},{4,12},{8,0},{12,4},{16,24},{20,28},{24,16},{28,20},{1,9},{5... | collective-permute-start | bytes 540680 | tf_op jit(solution)/shard_map/ppermute | solution.py:817
  230.1 16.9 %collective-permute-start.29 = (bf16[176,512]{1,0:T(8,128)(2,1)}, bf16[176,512]{1,0:T(8,128)(2,1)S(1)}, u32[]{:S(2)}, u32[]{:S(2)}) collective-permute-start(bf16[176,512]{1,0:T(8,128)(2,1)} %get-tuple-element.180), channel_id=1, source_target_pairs={{0,16},{4,20},{8,24},{12,28},{16,0},{20,4},{24,8},{28,12},{1,17},{... | collective-permute-start | bytes 540680 | tf_op jit(solution)/shard_map/ppermute | solution.py:817
  232.8 14.2 %collective-permute-start.30 = (bf16[176,512]{1,0:T(8,128)(2,1)}, bf16[176,512]{1,0:T(8,128)(2,1)S(1)}, u32[]{:S(2)}, u32[]{:S(2)}) collective-permute-start(bf16[176,512]{1,0:T(8,128)(2,1)} %get-tuple-element.181), channel_id=1, source_target_pairs={{0,24},{4,28},{8,16},{12,20},{16,8},{20,12},{24,0},{28,4},{1,25},{... | collective-permute-start | bytes 540680 | tf_op jit(solution)/shard_map/ppermute | solution.py:817
  247.0 6.1 %collective-permute-start.31 = (bf16[2,4,64,1024]{3,2,1,0:T(8,128)(2,1)}, bf16[2,4,64,1024]{3,2,1,0:T(8,128)(2,1)}, u32[]{:S(2)}, u32[]{:S(2)}) collective-permute-start(bf16[2,4,64,1024]{3,2,1,0:T(8,128)(2,1)} %get-tuple-element.182), channel_id=1, source_target_pairs={{0,1},{1,0},{2,3},{3,2},{4,5},{5,4},{6,7},{7,6},{8,9},{9,8},{10,11... | collective-permute-start | bytes 3145736 | tf_op jit(solution)/shard_map/ppermute | solution.py:817
  247.1 33.6 %all-to-all-start.3 = ((bf16[32,32,512]{2,1,0:T(8,128)(2,1)}), bf16[32,32,512]{2,1,0:T(8,128)(2,1)S(1)}, u32[]{:S(2)}, u32[]{:S(2)}) async-start(bf16[32,32,512]{2,1,0:T(8,128)(2,1)} %bitcast.49), calls=%async_computation.3 | async-start | bytes 2097152 | tf_op jit(solution)/shard_map/all_to_all | solution.py:1081
  256.9 6.6 %collective-permute-start.32 = (bf16[32,512]{1,0:T(8,128)(2,1)S(1)}, bf16[32,512]{1,0:T(8,128)(2,1)S(1)}, u32[]{:S(2)}, u32[]{:S(2)}) collective-permute-start(bf16[32,512]{1,0:T(8,128)(2,1)S(1)} %get-tuple-element.187), channel_id=1, source_target_pairs={{0,3},{1,2},{2,1},{3,0},{4,7},{5,6},{6,5},{7,4},{8,11},{9,10},{10,... | collective-permute-start | bytes 98312 | tf_op jit(solution)/shard_map/ppermute | solution.py:817
  258.5 24.4 %collective-permute-start.33 = (bf16[4,64,1024]{2,1,0:T(8,128)(2,1)}, bf16[4,64,1024]{2,1,0:T(8,128)(2,1)}, u32[]{:S(2)}, u32[]{:S(2)}) collective-permute-start(bf16[4,64,1024]{2,1,0:T(8,128)(2,1)} %fusion.3), channel_id=1, source_target_pairs={{0,2},{1,3},{2,0},{3,1},{4,6},{5,7},{6,4},{7,5},{8,10},{9,11},{10,... | collective-permute-start | bytes 1572872 | tf_op jit(solution)/shard_map/ppermute | solution.py:817
  258.9 14.4 %collective-permute-start.34 = (bf16[32,512]{1,0:T(8,128)(2,1)S(1)}, bf16[32,512]{1,0:T(8,128)(2,1)S(1)}, u32[]{:S(2)}, u32[]{:S(2)}) collective-permute-start(bf16[32,512]{1,0:T(8,128)(2,1)S(1)} %get-tuple-element.192), channel_id=1, source_target_pairs={{0,1},{1,0},{2,3},{3,2},{4,5},{5,4},{6,7},{7,6},{8,9},{9,8},{10,11... | collective-permute-start | bytes 98312 | tf_op jit(solution)/shard_map/ppermute | solution.py:817
  258.9 21.8 %collective-permute-start.35 = (bf16[32,512]{1,0:T(8,128)(2,1)S(1)}, bf16[32,512]{1,0:T(8,128)(2,1)S(1)}, u32[]{:S(2)}, u32[]{:S(2)}) collective-permute-start(bf16[32,512]{1,0:T(8,128)(2,1)S(1)} %get-tuple-element.193), channel_id=1, source_target_pairs={{0,2},{1,3},{2,0},{3,1},{4,6},{5,7},{6,4},{7,5},{8,10},{9,11},{10,... | collective-permute-start | bytes 98312 | tf_op jit(solution)/shard_map/ppermute | solution.py:817
  263.5 6.6 %collective-permute-start.36 = (f32[192,128]{1,0:T(8,128)S(1)}, f32[192,128]{1,0:T(8,128)S(1)}, u32[]{:S(2)}, u32[]{:S(2)}) collective-permute-start(f32[192,128]{1,0:T(8,128)S(1)} %get-tuple-element.198), channel_id=1, source_target_pairs={{0,4},{4,0},{8,12},{12,8},{16,20},{20,16},{24,28},{28,24},{1,5},{5... | collective-permute-start | bytes 294920 | tf_op jit(solution)/shard_map/ppermute | solution.py:817
  (41 other events, 248.1 us)

commit v6 on v5

--- a/solution.py
+++ b/solution.py
@@ -828,9 +828,7 @@
             select_weight.T,
             decay_log,
             kernel_weight,
-            kernel_offset[None],
-            timestep_bias[None],
-            skip_gain[None],
+            jnp.concatenate([kernel_offset, timestep_bias, skip_gain]).reshape(3, own),
             jnp.zeros((small_rows - 183, own), bf16),
         ],
         axis=0,
@@ -845,7 +843,7 @@
     halves = halves.reshape(groups, 2 * slice_rows, group_width)
     halves = jnp.concatenate([halves, jnp.broadcast_to(gain_line, (groups,) + gain_line.shape[1:])], axis=1)
     exit_block = jnp.concatenate([exit_weight, jnp.pad(packed.reshape(-1), (0, -packed.size % (16 * width))).reshape(-1, width)])
-    halves, exit_block, tokens = rounds(halves, exit_block, tokens)
+    halves, exit_block = rounds(halves, exit_block)
     halves = lax.all_to_all(halves, "grp", split_axis=0, concat_axis=0, tiled=True)
     exit_side = side_blocks(exit_block)
     token_pair = flipped(tokens, "grp", 2)

time: 287 us -> 286 us (level)
  transfers between devices with their start and end apart: 40 -> 40, of which waited for: 12 -> 12; matrix products, arithmetic and copies ran while one was open for 7% -> 10% of each run, Pallas kernels for 24% -> 24%
where the time goes in v6:
time: 286 us; the launch traced here: 284 us
  Pallas kernels  120 us (42%)
  starting transfers between devices  63.9 us (22%)
  waiting for transfers between devices  32.5 us (11%)
  local copies, waits for them, and re-layouts  28 us (10%)
  blocking collectives  21.6 us (8%)
  other arithmetic  16.6 us (6%)
    pallas_call x12, Pallas kernels, kernel_call(): pl.pallas_call(body, out_shape=[jax.ShapeDtypeStruct(shape, kind) for sha...  120 us
    ppermute x34, starting transfers between devices, flipped(): lax.ppermute(value, axis, [(i, i ^ bits) for i in range(lax.axis_size(axi...  41.2 us
    ppermute x34, waiting for transfers between devices, flipped(): lax.ppermute(value, axis, [(i, i ^ bits) for i in range(lax.axis_size(axi...  32 us
    all_to_all x1, blocking collectives, local(): came = lax.all_to_all(loads, 'blk', split_axis=0, concat_axis=0, tiled=True)  21.6 us
    unnamed x104, local copies, waits for them, and re-layouts  16 us
    all_to_all x1, starting transfers between devices, local(): lax.all_to_all(inner_entry.reshape(pieces * groups, slice_rows, group_wid...  6.03 us
  transfers between devices with their start and end apart: 40, of which 12 were waited for; matrix products, arithmetic and copies ran while one was open for 10% of the time, Pallas kernels for 24%

profile of v6, /device:TPU:0, one launch (start us, length us, event | category | flops | bytes accessed | tf_op | source)
XLA Modules:
  0.0 284.4 jit_solution(2383848373280285487)
XLA Ops:
  0.7 3.0 %collective-permute-start = (bf16[4,64,1024]{2,1,0:T(8,128)(2,1)}, bf16[4,64,1024]{2,1,0:T(8,128)(2,1)S(1)}, u32[]{:S(2)}, u32[]{:S(2)}) collective-permute-start(bf16[4,64,1024]{2,1,0:T(8,128)(2,1)} %tokens_ref), channel_id=1, source_target_pairs={{0,2},{1,3},{2,0},{3,1},{4,6},{5,7},{6,4},{7,5},{8,10},{9,11},{10,... | collective-permute-start | bytes 1572872 | tf_op jit(solution)/shard_map/ppermute | solution.py:817
  9.0 1.5 reshape.112
  11.7 3.6 %collective-permute-start.3 = (bf16[80,1024]{1,0:T(8,128)(2,1)S(1)}, bf16[80,1024]{1,0:T(8,128)(2,1)S(1)}, u32[]{:S(2)}, u32[]{:S(2)}) collective-permute-start(bf16[80,1024]{1,0:T(8,128)(2,1)S(1)} %pad_maximum_fusion.5), channel_id=1, source_target_pairs={{0,24},{4,28},{8,16},{12,20},{16,8},{20,12},{24,0},{28,4},{1,25},{... | collective-permute-start | bytes 491528 | tf_op jit(solution)/shard_map/ppermute | solution.py:817
  16.1 3.4 %collective-permute-start.12 = (s32[4,3]{1,0:T(4,128)S(1)}, s32[4,3]{1,0:T(4,128)S(1)}, u32[]{:S(2)}, u32[]{:S(2)}) collective-permute-start(s32[4,3]{1,0:T(4,128)S(1)} %slice.106), channel_id=1, source_target_pairs={{0,4},{4,8},{8,12},{12,16},{16,20},{20,24},{24,28},{1,5},{5,9},{9,... | collective-permute-start | bytes 152 | tf_op jit(solution)/shard_map/ppermute | solution.py:882
  19.5 3.5 %all-to-all-start = ((bf16[4,72,512]{2,1,0:T(8,128)(2,1)}), bf16[4,72,512]{2,1,0:T(8,128)(2,1)S(1)}, u32[]{:S(2)}, u32[]{:S(2)}) async-start(bf16[4,72,512]{2,1,0:T(8,128)(2,1)} %pad_maximum_fusion.3), calls=%async_computation | async-start | bytes 589824 | tf_op jit(solution)/shard_map/all_to_all | solution.py:847
  23.1 5.7 %collective-permute-done.2 = bf16[80,1024]{1,0:T(8,128)(2,1)S(1)} collective-permute-done((bf16[80,1024]{1,0:T(8,128)(2,1)S(1)}, bf16[80,1024]{1,0:T(8,128)(2,1)S(1)}, u32[]{:S(2)}, u32[]{:S(2)}) %collective-permute-start.2) | collective-permute-done | bytes 163872 | tf_op jit(solution)/shard_map/ppermute | solution.py:817
  30.2 1.3 collective-permute-start.4
  31.5 2.5 collective-permute-start.7
  35.1 3.4 %collective-permute-done.7 = bf16[136,512]{1,0:T(8,128)(2,1)S(1)} collective-permute-done((bf16[136,512]{1,0:T(8,128)(2,1)S(1)}, bf16[136,512]{1,0:T(8,128)(2,1)S(1)}, u32[]{:S(2)}, u32[]{:S(2)}) %collective-permute-start.7) | collective-permute-done | bytes 139296 | tf_op jit(solution)/shard_map/ppermute | solution.py:817
  38.5 6.5 %collective-permute-start.5 = (bf16[136,512]{1,0:T(8,128)(2,1)S(1)}, bf16[136,512]{1,0:T(8,128)(2,1)}, u32[]{:S(2)}, u32[]{:S(2)}) collective-permute-start(bf16[136,512]{1,0:T(8,128)(2,1)S(1)} %pad_maximum_fusion.6), channel_id=1, source_target_pairs={{0,8},{4,12},{8,0},{12,4},{16,24},{20,28},{24,16},{28,20},{1,9},{5... | collective-permute-start | bytes 417800 | tf_op jit(solution)/shard_map/ppermute | solution.py:817
  45.4 1.3 collective-permute-done.6
  46.7 3.0 %collective-permute-done.5 = bf16[136,512]{1,0:T(8,128)(2,1)} collective-permute-done((bf16[136,512]{1,0:T(8,128)(2,1)S(1)}, bf16[136,512]{1,0:T(8,128)(2,1)}, u32[]{:S(2)}, u32[]{:S(2)}) %collective-permute-start.5) | collective-permute-done | bytes 139296 | tf_op jit(solution)/shard_map/ppermute | solution.py:817
  52.9 2.6 collective-permute-start.20
  55.5 1.8 collective-permute-start.18
  62.9 3.9 %collective-permute-start.10 = (bf16[12,1024]{1,0:T(8,128)(2,1)S(1)}, bf16[12,1024]{1,0:T(8,128)(2,1)S(1)}, u32[]{:S(2)}, u32[]{:S(2)}) collective-permute-start(bf16[12,1024]{1,0:T(8,128)(2,1)S(1)} %reshape.120), channel_id=1, source_target_pairs={{0,4},{4,8},{8,12},{12,16},{16,20},{20,24},{24,28},{1,5},{5,9},{9,... | collective-permute-start | bytes 73736 | tf_op jit(solution)/shard_map/ppermute | solution.py:877
  68.8 3.2 %collective-permute-done.16.slab2_ref = bf16[4,64,1024]{2,1,0:T(8,128)(2,1)} collective-permute-done((bf16[4,64,1024]{2,1,0:T(8,128)(2,1)}, bf16[4,64,1024]{2,1,0:T(8,128)(2,1)}, u32[]{:S(2)}, u32[]{:S(2)}) %collective-permute-start.16) | collective-permute-done | bytes 524320 | tf_op jit(solution)/shard_map/ppermute | solution.py:817
  72.9 8.7 %shard_map.220 = (bf16[1024,1024]{1,0:T(8,128)(2,1)S(1)}, bf16[1072,512]{1,0:T(8,128)(2,1)S(1)}, f32[1024,512]{1,0:T(8,128)S(1)}, bf16[96,1024]{1,0:T(8,128)(2,1)S(1)}) custom-call(s32[2]{0:T(128)S(1)} %pad_add_fusion.1.place_ref, bf16[4,64,1024]{2,1,0:T(8,128)(2,1)S(1)} %copy-done, bf16[4,64,1024]{2,1,0:T(8,128)(2,1)} %collective-permute-done.8.slab1_ref, ...), custom_call_target="tpu_custom_call" | custom-call | flops 10350000128 | bytes 8000000 | tf_op jit(solution)/shard_map/pallas_call | solution.py:59
  85.0 6.5 %shard_map.221 = (bf16[1024,1024]{1,0:T(8,128)(2,1)S(1)}, f32[1024,512]{1,0:T(8,128)S(1)}, f32[1024,512]{1,0:T(8,128)S(1)}, f32[1024,512]{1,0:T(8,128)S(1)}) custom-call(s32[2]{0:T(128)S(1)} %pad_add_fusion.1.place_ref, bf16[4,64,1024]{2,1,0:T(8,128)(2,1)S(1)} %copy-done.13, bf16[4,64,1024]{2,1,0:T(8,128)(2,1)S(1)} %collective-permute-done.15.slab1_ref, ...), custom_call_target="tpu_custom_call" | custom-call | flops 9200000000 | bytes 8000000 | tf_op jit(solution)/shard_map/pallas_call | solution.py:59
  91.5 19.6 %shard_map.222 = (f32[64,16,128]{2,1,0:T(8,128)S(1)}, f32[64,16,512]{2,1,0:T(8,128)S(1)}, f32[64,16,512]{2,1,0:T(8,128)S(1)}, f32[16,16,512]{2,1,0:T(8,128)S(1)}...) custom-call(s32[2]{0:T(128)S(1)} %pad_add_fusion.1.place_ref, ...), custom_call_target="tpu_custom_call" | custom-call | flops 26449999872 | bytes 8000000 | tf_op jit(solution)/shard_map/pallas_call | solution.py:59
  111.1 1.3 copy-done.32
  112.4 21.6 %all_to_all.20.came_ref = bf16[8,72,512]{2,1,0:T(8,128)(2,1)S(1)} all-to-all(bf16[8,72,512]{2,1,0:T(8,128)(2,1)S(1)} %get-tuple-element.132), channel_id=1, replica_groups=mesh['blk'=8,'grp'=4] {'blk'}, dimensions={0} | all-to-all | bytes 1179648 | tf_op jit(solution)/shard_map/all_to_all | solution.py:964
  134.0 21.5 %shard_map.223 = (f32[64,16,512]{2,1,0:T(8,128)S(1)}, f32[64,16,128]{2,1,0:T(8,128)S(1)}, f32[16,16,16,512]{3,2,1,0:T(8,128)}, f32[16,16,512]{2,1,0:T(8,128)S(1)}) custom-call(s32[2]{0:T(128)S(1)} %pad_add_fusion.1.place_ref, bf16[8,72,512]{2,1,0:T(8,128)(2,1)S(1)} %all_to_all.20.came_ref, f32[64,16,128]{2,1,0:T(8,128)S(1)} %get-tuple-element.133.gates_ref, ...), custom_call_target="tpu_custom_call" | custom-call | flops 20700000256 | bytes 8000000 | tf_op jit(solution)/shard_map/pallas_call | solution.py:59
  155.5 8.1 %shard_map.224 = (bf16[1024,512]{1,0:T(8,128)(2,1)S(1)}, bf16[2,4,64,1024]{3,2,1,0:T(8,128)(2,1)S(1)}, bf16[2,4,64,1024]{3,2,1,0:T(8,128)(2,1)}, bf16[512,1024]{...) custom-call(s32[2]{0:T(128)S(1)} %pad_add_fusion.1.place_ref, ...), custom_call_target="tpu_custom_call" | custom-call | flops 13799999488 | bytes 8000000 | tf_op jit(solution)/shard_map/pallas_call | solution.py:59
  165.5 4.4 %all-to-all-start.2 = ((bf16[8,64,1024]{2,1,0:T(8,128)(2,1)}), bf16[8,64,1024]{2,1,0:T(8,128)(2,1)}, u32[]{:S(2)}, u32[]{:S(2)}) async-start(bf16[8,64,1024]{2,1,0:T(8,128)(2,1)} %bitcast.40), calls=%async_computation.2 | async-start | bytes 2097152 | tf_op jit(solution)/shard_map/all_to_all | solution.py:1002
  169.9 1.9 collective-permute-start.22
  173.9 32.0 %shard_map.225 = (f32[64,16,512]{2,1,0:T(8,128)}, f32[64,512]{1,0:T(8,128)S(1)}, bf16[96,1024]{1,0:T(8,128)(2,1)S(1)}, f32[16,512]{1,0:T(8,128)S(1)}, f32[1,512]{1,0:T(1,128)S(1)}, /*index=5*/f32[1,512]{1,0:T(1,128)S(1)}) custom-call(f32[64,16,128]{2,1,0:T(8,128)S(1)} %copy-done.34, bf16[192,512]{1,0:T(8,128)(2,1)S(1)} %copy.41.small_ref, ...), custom_call_target="tpu_custom_call" | custom-call | flops 40249999360 | bytes 8000000 | tf_op jit(solution)/shard_map/pallas_call | solution.py:59
  206.0 1.4 collective-permute-done.24
  207.6 1.4 collective-permute-start.25
  209.0 2.0 fusion.2
  211.0 2.1 convert_reduce_fusion
  215.2 9.6 %shard_map.226 = (bf16[1024,512]{1,0:T(8,128)(2,1)}, f32[3,16,512]{2,1,0:T(8,128)}, f32[3,4,512]{2,1,0:T(4,128)}, f32[192,512]{1,0:T(8,128)}, f32[176,512]{1,0:T...) custom-call(s32[2]{0:T(128)} %copy-done.19, bf16[96,1024]{1,0:T(8,128)(2,1)} %copy-done.42, ...), custom_call_target="tpu_custom_call" | custom-call | flops 6899999744 | bytes 8000000 | tf_op jit(solution)/shard_map/pallas_call | solution.py:59
  224.9 1.5 collective-permute-start.26
  226.4 2.3 collective-permute-start.28
  228.7 2.7 collective-permute-start.29
  231.4 1.6 copy-done.22
  235.2 2.3 shard_map.227
  237.5 7.2 %shard_map.228 = (bf16[2,4,64,1024]{3,2,1,0:T(8,128)(2,1)S(1)}, bf16[2,4,64,1024]{3,2,1,0:T(8,128)(2,1)}) custom-call(s32[2]{0:T(128)S(1)} %copy-done.20, bf16[1024,512]{1,0:T(8,128)(2,1)S(1)} %get-tuple-element.173.inner_ref, bf16[1024,512]{1,0:T(8,128)(2,1)S(1)} %copy-done.28, bf16[4,136,512]{2,1,0:T(8,128)(2,1)S(1)} %pad_maximum_fusion.1.near_ref, ...), custom_call_target="tpu_custom_call" | custom-call | flops 11500000256 | bytes 8000000 | tf_op jit(solution)/shard_map/pallas_call | solution.py:59
  245.7 6.0 %all-to-all-start.3 = ((bf16[32,32,512]{2,1,0:T(8,128)(2,1)}), bf16[32,32,512]{2,1,0:T(8,128)(2,1)S(1)}, u32[]{:S(2)}, u32[]{:S(2)}) async-start(bf16[32,32,512]{2,1,0:T(8,128)(2,1)} %bitcast.46), calls=%async_computation.3 | async-start | bytes 2097152 | tf_op jit(solution)/shard_map/all_to_all | solution.py:1079
  251.7 2.2 fusion.3
  255.6 1.6 collective-permute-start.32
  257.6 1.7 collective-permute-start.35
  259.3 2.8 %collective-permute-done.32.gate3_ref = bf16[32,512]{1,0:T(8,128)(2,1)S(1)} collective-permute-done((bf16[32,512]{1,0:T(8,128)(2,1)S(1)}, bf16[32,512]{1,0:T(8,128)(2,1)S(1)}, u32[]{:S(2)}, u32[]{:S(2)}) %collective-permute-start.32) | collective-permute-done | bytes 32800 | tf_op jit(solution)/shard_map/ppermute | solution.py:817
  262.1 2.4 collective-permute-start.36
  264.6 2.4 fusion.1
  266.9 1.9 collective-permute-done.36
  271.9 7.4 %collective-permute-done.35.gate2_ref = bf16[32,512]{1,0:T(8,128)(2,1)S(1)} collective-permute-done((bf16[32,512]{1,0:T(8,128)(2,1)S(1)}, bf16[32,512]{1,0:T(8,128)(2,1)S(1)}, u32[]{:S(2)}, u32[]{:S(2)}) %collective-permute-start.35) | collective-permute-done | bytes 32800 | tf_op jit(solution)/shard_map/ppermute | solution.py:817
  279.4 1.6 shard_map.230
  281.6 2.8 shard_map.231
  (214 shorter events, 40.2 us)
Async XLA Ops:
  0.7 28.7 %collective-permute-start = (bf16[4,64,1024]{2,1,0:T(8,128)(2,1)}, bf16[4,64,1024]{2,1,0:T(8,128)(2,1)S(1)}, u32[]{:S(2)}, u32[]{:S(2)}) collective-permute-start(bf16[4,64,1024]{2,1,0:T(8,128)(2,1)} %tokens_ref), channel_id=1, source_target_pairs={{0,2},{1,3},{2,0},{3,1},{4,6},{5,7},{6,4},{7,5},{8,10},{9,11},{10,... | collective-permute-start | bytes 1572872 | tf_op jit(solution)/shard_map/ppermute | solution.py:817
  11.7 11.5 %collective-permute-start.3 = (bf16[80,1024]{1,0:T(8,128)(2,1)S(1)}, bf16[80,1024]{1,0:T(8,128)(2,1)S(1)}, u32[]{:S(2)}, u32[]{:S(2)}) collective-permute-start(bf16[80,1024]{1,0:T(8,128)(2,1)S(1)} %pad_maximum_fusion.5), channel_id=1, source_target_pairs={{0,24},{4,28},{8,16},{12,20},{16,8},{20,12},{24,0},{28,4},{1,25},{... | collective-permute-start | bytes 491528 | tf_op jit(solution)/shard_map/ppermute | solution.py:817
  15.3 13.6 %collective-permute-start.2 = (bf16[80,1024]{1,0:T(8,128)(2,1)S(1)}, bf16[80,1024]{1,0:T(8,128)(2,1)S(1)}, u32[]{:S(2)}, u32[]{:S(2)}) collective-permute-start(bf16[80,1024]{1,0:T(8,128)(2,1)S(1)} %pad_maximum_fusion.5), channel_id=1, source_target_pairs={{0,16},{4,20},{8,24},{12,28},{16,0},{20,4},{24,8},{28,12},{1,17},{... | collective-permute-start | bytes 491528 | tf_op jit(solution)/shard_map/ppermute | solution.py:817
  15.3 13.6 %collective-permute-start.1 = (bf16[80,1024]{1,0:T(8,128)(2,1)S(1)}, bf16[80,1024]{1,0:T(8,128)(2,1)S(1)}, u32[]{:S(2)}, u32[]{:S(2)}) collective-permute-start(bf16[80,1024]{1,0:T(8,128)(2,1)S(1)} %pad_maximum_fusion.5), channel_id=1, source_target_pairs={{0,8},{4,12},{8,0},{12,4},{16,24},{20,28},{24,16},{28,20},{1,9},{5... | collective-permute-start | bytes 491528 | tf_op jit(solution)/shard_map/ppermute | solution.py:817
  16.1 6.9 %collective-permute-start.12 = (s32[4,3]{1,0:T(4,128)S(1)}, s32[4,3]{1,0:T(4,128)S(1)}, u32[]{:S(2)}, u32[]{:S(2)}) collective-permute-start(s32[4,3]{1,0:T(4,128)S(1)} %slice.106), channel_id=1, source_target_pairs={{0,4},{4,8},{8,12},{12,16},{16,20},{20,24},{24,28},{1,5},{5,9},{9,... | collective-permute-start | bytes 152 | tf_op jit(solution)/shard_map/ppermute | solution.py:882
  19.5 9.8 %all-to-all-start = ((bf16[4,72,512]{2,1,0:T(8,128)(2,1)}), bf16[4,72,512]{2,1,0:T(8,128)(2,1)S(1)}, u32[]{:S(2)}, u32[]{:S(2)}) async-start(bf16[4,72,512]{2,1,0:T(8,128)(2,1)} %pad_maximum_fusion.3), calls=%async_computation | async-start | bytes 589824 | tf_op jit(solution)/shard_map/all_to_all | solution.py:847
  23.1 132.5 %copy-start.19 = (s32[2]{0:T(128)}, s32[2]{0:T(128)S(1)}, u32[]{:S(2)}) copy-start(s32[2]{0:T(128)S(1)} %pad_add_fusion.1.place_ref) | copy-start | bytes 28
  30.2 19.5 %collective-permute-start.4 = (bf16[4,80,1024]{2,1,0:T(8,128)(2,1)S(1)}, bf16[4,80,1024]{2,1,0:T(8,128)(2,1)S(1)}, u32[]{:S(2)}, u32[]{:S(2)}) collective-permute-start(bf16[4,80,1024]{2,1,0:T(8,128)(2,1)S(1)} %pad_maximum_fusion.exit_near_ref), channel_id=1, source_target_pairs={{0,4},{4,0},{8,12},{12,8},{16,20},{20,16},{24,28},{28,24},{1,5},{5... | collective-permute-start | bytes 1966088 | tf_op jit(solution)/shard_map/ppermute | solution.py:817
  31.5 7.0 %collective-permute-start.7 = (bf16[136,512]{1,0:T(8,128)(2,1)S(1)}, bf16[136,512]{1,0:T(8,128)(2,1)S(1)}, u32[]{:S(2)}, u32[]{:S(2)}) collective-permute-start(bf16[136,512]{1,0:T(8,128)(2,1)S(1)} %pad_maximum_fusion.6), channel_id=1, source_target_pairs={{0,24},{4,28},{8,16},{12,20},{16,8},{20,12},{24,0},{28,4},{1,25},{... | collective-permute-start | bytes 417800 | tf_op jit(solution)/shard_map/ppermute | solution.py:817
  33.9 15.8 %collective-permute-start.9 = (bf16[4,64,1024]{2,1,0:T(8,128)(2,1)S(1)}, bf16[4,64,1024]{2,1,0:T(8,128)(2,1)}, u32[]{:S(2)}, u32[]{:S(2)}) collective-permute-start(bf16[4,64,1024]{2,1,0:T(8,128)(2,1)S(1)} %collective-permute-done.slab2_ref), channel_id=1, source_target_pairs={{0,1},{1,0},{2,3},{3,2},{4,5},{5,4},{6,7},{7,6},{8,9},{9,8},{10,11... | collective-permute-start | bytes 1572872 | tf_op jit(solution)/shard_map/ppermute | solution.py:817
  34.0 15.8 %collective-permute-start.8 = (bf16[4,64,1024]{2,1,0:T(8,128)(2,1)S(1)}, bf16[4,64,1024]{2,1,0:T(8,128)(2,1)}, u32[]{:S(2)}, u32[]{:S(2)}) collective-permute-start(bf16[4,64,1024]{2,1,0:T(8,128)(2,1)S(1)} %copy-done), channel_id=1, source_target_pairs={{0,1},{1,0},{2,3},{3,2},{4,5},{5,4},{6,7},{7,6},{8,9},{9,8},{10,11... | collective-permute-start | bytes 1572872 | tf_op jit(solution)/shard_map/ppermute | solution.py:817
  34.5 12.2 %collective-permute-start.6 = (bf16[136,512]{1,0:T(8,128)(2,1)S(1)}, bf16[136,512]{1,0:T(8,128)(2,1)S(1)}, u32[]{:S(2)}, u32[]{:S(2)}) collective-permute-start(bf16[136,512]{1,0:T(8,128)(2,1)S(1)} %pad_maximum_fusion.6), channel_id=1, source_target_pairs={{0,16},{4,20},{8,24},{12,28},{16,0},{20,4},{24,8},{28,12},{1,17},{... | collective-permute-start | bytes 417800 | tf_op jit(solution)/shard_map/ppermute | solution.py:817
  38.5 11.2 %collective-permute-start.5 = (bf16[136,512]{1,0:T(8,128)(2,1)S(1)}, bf16[136,512]{1,0:T(8,128)(2,1)}, u32[]{:S(2)}, u32[]{:S(2)}) collective-permute-start(bf16[136,512]{1,0:T(8,128)(2,1)S(1)} %pad_maximum_fusion.6), channel_id=1, source_target_pairs={{0,8},{4,12},{8,0},{12,4},{16,24},{20,28},{24,16},{28,20},{1,9},{5... | collective-permute-start | bytes 417800 | tf_op jit(solution)/shard_map/ppermute | solution.py:817
  45.4 46.1 %copy-start.2 = (f32[4,4,64,4]{3,0,1,2:T(4,128)}, f32[4,4,64,4]{3,0,1,2:T(4,128)S(1)}, u32[]{:S(2)}) copy-start(f32[4,4,64,4]{3,0,1,2:T(4,128)S(1)} %copy.38) | copy-start | bytes 49156
  52.9 10.0 %collective-permute-start.20 = (bf16[128,512]{1,0:T(8,128)(2,1)}, bf16[128,512]{1,0:T(8,128)(2,1)}, u32[]{:S(2)}, u32[]{:S(2)}) collective-permute-start(bf16[128,512]{1,0:T(8,128)(2,1)} %bitcast.108), channel_id=1, source_target_pairs={{0,24},{4,28},{8,16},{12,20},{16,8},{20,12},{24,0},{28,4},{1,25},{... | collective-permute-start | bytes 393224 | tf_op jit(solution)/shard_map/ppermute | solution.py:817
  55.5 11.3 %collective-permute-start.19 = (bf16[128,512]{1,0:T(8,128)(2,1)}, bf16[128,512]{1,0:T(8,128)(2,1)}, u32[]{:S(2)}, u32[]{:S(2)}) collective-permute-start(bf16[128,512]{1,0:T(8,128)(2,1)} %bitcast.109), channel_id=1, source_target_pairs={{0,16},{4,20},{8,24},{12,28},{16,0},{20,4},{24,8},{28,12},{1,17},{... | collective-permute-start | bytes 393224 | tf_op jit(solution)/shard_map/ppermute | solution.py:817
  55.5 11.4 %collective-permute-start.18 = (bf16[128,512]{1,0:T(8,128)(2,1)}, bf16[128,512]{1,0:T(8,128)(2,1)}, u32[]{:S(2)}, u32[]{:S(2)}) collective-permute-start(bf16[128,512]{1,0:T(8,128)(2,1)} %bitcast.110), channel_id=1, source_target_pairs={{0,8},{4,12},{8,0},{12,4},{16,24},{20,28},{24,16},{28,20},{1,9},{5... | collective-permute-start | bytes 393224 | tf_op jit(solution)/shard_map/ppermute | solution.py:817
  57.3 14.7 %collective-permute-start.11 = (bf16[4,136,512]{2,1,0:T(8,128)(2,1)S(1)}, bf16[4,136,512]{2,1,0:T(8,128)(2,1)}, u32[]{:S(2)}, u32[]{:S(2)}) collective-permute-start(bf16[4,136,512]{2,1,0:T(8,128)(2,1)S(1)} %pad_maximum_fusion.1.near_ref), channel_id=1, source_target_pairs={{0,4},{4,0},{8,12},{12,8},{16,20},{20,16},{24,28},{28,24},{1,5},{5... | collective-permute-start | bytes 1671176 | tf_op jit(solution)/shard_map/ppermute | solution.py:817
  58.7 13.3 %collective-permute-start.16 = (bf16[4,64,1024]{2,1,0:T(8,128)(2,1)}, bf16[4,64,1024]{2,1,0:T(8,128)(2,1)}, u32[]{:S(2)}, u32[]{:S(2)}) collective-permute-start(bf16[4,64,1024]{2,1,0:T(8,128)(2,1)} %cotangent_ref), channel_id=1, source_target_pairs={{0,2},{1,3},{2,0},{3,1},{4,6},{5,7},{6,4},{7,5},{8,10},{9,11},{10,... | collective-permute-start | bytes 1572872 | tf_op jit(solution)/shard_map/ppermute | solution.py:817
  62.8 109.0 %copy-start.8 = (bf16[192,512]{1,0:T(8,128)(2,1)}, bf16[192,512]{1,0:T(8,128)(2,1)S(1)}, u32[]{:S(2)}) copy-start(bf16[192,512]{1,0:T(8,128)(2,1)S(1)} %copy.41.small_ref) | copy-start | bytes 589828
  62.9 10.0 %collective-permute-start.10 = (bf16[12,1024]{1,0:T(8,128)(2,1)S(1)}, bf16[12,1024]{1,0:T(8,128)(2,1)S(1)}, u32[]{:S(2)}, u32[]{:S(2)}) collective-permute-start(bf16[12,1024]{1,0:T(8,128)(2,1)S(1)} %reshape.120), channel_id=1, source_target_pairs={{0,4},{4,8},{8,12},{12,16},{16,20},{20,24},{24,28},{1,5},{5,9},{9,... | collective-permute-start | bytes 73736 | tf_op jit(solution)/shard_map/ppermute | solution.py:877
  66.8 18.1 %collective-permute-start.15 = (bf16[4,64,1024]{2,1,0:T(8,128)(2,1)}, bf16[4,64,1024]{2,1,0:T(8,128)(2,1)S(1)}, u32[]{:S(2)}, u32[]{:S(2)}) collective-permute-start(bf16[4,64,1024]{2,1,0:T(8,128)(2,1)} %cotangent_ref), channel_id=1, source_target_pairs={{0,1},{1,0},{2,3},{3,2},{4,5},{5,4},{6,7},{7,6},{8,9},{9,8},{10,11... | collective-permute-start | bytes 1572872 | tf_op jit(solution)/shard_map/ppermute | solution.py:817
  68.1 16.8 %collective-permute-start.21 = (bf16[4,128,512]{2,1,0:T(8,128)(2,1)S(1)}, bf16[4,128,512]{2,1,0:T(8,128)(2,1)S(1)}, u32[]{:S(2)}, u32[]{:S(2)}) collective-permute-start(bf16[4,128,512]{2,1,0:T(8,128)(2,1)S(1)} %pad_maximum_fusion.2.near_ref.gate_near_ref), channel_id=1, source_target_pairs={{0,4},{4,0},{8,12},{12,8},{16,20},{20,16},{24,28},{28,24},{1,5},{5... | collective-permute-start | bytes 1572872 | tf_op jit(solution)/shard_map/ppermute | solution.py:817
  72.0 12.9 %collective-permute-start.17 = (bf16[4,64,1024]{2,1,0:T(8,128)(2,1)}, bf16[4,64,1024]{2,1,0:T(8,128)(2,1)S(1)}, u32[]{:S(2)}, u32[]{:S(2)}) collective-permute-start(bf16[4,64,1024]{2,1,0:T(8,128)(2,1)} %collective-permute-done.16.slab2_ref), channel_id=1, source_target_pairs={{0,1},{1,0},{2,3},{3,2},{4,5},{5,4},{6,7},{7,6},{8,9},{9,8},{10,11... | collective-permute-start | bytes 1572872 | tf_op jit(solution)/shard_map/ppermute | solution.py:817
  82.6 51.4 %copy-start.17 = (f32[1024,512]{1,0:T(8,128)}, f32[1024,512]{1,0:T(8,128)S(1)}, u32[]{:S(2)}) copy-start(f32[1024,512]{1,0:T(8,128)S(1)} %get-tuple-element.125.filter_ref) | copy-start | bytes 6291460
  82.6 72.9 %copy-start.21 = (bf16[1024,1024]{1,0:T(8,128)(2,1)}, bf16[1024,1024]{1,0:T(8,128)(2,1)S(1)}, u32[]{:S(2)}) copy-start(bf16[1024,1024]{1,0:T(8,128)(2,1)S(1)} %get-tuple-element.129.normed_ref) | copy-start | bytes 6291460
  82.6 1.6 collective-permute-start.13
  84.2 7.3 %collective-permute-start.14 = (bf16[96,1024]{1,0:T(8,128)(2,1)S(1)}, bf16[96,1024]{1,0:T(8,128)(2,1)S(1)}, u32[]{:S(2)}, u32[]{:S(2)}) collective-permute-start(bf16[96,1024]{1,0:T(8,128)(2,1)S(1)} %add_convert_fusion.3.chosen_ref), channel_id=1, source_target_pairs={{0,2},{1,3},{2,0},{3,1},{4,6},{5,7},{6,4},{7,5},{8,10},{9,11},{10,... | collective-permute-start | bytes 589832 | tf_op jit(solution)/shard_map/ppermute | solution.py:817
  91.5 42.5 %copy-start.18 = (f32[1024,512]{1,0:T(8,128)}, f32[1024,512]{1,0:T(8,128)S(1)}, u32[]{:S(2)}) copy-start(f32[1024,512]{1,0:T(8,128)S(1)} %get-tuple-element.145) | copy-start | bytes 6291460
  112.4 43.1 %copy-start.30 = (f32[64,16,512]{2,1,0:T(8,128)}, f32[64,16,512]{2,1,0:T(8,128)S(1)}, u32[]{:S(2)}) copy-start(f32[64,16,512]{2,1,0:T(8,128)S(1)} %get-tuple-element.134.step_ref) | copy-start | bytes 6291460
  112.4 43.1 %copy-start.33 = (f32[64,16,128]{2,1,0:T(8,128)}, f32[64,16,128]{2,1,0:T(8,128)S(1)}, u32[]{:S(2)}) copy-start(f32[64,16,128]{2,1,0:T(8,128)S(1)} %get-tuple-element.133.gates_ref) | copy-start | bytes 1572868
  165.5 40.5 %collective-permute-start.23 = (bf16[2,4,64,1024]{3,2,1,0:T(8,128)(2,1)}, bf16[2,4,64,1024]{3,2,1,0:T(8,128)(2,1)}, u32[]{:S(2)}, u32[]{:S(2)}) collective-permute-start(bf16[2,4,64,1024]{3,2,1,0:T(8,128)(2,1)} %get-tuple-element.144), channel_id=1, source_target_pairs={{0,1},{1,0},{2,3},{3,2},{4,5},{5,4},{6,7},{7,6},{8,9},{9,8},{10,11... | collective-permute-start | bytes 3145736 | tf_op jit(solution)/shard_map/ppermute | solution.py:817
  165.5 40.5 %all-to-all-start.2 = ((bf16[8,64,1024]{2,1,0:T(8,128)(2,1)}), bf16[8,64,1024]{2,1,0:T(8,128)(2,1)}, u32[]{:S(2)}, u32[]{:S(2)}) async-start(bf16[8,64,1024]{2,1,0:T(8,128)(2,1)} %bitcast.40), calls=%async_computation.2 | async-start | bytes 2097152 | tf_op jit(solution)/shard_map/all_to_all | solution.py:1002
  169.9 36.0 %collective-permute-start.22 = (bf16[4,128,512]{2,1,0:T(8,128)(2,1)}, bf16[4,128,512]{2,1,0:T(8,128)(2,1)}, u32[]{:S(2)}, u32[]{:S(2)}) collective-permute-start(bf16[4,128,512]{2,1,0:T(8,128)(2,1)} %get-tuple-element.151), channel_id=1, source_target_pairs={{0,4},{4,0},{8,12},{12,8},{16,20},{20,16},{24,28},{28,24},{1,5},{5... | collective-permute-start | bytes 1572872 | tf_op jit(solution)/shard_map/ppermute | solution.py:817
  206.0 1.5 collective-permute-start.24
  207.6 7.0 %collective-permute-start.25 = (bf16[96,1024]{1,0:T(8,128)(2,1)S(1)}, bf16[96,1024]{1,0:T(8,128)(2,1)S(1)}, u32[]{:S(2)}, u32[]{:S(2)}) collective-permute-start(bf16[96,1024]{1,0:T(8,128)(2,1)S(1)} %add_convert_fusion.2.chosen_ref), channel_id=1, source_target_pairs={{0,2},{1,3},{2,0},{3,1},{4,6},{5,7},{6,4},{7,5},{8,10},{9,11},{10,... | collective-permute-start | bytes 589832 | tf_op jit(solution)/shard_map/ppermute | solution.py:817
  213.2 24.3 %collective-permute-start.27 = (bf16[4,64,1024]{2,1,0:T(8,128)(2,1)}, bf16[4,64,1024]{2,1,0:T(8,128)(2,1)}, u32[]{:S(2)}, u32[]{:S(2)}) collective-permute-start(bf16[4,64,1024]{2,1,0:T(8,128)(2,1)} %fusion.2), channel_id=1, source_target_pairs={{0,2},{1,3},{2,0},{3,1},{4,6},{5,7},{6,4},{7,5},{8,10},{9,11},{10,... | collective-permute-start | bytes 1572872 | tf_op jit(solution)/shard_map/ppermute | solution.py:817
  224.9 6.6 %collective-permute-start.26 = (f32[3,4,512]{2,1,0:T(4,128)}, f32[3,4,512]{2,1,0:T(4,128)S(1)}, u32[]{:S(2)}, u32[]{:S(2)}) collective-permute-start(f32[3,4,512]{2,1,0:T(4,128)} %get-tuple-element.167), channel_id=1, source_target_pairs={{4,0},{8,4},{12,8},{16,12},{20,16},{24,20},{28,24},{5,1},{9,5},{13... | collective-permute-start | bytes 73736 | tf_op jit(solution)/shard_map/ppermute | solution.py:1068
  226.4 19.2 %collective-permute-start.28 = (bf16[176,512]{1,0:T(8,128)(2,1)}, bf16[176,512]{1,0:T(8,128)(2,1)S(1)}, u32[]{:S(2)}, u32[]{:S(2)}) collective-permute-start(bf16[176,512]{1,0:T(8,128)(2,1)} %get-tuple-element.177), channel_id=1, source_target_pairs={{0,8},{4,12},{8,0},{12,4},{16,24},{20,28},{24,16},{28,20},{1,9},{5... | collective-permute-start | bytes 540680 | tf_op jit(solution)/shard_map/ppermute | solution.py:817
  228.7 16.9 %collective-permute-start.29 = (bf16[176,512]{1,0:T(8,128)(2,1)}, bf16[176,512]{1,0:T(8,128)(2,1)S(1)}, u32[]{:S(2)}, u32[]{:S(2)}) collective-permute-start(bf16[176,512]{1,0:T(8,128)(2,1)} %get-tuple-element.178), channel_id=1, source_target_pairs={{0,16},{4,20},{8,24},{12,28},{16,0},{20,4},{24,8},{28,12},{1,17},{... | collective-permute-start | bytes 540680 | tf_op jit(solution)/shard_map/ppermute | solution.py:817
  231.4 14.2 %collective-permute-start.30 = (bf16[176,512]{1,0:T(8,128)(2,1)}, bf16[176,512]{1,0:T(8,128)(2,1)S(1)}, u32[]{:S(2)}, u32[]{:S(2)}) collective-permute-start(bf16[176,512]{1,0:T(8,128)(2,1)} %get-tuple-element.179), channel_id=1, source_target_pairs={{0,24},{4,28},{8,16},{12,20},{16,8},{20,12},{24,0},{28,4},{1,25},{... | collective-permute-start | bytes 540680 | tf_op jit(solution)/shard_map/ppermute | solution.py:817
  245.6 6.1 %collective-permute-start.31 = (bf16[2,4,64,1024]{3,2,1,0:T(8,128)(2,1)}, bf16[2,4,64,1024]{3,2,1,0:T(8,128)(2,1)}, u32[]{:S(2)}, u32[]{:S(2)}) collective-permute-start(bf16[2,4,64,1024]{3,2,1,0:T(8,128)(2,1)} %get-tuple-element.180), channel_id=1, source_target_pairs={{0,1},{1,0},{2,3},{3,2},{4,5},{5,4},{6,7},{7,6},{8,9},{9,8},{10,11... | collective-permute-start | bytes 3145736 | tf_op jit(solution)/shard_map/ppermute | solution.py:817
  245.7 33.6 %all-to-all-start.3 = ((bf16[32,32,512]{2,1,0:T(8,128)(2,1)}), bf16[32,32,512]{2,1,0:T(8,128)(2,1)S(1)}, u32[]{:S(2)}, u32[]{:S(2)}) async-start(bf16[32,32,512]{2,1,0:T(8,128)(2,1)} %bitcast.46), calls=%async_computation.3 | async-start | bytes 2097152 | tf_op jit(solution)/shard_map/all_to_all | solution.py:1079
  255.6 6.6 %collective-permute-start.32 = (bf16[32,512]{1,0:T(8,128)(2,1)S(1)}, bf16[32,512]{1,0:T(8,128)(2,1)S(1)}, u32[]{:S(2)}, u32[]{:S(2)}) collective-permute-start(bf16[32,512]{1,0:T(8,128)(2,1)S(1)} %get-tuple-element.185), channel_id=1, source_target_pairs={{0,3},{1,2},{2,1},{3,0},{4,7},{5,6},{6,5},{7,4},{8,11},{9,10},{10,... | collective-permute-start | bytes 98312 | tf_op jit(solution)/shard_map/ppermute | solution.py:817
  257.2 24.4 %collective-permute-start.33 = (bf16[4,64,1024]{2,1,0:T(8,128)(2,1)}, bf16[4,64,1024]{2,1,0:T(8,128)(2,1)}, u32[]{:S(2)}, u32[]{:S(2)}) collective-permute-start(bf16[4,64,1024]{2,1,0:T(8,128)(2,1)} %fusion.3), channel_id=1, source_target_pairs={{0,2},{1,3},{2,0},{3,1},{4,6},{5,7},{6,4},{7,5},{8,10},{9,11},{10,... | collective-permute-start | bytes 1572872 | tf_op jit(solution)/shard_map/ppermute | solution.py:817
  257.5 14.4 %collective-permute-start.34 = (bf16[32,512]{1,0:T(8,128)(2,1)S(1)}, bf16[32,512]{1,0:T(8,128)(2,1)S(1)}, u32[]{:S(2)}, u32[]{:S(2)}) collective-permute-start(bf16[32,512]{1,0:T(8,128)(2,1)S(1)} %get-tuple-element.190), channel_id=1, source_target_pairs={{0,1},{1,0},{2,3},{3,2},{4,5},{5,4},{6,7},{7,6},{8,9},{9,8},{10,11... | collective-permute-start | bytes 98312 | tf_op jit(solution)/shard_map/ppermute | solution.py:817
  257.6 21.8 %collective-permute-start.35 = (bf16[32,512]{1,0:T(8,128)(2,1)S(1)}, bf16[32,512]{1,0:T(8,128)(2,1)S(1)}, u32[]{:S(2)}, u32[]{:S(2)}) collective-permute-start(bf16[32,512]{1,0:T(8,128)(2,1)S(1)} %get-tuple-element.191), channel_id=1, source_target_pairs={{0,2},{1,3},{2,0},{3,1},{4,6},{5,7},{6,4},{7,5},{8,10},{9,11},{10,... | collective-permute-start | bytes 98312 | tf_op jit(solution)/shard_map/ppermute | solution.py:817
  262.1 6.6 %collective-permute-start.36 = (f32[192,128]{1,0:T(8,128)S(1)}, f32[192,128]{1,0:T(8,128)S(1)}, u32[]{:S(2)}, u32[]{:S(2)}) collective-permute-start(f32[192,128]{1,0:T(8,128)S(1)} %get-tuple-element.196), channel_id=1, source_target_pairs={{0,4},{4,0},{8,12},{12,8},{16,20},{20,16},{24,28},{28,24},{1,5},{5... | collective-permute-start | bytes 294920 | tf_op jit(solution)/shard_map/ppermute | solution.py:817
  (41 other events, 262.5 us)

commit v7 on v6

--- a/solution.py
+++ b/solution.py
@@ -249,7 +249,7 @@
     end_ref[...] = jnp.zeros_like(end_ref)
     give_ref[...] = jnp.zeros_like(give_ref)
     keep_ref[...] = jnp.ones_like(keep_ref)
-    span = 4
+    span = 8
     lanes = lane_slices(width)
     spots = [(j, i) for j in range(span) for i in range(len(lanes))]
 

time: 286 us -> 285 us (level)
  no operation moved by 1% of the time
where the time goes in v7:
time: 285 us; the launch traced here: 283 us
  Pallas kernels  119 us (42%)
  starting transfers between devices  63.9 us (22%)
  waiting for transfers between devices  32.5 us (11%)
  local copies, waits for them, and re-layouts  28 us (10%)
  blocking collectives  21.6 us (8%)
  other arithmetic  16.6 us (6%)
    pallas_call x12, Pallas kernels, kernel_call(): pl.pallas_call(body, out_shape=[jax.ShapeDtypeStruct(shape, kind) for sha...  119 us
    ppermute x34, starting transfers between devices, flipped(): lax.ppermute(value, axis, [(i, i ^ bits) for i in range(lax.axis_size(axi...  41.2 us
    ppermute x34, waiting for transfers between devices, flipped(): lax.ppermute(value, axis, [(i, i ^ bits) for i in range(lax.axis_size(axi...  32 us
    all_to_all x1, blocking collectives, local(): came = lax.all_to_all(loads, 'blk', split_axis=0, concat_axis=0, tiled=True)  21.6 us
    unnamed x104, local copies, waits for them, and re-layouts  16 us
    all_to_all x1, starting transfers between devices, local(): lax.all_to_all(inner_entry.reshape(pieces * groups, slice_rows, group_wid...  6.01 us
  transfers between devices with their start and end apart: 40, of which 12 were waited for; matrix products, arithmetic and copies ran while one was open for 10% of the time, Pallas kernels for 24%

profile of v7, /device:TPU:0, one launch (start us, length us, event | category | flops | bytes accessed | tf_op | source)
XLA Modules:
  0.0 283.2 jit_solution(12642670951616439459)
XLA Ops:
  0.7 3.0 %collective-permute-start = (bf16[4,64,1024]{2,1,0:T(8,128)(2,1)}, bf16[4,64,1024]{2,1,0:T(8,128)(2,1)S(1)}, u32[]{:S(2)}, u32[]{:S(2)}) collective-permute-start(bf16[4,64,1024]{2,1,0:T(8,128)(2,1)} %tokens_ref), channel_id=1, source_target_pairs={{0,2},{1,3},{2,0},{3,1},{4,6},{5,7},{6,4},{7,5},{8,10},{9,11},{10,... | collective-permute-start | bytes 1572872 | tf_op jit(solution)/shard_map/ppermute | solution.py:817
  9.0 1.5 reshape.112
  11.7 3.6 %collective-permute-start.3 = (bf16[80,1024]{1,0:T(8,128)(2,1)S(1)}, bf16[80,1024]{1,0:T(8,128)(2,1)S(1)}, u32[]{:S(2)}, u32[]{:S(2)}) collective-permute-start(bf16[80,1024]{1,0:T(8,128)(2,1)S(1)} %pad_maximum_fusion.5), channel_id=1, source_target_pairs={{0,24},{4,28},{8,16},{12,20},{16,8},{20,12},{24,0},{28,4},{1,25},{... | collective-permute-start | bytes 491528 | tf_op jit(solution)/shard_map/ppermute | solution.py:817
  16.1 3.4 %collective-permute-start.12 = (s32[4,3]{1,0:T(4,128)S(1)}, s32[4,3]{1,0:T(4,128)S(1)}, u32[]{:S(2)}, u32[]{:S(2)}) collective-permute-start(s32[4,3]{1,0:T(4,128)S(1)} %slice.106), channel_id=1, source_target_pairs={{0,4},{4,8},{8,12},{12,16},{16,20},{20,24},{24,28},{1,5},{5,9},{9,... | collective-permute-start | bytes 152 | tf_op jit(solution)/shard_map/ppermute | solution.py:882
  19.5 3.5 %all-to-all-start = ((bf16[4,72,512]{2,1,0:T(8,128)(2,1)}), bf16[4,72,512]{2,1,0:T(8,128)(2,1)S(1)}, u32[]{:S(2)}, u32[]{:S(2)}) async-start(bf16[4,72,512]{2,1,0:T(8,128)(2,1)} %pad_maximum_fusion.3), calls=%async_computation | async-start | bytes 589824 | tf_op jit(solution)/shard_map/all_to_all | solution.py:847
  23.1 5.7 %collective-permute-done.2 = bf16[80,1024]{1,0:T(8,128)(2,1)S(1)} collective-permute-done((bf16[80,1024]{1,0:T(8,128)(2,1)S(1)}, bf16[80,1024]{1,0:T(8,128)(2,1)S(1)}, u32[]{:S(2)}, u32[]{:S(2)}) %collective-permute-start.2) | collective-permute-done | bytes 163872 | tf_op jit(solution)/shard_map/ppermute | solution.py:817
  30.2 1.3 collective-permute-start.4
  31.5 2.5 collective-permute-start.7
  35.1 3.4 %collective-permute-done.7 = bf16[136,512]{1,0:T(8,128)(2,1)S(1)} collective-permute-done((bf16[136,512]{1,0:T(8,128)(2,1)S(1)}, bf16[136,512]{1,0:T(8,128)(2,1)S(1)}, u32[]{:S(2)}, u32[]{:S(2)}) %collective-permute-start.7) | collective-permute-done | bytes 139296 | tf_op jit(solution)/shard_map/ppermute | solution.py:817
  38.5 6.5 %collective-permute-start.5 = (bf16[136,512]{1,0:T(8,128)(2,1)S(1)}, bf16[136,512]{1,0:T(8,128)(2,1)}, u32[]{:S(2)}, u32[]{:S(2)}) collective-permute-start(bf16[136,512]{1,0:T(8,128)(2,1)S(1)} %pad_maximum_fusion.6), channel_id=1, source_target_pairs={{0,8},{4,12},{8,0},{12,4},{16,24},{20,28},{24,16},{28,20},{1,9},{5... | collective-permute-start | bytes 417800 | tf_op jit(solution)/shard_map/ppermute | solution.py:817
  45.4 1.3 collective-permute-done.6
  46.7 3.0 %collective-permute-done.5 = bf16[136,512]{1,0:T(8,128)(2,1)} collective-permute-done((bf16[136,512]{1,0:T(8,128)(2,1)S(1)}, bf16[136,512]{1,0:T(8,128)(2,1)}, u32[]{:S(2)}, u32[]{:S(2)}) %collective-permute-start.5) | collective-permute-done | bytes 139296 | tf_op jit(solution)/shard_map/ppermute | solution.py:817
  52.9 2.6 collective-permute-start.20
  55.5 1.8 collective-permute-start.18
  62.9 3.9 %collective-permute-start.10 = (bf16[12,1024]{1,0:T(8,128)(2,1)S(1)}, bf16[12,1024]{1,0:T(8,128)(2,1)S(1)}, u32[]{:S(2)}, u32[]{:S(2)}) collective-permute-start(bf16[12,1024]{1,0:T(8,128)(2,1)S(1)} %reshape.120), channel_id=1, source_target_pairs={{0,4},{4,8},{8,12},{12,16},{16,20},{20,24},{24,28},{1,5},{5,9},{9,... | collective-permute-start | bytes 73736 | tf_op jit(solution)/shard_map/ppermute | solution.py:877
  68.8 3.2 %collective-permute-done.16.slab2_ref = bf16[4,64,1024]{2,1,0:T(8,128)(2,1)} collective-permute-done((bf16[4,64,1024]{2,1,0:T(8,128)(2,1)}, bf16[4,64,1024]{2,1,0:T(8,128)(2,1)}, u32[]{:S(2)}, u32[]{:S(2)}) %collective-permute-start.16) | collective-permute-done | bytes 524320 | tf_op jit(solution)/shard_map/ppermute | solution.py:817
  72.9 8.7 %shard_map.220 = (bf16[1024,1024]{1,0:T(8,128)(2,1)S(1)}, bf16[1072,512]{1,0:T(8,128)(2,1)S(1)}, f32[1024,512]{1,0:T(8,128)S(1)}, bf16[96,1024]{1,0:T(8,128)(2,1)S(1)}) custom-call(s32[2]{0:T(128)S(1)} %pad_add_fusion.1.place_ref, bf16[4,64,1024]{2,1,0:T(8,128)(2,1)S(1)} %copy-done, bf16[4,64,1024]{2,1,0:T(8,128)(2,1)} %collective-permute-done.8.slab1_ref, ...), custom_call_target="tpu_custom_call" | custom-call | flops 10350000128 | bytes 8000000 | tf_op jit(solution)/shard_map/pallas_call | solution.py:59
  85.0 6.5 %shard_map.221 = (bf16[1024,1024]{1,0:T(8,128)(2,1)S(1)}, f32[1024,512]{1,0:T(8,128)S(1)}, f32[1024,512]{1,0:T(8,128)S(1)}, f32[1024,512]{1,0:T(8,128)S(1)}) custom-call(s32[2]{0:T(128)S(1)} %pad_add_fusion.1.place_ref, bf16[4,64,1024]{2,1,0:T(8,128)(2,1)S(1)} %copy-done.13, bf16[4,64,1024]{2,1,0:T(8,128)(2,1)S(1)} %collective-permute-done.15.slab1_ref, ...), custom_call_target="tpu_custom_call" | custom-call | flops 9200000000 | bytes 8000000 | tf_op jit(solution)/shard_map/pallas_call | solution.py:59
  91.5 18.3 %shard_map.222 = (f32[64,16,128]{2,1,0:T(8,128)S(1)}, f32[64,16,512]{2,1,0:T(8,128)S(1)}, f32[64,16,512]{2,1,0:T(8,128)S(1)}, f32[16,16,512]{2,1,0:T(8,128)S(1)}...) custom-call(s32[2]{0:T(128)S(1)} %pad_add_fusion.1.place_ref, ...), custom_call_target="tpu_custom_call" | custom-call | flops 26449999872 | bytes 8000000 | tf_op jit(solution)/shard_map/pallas_call | solution.py:59
  109.9 1.3 copy-done.32
  111.2 21.6 %all_to_all.20.came_ref = bf16[8,72,512]{2,1,0:T(8,128)(2,1)S(1)} all-to-all(bf16[8,72,512]{2,1,0:T(8,128)(2,1)S(1)} %get-tuple-element.132), channel_id=1, replica_groups=mesh['blk'=8,'grp'=4] {'blk'}, dimensions={0} | all-to-all | bytes 1179648 | tf_op jit(solution)/shard_map/all_to_all | solution.py:964
  132.8 21.5 %shard_map.223 = (f32[64,16,512]{2,1,0:T(8,128)S(1)}, f32[64,16,128]{2,1,0:T(8,128)S(1)}, f32[16,16,16,512]{3,2,1,0:T(8,128)}, f32[16,16,512]{2,1,0:T(8,128)S(1)}) custom-call(s32[2]{0:T(128)S(1)} %pad_add_fusion.1.place_ref, bf16[8,72,512]{2,1,0:T(8,128)(2,1)S(1)} %all_to_all.20.came_ref, f32[64,16,128]{2,1,0:T(8,128)S(1)} %get-tuple-element.133.gates_ref, ...), custom_call_target="tpu_custom_call" | custom-call | flops 20700000256 | bytes 8000000 | tf_op jit(solution)/shard_map/pallas_call | solution.py:59
  154.3 8.1 %shard_map.224 = (bf16[1024,512]{1,0:T(8,128)(2,1)S(1)}, bf16[2,4,64,1024]{3,2,1,0:T(8,128)(2,1)S(1)}, bf16[2,4,64,1024]{3,2,1,0:T(8,128)(2,1)}, bf16[512,1024]{...) custom-call(s32[2]{0:T(128)S(1)} %pad_add_fusion.1.place_ref, ...), custom_call_target="tpu_custom_call" | custom-call | flops 13799999488 | bytes 8000000 | tf_op jit(solution)/shard_map/pallas_call | solution.py:59
  164.3 4.4 %all-to-all-start.2 = ((bf16[8,64,1024]{2,1,0:T(8,128)(2,1)}), bf16[8,64,1024]{2,1,0:T(8,128)(2,1)}, u32[]{:S(2)}, u32[]{:S(2)}) async-start(bf16[8,64,1024]{2,1,0:T(8,128)(2,1)} %bitcast.40), calls=%async_computation.2 | async-start | bytes 2097152 | tf_op jit(solution)/shard_map/all_to_all | solution.py:1002
  168.7 1.9 collective-permute-start.22
  172.7 32.0 %shard_map.225 = (f32[64,16,512]{2,1,0:T(8,128)}, f32[64,512]{1,0:T(8,128)S(1)}, bf16[96,1024]{1,0:T(8,128)(2,1)S(1)}, f32[16,512]{1,0:T(8,128)S(1)}, f32[1,512]{1,0:T(1,128)S(1)}, /*index=5*/f32[1,512]{1,0:T(1,128)S(1)}) custom-call(f32[64,16,128]{2,1,0:T(8,128)S(1)} %copy-done.34, bf16[192,512]{1,0:T(8,128)(2,1)S(1)} %copy.41.small_ref, ...), custom_call_target="tpu_custom_call" | custom-call | flops 40249999360 | bytes 8000000 | tf_op jit(solution)/shard_map/pallas_call | solution.py:59
  204.8 1.4 collective-permute-done.24
  206.3 1.4 collective-permute-start.25
  207.8 2.0 fusion.2
  209.8 2.1 convert_reduce_fusion
  214.0 9.6 %shard_map.226 = (bf16[1024,512]{1,0:T(8,128)(2,1)}, f32[3,16,512]{2,1,0:T(8,128)}, f32[3,4,512]{2,1,0:T(4,128)}, f32[192,512]{1,0:T(8,128)}, f32[176,512]{1,0:T...) custom-call(s32[2]{0:T(128)} %copy-done.19, bf16[96,1024]{1,0:T(8,128)(2,1)} %copy-done.42, ...), custom_call_target="tpu_custom_call" | custom-call | flops 6899999744 | bytes 8000000 | tf_op jit(solution)/shard_map/pallas_call | solution.py:59
  223.6 1.5 collective-permute-start.26
  225.1 2.4 collective-permute-start.28
  227.5 2.7 collective-permute-start.29
  230.2 1.6 copy-done.22
  234.0 2.3 shard_map.227
  236.2 7.2 %shard_map.228 = (bf16[2,4,64,1024]{3,2,1,0:T(8,128)(2,1)S(1)}, bf16[2,4,64,1024]{3,2,1,0:T(8,128)(2,1)}) custom-call(s32[2]{0:T(128)S(1)} %copy-done.20, bf16[1024,512]{1,0:T(8,128)(2,1)S(1)} %get-tuple-element.173.inner_ref, bf16[1024,512]{1,0:T(8,128)(2,1)S(1)} %copy-done.28, bf16[4,136,512]{2,1,0:T(8,128)(2,1)S(1)} %pad_maximum_fusion.1.near_ref, ...), custom_call_target="tpu_custom_call" | custom-call | flops 11500000256 | bytes 8000000 | tf_op jit(solution)/shard_map/pallas_call | solution.py:59
  244.5 6.0 %all-to-all-start.3 = ((bf16[32,32,512]{2,1,0:T(8,128)(2,1)}), bf16[32,32,512]{2,1,0:T(8,128)(2,1)S(1)}, u32[]{:S(2)}, u32[]{:S(2)}) async-start(bf16[32,32,512]{2,1,0:T(8,128)(2,1)} %bitcast.46), calls=%async_computation.3 | async-start | bytes 2097152 | tf_op jit(solution)/shard_map/all_to_all | solution.py:1079
  250.5 2.2 fusion.3
  254.4 1.6 collective-permute-start.32
  256.3 1.7 collective-permute-start.35
  258.1 2.8 %collective-permute-done.32.gate3_ref = bf16[32,512]{1,0:T(8,128)(2,1)S(1)} collective-permute-done((bf16[32,512]{1,0:T(8,128)(2,1)S(1)}, bf16[32,512]{1,0:T(8,128)(2,1)S(1)}, u32[]{:S(2)}, u32[]{:S(2)}) %collective-permute-start.32) | collective-permute-done | bytes 32800 | tf_op jit(solution)/shard_map/ppermute | solution.py:817
  260.9 2.4 collective-permute-start.36
  263.3 2.4 fusion.1
  265.7 1.9 collective-permute-done.36
  270.7 7.4 %collective-permute-done.35.gate2_ref = bf16[32,512]{1,0:T(8,128)(2,1)S(1)} collective-permute-done((bf16[32,512]{1,0:T(8,128)(2,1)S(1)}, bf16[32,512]{1,0:T(8,128)(2,1)S(1)}, u32[]{:S(2)}, u32[]{:S(2)}) %collective-permute-start.35) | collective-permute-done | bytes 32800 | tf_op jit(solution)/shard_map/ppermute | solution.py:817
  278.1 1.6 shard_map.230
  280.4 2.8 shard_map.231
  (214 shorter events, 40.2 us)
Async XLA Ops:
  0.7 28.7 %collective-permute-start = (bf16[4,64,1024]{2,1,0:T(8,128)(2,1)}, bf16[4,64,1024]{2,1,0:T(8,128)(2,1)S(1)}, u32[]{:S(2)}, u32[]{:S(2)}) collective-permute-start(bf16[4,64,1024]{2,1,0:T(8,128)(2,1)} %tokens_ref), channel_id=1, source_target_pairs={{0,2},{1,3},{2,0},{3,1},{4,6},{5,7},{6,4},{7,5},{8,10},{9,11},{10,... | collective-permute-start | bytes 1572872 | tf_op jit(solution)/shard_map/ppermute | solution.py:817
  11.7 11.5 %collective-permute-start.3 = (bf16[80,1024]{1,0:T(8,128)(2,1)S(1)}, bf16[80,1024]{1,0:T(8,128)(2,1)S(1)}, u32[]{:S(2)}, u32[]{:S(2)}) collective-permute-start(bf16[80,1024]{1,0:T(8,128)(2,1)S(1)} %pad_maximum_fusion.5), channel_id=1, source_target_pairs={{0,24},{4,28},{8,16},{12,20},{16,8},{20,12},{24,0},{28,4},{1,25},{... | collective-permute-start | bytes 491528 | tf_op jit(solution)/shard_map/ppermute | solution.py:817
  15.3 13.6 %collective-permute-start.2 = (bf16[80,1024]{1,0:T(8,128)(2,1)S(1)}, bf16[80,1024]{1,0:T(8,128)(2,1)S(1)}, u32[]{:S(2)}, u32[]{:S(2)}) collective-permute-start(bf16[80,1024]{1,0:T(8,128)(2,1)S(1)} %pad_maximum_fusion.5), channel_id=1, source_target_pairs={{0,16},{4,20},{8,24},{12,28},{16,0},{20,4},{24,8},{28,12},{1,17},{... | collective-permute-start | bytes 491528 | tf_op jit(solution)/shard_map/ppermute | solution.py:817
  15.3 13.6 %collective-permute-start.1 = (bf16[80,1024]{1,0:T(8,128)(2,1)S(1)}, bf16[80,1024]{1,0:T(8,128)(2,1)S(1)}, u32[]{:S(2)}, u32[]{:S(2)}) collective-permute-start(bf16[80,1024]{1,0:T(8,128)(2,1)S(1)} %pad_maximum_fusion.5), channel_id=1, source_target_pairs={{0,8},{4,12},{8,0},{12,4},{16,24},{20,28},{24,16},{28,20},{1,9},{5... | collective-permute-start | bytes 491528 | tf_op jit(solution)/shard_map/ppermute | solution.py:817
  16.1 6.9 %collective-permute-start.12 = (s32[4,3]{1,0:T(4,128)S(1)}, s32[4,3]{1,0:T(4,128)S(1)}, u32[]{:S(2)}, u32[]{:S(2)}) collective-permute-start(s32[4,3]{1,0:T(4,128)S(1)} %slice.106), channel_id=1, source_target_pairs={{0,4},{4,8},{8,12},{12,16},{16,20},{20,24},{24,28},{1,5},{5,9},{9,... | collective-permute-start | bytes 152 | tf_op jit(solution)/shard_map/ppermute | solution.py:882
  19.5 9.8 %all-to-all-start = ((bf16[4,72,512]{2,1,0:T(8,128)(2,1)}), bf16[4,72,512]{2,1,0:T(8,128)(2,1)S(1)}, u32[]{:S(2)}, u32[]{:S(2)}) async-start(bf16[4,72,512]{2,1,0:T(8,128)(2,1)} %pad_maximum_fusion.3), calls=%async_computation | async-start | bytes 589824 | tf_op jit(solution)/shard_map/all_to_all | solution.py:847
  23.1 131.2 %copy-start.19 = (s32[2]{0:T(128)}, s32[2]{0:T(128)S(1)}, u32[]{:S(2)}) copy-start(s32[2]{0:T(128)S(1)} %pad_add_fusion.1.place_ref) | copy-start | bytes 28
  30.2 19.5 %collective-permute-start.4 = (bf16[4,80,1024]{2,1,0:T(8,128)(2,1)S(1)}, bf16[4,80,1024]{2,1,0:T(8,128)(2,1)S(1)}, u32[]{:S(2)}, u32[]{:S(2)}) collective-permute-start(bf16[4,80,1024]{2,1,0:T(8,128)(2,1)S(1)} %pad_maximum_fusion.exit_near_ref), channel_id=1, source_target_pairs={{0,4},{4,0},{8,12},{12,8},{16,20},{20,16},{24,28},{28,24},{1,5},{5... | collective-permute-start | bytes 1966088 | tf_op jit(solution)/shard_map/ppermute | solution.py:817
  31.5 7.0 %collective-permute-start.7 = (bf16[136,512]{1,0:T(8,128)(2,1)S(1)}, bf16[136,512]{1,0:T(8,128)(2,1)S(1)}, u32[]{:S(2)}, u32[]{:S(2)}) collective-permute-start(bf16[136,512]{1,0:T(8,128)(2,1)S(1)} %pad_maximum_fusion.6), channel_id=1, source_target_pairs={{0,24},{4,28},{8,16},{12,20},{16,8},{20,12},{24,0},{28,4},{1,25},{... | collective-permute-start | bytes 417800 | tf_op jit(solution)/shard_map/ppermute | solution.py:817
  33.9 15.8 %collective-permute-start.9 = (bf16[4,64,1024]{2,1,0:T(8,128)(2,1)S(1)}, bf16[4,64,1024]{2,1,0:T(8,128)(2,1)}, u32[]{:S(2)}, u32[]{:S(2)}) collective-permute-start(bf16[4,64,1024]{2,1,0:T(8,128)(2,1)S(1)} %collective-permute-done.slab2_ref), channel_id=1, source_target_pairs={{0,1},{1,0},{2,3},{3,2},{4,5},{5,4},{6,7},{7,6},{8,9},{9,8},{10,11... | collective-permute-start | bytes 1572872 | tf_op jit(solution)/shard_map/ppermute | solution.py:817
  34.0 15.8 %collective-permute-start.8 = (bf16[4,64,1024]{2,1,0:T(8,128)(2,1)S(1)}, bf16[4,64,1024]{2,1,0:T(8,128)(2,1)}, u32[]{:S(2)}, u32[]{:S(2)}) collective-permute-start(bf16[4,64,1024]{2,1,0:T(8,128)(2,1)S(1)} %copy-done), channel_id=1, source_target_pairs={{0,1},{1,0},{2,3},{3,2},{4,5},{5,4},{6,7},{7,6},{8,9},{9,8},{10,11... | collective-permute-start | bytes 1572872 | tf_op jit(solution)/shard_map/ppermute | solution.py:817
  34.5 12.2 %collective-permute-start.6 = (bf16[136,512]{1,0:T(8,128)(2,1)S(1)}, bf16[136,512]{1,0:T(8,128)(2,1)S(1)}, u32[]{:S(2)}, u32[]{:S(2)}) collective-permute-start(bf16[136,512]{1,0:T(8,128)(2,1)S(1)} %pad_maximum_fusion.6), channel_id=1, source_target_pairs={{0,16},{4,20},{8,24},{12,28},{16,0},{20,4},{24,8},{28,12},{1,17},{... | collective-permute-start | bytes 417800 | tf_op jit(solution)/shard_map/ppermute | solution.py:817
  38.5 11.2 %collective-permute-start.5 = (bf16[136,512]{1,0:T(8,128)(2,1)S(1)}, bf16[136,512]{1,0:T(8,128)(2,1)}, u32[]{:S(2)}, u32[]{:S(2)}) collective-permute-start(bf16[136,512]{1,0:T(8,128)(2,1)S(1)} %pad_maximum_fusion.6), channel_id=1, source_target_pairs={{0,8},{4,12},{8,0},{12,4},{16,24},{20,28},{24,16},{28,20},{1,9},{5... | collective-permute-start | bytes 417800 | tf_op jit(solution)/shard_map/ppermute | solution.py:817
  45.4 46.1 %copy-start.2 = (f32[4,4,64,4]{3,0,1,2:T(4,128)}, f32[4,4,64,4]{3,0,1,2:T(4,128)S(1)}, u32[]{:S(2)}) copy-start(f32[4,4,64,4]{3,0,1,2:T(4,128)S(1)} %copy.38) | copy-start | bytes 49156
  52.9 10.0 %collective-permute-start.20 = (bf16[128,512]{1,0:T(8,128)(2,1)}, bf16[128,512]{1,0:T(8,128)(2,1)}, u32[]{:S(2)}, u32[]{:S(2)}) collective-permute-start(bf16[128,512]{1,0:T(8,128)(2,1)} %bitcast.108), channel_id=1, source_target_pairs={{0,24},{4,28},{8,16},{12,20},{16,8},{20,12},{24,0},{28,4},{1,25},{... | collective-permute-start | bytes 393224 | tf_op jit(solution)/shard_map/ppermute | solution.py:817
  55.5 11.3 %collective-permute-start.19 = (bf16[128,512]{1,0:T(8,128)(2,1)}, bf16[128,512]{1,0:T(8,128)(2,1)}, u32[]{:S(2)}, u32[]{:S(2)}) collective-permute-start(bf16[128,512]{1,0:T(8,128)(2,1)} %bitcast.109), channel_id=1, source_target_pairs={{0,16},{4,20},{8,24},{12,28},{16,0},{20,4},{24,8},{28,12},{1,17},{... | collective-permute-start | bytes 393224 | tf_op jit(solution)/shard_map/ppermute | solution.py:817
  55.5 11.4 %collective-permute-start.18 = (bf16[128,512]{1,0:T(8,128)(2,1)}, bf16[128,512]{1,0:T(8,128)(2,1)}, u32[]{:S(2)}, u32[]{:S(2)}) collective-permute-start(bf16[128,512]{1,0:T(8,128)(2,1)} %bitcast.110), channel_id=1, source_target_pairs={{0,8},{4,12},{8,0},{12,4},{16,24},{20,28},{24,16},{28,20},{1,9},{5... | collective-permute-start | bytes 393224 | tf_op jit(solution)/shard_map/ppermute | solution.py:817
  57.3 14.7 %collective-permute-start.11 = (bf16[4,136,512]{2,1,0:T(8,128)(2,1)S(1)}, bf16[4,136,512]{2,1,0:T(8,128)(2,1)}, u32[]{:S(2)}, u32[]{:S(2)}) collective-permute-start(bf16[4,136,512]{2,1,0:T(8,128)(2,1)S(1)} %pad_maximum_fusion.1.near_ref), channel_id=1, source_target_pairs={{0,4},{4,0},{8,12},{12,8},{16,20},{20,16},{24,28},{28,24},{1,5},{5... | collective-permute-start | bytes 1671176 | tf_op jit(solution)/shard_map/ppermute | solution.py:817
  58.7 13.3 %collective-permute-start.16 = (bf16[4,64,1024]{2,1,0:T(8,128)(2,1)}, bf16[4,64,1024]{2,1,0:T(8,128)(2,1)}, u32[]{:S(2)}, u32[]{:S(2)}) collective-permute-start(bf16[4,64,1024]{2,1,0:T(8,128)(2,1)} %cotangent_ref), channel_id=1, source_target_pairs={{0,2},{1,3},{2,0},{3,1},{4,6},{5,7},{6,4},{7,5},{8,10},{9,11},{10,... | collective-permute-start | bytes 1572872 | tf_op jit(solution)/shard_map/ppermute | solution.py:817
  62.8 107.8 %copy-start.8 = (bf16[192,512]{1,0:T(8,128)(2,1)}, bf16[192,512]{1,0:T(8,128)(2,1)S(1)}, u32[]{:S(2)}) copy-start(bf16[192,512]{1,0:T(8,128)(2,1)S(1)} %copy.41.small_ref) | copy-start | bytes 589828
  62.9 10.0 %collective-permute-start.10 = (bf16[12,1024]{1,0:T(8,128)(2,1)S(1)}, bf16[12,1024]{1,0:T(8,128)(2,1)S(1)}, u32[]{:S(2)}, u32[]{:S(2)}) collective-permute-start(bf16[12,1024]{1,0:T(8,128)(2,1)S(1)} %reshape.120), channel_id=1, source_target_pairs={{0,4},{4,8},{8,12},{12,16},{16,20},{20,24},{24,28},{1,5},{5,9},{9,... | collective-permute-start | bytes 73736 | tf_op jit(solution)/shard_map/ppermute | solution.py:877
  66.8 18.1 %collective-permute-start.15 = (bf16[4,64,1024]{2,1,0:T(8,128)(2,1)}, bf16[4,64,1024]{2,1,0:T(8,128)(2,1)S(1)}, u32[]{:S(2)}, u32[]{:S(2)}) collective-permute-start(bf16[4,64,1024]{2,1,0:T(8,128)(2,1)} %cotangent_ref), channel_id=1, source_target_pairs={{0,1},{1,0},{2,3},{3,2},{4,5},{5,4},{6,7},{7,6},{8,9},{9,8},{10,11... | collective-permute-start | bytes 1572872 | tf_op jit(solution)/shard_map/ppermute | solution.py:817
  68.1 16.8 %collective-permute-start.21 = (bf16[4,128,512]{2,1,0:T(8,128)(2,1)S(1)}, bf16[4,128,512]{2,1,0:T(8,128)(2,1)S(1)}, u32[]{:S(2)}, u32[]{:S(2)}) collective-permute-start(bf16[4,128,512]{2,1,0:T(8,128)(2,1)S(1)} %pad_maximum_fusion.2.near_ref.gate_near_ref), channel_id=1, source_target_pairs={{0,4},{4,0},{8,12},{12,8},{16,20},{20,16},{24,28},{28,24},{1,5},{5... | collective-permute-start | bytes 1572872 | tf_op jit(solution)/shard_map/ppermute | solution.py:817
  72.0 12.9 %collective-permute-start.17 = (bf16[4,64,1024]{2,1,0:T(8,128)(2,1)}, bf16[4,64,1024]{2,1,0:T(8,128)(2,1)S(1)}, u32[]{:S(2)}, u32[]{:S(2)}) collective-permute-start(bf16[4,64,1024]{2,1,0:T(8,128)(2,1)} %collective-permute-done.16.slab2_ref), channel_id=1, source_target_pairs={{0,1},{1,0},{2,3},{3,2},{4,5},{5,4},{6,7},{7,6},{8,9},{9,8},{10,11... | collective-permute-start | bytes 1572872 | tf_op jit(solution)/shard_map/ppermute | solution.py:817
  82.6 50.2 %copy-start.17 = (f32[1024,512]{1,0:T(8,128)}, f32[1024,512]{1,0:T(8,128)S(1)}, u32[]{:S(2)}) copy-start(f32[1024,512]{1,0:T(8,128)S(1)} %get-tuple-element.125.filter_ref) | copy-start | bytes 6291460
  82.6 71.7 %copy-start.21 = (bf16[1024,1024]{1,0:T(8,128)(2,1)}, bf16[1024,1024]{1,0:T(8,128)(2,1)S(1)}, u32[]{:S(2)}) copy-start(bf16[1024,1024]{1,0:T(8,128)(2,1)S(1)} %get-tuple-element.129.normed_ref) | copy-start | bytes 6291460
  82.6 1.6 collective-permute-start.13
  84.2 7.3 %collective-permute-start.14 = (bf16[96,1024]{1,0:T(8,128)(2,1)S(1)}, bf16[96,1024]{1,0:T(8,128)(2,1)S(1)}, u32[]{:S(2)}, u32[]{:S(2)}) collective-permute-start(bf16[96,1024]{1,0:T(8,128)(2,1)S(1)} %add_convert_fusion.3.chosen_ref), channel_id=1, source_target_pairs={{0,2},{1,3},{2,0},{3,1},{4,6},{5,7},{6,4},{7,5},{8,10},{9,11},{10,... | collective-permute-start | bytes 589832 | tf_op jit(solution)/shard_map/ppermute | solution.py:817
  91.5 41.3 %copy-start.18 = (f32[1024,512]{1,0:T(8,128)}, f32[1024,512]{1,0:T(8,128)S(1)}, u32[]{:S(2)}) copy-start(f32[1024,512]{1,0:T(8,128)S(1)} %get-tuple-element.145) | copy-start | bytes 6291460
  111.2 43.1 %copy-start.30 = (f32[64,16,512]{2,1,0:T(8,128)}, f32[64,16,512]{2,1,0:T(8,128)S(1)}, u32[]{:S(2)}) copy-start(f32[64,16,512]{2,1,0:T(8,128)S(1)} %get-tuple-element.134.step_ref) | copy-start | bytes 6291460
  111.2 43.1 %copy-start.33 = (f32[64,16,128]{2,1,0:T(8,128)}, f32[64,16,128]{2,1,0:T(8,128)S(1)}, u32[]{:S(2)}) copy-start(f32[64,16,128]{2,1,0:T(8,128)S(1)} %get-tuple-element.133.gates_ref) | copy-start | bytes 1572868
  164.3 40.4 %collective-permute-start.23 = (bf16[2,4,64,1024]{3,2,1,0:T(8,128)(2,1)}, bf16[2,4,64,1024]{3,2,1,0:T(8,128)(2,1)}, u32[]{:S(2)}, u32[]{:S(2)}) collective-permute-start(bf16[2,4,64,1024]{3,2,1,0:T(8,128)(2,1)} %get-tuple-element.144), channel_id=1, source_target_pairs={{0,1},{1,0},{2,3},{3,2},{4,5},{5,4},{6,7},{7,6},{8,9},{9,8},{10,11... | collective-permute-start | bytes 3145736 | tf_op jit(solution)/shard_map/ppermute | solution.py:817
  164.3 40.4 %all-to-all-start.2 = ((bf16[8,64,1024]{2,1,0:T(8,128)(2,1)}), bf16[8,64,1024]{2,1,0:T(8,128)(2,1)}, u32[]{:S(2)}, u32[]{:S(2)}) async-start(bf16[8,64,1024]{2,1,0:T(8,128)(2,1)} %bitcast.40), calls=%async_computation.2 | async-start | bytes 2097152 | tf_op jit(solution)/shard_map/all_to_all | solution.py:1002
  168.7 36.0 %collective-permute-start.22 = (bf16[4,128,512]{2,1,0:T(8,128)(2,1)}, bf16[4,128,512]{2,1,0:T(8,128)(2,1)}, u32[]{:S(2)}, u32[]{:S(2)}) collective-permute-start(bf16[4,128,512]{2,1,0:T(8,128)(2,1)} %get-tuple-element.151), channel_id=1, source_target_pairs={{0,4},{4,0},{8,12},{12,8},{16,20},{20,16},{24,28},{28,24},{1,5},{5... | collective-permute-start | bytes 1572872 | tf_op jit(solution)/shard_map/ppermute | solution.py:817
  204.7 1.5 collective-permute-start.24
  206.3 7.0 %collective-permute-start.25 = (bf16[96,1024]{1,0:T(8,128)(2,1)S(1)}, bf16[96,1024]{1,0:T(8,128)(2,1)S(1)}, u32[]{:S(2)}, u32[]{:S(2)}) collective-permute-start(bf16[96,1024]{1,0:T(8,128)(2,1)S(1)} %add_convert_fusion.2.chosen_ref), channel_id=1, source_target_pairs={{0,2},{1,3},{2,0},{3,1},{4,6},{5,7},{6,4},{7,5},{8,10},{9,11},{10,... | collective-permute-start | bytes 589832 | tf_op jit(solution)/shard_map/ppermute | solution.py:817
  211.9 24.3 %collective-permute-start.27 = (bf16[4,64,1024]{2,1,0:T(8,128)(2,1)}, bf16[4,64,1024]{2,1,0:T(8,128)(2,1)}, u32[]{:S(2)}, u32[]{:S(2)}) collective-permute-start(bf16[4,64,1024]{2,1,0:T(8,128)(2,1)} %fusion.2), channel_id=1, source_target_pairs={{0,2},{1,3},{2,0},{3,1},{4,6},{5,7},{6,4},{7,5},{8,10},{9,11},{10,... | collective-permute-start | bytes 1572872 | tf_op jit(solution)/shard_map/ppermute | solution.py:817
  223.6 6.6 %collective-permute-start.26 = (f32[3,4,512]{2,1,0:T(4,128)}, f32[3,4,512]{2,1,0:T(4,128)S(1)}, u32[]{:S(2)}, u32[]{:S(2)}) collective-permute-start(f32[3,4,512]{2,1,0:T(4,128)} %get-tuple-element.167), channel_id=1, source_target_pairs={{4,0},{8,4},{12,8},{16,12},{20,16},{24,20},{28,24},{5,1},{9,5},{13... | collective-permute-start | bytes 73736 | tf_op jit(solution)/shard_map/ppermute | solution.py:1068
  225.1 19.2 %collective-permute-start.28 = (bf16[176,512]{1,0:T(8,128)(2,1)}, bf16[176,512]{1,0:T(8,128)(2,1)S(1)}, u32[]{:S(2)}, u32[]{:S(2)}) collective-permute-start(bf16[176,512]{1,0:T(8,128)(2,1)} %get-tuple-element.177), channel_id=1, source_target_pairs={{0,8},{4,12},{8,0},{12,4},{16,24},{20,28},{24,16},{28,20},{1,9},{5... | collective-permute-start | bytes 540680 | tf_op jit(solution)/shard_map/ppermute | solution.py:817
  227.5 16.9 %collective-permute-start.29 = (bf16[176,512]{1,0:T(8,128)(2,1)}, bf16[176,512]{1,0:T(8,128)(2,1)S(1)}, u32[]{:S(2)}, u32[]{:S(2)}) collective-permute-start(bf16[176,512]{1,0:T(8,128)(2,1)} %get-tuple-element.178), channel_id=1, source_target_pairs={{0,16},{4,20},{8,24},{12,28},{16,0},{20,4},{24,8},{28,12},{1,17},{... | collective-permute-start | bytes 540680 | tf_op jit(solution)/shard_map/ppermute | solution.py:817
  230.2 14.2 %collective-permute-start.30 = (bf16[176,512]{1,0:T(8,128)(2,1)}, bf16[176,512]{1,0:T(8,128)(2,1)S(1)}, u32[]{:S(2)}, u32[]{:S(2)}) collective-permute-start(bf16[176,512]{1,0:T(8,128)(2,1)} %get-tuple-element.179), channel_id=1, source_target_pairs={{0,24},{4,28},{8,16},{12,20},{16,8},{20,12},{24,0},{28,4},{1,25},{... | collective-permute-start | bytes 540680 | tf_op jit(solution)/shard_map/ppermute | solution.py:817
  244.4 6.1 %collective-permute-start.31 = (bf16[2,4,64,1024]{3,2,1,0:T(8,128)(2,1)}, bf16[2,4,64,1024]{3,2,1,0:T(8,128)(2,1)}, u32[]{:S(2)}, u32[]{:S(2)}) collective-permute-start(bf16[2,4,64,1024]{3,2,1,0:T(8,128)(2,1)} %get-tuple-element.180), channel_id=1, source_target_pairs={{0,1},{1,0},{2,3},{3,2},{4,5},{5,4},{6,7},{7,6},{8,9},{9,8},{10,11... | collective-permute-start | bytes 3145736 | tf_op jit(solution)/shard_map/ppermute | solution.py:817
  244.5 33.6 %all-to-all-start.3 = ((bf16[32,32,512]{2,1,0:T(8,128)(2,1)}), bf16[32,32,512]{2,1,0:T(8,128)(2,1)S(1)}, u32[]{:S(2)}, u32[]{:S(2)}) async-start(bf16[32,32,512]{2,1,0:T(8,128)(2,1)} %bitcast.46), calls=%async_computation.3 | async-start | bytes 2097152 | tf_op jit(solution)/shard_map/all_to_all | solution.py:1079
  254.4 6.6 %collective-permute-start.32 = (bf16[32,512]{1,0:T(8,128)(2,1)S(1)}, bf16[32,512]{1,0:T(8,128)(2,1)S(1)}, u32[]{:S(2)}, u32[]{:S(2)}) collective-permute-start(bf16[32,512]{1,0:T(8,128)(2,1)S(1)} %get-tuple-element.185), channel_id=1, source_target_pairs={{0,3},{1,2},{2,1},{3,0},{4,7},{5,6},{6,5},{7,4},{8,11},{9,10},{10,... | collective-permute-start | bytes 98312 | tf_op jit(solution)/shard_map/ppermute | solution.py:817
  255.9 24.4 %collective-permute-start.33 = (bf16[4,64,1024]{2,1,0:T(8,128)(2,1)}, bf16[4,64,1024]{2,1,0:T(8,128)(2,1)}, u32[]{:S(2)}, u32[]{:S(2)}) collective-permute-start(bf16[4,64,1024]{2,1,0:T(8,128)(2,1)} %fusion.3), channel_id=1, source_target_pairs={{0,2},{1,3},{2,0},{3,1},{4,6},{5,7},{6,4},{7,5},{8,10},{9,11},{10,... | collective-permute-start | bytes 1572872 | tf_op jit(solution)/shard_map/ppermute | solution.py:817
  256.3 14.4 %collective-permute-start.34 = (bf16[32,512]{1,0:T(8,128)(2,1)S(1)}, bf16[32,512]{1,0:T(8,128)(2,1)S(1)}, u32[]{:S(2)}, u32[]{:S(2)}) collective-permute-start(bf16[32,512]{1,0:T(8,128)(2,1)S(1)} %get-tuple-element.190), channel_id=1, source_target_pairs={{0,1},{1,0},{2,3},{3,2},{4,5},{5,4},{6,7},{7,6},{8,9},{9,8},{10,11... | collective-permute-start | bytes 98312 | tf_op jit(solution)/shard_map/ppermute | solution.py:817
  256.3 21.8 %collective-permute-start.35 = (bf16[32,512]{1,0:T(8,128)(2,1)S(1)}, bf16[32,512]{1,0:T(8,128)(2,1)S(1)}, u32[]{:S(2)}, u32[]{:S(2)}) collective-permute-start(bf16[32,512]{1,0:T(8,128)(2,1)S(1)} %get-tuple-element.191), channel_id=1, source_target_pairs={{0,2},{1,3},{2,0},{3,1},{4,6},{5,7},{6,4},{7,5},{8,10},{9,11},{10,... | collective-permute-start | bytes 98312 | tf_op jit(solution)/shard_map/ppermute | solution.py:817
  260.9 6.6 %collective-permute-start.36 = (f32[192,128]{1,0:T(8,128)S(1)}, f32[192,128]{1,0:T(8,128)S(1)}, u32[]{:S(2)}, u32[]{:S(2)}) collective-permute-start(f32[192,128]{1,0:T(8,128)S(1)} %get-tuple-element.196), channel_id=1, source_target_pairs={{0,4},{4,0},{8,12},{12,8},{16,20},{20,16},{24,28},{28,24},{1,5},{5... | collective-permute-start | bytes 294920 | tf_op jit(solution)/shard_map/ppermute | solution.py:817
  (41 other events, 262.5 us)

commit v8 on v7

--- a/solution.py
+++ b/solution.py
@@ -379,7 +379,7 @@
                 arrive_ref[n, other, :] = back
                 back = give_ref[n, other, :] + keep_ref[n, other, :] * back
 
-    span = 4
+    span = 8
     lanes = lane_slices(width)
     spots = [(j, i) for j in range(span) for i in range(len(lanes))]
 
@@ -970,7 +970,7 @@
         pltpu.VMEM((4 * states, 2 * states * 128), bf16),
     ]
     product_scratch = [pltpu.VMEM((steps * 8, states * 128), bf16), pltpu.VMEM((states * 128, 128), bf16)]
-    starts = (steps // 4, states, chunks, group_width)
+    starts = (steps // 8, states, chunks, group_width)
     scan_out, read_sums, block_starts, arrive = kernel_call(
         forward_kernel,
         18,

time: 285 us -> 279 us (0.979)
  Pallas kernels: 119 us -> 114 us
    pallas_call x12, Pallas kernels: 119 us -> 114 us  [kernel_call(): pl.pallas_call(body, out_shape=[jax.ShapeDtypeStruct(shape, kind) for sha...]
    unnamed x104 -> x106, local copies, waits for them, and re-layouts: 16 us -> 15.9 us
where the time goes in v8:
time: 279 us; the launch traced here: 278 us
  Pallas kernels  114 us (41%)
  starting transfers between devices  63.9 us (23%)
  waiting for transfers between devices  32.5 us (12%)
  local copies, waits for them, and re-layouts  27.9 us (10%)
  blocking collectives  21.6 us (8%)
  other arithmetic  16.6 us (6%)
    pallas_call x12, Pallas kernels, kernel_call(): pl.pallas_call(body, out_shape=[jax.ShapeDtypeStruct(shape, kind) for sha...  114 us
    ppermute x34, starting transfers between devices, flipped(): lax.ppermute(value, axis, [(i, i ^ bits) for i in range(lax.axis_size(axi...  41.2 us
    ppermute x34, waiting for transfers between devices, flipped(): lax.ppermute(value, axis, [(i, i ^ bits) for i in range(lax.axis_size(axi...  32 us
    all_to_all x1, blocking collectives, local(): came = lax.all_to_all(loads, 'blk', split_axis=0, concat_axis=0, tiled=True)  21.6 us
    unnamed x106, local copies, waits for them, and re-layouts  15.9 us
    all_to_all x1, starting transfers between devices, local(): lax.all_to_all(inner_entry.reshape(pieces * groups, slice_rows, group_wid...  6.01 us
  transfers between devices with their start and end apart: 40, of which 12 were waited for; matrix products, arithmetic and copies ran while one was open for 10% of the time, Pallas kernels for 24%

profile of v8, /device:TPU:0, one launch (start us, length us, event | category | flops | bytes accessed | tf_op | source)
XLA Modules:
  0.0 277.7 jit_solution(1233314386882233496)
XLA Ops:
  0.7 3.0 %collective-permute-start = (bf16[4,64,1024]{2,1,0:T(8,128)(2,1)}, bf16[4,64,1024]{2,1,0:T(8,128)(2,1)S(1)}, u32[]{:S(2)}, u32[]{:S(2)}) collective-permute-start(bf16[4,64,1024]{2,1,0:T(8,128)(2,1)} %tokens_ref), channel_id=1, source_target_pairs={{0,2},{1,3},{2,0},{3,1},{4,6},{5,7},{6,4},{7,5},{8,10},{9,11},{10,... | collective-permute-start | bytes 1572872 | tf_op jit(solution)/shard_map/ppermute | solution.py:817
  9.0 1.5 reshape.112
  11.7 3.6 %collective-permute-start.3 = (bf16[80,1024]{1,0:T(8,128)(2,1)S(1)}, bf16[80,1024]{1,0:T(8,128)(2,1)S(1)}, u32[]{:S(2)}, u32[]{:S(2)}) collective-permute-start(bf16[80,1024]{1,0:T(8,128)(2,1)S(1)} %pad_maximum_fusion.5), channel_id=1, source_target_pairs={{0,24},{4,28},{8,16},{12,20},{16,8},{20,12},{24,0},{28,4},{1,25},{... | collective-permute-start | bytes 491528 | tf_op jit(solution)/shard_map/ppermute | solution.py:817
  16.1 3.4 %collective-permute-start.12 = (s32[4,3]{1,0:T(4,128)S(1)}, s32[4,3]{1,0:T(4,128)S(1)}, u32[]{:S(2)}, u32[]{:S(2)}) collective-permute-start(s32[4,3]{1,0:T(4,128)S(1)} %slice.106), channel_id=1, source_target_pairs={{0,4},{4,8},{8,12},{12,16},{16,20},{20,24},{24,28},{1,5},{5,9},{9,... | collective-permute-start | bytes 152 | tf_op jit(solution)/shard_map/ppermute | solution.py:882
  19.5 3.5 %all-to-all-start = ((bf16[4,72,512]{2,1,0:T(8,128)(2,1)}), bf16[4,72,512]{2,1,0:T(8,128)(2,1)S(1)}, u32[]{:S(2)}, u32[]{:S(2)}) async-start(bf16[4,72,512]{2,1,0:T(8,128)(2,1)} %pad_maximum_fusion.3), calls=%async_computation | async-start | bytes 589824 | tf_op jit(solution)/shard_map/all_to_all | solution.py:847
  23.1 5.7 %collective-permute-done.2 = bf16[80,1024]{1,0:T(8,128)(2,1)S(1)} collective-permute-done((bf16[80,1024]{1,0:T(8,128)(2,1)S(1)}, bf16[80,1024]{1,0:T(8,128)(2,1)S(1)}, u32[]{:S(2)}, u32[]{:S(2)}) %collective-permute-start.2) | collective-permute-done | bytes 163872 | tf_op jit(solution)/shard_map/ppermute | solution.py:817
  30.2 1.3 collective-permute-start.4
  31.5 2.5 collective-permute-start.7
  35.1 3.4 %collective-permute-done.7 = bf16[136,512]{1,0:T(8,128)(2,1)S(1)} collective-permute-done((bf16[136,512]{1,0:T(8,128)(2,1)S(1)}, bf16[136,512]{1,0:T(8,128)(2,1)S(1)}, u32[]{:S(2)}, u32[]{:S(2)}) %collective-permute-start.7) | collective-permute-done | bytes 139296 | tf_op jit(solution)/shard_map/ppermute | solution.py:817
  38.5 6.5 %collective-permute-start.5 = (bf16[136,512]{1,0:T(8,128)(2,1)S(1)}, bf16[136,512]{1,0:T(8,128)(2,1)}, u32[]{:S(2)}, u32[]{:S(2)}) collective-permute-start(bf16[136,512]{1,0:T(8,128)(2,1)S(1)} %pad_maximum_fusion.6), channel_id=1, source_target_pairs={{0,8},{4,12},{8,0},{12,4},{16,24},{20,28},{24,16},{28,20},{1,9},{5... | collective-permute-start | bytes 417800 | tf_op jit(solution)/shard_map/ppermute | solution.py:817
  45.4 1.3 collective-permute-done.6
  46.7 3.0 %collective-permute-done.5 = bf16[136,512]{1,0:T(8,128)(2,1)} collective-permute-done((bf16[136,512]{1,0:T(8,128)(2,1)S(1)}, bf16[136,512]{1,0:T(8,128)(2,1)}, u32[]{:S(2)}, u32[]{:S(2)}) %collective-permute-start.5) | collective-permute-done | bytes 139296 | tf_op jit(solution)/shard_map/ppermute | solution.py:817
  52.9 2.6 collective-permute-start.20
  55.5 1.8 collective-permute-start.18
  62.9 3.9 %collective-permute-start.10 = (bf16[12,1024]{1,0:T(8,128)(2,1)S(1)}, bf16[12,1024]{1,0:T(8,128)(2,1)S(1)}, u32[]{:S(2)}, u32[]{:S(2)}) collective-permute-start(bf16[12,1024]{1,0:T(8,128)(2,1)S(1)} %reshape.120), channel_id=1, source_target_pairs={{0,4},{4,8},{8,12},{12,16},{16,20},{20,24},{24,28},{1,5},{5,9},{9,... | collective-permute-start | bytes 73736 | tf_op jit(solution)/shard_map/ppermute | solution.py:877
  68.8 3.2 %collective-permute-done.16.slab2_ref = bf16[4,64,1024]{2,1,0:T(8,128)(2,1)} collective-permute-done((bf16[4,64,1024]{2,1,0:T(8,128)(2,1)}, bf16[4,64,1024]{2,1,0:T(8,128)(2,1)}, u32[]{:S(2)}, u32[]{:S(2)}) %collective-permute-start.16) | collective-permute-done | bytes 524320 | tf_op jit(solution)/shard_map/ppermute | solution.py:817
  72.9 8.7 %shard_map.220 = (bf16[1024,1024]{1,0:T(8,128)(2,1)S(1)}, bf16[1072,512]{1,0:T(8,128)(2,1)S(1)}, f32[1024,512]{1,0:T(8,128)S(1)}, bf16[96,1024]{1,0:T(8,128)(2,1)S(1)}) custom-call(s32[2]{0:T(128)S(1)} %pad_add_fusion.1.place_ref, bf16[4,64,1024]{2,1,0:T(8,128)(2,1)S(1)} %copy-done, bf16[4,64,1024]{2,1,0:T(8,128)(2,1)} %collective-permute-done.8.slab1_ref, ...), custom_call_target="tpu_custom_call" | custom-call | flops 10350000128 | bytes 8000000 | tf_op jit(solution)/shard_map/pallas_call | solution.py:59
  84.9 6.5 %shard_map.221 = (bf16[1024,1024]{1,0:T(8,128)(2,1)S(1)}, f32[1024,512]{1,0:T(8,128)S(1)}, f32[1024,512]{1,0:T(8,128)S(1)}, f32[1024,512]{1,0:T(8,128)S(1)}) custom-call(s32[2]{0:T(128)S(1)} %pad_add_fusion.1.place_ref, bf16[4,64,1024]{2,1,0:T(8,128)(2,1)S(1)} %copy-done.13, bf16[4,64,1024]{2,1,0:T(8,128)(2,1)S(1)} %collective-permute-done.15.slab1_ref, ...), custom_call_target="tpu_custom_call" | custom-call | flops 9200000000 | bytes 8000000 | tf_op jit(solution)/shard_map/pallas_call | solution.py:59
  91.5 18.3 %shard_map.222 = (f32[64,16,128]{2,1,0:T(8,128)S(1)}, f32[64,16,512]{2,1,0:T(8,128)S(1)}, f32[64,16,512]{2,1,0:T(8,128)S(1)}, f32[16,16,512]{2,1,0:T(8,128)S(1)}...) custom-call(s32[2]{0:T(128)S(1)} %pad_add_fusion.1.place_ref, ...), custom_call_target="tpu_custom_call" | custom-call | flops 26449999872 | bytes 8000000 | tf_op jit(solution)/shard_map/pallas_call | solution.py:59
  109.9 1.3 copy-done.33
  111.2 21.6 %all_to_all.20.came_ref = bf16[8,72,512]{2,1,0:T(8,128)(2,1)S(1)} all-to-all(bf16[8,72,512]{2,1,0:T(8,128)(2,1)S(1)} %get-tuple-element.132), channel_id=1, replica_groups=mesh['blk'=8,'grp'=4] {'blk'}, dimensions={0} | all-to-all | bytes 1179648 | tf_op jit(solution)/shard_map/all_to_all | solution.py:964
  132.8 18.3 %shard_map.223 = (f32[64,16,512]{2,1,0:T(8,128)S(1)}, f32[64,16,128]{2,1,0:T(8,128)S(1)}, f32[8,16,16,512]{3,2,1,0:T(8,128)S(1)}, f32[16,16,512]{2,1,0:T(8,128)S(1)}) custom-call(s32[2]{0:T(128)S(1)} %pad_add_fusion.1.place_ref, bf16[8,72,512]{2,1,0:T(8,128)(2,1)S(1)} %all_to_all.20.came_ref, f32[64,16,128]{2,1,0:T(8,128)S(1)} %get-tuple-element.133.gates_ref, ...), custom_call_target="tpu_custom_call" | custom-call | flops 20700000256 | bytes 8000000 | tf_op jit(solution)/shard_map/pallas_call | solution.py:59
  151.1 8.1 %shard_map.224 = (bf16[1024,512]{1,0:T(8,128)(2,1)S(1)}, bf16[2,4,64,1024]{3,2,1,0:T(8,128)(2,1)S(1)}, bf16[2,4,64,1024]{3,2,1,0:T(8,128)(2,1)}, bf16[512,1024]{...) custom-call(s32[2]{0:T(128)S(1)} %pad_add_fusion.1.place_ref, ...), custom_call_target="tpu_custom_call" | custom-call | flops 13799999488 | bytes 8000000 | tf_op jit(solution)/shard_map/pallas_call | solution.py:59
  161.0 4.4 %all-to-all-start.2 = ((bf16[8,64,1024]{2,1,0:T(8,128)(2,1)}), bf16[8,64,1024]{2,1,0:T(8,128)(2,1)}, u32[]{:S(2)}, u32[]{:S(2)}) async-start(bf16[8,64,1024]{2,1,0:T(8,128)(2,1)} %bitcast.40), calls=%async_computation.2 | async-start | bytes 2097152 | tf_op jit(solution)/shard_map/all_to_all | solution.py:1002
  165.3 1.9 collective-permute-start.22
  169.3 29.9 %shard_map.225 = (f32[64,16,512]{2,1,0:T(8,128)}, f32[64,512]{1,0:T(8,128)S(1)}, bf16[96,1024]{1,0:T(8,128)(2,1)S(1)}, f32[16,512]{1,0:T(8,128)S(1)}, f32[1,512]{1,0:T(1,128)S(1)}, /*index=5*/f32[1,512]{1,0:T(1,128)S(1)}) custom-call(f32[64,16,128]{2,1,0:T(8,128)S(1)} %copy-done.35, bf16[192,512]{1,0:T(8,128)(2,1)S(1)} %copy.41.small_ref, ...), custom_call_target="tpu_custom_call" | custom-call | flops 40249999360 | bytes 8000000 | tf_op jit(solution)/shard_map/pallas_call | solution.py:59
  199.4 1.4 collective-permute-done.24
  200.9 1.4 collective-permute-start.25
  202.3 2.0 fusion.2
  204.3 2.1 convert_reduce_fusion
  208.6 9.6 %shard_map.226 = (bf16[1024,512]{1,0:T(8,128)(2,1)}, f32[3,16,512]{2,1,0:T(8,128)}, f32[3,4,512]{2,1,0:T(4,128)}, f32[192,512]{1,0:T(8,128)}, f32[176,512]{1,0:T...) custom-call(s32[2]{0:T(128)} %copy-done.19, bf16[96,1024]{1,0:T(8,128)(2,1)} %copy-done.43, ...), custom_call_target="tpu_custom_call" | custom-call | flops 6899999744 | bytes 8000000 | tf_op jit(solution)/shard_map/pallas_call | solution.py:59
  218.2 1.5 collective-permute-start.26
  219.7 2.3 collective-permute-start.28
  222.1 2.7 collective-permute-start.29
  224.8 1.6 copy-done.22
  228.5 2.3 shard_map.227
  230.8 7.2 %shard_map.228 = (bf16[2,4,64,1024]{3,2,1,0:T(8,128)(2,1)S(1)}, bf16[2,4,64,1024]{3,2,1,0:T(8,128)(2,1)}) custom-call(s32[2]{0:T(128)S(1)} %copy-done.20, bf16[1024,512]{1,0:T(8,128)(2,1)S(1)} %get-tuple-element.173.inner_ref, bf16[1024,512]{1,0:T(8,128)(2,1)S(1)} %copy-done.29, bf16[4,136,512]{2,1,0:T(8,128)(2,1)S(1)} %pad_maximum_fusion.1.near_ref, ...), custom_call_target="tpu_custom_call" | custom-call | flops 11500000256 | bytes 8000000 | tf_op jit(solution)/shard_map/pallas_call | solution.py:59
  239.1 6.0 %all-to-all-start.3 = ((bf16[32,32,512]{2,1,0:T(8,128)(2,1)}), bf16[32,32,512]{2,1,0:T(8,128)(2,1)S(1)}, u32[]{:S(2)}, u32[]{:S(2)}) async-start(bf16[32,32,512]{2,1,0:T(8,128)(2,1)} %bitcast.46), calls=%async_computation.3 | async-start | bytes 2097152 | tf_op jit(solution)/shard_map/all_to_all | solution.py:1079
  245.1 2.2 fusion.3
  248.9 1.6 collective-permute-start.32
  250.9 1.7 collective-permute-start.35
  252.6 2.8 %collective-permute-done.32.gate3_ref = bf16[32,512]{1,0:T(8,128)(2,1)S(1)} collective-permute-done((bf16[32,512]{1,0:T(8,128)(2,1)S(1)}, bf16[32,512]{1,0:T(8,128)(2,1)S(1)}, u32[]{:S(2)}, u32[]{:S(2)}) %collective-permute-start.32) | collective-permute-done | bytes 32800 | tf_op jit(solution)/shard_map/ppermute | solution.py:817
  255.5 2.4 collective-permute-start.36
  257.9 2.4 fusion.1
  260.3 1.9 collective-permute-done.36
  265.3 7.4 %collective-permute-done.35.gate2_ref = bf16[32,512]{1,0:T(8,128)(2,1)S(1)} collective-permute-done((bf16[32,512]{1,0:T(8,128)(2,1)S(1)}, bf16[32,512]{1,0:T(8,128)(2,1)S(1)}, u32[]{:S(2)}, u32[]{:S(2)}) %collective-permute-start.35) | collective-permute-done | bytes 32800 | tf_op jit(solution)/shard_map/ppermute | solution.py:817
  272.7 1.6 shard_map.230
  275.0 2.8 shard_map.231
  (216 shorter events, 40.1 us)
Async XLA Ops:
  0.7 28.7 %collective-permute-start = (bf16[4,64,1024]{2,1,0:T(8,128)(2,1)}, bf16[4,64,1024]{2,1,0:T(8,128)(2,1)S(1)}, u32[]{:S(2)}, u32[]{:S(2)}) collective-permute-start(bf16[4,64,1024]{2,1,0:T(8,128)(2,1)} %tokens_ref), channel_id=1, source_target_pairs={{0,2},{1,3},{2,0},{3,1},{4,6},{5,7},{6,4},{7,5},{8,10},{9,11},{10,... | collective-permute-start | bytes 1572872 | tf_op jit(solution)/shard_map/ppermute | solution.py:817
  11.7 11.5 %collective-permute-start.3 = (bf16[80,1024]{1,0:T(8,128)(2,1)S(1)}, bf16[80,1024]{1,0:T(8,128)(2,1)S(1)}, u32[]{:S(2)}, u32[]{:S(2)}) collective-permute-start(bf16[80,1024]{1,0:T(8,128)(2,1)S(1)} %pad_maximum_fusion.5), channel_id=1, source_target_pairs={{0,24},{4,28},{8,16},{12,20},{16,8},{20,12},{24,0},{28,4},{1,25},{... | collective-permute-start | bytes 491528 | tf_op jit(solution)/shard_map/ppermute | solution.py:817
  15.3 13.6 %collective-permute-start.2 = (bf16[80,1024]{1,0:T(8,128)(2,1)S(1)}, bf16[80,1024]{1,0:T(8,128)(2,1)S(1)}, u32[]{:S(2)}, u32[]{:S(2)}) collective-permute-start(bf16[80,1024]{1,0:T(8,128)(2,1)S(1)} %pad_maximum_fusion.5), channel_id=1, source_target_pairs={{0,16},{4,20},{8,24},{12,28},{16,0},{20,4},{24,8},{28,12},{1,17},{... | collective-permute-start | bytes 491528 | tf_op jit(solution)/shard_map/ppermute | solution.py:817
  15.3 13.6 %collective-permute-start.1 = (bf16[80,1024]{1,0:T(8,128)(2,1)S(1)}, bf16[80,1024]{1,0:T(8,128)(2,1)S(1)}, u32[]{:S(2)}, u32[]{:S(2)}) collective-permute-start(bf16[80,1024]{1,0:T(8,128)(2,1)S(1)} %pad_maximum_fusion.5), channel_id=1, source_target_pairs={{0,8},{4,12},{8,0},{12,4},{16,24},{20,28},{24,16},{28,20},{1,9},{5... | collective-permute-start | bytes 491528 | tf_op jit(solution)/shard_map/ppermute | solution.py:817
  16.1 6.9 %collective-permute-start.12 = (s32[4,3]{1,0:T(4,128)S(1)}, s32[4,3]{1,0:T(4,128)S(1)}, u32[]{:S(2)}, u32[]{:S(2)}) collective-permute-start(s32[4,3]{1,0:T(4,128)S(1)} %slice.106), channel_id=1, source_target_pairs={{0,4},{4,8},{8,12},{12,16},{16,20},{20,24},{24,28},{1,5},{5,9},{9,... | collective-permute-start | bytes 152 | tf_op jit(solution)/shard_map/ppermute | solution.py:882
  19.5 9.8 %all-to-all-start = ((bf16[4,72,512]{2,1,0:T(8,128)(2,1)}), bf16[4,72,512]{2,1,0:T(8,128)(2,1)S(1)}, u32[]{:S(2)}, u32[]{:S(2)}) async-start(bf16[4,72,512]{2,1,0:T(8,128)(2,1)} %pad_maximum_fusion.3), calls=%async_computation | async-start | bytes 589824 | tf_op jit(solution)/shard_map/all_to_all | solution.py:847
  23.1 128.0 %copy-start.19 = (s32[2]{0:T(128)}, s32[2]{0:T(128)S(1)}, u32[]{:S(2)}) copy-start(s32[2]{0:T(128)S(1)} %pad_add_fusion.1.place_ref) | copy-start | bytes 28
  30.2 19.5 %collective-permute-start.4 = (bf16[4,80,1024]{2,1,0:T(8,128)(2,1)S(1)}, bf16[4,80,1024]{2,1,0:T(8,128)(2,1)S(1)}, u32[]{:S(2)}, u32[]{:S(2)}) collective-permute-start(bf16[4,80,1024]{2,1,0:T(8,128)(2,1)S(1)} %pad_maximum_fusion.exit_near_ref), channel_id=1, source_target_pairs={{0,4},{4,0},{8,12},{12,8},{16,20},{20,16},{24,28},{28,24},{1,5},{5... | collective-permute-start | bytes 1966088 | tf_op jit(solution)/shard_map/ppermute | solution.py:817
  31.5 7.0 %collective-permute-start.7 = (bf16[136,512]{1,0:T(8,128)(2,1)S(1)}, bf16[136,512]{1,0:T(8,128)(2,1)S(1)}, u32[]{:S(2)}, u32[]{:S(2)}) collective-permute-start(bf16[136,512]{1,0:T(8,128)(2,1)S(1)} %pad_maximum_fusion.6), channel_id=1, source_target_pairs={{0,24},{4,28},{8,16},{12,20},{16,8},{20,12},{24,0},{28,4},{1,25},{... | collective-permute-start | bytes 417800 | tf_op jit(solution)/shard_map/ppermute | solution.py:817
  33.9 15.8 %collective-permute-start.9 = (bf16[4,64,1024]{2,1,0:T(8,128)(2,1)S(1)}, bf16[4,64,1024]{2,1,0:T(8,128)(2,1)}, u32[]{:S(2)}, u32[]{:S(2)}) collective-permute-start(bf16[4,64,1024]{2,1,0:T(8,128)(2,1)S(1)} %collective-permute-done.slab2_ref), channel_id=1, source_target_pairs={{0,1},{1,0},{2,3},{3,2},{4,5},{5,4},{6,7},{7,6},{8,9},{9,8},{10,11... | collective-permute-start | bytes 1572872 | tf_op jit(solution)/shard_map/ppermute | solution.py:817
  34.0 15.8 %collective-permute-start.8 = (bf16[4,64,1024]{2,1,0:T(8,128)(2,1)S(1)}, bf16[4,64,1024]{2,1,0:T(8,128)(2,1)}, u32[]{:S(2)}, u32[]{:S(2)}) collective-permute-start(bf16[4,64,1024]{2,1,0:T(8,128)(2,1)S(1)} %copy-done), channel_id=1, source_target_pairs={{0,1},{1,0},{2,3},{3,2},{4,5},{5,4},{6,7},{7,6},{8,9},{9,8},{10,11... | collective-permute-start | bytes 1572872 | tf_op jit(solution)/shard_map/ppermute | solution.py:817
  34.5 12.2 %collective-permute-start.6 = (bf16[136,512]{1,0:T(8,128)(2,1)S(1)}, bf16[136,512]{1,0:T(8,128)(2,1)S(1)}, u32[]{:S(2)}, u32[]{:S(2)}) collective-permute-start(bf16[136,512]{1,0:T(8,128)(2,1)S(1)} %pad_maximum_fusion.6), channel_id=1, source_target_pairs={{0,16},{4,20},{8,24},{12,28},{16,0},{20,4},{24,8},{28,12},{1,17},{... | collective-permute-start | bytes 417800 | tf_op jit(solution)/shard_map/ppermute | solution.py:817
  38.5 11.2 %collective-permute-start.5 = (bf16[136,512]{1,0:T(8,128)(2,1)S(1)}, bf16[136,512]{1,0:T(8,128)(2,1)}, u32[]{:S(2)}, u32[]{:S(2)}) collective-permute-start(bf16[136,512]{1,0:T(8,128)(2,1)S(1)} %pad_maximum_fusion.6), channel_id=1, source_target_pairs={{0,8},{4,12},{8,0},{12,4},{16,24},{20,28},{24,16},{28,20},{1,9},{5... | collective-permute-start | bytes 417800 | tf_op jit(solution)/shard_map/ppermute | solution.py:817
  45.4 46.1 %copy-start.2 = (f32[4,4,64,4]{3,0,1,2:T(4,128)}, f32[4,4,64,4]{3,0,1,2:T(4,128)S(1)}, u32[]{:S(2)}) copy-start(f32[4,4,64,4]{3,0,1,2:T(4,128)S(1)} %copy.38) | copy-start | bytes 49156
  52.9 10.0 %collective-permute-start.20 = (bf16[128,512]{1,0:T(8,128)(2,1)}, bf16[128,512]{1,0:T(8,128)(2,1)}, u32[]{:S(2)}, u32[]{:S(2)}) collective-permute-start(bf16[128,512]{1,0:T(8,128)(2,1)} %bitcast.108), channel_id=1, source_target_pairs={{0,24},{4,28},{8,16},{12,20},{16,8},{20,12},{24,0},{28,4},{1,25},{... | collective-permute-start | bytes 393224 | tf_op jit(solution)/shard_map/ppermute | solution.py:817
  55.5 11.3 %collective-permute-start.19 = (bf16[128,512]{1,0:T(8,128)(2,1)}, bf16[128,512]{1,0:T(8,128)(2,1)}, u32[]{:S(2)}, u32[]{:S(2)}) collective-permute-start(bf16[128,512]{1,0:T(8,128)(2,1)} %bitcast.109), channel_id=1, source_target_pairs={{0,16},{4,20},{8,24},{12,28},{16,0},{20,4},{24,8},{28,12},{1,17},{... | collective-permute-start | bytes 393224 | tf_op jit(solution)/shard_map/ppermute | solution.py:817
  55.5 11.4 %collective-permute-start.18 = (bf16[128,512]{1,0:T(8,128)(2,1)}, bf16[128,512]{1,0:T(8,128)(2,1)}, u32[]{:S(2)}, u32[]{:S(2)}) collective-permute-start(bf16[128,512]{1,0:T(8,128)(2,1)} %bitcast.110), channel_id=1, source_target_pairs={{0,8},{4,12},{8,0},{12,4},{16,24},{20,28},{24,16},{28,20},{1,9},{5... | collective-permute-start | bytes 393224 | tf_op jit(solution)/shard_map/ppermute | solution.py:817
  57.3 14.7 %collective-permute-start.11 = (bf16[4,136,512]{2,1,0:T(8,128)(2,1)S(1)}, bf16[4,136,512]{2,1,0:T(8,128)(2,1)}, u32[]{:S(2)}, u32[]{:S(2)}) collective-permute-start(bf16[4,136,512]{2,1,0:T(8,128)(2,1)S(1)} %pad_maximum_fusion.1.near_ref), channel_id=1, source_target_pairs={{0,4},{4,0},{8,12},{12,8},{16,20},{20,16},{24,28},{28,24},{1,5},{5... | collective-permute-start | bytes 1671176 | tf_op jit(solution)/shard_map/ppermute | solution.py:817
  58.7 13.3 %collective-permute-start.16 = (bf16[4,64,1024]{2,1,0:T(8,128)(2,1)}, bf16[4,64,1024]{2,1,0:T(8,128)(2,1)}, u32[]{:S(2)}, u32[]{:S(2)}) collective-permute-start(bf16[4,64,1024]{2,1,0:T(8,128)(2,1)} %cotangent_ref), channel_id=1, source_target_pairs={{0,2},{1,3},{2,0},{3,1},{4,6},{5,7},{6,4},{7,5},{8,10},{9,11},{10,... | collective-permute-start | bytes 1572872 | tf_op jit(solution)/shard_map/ppermute | solution.py:817
  62.9 104.4 %copy-start.8 = (bf16[192,512]{1,0:T(8,128)(2,1)}, bf16[192,512]{1,0:T(8,128)(2,1)S(1)}, u32[]{:S(2)}) copy-start(bf16[192,512]{1,0:T(8,128)(2,1)S(1)} %copy.41.small_ref) | copy-start | bytes 589828
  62.9 9.9 %collective-permute-start.10 = (bf16[12,1024]{1,0:T(8,128)(2,1)S(1)}, bf16[12,1024]{1,0:T(8,128)(2,1)S(1)}, u32[]{:S(2)}, u32[]{:S(2)}) collective-permute-start(bf16[12,1024]{1,0:T(8,128)(2,1)S(1)} %reshape.120), channel_id=1, source_target_pairs={{0,4},{4,8},{8,12},{12,16},{16,20},{20,24},{24,28},{1,5},{5,9},{9,... | collective-permute-start | bytes 73736 | tf_op jit(solution)/shard_map/ppermute | solution.py:877
  66.8 18.1 %collective-permute-start.15 = (bf16[4,64,1024]{2,1,0:T(8,128)(2,1)}, bf16[4,64,1024]{2,1,0:T(8,128)(2,1)S(1)}, u32[]{:S(2)}, u32[]{:S(2)}) collective-permute-start(bf16[4,64,1024]{2,1,0:T(8,128)(2,1)} %cotangent_ref), channel_id=1, source_target_pairs={{0,1},{1,0},{2,3},{3,2},{4,5},{5,4},{6,7},{7,6},{8,9},{9,8},{10,11... | collective-permute-start | bytes 1572872 | tf_op jit(solution)/shard_map/ppermute | solution.py:817
  68.1 16.8 %collective-permute-start.21 = (bf16[4,128,512]{2,1,0:T(8,128)(2,1)S(1)}, bf16[4,128,512]{2,1,0:T(8,128)(2,1)S(1)}, u32[]{:S(2)}, u32[]{:S(2)}) collective-permute-start(bf16[4,128,512]{2,1,0:T(8,128)(2,1)S(1)} %pad_maximum_fusion.2.near_ref.gate_near_ref), channel_id=1, source_target_pairs={{0,4},{4,0},{8,12},{12,8},{16,20},{20,16},{24,28},{28,24},{1,5},{5... | collective-permute-start | bytes 1572872 | tf_op jit(solution)/shard_map/ppermute | solution.py:817
  72.0 12.9 %collective-permute-start.17 = (bf16[4,64,1024]{2,1,0:T(8,128)(2,1)}, bf16[4,64,1024]{2,1,0:T(8,128)(2,1)S(1)}, u32[]{:S(2)}, u32[]{:S(2)}) collective-permute-start(bf16[4,64,1024]{2,1,0:T(8,128)(2,1)} %collective-permute-done.16.slab2_ref), channel_id=1, source_target_pairs={{0,1},{1,0},{2,3},{3,2},{4,5},{5,4},{6,7},{7,6},{8,9},{9,8},{10,11... | collective-permute-start | bytes 1572872 | tf_op jit(solution)/shard_map/ppermute | solution.py:817
  82.5 50.2 %copy-start.17 = (f32[1024,512]{1,0:T(8,128)}, f32[1024,512]{1,0:T(8,128)S(1)}, u32[]{:S(2)}) copy-start(f32[1024,512]{1,0:T(8,128)S(1)} %get-tuple-element.125.filter_ref) | copy-start | bytes 6291460
  82.5 68.5 %copy-start.21 = (bf16[1024,1024]{1,0:T(8,128)(2,1)}, bf16[1024,1024]{1,0:T(8,128)(2,1)S(1)}, u32[]{:S(2)}) copy-start(bf16[1024,1024]{1,0:T(8,128)(2,1)S(1)} %get-tuple-element.129.normed_ref) | copy-start | bytes 6291460
  82.5 1.6 collective-permute-start.13
  84.2 7.3 %collective-permute-start.14 = (bf16[96,1024]{1,0:T(8,128)(2,1)S(1)}, bf16[96,1024]{1,0:T(8,128)(2,1)S(1)}, u32[]{:S(2)}, u32[]{:S(2)}) collective-permute-start(bf16[96,1024]{1,0:T(8,128)(2,1)S(1)} %add_convert_fusion.3.chosen_ref), channel_id=1, source_target_pairs={{0,2},{1,3},{2,0},{3,1},{4,6},{5,7},{6,4},{7,5},{8,10},{9,11},{10,... | collective-permute-start | bytes 589832 | tf_op jit(solution)/shard_map/ppermute | solution.py:817
  91.5 41.3 %copy-start.18 = (f32[1024,512]{1,0:T(8,128)}, f32[1024,512]{1,0:T(8,128)S(1)}, u32[]{:S(2)}) copy-start(f32[1024,512]{1,0:T(8,128)S(1)} %get-tuple-element.145) | copy-start | bytes 6291460
  111.2 39.8 %copy-start.31 = (f32[64,16,512]{2,1,0:T(8,128)}, f32[64,16,512]{2,1,0:T(8,128)S(1)}, u32[]{:S(2)}) copy-start(f32[64,16,512]{2,1,0:T(8,128)S(1)} %get-tuple-element.134.step_ref) | copy-start | bytes 6291460
  111.2 39.8 %copy-start.34 = (f32[64,16,128]{2,1,0:T(8,128)}, f32[64,16,128]{2,1,0:T(8,128)S(1)}, u32[]{:S(2)}) copy-start(f32[64,16,128]{2,1,0:T(8,128)S(1)} %get-tuple-element.133.gates_ref) | copy-start | bytes 1572868
  160.9 38.3 %collective-permute-start.23 = (bf16[2,4,64,1024]{3,2,1,0:T(8,128)(2,1)}, bf16[2,4,64,1024]{3,2,1,0:T(8,128)(2,1)}, u32[]{:S(2)}, u32[]{:S(2)}) collective-permute-start(bf16[2,4,64,1024]{3,2,1,0:T(8,128)(2,1)} %get-tuple-element.144), channel_id=1, source_target_pairs={{0,1},{1,0},{2,3},{3,2},{4,5},{5,4},{6,7},{7,6},{8,9},{9,8},{10,11... | collective-permute-start | bytes 3145736 | tf_op jit(solution)/shard_map/ppermute | solution.py:817
  161.0 38.3 %all-to-all-start.2 = ((bf16[8,64,1024]{2,1,0:T(8,128)(2,1)}), bf16[8,64,1024]{2,1,0:T(8,128)(2,1)}, u32[]{:S(2)}, u32[]{:S(2)}) async-start(bf16[8,64,1024]{2,1,0:T(8,128)(2,1)} %bitcast.40), calls=%async_computation.2 | async-start | bytes 2097152 | tf_op jit(solution)/shard_map/all_to_all | solution.py:1002
  165.3 33.9 %collective-permute-start.22 = (bf16[4,128,512]{2,1,0:T(8,128)(2,1)}, bf16[4,128,512]{2,1,0:T(8,128)(2,1)}, u32[]{:S(2)}, u32[]{:S(2)}) collective-permute-start(bf16[4,128,512]{2,1,0:T(8,128)(2,1)} %get-tuple-element.151), channel_id=1, source_target_pairs={{0,4},{4,0},{8,12},{12,8},{16,20},{20,16},{24,28},{28,24},{1,5},{5... | collective-permute-start | bytes 1572872 | tf_op jit(solution)/shard_map/ppermute | solution.py:817
  199.3 1.5 collective-permute-start.24
  200.9 7.0 %collective-permute-start.25 = (bf16[96,1024]{1,0:T(8,128)(2,1)S(1)}, bf16[96,1024]{1,0:T(8,128)(2,1)S(1)}, u32[]{:S(2)}, u32[]{:S(2)}) collective-permute-start(bf16[96,1024]{1,0:T(8,128)(2,1)S(1)} %add_convert_fusion.2.chosen_ref), channel_id=1, source_target_pairs={{0,2},{1,3},{2,0},{3,1},{4,6},{5,7},{6,4},{7,5},{8,10},{9,11},{10,... | collective-permute-start | bytes 589832 | tf_op jit(solution)/shard_map/ppermute | solution.py:817
  206.5 24.3 %collective-permute-start.27 = (bf16[4,64,1024]{2,1,0:T(8,128)(2,1)}, bf16[4,64,1024]{2,1,0:T(8,128)(2,1)}, u32[]{:S(2)}, u32[]{:S(2)}) collective-permute-start(bf16[4,64,1024]{2,1,0:T(8,128)(2,1)} %fusion.2), channel_id=1, source_target_pairs={{0,2},{1,3},{2,0},{3,1},{4,6},{5,7},{6,4},{7,5},{8,10},{9,11},{10,... | collective-permute-start | bytes 1572872 | tf_op jit(solution)/shard_map/ppermute | solution.py:817
  218.2 6.6 %collective-permute-start.26 = (f32[3,4,512]{2,1,0:T(4,128)}, f32[3,4,512]{2,1,0:T(4,128)S(1)}, u32[]{:S(2)}, u32[]{:S(2)}) collective-permute-start(f32[3,4,512]{2,1,0:T(4,128)} %get-tuple-element.167), channel_id=1, source_target_pairs={{4,0},{8,4},{12,8},{16,12},{20,16},{24,20},{28,24},{5,1},{9,5},{13... | collective-permute-start | bytes 73736 | tf_op jit(solution)/shard_map/ppermute | solution.py:1068
  219.7 19.2 %collective-permute-start.28 = (bf16[176,512]{1,0:T(8,128)(2,1)}, bf16[176,512]{1,0:T(8,128)(2,1)S(1)}, u32[]{:S(2)}, u32[]{:S(2)}) collective-permute-start(bf16[176,512]{1,0:T(8,128)(2,1)} %get-tuple-element.177), channel_id=1, source_target_pairs={{0,8},{4,12},{8,0},{12,4},{16,24},{20,28},{24,16},{28,20},{1,9},{5... | collective-permute-start | bytes 540680 | tf_op jit(solution)/shard_map/ppermute | solution.py:817
  222.1 16.9 %collective-permute-start.29 = (bf16[176,512]{1,0:T(8,128)(2,1)}, bf16[176,512]{1,0:T(8,128)(2,1)S(1)}, u32[]{:S(2)}, u32[]{:S(2)}) collective-permute-start(bf16[176,512]{1,0:T(8,128)(2,1)} %get-tuple-element.178), channel_id=1, source_target_pairs={{0,16},{4,20},{8,24},{12,28},{16,0},{20,4},{24,8},{28,12},{1,17},{... | collective-permute-start | bytes 540680 | tf_op jit(solution)/shard_map/ppermute | solution.py:817
  224.8 14.2 %collective-permute-start.30 = (bf16[176,512]{1,0:T(8,128)(2,1)}, bf16[176,512]{1,0:T(8,128)(2,1)S(1)}, u32[]{:S(2)}, u32[]{:S(2)}) collective-permute-start(bf16[176,512]{1,0:T(8,128)(2,1)} %get-tuple-element.179), channel_id=1, source_target_pairs={{0,24},{4,28},{8,16},{12,20},{16,8},{20,12},{24,0},{28,4},{1,25},{... | collective-permute-start | bytes 540680 | tf_op jit(solution)/shard_map/ppermute | solution.py:817
  239.0 6.1 %collective-permute-start.31 = (bf16[2,4,64,1024]{3,2,1,0:T(8,128)(2,1)}, bf16[2,4,64,1024]{3,2,1,0:T(8,128)(2,1)}, u32[]{:S(2)}, u32[]{:S(2)}) collective-permute-start(bf16[2,4,64,1024]{3,2,1,0:T(8,128)(2,1)} %get-tuple-element.180), channel_id=1, source_target_pairs={{0,1},{1,0},{2,3},{3,2},{4,5},{5,4},{6,7},{7,6},{8,9},{9,8},{10,11... | collective-permute-start | bytes 3145736 | tf_op jit(solution)/shard_map/ppermute | solution.py:817
  239.1 33.6 %all-to-all-start.3 = ((bf16[32,32,512]{2,1,0:T(8,128)(2,1)}), bf16[32,32,512]{2,1,0:T(8,128)(2,1)S(1)}, u32[]{:S(2)}, u32[]{:S(2)}) async-start(bf16[32,32,512]{2,1,0:T(8,128)(2,1)} %bitcast.46), calls=%async_computation.3 | async-start | bytes 2097152 | tf_op jit(solution)/shard_map/all_to_all | solution.py:1079
  248.9 6.6 %collective-permute-start.32 = (bf16[32,512]{1,0:T(8,128)(2,1)S(1)}, bf16[32,512]{1,0:T(8,128)(2,1)S(1)}, u32[]{:S(2)}, u32[]{:S(2)}) collective-permute-start(bf16[32,512]{1,0:T(8,128)(2,1)S(1)} %get-tuple-element.185), channel_id=1, source_target_pairs={{0,3},{1,2},{2,1},{3,0},{4,7},{5,6},{6,5},{7,4},{8,11},{9,10},{10,... | collective-permute-start | bytes 98312 | tf_op jit(solution)/shard_map/ppermute | solution.py:817
  250.5 24.4 %collective-permute-start.33 = (bf16[4,64,1024]{2,1,0:T(8,128)(2,1)}, bf16[4,64,1024]{2,1,0:T(8,128)(2,1)}, u32[]{:S(2)}, u32[]{:S(2)}) collective-permute-start(bf16[4,64,1024]{2,1,0:T(8,128)(2,1)} %fusion.3), channel_id=1, source_target_pairs={{0,2},{1,3},{2,0},{3,1},{4,6},{5,7},{6,4},{7,5},{8,10},{9,11},{10,... | collective-permute-start | bytes 1572872 | tf_op jit(solution)/shard_map/ppermute | solution.py:817
  250.9 14.4 %collective-permute-start.34 = (bf16[32,512]{1,0:T(8,128)(2,1)S(1)}, bf16[32,512]{1,0:T(8,128)(2,1)S(1)}, u32[]{:S(2)}, u32[]{:S(2)}) collective-permute-start(bf16[32,512]{1,0:T(8,128)(2,1)S(1)} %get-tuple-element.190), channel_id=1, source_target_pairs={{0,1},{1,0},{2,3},{3,2},{4,5},{5,4},{6,7},{7,6},{8,9},{9,8},{10,11... | collective-permute-start | bytes 98312 | tf_op jit(solution)/shard_map/ppermute | solution.py:817
  250.9 21.8 %collective-permute-start.35 = (bf16[32,512]{1,0:T(8,128)(2,1)S(1)}, bf16[32,512]{1,0:T(8,128)(2,1)S(1)}, u32[]{:S(2)}, u32[]{:S(2)}) collective-permute-start(bf16[32,512]{1,0:T(8,128)(2,1)S(1)} %get-tuple-element.191), channel_id=1, source_target_pairs={{0,2},{1,3},{2,0},{3,1},{4,6},{5,7},{6,4},{7,5},{8,10},{9,11},{10,... | collective-permute-start | bytes 98312 | tf_op jit(solution)/shard_map/ppermute | solution.py:817
  255.5 6.6 %collective-permute-start.36 = (f32[192,128]{1,0:T(8,128)S(1)}, f32[192,128]{1,0:T(8,128)S(1)}, u32[]{:S(2)}, u32[]{:S(2)}) collective-permute-start(f32[192,128]{1,0:T(8,128)S(1)} %get-tuple-element.196), channel_id=1, source_target_pairs={{0,4},{4,0},{8,12},{12,8},{16,20},{20,16},{24,28},{28,24},{1,5},{5... | collective-permute-start | bytes 294920 | tf_op jit(solution)/shard_map/ppermute | solution.py:817
  (42 other events, 270.4 us)
